TPU v7x, 32 devices: a whole 2x2x4 slice. The times are simulated.
32 devices in a mesh: ep: 4 (over z), split: 2 (over x), tp: 4 (over y, core).
Axes of the slice: x: 2, y: 2, z: 4, core: 2. Of those that a mesh axis runs over, the one named last changes fastest.
Arguments:
- feats: bfloat16 [2, 16, 1024, 100], P('split', 'ep', 'tp'), may hold values from -6 to 6
- counts: int32 [16, 2], P('ep'), may hold values from 256 to 1024, as said below
- feat_mask: int32 [16, 100], P('ep'), may hold values from 0 to 1, as said below
- cotangent: bfloat16 [2, 16, 1024, 512], P('split', 'ep', 'tp'), may hold values from -6 to 6
- block_weights: float32 [512, 4, 1024], P(('ep', 'split'), 'tp'), may hold values from -4 to 4
- block_moments: float32 [2, 512, 4, 1024], P(None, ('ep', 'split'), 'tp'), may hold values from -1 to 1, as said below
- head_biases: float32 [512, 4], P(('ep', 'split'), 'tp'), may hold values from -1.75 to 1.75
- bias_moments: float32 [2, 512, 4], P(None, ('ep', 'split'), 'tp'), may hold values from -1 to 1, as said below
- encoder: float32 [512, 100], P(('ep', 'split', 'tp')), may hold values from -0.625 to 0.625
- encoder_moments: float32 [2, 512, 100], P(None, ('ep', 'split', 'tp')), may hold values from -1 to 1, as said below
- shared_vectors: float32 [512, 7], P(('ep', 'split', 'tp')), may hold values from -1 to 3
- vector_moments: float32 [2, 512, 7], P(None, ('ep', 'split', 'tp')), may hold values from -1 to 1, as said below
- prompt: float32 [512, 1000], P(('ep', 'split', 'tp')), may hold values from -6 to 6
- prompt_moments: float32 [2, 512, 1000], P(None, ('ep', 'split', 'tp')), may hold values from -1 to 1, as said below
Outputs:
- output: bfloat16 [2, 16, 1024, 512], P('split', 'ep', 'tp')
- input_grad: float32 [2, 16, 1024, 100], P('split', 'ep', 'tp')
- grad_norm: float32 [], replicated
- block_new: float32 [512, 4, 1024], P(('ep', 'split'), 'tp')
- block_first_new: float32 [512, 4, 1024], P(('ep', 'split'), 'tp')
- block_second_new: float32 [512, 4, 1024], P(('ep', 'split'), 'tp')
- block_copy: bfloat16 [512, 4, 1024], P(('ep', 'split'), 'tp')
- biases_new: float32 [512, 4], P(('ep', 'split'), 'tp')
- bias_first_new: float32 [512, 4], P(('ep', 'split'), 'tp')
- bias_second_new: float32 [512, 4], P(('ep', 'split'), 'tp')
- biases_copy: bfloat16 [512, 4], P(('ep', 'split'), 'tp')
- encoder_new: float32 [512, 100], P(('ep', 'split', 'tp'))
- encoder_first_new: float32 [512, 100], P(('ep', 'split', 'tp'))
- encoder_second_new: float32 [512, 100], P(('ep', 'split', 'tp'))
- encoder_copy: bfloat16 [512, 100], P(('ep', 'split', 'tp'))
- vectors_new: float32 [512, 7], P(('ep', 'split', 'tp'))
- vector_first_new: float32 [512, 7], P(('ep', 'split', 'tp'))
- vector_second_new: float32 [512, 7], P(('ep', 'split', 'tp'))
- vectors_copy: bfloat16 [512, 7], P(('ep', 'split', 'tp'))
- prompt_new: float32 [512, 1000], P(('ep', 'split', 'tp'))
- prompt_first_new: float32 [512, 1000], P(('ep', 'split', 'tp'))
- prompt_second_new: float32 [512, 1000], P(('ep', 'split', 'tp'))
- prompt_copy: bfloat16 [512, 1000], P(('ep', 'split', 'tp'))
Inputs may be any that keep to these rules, and one draw needn't show every extreme that they name: Column 0 counts an episode's filled context slots and column 1 its filled test slots; filled slots come first. In every draw one episode has every slot filled and another has 256 in both columns. `feat_mask`: an episode uses between 25 and 100 features; one episode uses all of them. `block_moments`: second moments are positive. `bias_moments`: second moments are positive. `encoder_moments`: second moments are positive. `vector_moments`: second moments are positive. `prompt_moments`: second moments are positive.
All inputs are finite; a program needn't handle non-finite values.
Results may differ from a plain program's by a relative error of at most 0.02.
The roundings to bfloat16 on the way count: a program that leaves them out, or rounds other values in their place, can miss the bound.
Values may be sent and summed in bfloat16 or wider, within the bound.
No kernel may reach another device: no remote copies, remote signals or barrier semaphores. Data moves between devices by JAX's collectives and lax.ppermute only.
A program may use at most 128 MiB of HBM per device.

v0:
```python
import jax
import jax.numpy as jnp
from jax import lax
from jax.sharding import PartitionSpec as P

HEADS = 4
HEAD = 128
FF = 1024
FEAT = 100
PROMPT = 1000
SLOTS = 1024
ADAM_STEP = 10


ln_eps = 1e-05
neg_big = -1e30
clip_norm = 1.0
beta_one = 0.9
beta_two = 0.999
adam_eps = 1e-08
rate_matrix = 0.15
rate_vector = 0.5
weight_decay = 0.01
highest = lax.Precision.HIGHEST


def broadcast(array, axis, root):
    mine = lax.axis_index(axis) == root
    return lax.psum(jnp.where(mine, array, jnp.zeros_like(array)), axis)


def passed_along(value, axis, steps):
    count = lax.axis_size(axis)
    first, last = (max(0, -steps), min(count, count - steps))
    return lax.ppermute(value, axis, [(source, source + steps) for source in range(first, last)])


def norm_rows(residual, norm_gain, norm_shift):
    centre = jnp.mean(residual, axis=-1, keepdims=True)
    centred = residual - centre
    spread = jnp.mean(centred * centred, axis=-1, keepdims=True)
    inverse = lax.rsqrt(spread + ln_eps)
    normed = centred * inverse
    return (normed * norm_gain + norm_shift, normed, inverse)


def norm_back(grad_out, normed, inverse, norm_gain):
    scaled = grad_out * norm_gain
    mean_plain = jnp.mean(scaled, axis=-1, keepdims=True)
    mean_mixed = jnp.mean(scaled * normed, axis=-1, keepdims=True)
    grad_in = inverse * (scaled - mean_plain - normed * mean_mixed)
    return (grad_in, jnp.sum(grad_out * normed, axis=(0, 1)), jnp.sum(grad_out, axis=(0, 1)))


def row_gather(rows_low):
    return lax.all_gather(rows_low, "tp", axis=1, tiled=True)


def row_reduce(partial_sum):
    return lax.psum_scatter(
        partial_sum.astype(jnp.bfloat16), "tp", scatter_dimension=1, tiled=True
    ).astype(jnp.float32)


def send_context(kv_values):
    return broadcast(kv_values, "split", 0)


def fetch_test(kv_terms):
    return passed_along(kv_terms.astype(jnp.bfloat16), "split", -1).astype(kv_terms.dtype)


def adam_update(weight, moments, gradient, factor, step_rate, decay_rate):
    clipped = gradient * factor
    first_moment = beta_one * moments[0] + (1.0 - beta_one) * clipped
    second_moment = beta_two * moments[1] + (1.0 - beta_two) * clipped * clipped
    first_hat = first_moment / (1.0 - beta_one**ADAM_STEP)
    second_hat = second_moment / (1.0 - beta_two**ADAM_STEP)
    updated = weight - step_rate * (
        first_hat / (jnp.sqrt(second_hat) + adam_eps) + decay_rate * weight
    )
    return (updated, first_moment, second_moment, updated.astype(jnp.bfloat16))


def shards(
    feats,
    counts,
    feat_mask,
    cotangent,
    block_weights,
    block_moments,
    head_biases,
    bias_moments,
    encoder,
    encoder_moments,
    shared_vectors,
    vector_moments,
    prompt,
    prompt_moments,
):
    part_block, part_bias = (
        lax.all_gather(block_weights.astype(jnp.bfloat16), ("ep", "split"), axis=0, tiled=True),
        lax.all_gather(head_biases.astype(jnp.bfloat16), ("ep", "split"), axis=0, tiled=True),
    )
    encoder_low, vector_low, prompt_low = (
        lax.all_gather(encoder.astype(jnp.bfloat16), ("ep", "split", "tp"), axis=0, tiled=True),
        lax.all_gather(
            shared_vectors.astype(jnp.bfloat16), ("ep", "split", "tp"), axis=0, tiled=True
        ),
        lax.all_gather(prompt.astype(jnp.bfloat16), ("ep", "split", "tp"), axis=0, tiled=True),
    )
    weights_low, biases_low = (part_block, part_bias)
    is_context = lax.axis_index("split") == 0
    episode_count = feats.shape[1]
    counts_here, mask_here = (counts, feat_mask)
    group_ids = jnp.reshape(lax.axis_index("split"), (1,))
    shard_rows = feats.shape[2]
    feats_flat = feats.reshape((episode_count,) + feats.shape[2:])
    cotan_flat = cotangent.reshape((episode_count,) + cotangent.shape[2:])
    vectors = vector_low.astype(jnp.float32)
    local_heads = weights_low.shape[1]
    model_width = weights_low.shape[0]
    hidden_units = FF // HEADS
    score_scale = HEAD ** (-0.5)
    w_query = weights_low[:, :, 0:HEAD]
    w_keyval = weights_low[:, :, HEAD : 3 * HEAD]
    w_output = weights_low[:, :, 3 * HEAD : 4 * HEAD]
    w_hidden = weights_low[:, :, 4 * HEAD : 4 * HEAD + hidden_units]
    w_return = weights_low[:, :, 4 * HEAD + hidden_units :]
    bias_rows = biases_low.astype(jnp.float32).T
    bias_query = bias_rows[:, 0:HEAD]
    bias_value = bias_rows[:, HEAD : 2 * HEAD]
    bias_hidden = bias_rows[:, 2 * HEAD :]
    slot_ids = lax.axis_index("tp") * shard_rows + jnp.arange(shard_rows, dtype=jnp.int32)
    own_count = jnp.where(
        group_ids[:, None] == 0, counts_here[None, :, 0], counts_here[None, :, 1]
    ).reshape(episode_count)
    row_live = (slot_ids[None, :] < own_count[:, None]).astype(jnp.float32)
    key_live = jnp.concatenate(
        [
            jnp.ones((episode_count, PROMPT), dtype=bool),
            jnp.arange(SLOTS, dtype=jnp.int32)[None, :] < counts_here[:, 0:1],
        ],
        axis=1,
    )
    mask_rows = mask_here.astype(jnp.float32)
    masked = feats_flat * mask_here.astype(jnp.bfloat16)[:, None, :]
    feat_ratio = FEAT / jnp.sum(mask_rows, axis=1)
    prompt_kv = jnp.einsum("dp,dhc->phc", prompt_low, w_keyval, preferred_element_type=jnp.float32)
    prompt_keys = prompt_kv[..., 0:HEAD].astype(jnp.bfloat16)
    prompt_values = (prompt_kv[..., HEAD:] + bias_value).astype(jnp.bfloat16)

    def attend_one(episode_item):
        queries, context_kv, live_keys = episode_item
        key_rows = jnp.concatenate([prompt_keys, context_kv[..., 0:HEAD]], axis=0)
        value_rows = jnp.concatenate([prompt_values, context_kv[..., HEAD:]], axis=0)
        scores = (
            jnp.einsum("shc,khc->hsk", queries, key_rows, preferred_element_type=jnp.float32)
            * score_scale
        )
        scores = jnp.where(live_keys[None, None, :], scores, neg_big)
        top_score = jnp.max(scores, axis=-1, keepdims=True)
        raised = jnp.exp(scores - top_score)
        exp_total = jnp.sum(raised, axis=-1, keepdims=True)
        attn_probs = (raised / exp_total).astype(jnp.bfloat16)
        attended = jnp.einsum(
            "hsk,khc->shc", attn_probs, value_rows, preferred_element_type=jnp.float32
        ).astype(jnp.bfloat16)
        return (attended, (top_score + jnp.log(exp_total))[..., 0])

    def attend_back(episode_item):
        queries, context_kv, live_keys, log_total, grad_attended = episode_item
        key_rows = jnp.concatenate([prompt_keys, context_kv[..., 0:HEAD]], axis=0)
        value_rows = jnp.concatenate([prompt_values, context_kv[..., HEAD:]], axis=0)
        scores = (
            jnp.einsum("shc,khc->hsk", queries, key_rows, preferred_element_type=jnp.float32)
            * score_scale
        )
        scores = jnp.where(live_keys[None, None, :], scores, neg_big)
        attn_probs = jnp.exp(scores - log_total[..., None])
        grad_probs = jnp.einsum(
            "shc,khc->hsk", grad_attended, value_rows, preferred_element_type=jnp.float32
        )
        row_delta = jnp.sum(attn_probs * grad_probs, axis=-1, keepdims=True)
        grad_scores = (attn_probs * (grad_probs - row_delta)).astype(jnp.bfloat16)
        grad_queries = (
            jnp.einsum("hsk,khc->shc", grad_scores, key_rows, preferred_element_type=jnp.float32)
            * score_scale
        ).astype(jnp.bfloat16)
        grad_keys = (
            jnp.einsum("hsk,shc->khc", grad_scores, queries, preferred_element_type=jnp.float32)
            * score_scale
        )
        grad_values = jnp.einsum(
            "hsk,shc->khc",
            attn_probs.astype(jnp.bfloat16),
            grad_attended,
            preferred_element_type=jnp.float32,
        )
        grad_kv = jnp.concatenate([grad_keys, grad_values], axis=-1)
        return (grad_queries, grad_kv[PROMPT:], grad_kv[0:PROMPT])

    def project_kv(rows):
        kv_both = jnp.einsum("esd,dhc->eshc", rows, w_keyval, preferred_element_type=jnp.float32)
        return jnp.concatenate(
            [kv_both[..., 0:HEAD], kv_both[..., HEAD:] + bias_value], axis=-1
        ).astype(jnp.bfloat16)

    def forward(masked_in):
        embedded = (
            feat_ratio[:, None, None]
            * jnp.einsum("erf,df->erd", masked_in, encoder_low, preferred_element_type=jnp.float32)
            + vectors[:, 6]
        )
        rows_low = row_gather(embedded.astype(jnp.bfloat16))
        queries = (
            jnp.einsum("esd,dhc->eshc", rows_low, w_query, preferred_element_type=jnp.float32)
            + bias_query
        ).astype(jnp.bfloat16)

        def empty_kv():
            return jnp.zeros(queries.shape[:-1] + (2 * HEAD,), jnp.bfloat16)

        own_kv = lax.cond(is_context, lambda: project_kv(rows_low), empty_kv)
        context_kv = send_context(own_kv)
        attended, log_total = lax.map(attend_one, (queries, context_kv, key_live))
        attn_out = (
            row_reduce(
                jnp.einsum("eshc,dhc->esd", attended, w_output, preferred_element_type=jnp.float32)
            )
            + vectors[:, 4]
        )
        normed_first, normed_one, inverse_one = norm_rows(
            embedded + attn_out, vectors[:, 0], vectors[:, 1]
        )
        first_low = row_gather(normed_first.astype(jnp.bfloat16))
        hidden_pre = (
            jnp.einsum("esd,dhf->eshf", first_low, w_hidden, preferred_element_type=jnp.float32)
            + bias_hidden
        )
        hidden_act = jax.nn.gelu(hidden_pre, approximate=False).astype(jnp.bfloat16)
        mlp_out = (
            row_reduce(
                jnp.einsum(
                    "eshf,dhf->esd", hidden_act, w_return, preferred_element_type=jnp.float32
                )
            )
            + vectors[:, 5]
        )
        normed_final, normed_two, inverse_two = norm_rows(
            normed_first + mlp_out, vectors[:, 2], vectors[:, 3]
        )
        output = normed_final * row_live[:, :, None]
        kept_state = (
            embedded,
            rows_low,
            queries,
            context_kv,
            attended,
            log_total,
            normed_one,
            inverse_one,
            first_low,
            hidden_pre,
            hidden_act,
            normed_two,
            inverse_two,
        )
        return (output, kept_state)

    output, kept_state = forward(masked)
    masked_again, unused = lax.optimization_barrier((masked, output))
    unused, kept_state = forward(masked_again)
    (
        embedded,
        rows_low,
        queries,
        context_kv,
        attended,
        log_total,
        normed_one,
        inverse_one,
        first_low,
        hidden_pre,
        hidden_act,
        normed_two,
        inverse_two,
    ) = kept_state
    grad_final = cotan_flat.astype(jnp.float32) * row_live[:, :, None]
    grad_two, gain_two, shift_two = norm_back(grad_final, normed_two, inverse_two, vectors[:, 2])
    grad_mlp_low = grad_two.astype(jnp.bfloat16)
    bias_two = jnp.sum(grad_mlp_low.astype(jnp.float32), axis=(0, 1))
    grad_mlp = row_gather(grad_mlp_low)
    grad_return = jnp.einsum(
        "esd,eshf->dhf", grad_mlp, hidden_act, preferred_element_type=jnp.float32
    )
    grad_act = jnp.einsum("esd,dhf->eshf", grad_mlp, w_return, preferred_element_type=jnp.float32)
    unused, gelu_pull = jax.vjp(
        lambda pre_value: jax.nn.gelu(pre_value, approximate=False), hidden_pre
    )
    grad_pre = gelu_pull(grad_act)[0].astype(jnp.bfloat16)
    grad_bias_hidden = jnp.sum(grad_pre.astype(jnp.float32), axis=(0, 1))
    grad_hidden = jnp.einsum(
        "esd,eshf->dhf", first_low, grad_pre, preferred_element_type=jnp.float32
    )
    grad_first = grad_two + row_reduce(
        jnp.einsum("eshf,dhf->esd", grad_pre, w_hidden, preferred_element_type=jnp.float32)
    )
    grad_one, gain_one, shift_one = norm_back(grad_first, normed_one, inverse_one, vectors[:, 0])
    grad_attn_low = grad_one.astype(jnp.bfloat16)
    bias_out = jnp.sum(grad_attn_low.astype(jnp.float32), axis=(0, 1))
    grad_attn = row_gather(grad_attn_low)
    grad_output = jnp.einsum(
        "esd,eshc->dhc", grad_attn, attended, preferred_element_type=jnp.float32
    )
    grad_attended = jnp.einsum(
        "esd,dhc->eshc", grad_attn, w_output, preferred_element_type=jnp.float32
    ).astype(jnp.bfloat16)
    grad_queries, grad_context, grad_prompt_all = lax.map(
        attend_back, (queries, context_kv, key_live, log_total, grad_attended)
    )
    grad_prompt_kv = jnp.sum(grad_prompt_all, axis=0)

    def kv_terms(rows_ctx, kv_total):
        kv_low = kv_total.astype(jnp.bfloat16)
        kv_project = jnp.einsum(
            "esd,eshc->dhc", rows_ctx, kv_low, preferred_element_type=jnp.float32
        )
        kv_back = jnp.einsum("eshc,dhc->esd", kv_low, w_keyval, preferred_element_type=jnp.float32)
        return (kv_project, kv_back, jnp.sum(kv_low[..., HEAD:].astype(jnp.float32), axis=(0, 1)))

    query_grad = jnp.einsum(
        "esd,eshc->dhc", rows_low, grad_queries, preferred_element_type=jnp.float32
    )
    back_rows = jnp.einsum(
        "eshc,dhc->esd", grad_queries, w_query, preferred_element_type=jnp.float32
    )
    grad_context_total = grad_context + fetch_test(grad_context)

    def no_terms():
        return (
            jnp.zeros((model_width, local_heads, 2 * HEAD), jnp.float32),
            jnp.zeros(back_rows.shape, jnp.float32),
            jnp.zeros((local_heads, HEAD), jnp.float32),
        )

    kv_project, kv_back, value_bias_rows = lax.cond(
        is_context, lambda: kv_terms(rows_low, grad_context_total), no_terms
    )
    back_rows = back_rows + kv_back
    grad_project = jnp.concatenate([query_grad, kv_project], axis=-1)
    prompt_float = prompt_low.astype(jnp.float32)
    grad_prompt_proj = jnp.einsum("dp,phc->dhc", prompt_float, grad_prompt_kv, precision=highest)
    grad_project = grad_project + jnp.concatenate(
        [jnp.zeros_like(grad_prompt_proj[..., 0:HEAD]), grad_prompt_proj], axis=-1
    )
    grad_prompt = jnp.einsum(
        "phc,dhc->dp", grad_prompt_kv, w_keyval.astype(jnp.float32), precision=highest
    )
    grad_bias_query = jnp.sum(grad_queries.astype(jnp.float32), axis=(0, 1))
    grad_bias_value = value_bias_rows + jnp.sum(grad_prompt_kv[..., HEAD:], axis=0)
    grad_input = grad_one + row_reduce(back_rows)
    grad_input_low = grad_input.astype(jnp.bfloat16)
    grad_encoder = jnp.einsum(
        "e,edf->df",
        feat_ratio,
        jnp.einsum("erd,erf->edf", grad_input_low, masked, preferred_element_type=jnp.float32),
        precision=highest,
    )
    grad_embed_bias = jnp.sum(grad_input_low.astype(jnp.float32), axis=(0, 1))
    input_grad = (
        feat_ratio[:, None, None]
        * jnp.einsum("erd,df->erf", grad_input_low, encoder_low, preferred_element_type=jnp.float32)
        * mask_rows[:, None, :]
    )
    grad_block = jnp.concatenate([grad_project, grad_output, grad_hidden, grad_return], axis=-1)
    grad_bias = jnp.concatenate([grad_bias_query, grad_bias_value, grad_bias_hidden], axis=-1).T
    grad_vectors = jnp.stack(
        [gain_one, shift_one, gain_two, shift_two, bias_out, bias_two, grad_embed_bias], axis=1
    )
    summed_block, summed_bias = (
        lax.psum_scatter(grad_block, ("ep", "split"), scatter_dimension=0, tiled=True),
        lax.psum_scatter(grad_bias, ("ep", "split"), scatter_dimension=0, tiled=True),
    )
    summed_encoder, summed_vectors, summed_prompt = (
        lax.psum_scatter(grad_encoder, ("ep", "split", "tp"), scatter_dimension=0, tiled=True),
        lax.psum_scatter(grad_vectors, ("ep", "split", "tp"), scatter_dimension=0, tiled=True),
        lax.psum_scatter(grad_prompt, ("ep", "split", "tp"), scatter_dimension=0, tiled=True),
    )
    local_squares = (
        jnp.sum(summed_block * summed_block)
        + jnp.sum(summed_bias * summed_bias)
        + jnp.sum(summed_encoder * summed_encoder)
        + jnp.sum(summed_vectors * summed_vectors)
        + jnp.sum(summed_prompt * summed_prompt)
    )
    grad_norm = jnp.sqrt(lax.psum(local_squares, ("ep", "split", "tp")))
    factor = jnp.minimum(1.0, clip_norm / (grad_norm + 1e-06))
    block_new, block_first_new, block_second_new, block_copy = adam_update(
        block_weights, block_moments, summed_block, factor, rate_matrix, weight_decay
    )
    biases_new, bias_first_new, bias_second_new, biases_copy = adam_update(
        head_biases, bias_moments, summed_bias, factor, rate_vector, 0.0
    )
    encoder_new, encoder_first_new, encoder_second_new, encoder_copy = adam_update(
        encoder, encoder_moments, summed_encoder, factor, rate_matrix, weight_decay
    )
    vectors_new, vector_first_new, vector_second_new, vectors_copy = adam_update(
        shared_vectors, vector_moments, summed_vectors, factor, rate_vector, 0.0
    )
    prompt_new, prompt_first_new, prompt_second_new, prompt_copy = adam_update(
        prompt, prompt_moments, summed_prompt, factor, rate_vector, weight_decay
    )
    output_final = output.astype(jnp.bfloat16)[None]
    input_final = input_grad[None]
    return (
        output_final,
        input_final,
        grad_norm,
        block_new,
        block_first_new,
        block_second_new,
        block_copy,
        biases_new,
        bias_first_new,
        bias_second_new,
        biases_copy,
        encoder_new,
        encoder_first_new,
        encoder_second_new,
        encoder_copy,
        vectors_new,
        vector_first_new,
        vector_second_new,
        vectors_copy,
        prompt_new,
        prompt_first_new,
        prompt_second_new,
        prompt_copy,
    )


def solution(mesh):
    placed = (
        P("split", "ep", "tp", None),
        P("ep", None),
        P("ep", None),
        P("split", "ep", "tp", None),
        P(("ep", "split"), "tp", None),
        P(None, ("ep", "split"), "tp", None),
        P(("ep", "split"), "tp"),
        P(None, ("ep", "split"), "tp"),
        P(("ep", "split", "tp"), None),
        P(None, ("ep", "split", "tp"), None),
        P(("ep", "split", "tp"), None),
        P(None, ("ep", "split", "tp"), None),
        P(("ep", "split", "tp"), None),
        P(None, ("ep", "split", "tp"), None),
    )
    return jax.shard_map(
        shards,
        mesh=mesh,
        in_specs=placed,
        out_specs=(
            P("split", "ep", "tp", None),
            P("split", "ep", "tp", None),
            P(),
            P(("ep", "split"), "tp", None),
            P(("ep", "split"), "tp", None),
            P(("ep", "split"), "tp", None),
            P(("ep", "split"), "tp", None),
            P(("ep", "split"), "tp"),
            P(("ep", "split"), "tp"),
            P(("ep", "split"), "tp"),
            P(("ep", "split"), "tp"),
            P(("ep", "split", "tp"), None),
            P(("ep", "split", "tp"), None),
            P(("ep", "split", "tp"), None),
            P(("ep", "split", "tp"), None),
            P(("ep", "split", "tp"), None),
            P(("ep", "split", "tp"), None),
            P(("ep", "split", "tp"), None),
            P(("ep", "split", "tp"), None),
            P(("ep", "split", "tp"), None),
            P(("ep", "split", "tp"), None),
            P(("ep", "split", "tp"), None),
            P(("ep", "split", "tp"), None),
        ),
        check_vma=False,
    )
```

profile of v0, /device:TPU:0, one launch (start us, length us, event | category | flops | bytes accessed | tf_op | source)
XLA Modules:
  0.0 1625.8 jit_solution(7999394525712691661)
XLA Ops:
  11.9 43.5 %all-gather = bf16[32,16,7]{1,2,0:T(8,128)(2,1)S(1)} all-gather(bf16[1,16,7]{1,2,0:T(8,128)(2,1)S(1)} %convert_bitcast_fusion.1), channel_id=1, replica_groups=mesh['ep'=4,'split'=2,'tp'=4] {'ep','split','tp'}, dimensions={0}, use_global_device_ids=true | all-gather | bytes 7392 | tf_op jit(solution)/shard_map/all_gather | solution.py:107
  55.7 37.0 %all_gather.33 = bf16[512,100]{1,0:T(8,128)(2,1)S(1)} all-gather(bf16[16,100]{1,0:T(8,128)(2,1)S(1)} %convert_element_type.245), channel_id=1, replica_groups=mesh['ep'=4,'split'=2,'tp'=4] {'ep','split','tp'}, dimensions={0}, use_global_device_ids=true | all-gather | bytes 105600 | tf_op jit(solution)/shard_map/all_gather | solution.py:106
  139.7 40.8 %all_gather.38 = bf16[512,1000]{1,0:T(8,128)(2,1)S(1)} all-gather(bf16[16,1000]{1,0:T(8,128)(2,1)S(1)} %convert_element_type.252), channel_id=1, replica_groups=mesh['ep'=4,'split'=2,'tp'=4] {'ep','split','tp'}, dimensions={0}, use_global_device_ids=true | all-gather | bytes 1056000 | tf_op jit(solution)/shard_map/all_gather | solution.py:110
  206.6 32.7 %while.36 = (s32[]{:T(128)}, bf16[4,1024,1,128]{1,3,2,0:T(8,128)(2,1)S(1)}, bf16[4,1024,1,256]{3,1,2,0:T(8,128)(2,1)}, bf16[1000,1,128]{2,0,1:T(8,128)(2,1)S(1)}...) while((s32[]{:T(128)}, ...), condition=%wide.region_7.8_spmd, body=%wide.region_4.7_spmd.sunk | while | flops 1088231424 | bytes 28559372 | solution.py:226
  243.7 44.6 %reduce-scatter.17.cloned.1.call-done = bf16[4,256,512]{2,1,0:T(8,128)(2,1)} async-done(((bf16[4,1024,512]{2,1,0:T(8,128)(2,1)}), bf16[4,256,512]{2,1,0:T(8,128)(2,1)}) %reduce-scatter.17.cloned.1.call-update) | async-done | bytes 1048592 | tf_op jit(solution)/shard_map/reduce_scatter | solution.py:60
  292.9 34.3 %all-gather.13.cloned.1.call-done = bf16[4,1024,512]{2,1,0:T(8,128)(2,1)} async-done(((bf16[4,256,512]{2,1,0:T(8,128)(2,1)}), bf16[4,1024,512]{2,1,0:T(8,128)(2,1)}) %all-gather.13.cloned.1.call-update) | async-done | bytes 4194320 | tf_op jit(solution)/shard_map/all_gather | solution.py:56
  344.1 44.6 %reduce-scatter.19.cloned.1.call-done = bf16[4,256,512]{2,1,0:T(8,128)(2,1)} async-done(((bf16[4,1024,512]{2,1,0:T(8,128)(2,1)}), bf16[4,256,512]{2,1,0:T(8,128)(2,1)}) %reduce-scatter.19.cloned.1.call-update) | async-done | bytes 1048592 | tf_op jit(solution)/shard_map/reduce_scatter | solution.py:60
  396.8 34.6 %all-gather.15.cloned.1.call-done = bf16[4,1024,512]{2,1,0:T(8,128)(2,1)} async-done(((bf16[4,256,512]{2,1,0:T(8,128)(2,1)}), bf16[4,1024,512]{2,1,0:T(8,128)(2,1)}) %all-gather.15.cloned.1.call-update) | async-done | bytes 4194320 | tf_op jit(solution)/shard_map/all_gather | solution.py:56
  445.3 58.1 %all-reduce.10.cloned.1.call-done = bf16[4,1024,1,256]{3,1,2,0:T(8,128)(2,1)} async-done(((bf16[4,1024,1,256]{3,1,2,0:T(8,128)(2,1)}), bf16[4,1024,1,256]{3,1,2,0:T(8,128)(2,1)}) %all-reduce.10.cloned.1.call-update) | async-done | bytes 2097168 | tf_op jit(solution)/shard_map/psum | solution.py:29
  503.5 29.1 %while.37 = (s32[]{:T(128)}, bf16[4,1024,1,128]{1,3,2,0:T(8,128)(2,1)S(1)}, f32[4,1,1024]{2,1,0:T(1,128)S(1)}, bf16[4,1024,1,256]{3,1,2,0:T(8,128)(2,1)}, bf16[1...) while((s32[]{:T(128)}, ...), condition=%wide.region_20.21_spmd, body=%wide.region_17.20_spmd.sunk | while | flops 1088232448 | bytes 28579888 | solution.py:226
  537.1 44.6 %reduce-scatter.21.cloned.1.call-done = bf16[4,256,512]{2,1,0:T(8,128)(2,1)} async-done(((bf16[4,1024,512]{2,1,0:T(8,128)(2,1)}), bf16[4,256,512]{2,1,0:T(8,128)(2,1)}) %reduce-scatter.21.cloned.1.call-update) | async-done | bytes 1048592 | tf_op jit(solution)/shard_map/reduce_scatter | solution.py:60
  586.2 34.4 %all-gather.17.cloned.1.call-done = bf16[4,1024,512]{2,1,0:T(8,128)(2,1)} async-done(((bf16[4,256,512]{2,1,0:T(8,128)(2,1)}), bf16[4,1024,512]{2,1,0:T(8,128)(2,1)}) %all-gather.17.cloned.1.call-update) | async-done | bytes 4194320 | tf_op jit(solution)/shard_map/all_gather | solution.py:56
  641.2 44.6 %reduce-scatter.23.cloned.1.call-done = bf16[4,256,512]{2,1,0:T(8,128)(2,1)} async-done(((bf16[4,1024,512]{2,1,0:T(8,128)(2,1)}), bf16[4,256,512]{2,1,0:T(8,128)(2,1)}) %reduce-scatter.23.cloned.1.call-update) | async-done | bytes 1048592 | tf_op jit(solution)/shard_map/reduce_scatter | solution.py:60
  692.5 34.6 %all-gather.19.cloned.1.call-done = bf16[4,1024,512]{2,1,0:T(8,128)(2,1)} async-done(((bf16[4,256,512]{2,1,0:T(8,128)(2,1)}), bf16[4,1024,512]{2,1,0:T(8,128)(2,1)}) %all-gather.19.cloned.1.call-update) | async-done | bytes 4194320 | tf_op jit(solution)/shard_map/all_gather | solution.py:56
  739.7 44.6 %reduce-scatter.25.cloned.1.call-done = bf16[4,256,512]{2,1,0:T(8,128)(2,1)} async-done(((bf16[4,1024,512]{2,1,0:T(8,128)(2,1)}), bf16[4,256,512]{2,1,0:T(8,128)(2,1)}) %reduce-scatter.25.cloned.1.call-update) | async-done | bytes 1048592 | tf_op jit(solution)/shard_map/reduce_scatter | solution.py:60
  791.2 34.3 %all-gather.21.cloned.1.call-done = bf16[4,1024,512]{2,1,0:T(8,128)(2,1)} async-done(((bf16[4,256,512]{2,1,0:T(8,128)(2,1)}), bf16[4,1024,512]{2,1,0:T(8,128)(2,1)}) %all-gather.21.cloned.1.call-update) | async-done | bytes 4194320 | tf_op jit(solution)/shard_map/all_gather | solution.py:56
  830.2 56.8 %while.38 = (s32[]{:T(128)}, bf16[4,1024,1,128]{1,3,2,0:T(8,128)(2,1)S(1)}, f32[4,1024,1,256]{3,1,2,0:T(8,128)}, f32[4,1000,1,256]{3,1,2,0:T(8,128)}, bf16[4,102...) while((s32[]{:T(128)}, ...), condition=%wide.region_34.35_spmd, body=%wide.region_32.34_spmd.sunk | while | flops 2688133120 | bytes 79663224 | solution.py:319
  895.0 45.7 %collective-permute-done = bf16[4,1024,1,256]{3,1,0,2:T(8,128)(2,1)} collective-permute-done((bf16[4,1024,1,256]{3,1,0,2:T(8,128)(2,1)}, bf16[4,1024,1,256]{3,1,0,2:T(8,128)(2,1)}, u32[]{:S(2)}, u32[]{:S(2)}) %collective-permute-start) | collective-permute-done | bytes 2097184 | tf_op jit(solution)/shard_map/ppermute | solution.py:35
  1015.1 136.6 %reduce-scatter.35.cloned.1.call-done = f32[16,1000]{1,0:T(8,128)} async-done(((f32[512,1000]{1,0:T(8,128)}), f32[16,1000]{1,0:T(8,128)}) %reduce-scatter.35.cloned.1.call-update) | async-done | bytes 64016 | tf_op jit(solution)/shard_map/reduce_scatter | solution.py:388
  1153.5 41.0 %reduce-scatter.27.cloned.1.call-done = bf16[4,256,512]{2,1,0:T(8,128)(2,1)} async-done(((bf16[4,1024,512]{2,1,0:T(8,128)(2,1)}), bf16[4,256,512]{2,1,0:T(8,128)(2,1)}) %reduce-scatter.27.cloned.1.call-update) | async-done | bytes 1048592 | tf_op jit(solution)/shard_map/reduce_scatter | solution.py:60
  1201.9 98.4 %all-reduce.12.cloned.1.call-done = f32[512,1,1024]{2,1,0:T(1,128)} async-done(((f32[512,1,1024]{2,1,0:T(1,128)}), f32[512,1,1024]{2,1,0:T(1,128)}) %all-reduce.12.cloned.1.call-update) | async-done | bytes 2097168
  1304.2 132.2 %reduce-scatter.33.cloned.1.call-done = f32[16,7]{1,0:T(8,128)} async-done(((f32[512,7]{1,0:T(8,128)}), f32[16,7]{1,0:T(8,128)}) %reduce-scatter.33.cloned.1.call-update) | async-done | bytes 464
  1437.8 130.6 %reduce-scatter.29.cloned.1.call-done = f32[16,100]{1,0:T(8,128)} async-done(((f32[512,100]{1,0:T(8,128)}), f32[16,100]{1,0:T(8,128)}) %reduce-scatter.29.cloned.1.call-update) | async-done | bytes 6416 | tf_op jit(solution)/shard_map/reduce_scatter | solution.py:386
  1572.6 36.8 %psum.23 = f32[]{:T(128)} all-reduce(f32[]{:T(128)S(6)} %add.405), channel_id=1, replica_groups=mesh['ep'=4,'split'=2,'tp'=4] {'ep','split','tp'}, use_global_device_ids=true, to_apply=%region_60.61 | all-reduce | flops 1 | bytes 8 | tf_op jit(solution)/shard_map/psum | solution.py:397
  (430 shorter events, 429.5 us)
Async XLA Ops:
  7.2 108.9 %all-gather.9.cloned.1.call-start = ((), (), s32[]{:S(2)}) async-start(), calls=%async_computation.10 | async-start | bytes 1179648 | tf_op jit(solution)/shard_map/all_gather | solution.py:102
  8.9 120.6 %all-gather.11.cloned.1.call-start = ((), (), s32[]{:S(2)}) async-start(), calls=%async_computation.11 | async-start | bytes 5242880 | tf_op jit(solution)/shard_map/all_gather | solution.py:56
  94.1 487.6 %copy-start.49 = (f32[4]{0:T(128)}, f32[4]{0:T(128)S(1)}, u32[]{:S(2)}) copy-start(f32[4]{0:T(128)S(1)} %broadcast_divide_fusion) | copy-start | bytes 52
  94.1 694.6 %copy-start.34 = (f32[512,1]{0,1:T(1,128)}, f32[512,1]{0,1:T(1,128)S(1)}, u32[]{:S(2)}) copy-start(f32[512,1]{0,1:T(1,128)S(1)} %get-tuple-element.625) | copy-start | bytes 6148
  97.4 109.1 %all-reduce.8.cloned.1.call-start = ((), (), s32[]{:S(2)}) async-start(), calls=%async_computation.12 | async-start | bytes 4194304 | tf_op jit(solution)/shard_map/psum | solution.py:29
  139.4 148.9 %reduce-scatter.17.cloned.1.call-start = ((), (), s32[]{:S(2)}) async-start(), calls=%async_computation.13 | async-start | bytes 5242880 | tf_op jit(solution)/shard_map/reduce_scatter | solution.py:60
  243.7 83.6 %all-gather.13.cloned.1.call-start = ((), (), s32[]{:S(2)}) async-start(), calls=%async_computation.14 | async-start | bytes 5242880 | tf_op jit(solution)/shard_map/all_gather | solution.py:56
  292.6 96.0 %reduce-scatter.19.cloned.1.call-start = ((), (), s32[]{:S(2)}) async-start(), calls=%async_computation.15 | async-start | bytes 5242880 | tf_op jit(solution)/shard_map/reduce_scatter | solution.py:60
  343.9 87.5 %all-gather.15.cloned.1.call-start = ((), (), s32[]{:S(2)}) async-start(), calls=%async_computation.16 | async-start | bytes 5242880 | tf_op jit(solution)/shard_map/all_gather | solution.py:56
  396.8 106.6 %all-reduce.10.cloned.1.call-start = ((), (), s32[]{:S(2)}) async-start(), calls=%async_computation.17 | async-start | bytes 4194304 | tf_op jit(solution)/shard_map/psum | solution.py:29
  441.2 140.5 %reduce-scatter.21.cloned.1.call-start = ((), (), s32[]{:S(2)}) async-start(), calls=%async_computation.18 | async-start | bytes 5242880 | tf_op jit(solution)/shard_map/reduce_scatter | solution.py:60
  537.0 83.6 %all-gather.17.cloned.1.call-start = ((), (), s32[]{:S(2)}) async-start(), calls=%async_computation.19 | async-start | bytes 5242880 | tf_op jit(solution)/shard_map/all_gather | solution.py:56
  586.0 99.8 %reduce-scatter.23.cloned.1.call-start = ((), (), s32[]{:S(2)}) async-start(), calls=%async_computation.20 | async-start | bytes 5242880 | tf_op jit(solution)/shard_map/reduce_scatter | solution.py:60
  641.1 86.0 %all-gather.19.cloned.1.call-start = ((), (), s32[]{:S(2)}) async-start(), calls=%async_computation.21 | async-start | bytes 5242880 | tf_op jit(solution)/shard_map/all_gather | solution.py:56
  692.5 91.9 %reduce-scatter.25.cloned.1.call-start = ((), (), s32[]{:S(2)}) async-start(), calls=%async_computation.22 | async-start | bytes 5242880 | tf_op jit(solution)/shard_map/reduce_scatter | solution.py:60
  739.7 85.9 %all-gather.21.cloned.1.call-start = ((), (), s32[]{:S(2)}) async-start(), calls=%async_computation.23 | async-start | bytes 5242880 | tf_op jit(solution)/shard_map/all_gather | solution.py:56
  791.0 222.7 %reduce-scatter.31.cloned.1.call-start = ((), (), s32[]{:S(2)}) async-start(), calls=%async_computation.26 | async-start | bytes 294912
  890.7 50.0 %collective-permute-start = (bf16[4,1024,1,256]{3,1,0,2:T(8,128)(2,1)}, bf16[4,1024,1,256]{3,1,0,2:T(8,128)(2,1)}, u32[]{:S(2)}, u32[]{:S(2)}) collective-permute-start(bf16[4,1024,1,256]{3,1,0,2:T(8,128)(2,1)} %bitcast_convert_fusion), channel_id=1, source_target_pairs={{4,0},{5,1},{6,2},{7,3},{12,8},{13,9},{14,10},{15,11},{20,16},{21,... | collective-permute-start | bytes 6291464 | tf_op jit(solution)/shard_map/ppermute | solution.py:35
  953.1 198.6 %reduce-scatter.35.cloned.1.call-start = ((), (), s32[]{:S(2)}) async-start(), calls=%async_computation.28 | async-start | bytes 2162688 | tf_op jit(solution)/shard_map/reduce_scatter | solution.py:388
  959.4 235.1 %reduce-scatter.27.cloned.1.call-start = ((), (), s32[]{:S(2)}) async-start(), calls=%async_computation.24 | async-start | bytes 5242880 | tf_op jit(solution)/shard_map/reduce_scatter | solution.py:60
  974.2 326.1 %all-reduce.12.cloned.1.call-start = ((), (), s32[]{:S(2)}) async-start(), calls=%async_computation.29 | async-start | bytes 4194304
  993.5 442.9 %reduce-scatter.33.cloned.1.call-start = ((), (), s32[]{:S(2)}) async-start(), calls=%async_computation.27 | async-start | bytes 270336
  1198.3 418.0 %copy-start.45 = (f32[16,100]{1,0:T(8,128)S(1)}, f32[16,100]{1,0:T(8,128)}, u32[]{:S(2)}) copy-start(f32[16,100]{1,0:T(8,128)} %param.34) | copy-start | bytes 19204
  1198.3 370.1 %reduce-scatter.29.cloned.1.call-start = ((), (), s32[]{:S(2)}) async-start(), calls=%async_computation.25 | async-start | bytes 270336 | tf_op jit(solution)/shard_map/reduce_scatter | solution.py:386
  (67 other events, 8452.0 us)
Sparse Core Ops, SparseCore 0:
  10.7 42.9 all-gather.8
  97.5 31.9 all-gather.10
  139.6 66.9 all-reduce.7
  243.8 44.5 reduce-scatter.16
  292.7 34.4 all-gather.12
  344.1 44.5 reduce-scatter.18
  396.9 34.4 all-gather.14
  441.4 62.0 all-reduce.9
  537.1 44.4 reduce-scatter.20
  586.1 34.4 all-gather.16
  641.3 44.5 reduce-scatter.22
  692.6 34.4 all-gather.18
  739.8 44.5 reduce-scatter.24
  791.1 34.4 all-gather.20
  953.2 60.3 reduce-scatter.30
  1015.8 135.8 reduce-scatter.34
  1154.1 40.3 reduce-scatter.26
  1198.4 101.8 all-reduce.11
  1303.2 133.1 reduce-scatter.32
  1439.0 129.3 reduce-scatter.28
where the time goes:
time: 1630 us
  waiting for transfers between devices  1090 us (67%)
  blocking collectives  175 us (11%)
  matrix products  161 us (10%)
  other arithmetic  123 us (8%)
  local copies, waits for them, and re-layouts  50.2 us (3%)
  between operations  22.1 us (1%)
    reduce_scatter x6, waiting for transfers between devices, row_reduce(): lax.psum_scatter(partial_sum.astype(jnp.bfloat16), 'tp', scatter_dimensio...  264 us
    unnamed x23, waiting for transfers between devices  249 us
    all_gather x6, waiting for transfers between devices, row_gather(): return lax.all_gather(rows_low, 'tp', axis=1, tiled=True)  185 us
    reduce_scatter x1, waiting for transfers between devices, shards(): lax.psum_scatter(grad_prompt, ('ep', 'split', 'tp'), scatter_dimension=0,...  137 us
    reduce_scatter x1, waiting for transfers between devices, shards(): lax.psum_scatter(grad_encoder, ('ep', 'split', 'tp'), scatter_dimension=0...  131 us
    psum x2, waiting for transfers between devices, broadcast(): return lax.psum(jnp.where(mine, array, jnp.zeros_like(array)), axis)  78.4 us
    ppermute x1, waiting for transfers between devices, passed_along(): lax.ppermute(value, axis, [(source, source + steps) for source in range(f...  45.7 us
    all_gather x1, blocking collectives, shards(): lax.all_gather(shared_vectors.astype(jnp.bfloat16), ('ep', 'split', 'tp')...  43.5 us
  transfers between devices with their start and end apart: 21, of which 20 were waited for; matrix products, arithmetic and copies ran while one was open for 5% of the time, Pallas kernels for 0%

commit v1 on v0

v1 whole, which is shorter than its diff:
```python
import jax
import jax.numpy as jnp
from jax import lax
from jax.sharding import PartitionSpec as P

HEADS = 4
HEAD = 128
FF = 1024
HID = FF // HEADS
FEAT = 100
PROMPT = 1000
SLOTS = 1024
ADAM_STEP = 10
PAD = 1024
WIDE = 128

ln_eps = 1e-05
neg_big = -1e30
clip_norm = 1.0
beta_one = 0.9
beta_two = 0.999
adam_eps = 1e-08
rate_matrix = 0.15
rate_vector = 0.5
weight_decay = 0.01
AXES = ("ep", "split", "tp")
bf16 = jnp.bfloat16
f32 = jnp.float32


def swap(value, ep=0, split=0, row=0, core=0):
    sizes = [lax.axis_size(a) for a in AXES]
    pairs = []
    for a in range(sizes[0]):
        for b in range(sizes[1]):
            for t in range(sizes[2]):
                other = ((a ^ ep) * sizes[1] + (b ^ split)) * sizes[2] + (t ^ (2 * row + core))
                pairs.append(((a * sizes[1] + b) * sizes[2] + t, other))
    return lax.ppermute(value, AXES, pairs)


def pick(low, high, bit):
    return jnp.where(bit == 0, low, high), jnp.where(bit == 0, high, low)


def plane_swap(piece):
    got = {}
    for b in (0, 1):
        for r in (0, 1):
            sent = piece(b, r)
            got[b, r] = sent if (b, r) == (0, 0) else swap(sent, split=b, row=r)
    return got


def gather_ep(shard):
    count = lax.axis_size("ep")
    if count > 4:
        return lax.all_gather(shard, "ep", axis=0)
    place = lax.axis_index("ep")
    parts = [shard] + [swap(shard, ep=k) for k in range(1, count)]
    bit = 1
    while bit < count:
        moved = list(parts)
        for k in range(count):
            if not k & bit:
                moved[k], moved[k | bit] = pick(parts[k], parts[k | bit], (place // bit) % 2)
        parts = moved
        bit *= 2
    return jnp.stack(parts)


def reduce_ep(parts):
    count = lax.axis_size("ep")
    if count > 4:
        return lax.psum_scatter(parts.astype(f32), "ep", scatter_dimension=0, tiled=True)[0]
    place = lax.axis_index("ep")
    total = lax.dynamic_index_in_dim(parts, place, 0, keepdims=False).astype(f32)
    for k in range(1, count):
        piece = lax.dynamic_index_in_dim(parts, place ^ k, 0, keepdims=False)
        total = total + swap(piece, ep=k).astype(f32)
    return total


def norm_rows(residual, norm_gain, norm_shift):
    centre = jnp.mean(residual, axis=-1, keepdims=True)
    centred = residual - centre
    spread = jnp.mean(centred * centred, axis=-1, keepdims=True)
    inverse = lax.rsqrt(spread + ln_eps)
    normed = centred * inverse
    return (normed * norm_gain + norm_shift, normed, inverse)


def norm_back(grad_out, normed, inverse, norm_gain):
    scaled = grad_out * norm_gain
    mean_plain = jnp.mean(scaled, axis=-1, keepdims=True)
    mean_mixed = jnp.mean(scaled * normed, axis=-1, keepdims=True)
    grad_in = inverse * (scaled - mean_plain - normed * mean_mixed)
    return (grad_in, jnp.sum(grad_out * normed, axis=0), jnp.sum(grad_out, axis=0))


def adam_update(weight, moments, gradient, factor, step_rate, decay_rate):
    clipped = gradient * factor
    first_moment = beta_one * moments[0] + (1.0 - beta_one) * clipped
    second_moment = beta_two * moments[1] + (1.0 - beta_two) * clipped * clipped
    first_hat = first_moment / (1.0 - beta_one**ADAM_STEP)
    second_hat = second_moment / (1.0 - beta_two**ADAM_STEP)
    updated = weight - step_rate * (
        first_hat / (jnp.sqrt(second_hat) + adam_eps) + decay_rate * weight
    )
    return (updated, first_moment, second_moment, updated.astype(bf16))


def dot(a, b, dims):
    return lax.dot_general(a, b, (dims, ((), ())), preferred_element_type=f32)


def split_dot(a, b, dims):
    high = a.astype(bf16)
    low = (a - high.astype(f32)).astype(bf16)
    return dot(high, b, dims) + dot(low, b, dims)


def attend(queries, keys, values, bias):
    scale = HEAD**-0.5

    def one(item):
        query, key, value = item
        scores = dot(query, key, ((1,), (1,))) * scale + bias
        top = jnp.max(scores, axis=-1, keepdims=True)
        raised = jnp.exp(scores - top)
        total = jnp.sum(raised, axis=-1, keepdims=True)
        probs = (raised / total).astype(bf16)
        return dot(probs, value, ((1,), (0,))).astype(bf16), top + jnp.log(total)

    return lax.map(one, (queries, keys, values))


def attend_back(queries, keys, values, bias, log_total, grad_out):
    scale = HEAD**-0.5

    def one(item):
        query, key, value, lse, grad = item
        scores = dot(query, key, ((1,), (1,))) * scale + bias
        probs = jnp.exp(scores - lse)
        grad_probs = dot(grad, value, ((1,), (1,)))
        delta = jnp.sum(probs * grad_probs, axis=-1, keepdims=True)
        grad_scores = (probs * (grad_probs - delta)).astype(bf16)
        grad_query = (dot(grad_scores, key, ((1,), (0,))) * scale).astype(bf16)
        grad_key = dot(grad_scores, query, ((0,), (0,))) * scale
        grad_value = dot(probs.astype(bf16), grad, ((0,), (0,)))
        return grad_query, grad_key, grad_value

    return lax.map(one, (queries, keys, values, log_total, grad_out))


def shards(
    feats,
    counts,
    feat_mask,
    cotangent,
    block_weights,
    block_moments,
    head_biases,
    bias_moments,
    encoder,
    encoder_moments,
    shared_vectors,
    vector_moments,
    prompt,
    prompt_moments,
):
    n_ep = lax.axis_size("ep")
    side = lax.axis_index("split")
    row = lax.axis_index("tp") // 2
    core = lax.axis_index("tp") % 2
    chip = side * 2 + row
    rows = feats.shape[2]
    half = 2 * rows
    width = cotangent.shape[3]
    slab = block_weights.shape[0]
    strip = encoder.shape[0]

    def canonical(got):
        first = [jnp.concatenate(pick(got[b, 0], got[b, 1], row), axis=0) for b in (0, 1)]
        return jnp.concatenate(pick(first[0], first[1], side), axis=0)

    def to_chip(array):
        return plane_swap(
            lambda b, r: lax.dynamic_index_in_dim(array[0], chip ^ (2 * b + r), 0, keepdims=False)
        )

    def from_chip(own_rows):
        blocks = own_rows.reshape((4, rows) + own_rows.shape[1:])
        got = plane_swap(
            lambda b, r: lax.dynamic_index_in_dim(blocks, chip ^ (2 * b + r), 0, keepdims=False)
        )
        first = [jnp.stack(pick(got[b, 0], got[b, 1], row)) for b in (0, 1)]
        return jnp.concatenate(pick(first[0], first[1], side), axis=0)[None]

    feats_own = canonical(to_chip(feats))
    mask_row = lax.dynamic_index_in_dim(feat_mask, chip, 0, keepdims=False)
    count_pair = lax.dynamic_index_in_dim(counts, chip, 0, keepdims=False)
    masked_own = feats_own * mask_row.astype(bf16)
    masked_other = swap(masked_own, core=1)
    mask_float = mask_row.astype(f32)
    feat_ratio = FEAT / jnp.sum(mask_float)

    block_low = block_weights[:, 0, :].astype(bf16)
    project_part = block_low[:, 0 : 3 * HEAD]
    rest_part = block_low[:, 3 * HEAD :]
    small_part = jnp.concatenate(
        [
            encoder.astype(bf16),
            shared_vectors.astype(bf16),
            head_biases.astype(bf16).reshape(strip, slab // strip),
        ],
        axis=1,
    )
    small_part = jnp.pad(small_part, ((0, 0), (0, WIDE - small_part.shape[1])))
    prompt_part = prompt.astype(bf16)

    def gather_heads(shard):
        along = gather_ep(shard)
        got = plane_swap(lambda b, r: along)
        return [
            jnp.stack(pick(got[0, r], got[1, r], side), axis=1).reshape(width, shard.shape[1])
            for r in (0, 1)
        ]

    def gather_strips(shard):
        along = gather_ep(shard)
        got = plane_swap(lambda b, r: along)
        by_row = [jnp.stack(pick(got[b, 0], got[b, 1], row), axis=1) for b in (0, 1)]
        both = jnp.stack(pick(by_row[0], by_row[1], side), axis=1)
        other = swap(both, core=1)
        return jnp.stack(pick(both, other, core), axis=3)

    small_all = gather_strips(small_part)
    prompt_low = gather_strips(prompt_part).reshape(width, PROMPT)
    encoder_low = small_all[..., 0:FEAT].reshape(width, FEAT)
    vectors = small_all[..., FEAT : FEAT + 7].reshape(width, 7).astype(f32)
    bias_all = small_all[..., FEAT + 7 : FEAT + 7 + slab // strip].astype(f32)
    bias_all = jnp.transpose(bias_all, (2, 3, 0, 1, 4, 5)).reshape(2, 2, width)

    def by_slot(table):
        rows_first = jnp.stack(pick(table[0], table[1], row))
        cores_first = jnp.stack(pick(rows_first[:, 0], rows_first[:, 1], core))
        return cores_first.reshape(4, table.shape[-1])

    bias_slots = by_slot(bias_all)
    bias_query = bias_slots[0:2, 0:HEAD]
    bias_value = bias_slots[0:2, HEAD : 2 * HEAD]
    bias_hidden = bias_slots[:, 2 * HEAD :].reshape(4 * HID)
    w_project = gather_heads(project_part)
    rest_own = gather_heads(rest_part)
    rest_own = jnp.stack(rest_own)
    rest_other = swap(rest_own, core=1)
    rest_all = jnp.concatenate([rest_own, rest_other], axis=0)
    w_output = jnp.concatenate([rest_all[k, :, 0:HEAD] for k in range(4)], axis=1)
    w_hidden = jnp.concatenate([rest_all[k, :, HEAD : HEAD + HID] for k in range(4)], axis=1)
    w_return = jnp.concatenate([rest_all[k, :, HEAD + HID :] for k in range(4)], axis=1)
    w_query = jnp.concatenate([w[:, 0:HEAD] for w in w_project], axis=1)
    w_key = jnp.concatenate([w[:, HEAD : 2 * HEAD] for w in w_project], axis=1)
    w_value = jnp.concatenate([w[:, 2 * HEAD :] for w in w_project], axis=1)

    masked_all = jnp.concatenate(
        [masked_own[0:half], masked_other[0:half], masked_own[half:], masked_other[half:]], axis=0
    )
    embed_all = feat_ratio * dot(masked_all, encoder_low, ((1,), (1,))) + vectors[:, 6]
    rows_low = embed_all.astype(bf16)
    embedded = jnp.concatenate([embed_all[0:half], embed_all[2 * half : 3 * half]], axis=0)
    context_low = rows_low[0:SLOTS]

    lane = jnp.arange(rows, dtype=jnp.int32)

    def slots_of(which_core):
        return jnp.concatenate([which_core * rows + lane, (2 + which_core) * rows + lane])

    own_slots = slots_of(core)
    key_slots = jnp.concatenate([own_slots, slots_of(1 - core)])
    key_live = jnp.concatenate([jnp.arange(PAD) < PROMPT, key_slots < count_pair[0]])
    key_bias = jnp.where(key_live, 0.0, neg_big)[None, :].astype(f32)
    row_live = jnp.concatenate([own_slots < count_pair[0], own_slots < count_pair[1]])
    row_live = row_live.astype(f32)[:, None]

    query = (dot(rows_low, w_query, ((1,), (0,))) + bias_query.reshape(-1)).astype(bf16)
    key_ctx = dot(context_low, w_key, ((1,), (0,))).astype(bf16)
    value_ctx = (dot(context_low, w_value, ((1,), (0,))) + bias_value.reshape(-1)).astype(bf16)
    key_prompt = dot(prompt_low, w_key, ((0,), (0,))).astype(bf16)
    value_prompt = (dot(prompt_low, w_value, ((0,), (0,))) + bias_value.reshape(-1)).astype(bf16)
    gap = ((0, PAD - PROMPT), (0, 0))
    keys = jnp.concatenate([jnp.pad(key_prompt, gap), key_ctx], axis=0)
    values = jnp.concatenate([jnp.pad(value_prompt, gap), value_ctx], axis=0)

    def heads_first(flat):
        return jnp.stack([flat[:, 0:HEAD], flat[:, HEAD:]])

    def chunked(flat):
        return heads_first(flat).reshape(4, SLOTS, HEAD)

    def doubled(flat):
        stacked = heads_first(flat)
        return jnp.stack([stacked[0], stacked[0], stacked[1], stacked[1]])

    queries = chunked(query)
    keys_four = doubled(keys)
    values_four = doubled(values)
    attended, log_total = attend(queries, keys_four, values_four, key_bias)
    attended = attended.reshape(2, 4, half, HEAD)

    def own_of(array):
        return jnp.concatenate([array[:, 0], array[:, 2]], axis=1)

    def other_of(array):
        return jnp.concatenate([array[:, 1], array[:, 3]], axis=1)

    attended_own = own_of(attended)
    attended_got = swap(other_of(attended), core=1)
    attended_rows = jnp.concatenate(
        [attended_own[0], attended_own[1], attended_got[0], attended_got[1]], axis=1
    )
    attn_out = dot(attended_rows, w_output, ((1,), (1,))) + vectors[:, 4]
    normed_first, normed_one, inverse_one = norm_rows(
        embedded + attn_out, vectors[:, 0], vectors[:, 1]
    )
    first_low = normed_first.astype(bf16)
    hidden_pre = dot(first_low, w_hidden, ((1,), (0,))) + bias_hidden
    hidden_value, gelu_pull = jax.vjp(
        lambda pre_value: jax.nn.gelu(pre_value, approximate=False), hidden_pre
    )
    hidden_act = hidden_value.astype(bf16)
    mlp_out = dot(hidden_act, w_return, ((1,), (1,))) + vectors[:, 5]
    normed_final, normed_two, inverse_two = norm_rows(
        normed_first + mlp_out, vectors[:, 2], vectors[:, 3]
    )
    output_final = from_chip((normed_final * row_live).astype(bf16))

    grad_final = canonical(to_chip(cotangent)).astype(f32) * row_live
    grad_two, gain_two, shift_two = norm_back(grad_final, normed_two, inverse_two, vectors[:, 2])
    grad_mlp = grad_two.astype(bf16)
    bias_two = jnp.sum(grad_mlp.astype(f32), axis=0)
    grad_return = dot(grad_mlp, hidden_act, ((0,), (0,)))
    grad_act = dot(grad_mlp, w_return, ((1,), (0,)))
    grad_pre = gelu_pull(grad_act)[0].astype(bf16)
    grad_bias_hidden = jnp.sum(grad_pre.astype(f32), axis=0)
    grad_hidden = dot(first_low, grad_pre, ((0,), (0,)))
    grad_first = grad_two + dot(grad_pre, w_hidden, ((1,), (1,)))
    grad_one, gain_one, shift_one = norm_back(grad_first, normed_one, inverse_one, vectors[:, 0])
    grad_attn = grad_one.astype(bf16)
    bias_out = jnp.sum(grad_attn.astype(f32), axis=0)
    grad_output = dot(grad_attn, attended_rows, ((0,), (0,)))
    grad_attended = dot(grad_attn, w_output, ((1,), (0,))).astype(bf16)

    def slot_grads(k):
        return jnp.concatenate(
            [
                grad_output[:, k * HEAD : (k + 1) * HEAD],
                grad_hidden[:, k * HID : (k + 1) * HID],
                grad_return[:, k * HID : (k + 1) * HID],
            ],
            axis=1,
        )

    rest_mine = jnp.stack([slot_grads(0), slot_grads(1)])
    rest_sent = jnp.stack([slot_grads(2), slot_grads(3)]).astype(bf16)
    rest_pair = (rest_mine + swap(rest_sent, core=1).astype(f32)).astype(bf16)

    def reduce_heads(pair):
        blocks = pair.reshape(2, n_ep, 2, slab, pair.shape[-1])
        got = plane_swap(
            lambda b, r: lax.dynamic_index_in_dim(blocks[r], side ^ b, 1, keepdims=False)
        )
        total = sum(part.astype(f32) for part in got.values())
        return reduce_ep(total.astype(pair.dtype))

    def reduce_strips(whole):
        blocks = whole.reshape(n_ep, 2, 2, 2, strip, whole.shape[-1])
        mine = lax.dynamic_index_in_dim(blocks, core, 3, keepdims=False)
        sent = lax.dynamic_index_in_dim(blocks, 1 - core, 3, keepdims=False)
        pair = (mine.astype(f32) + swap(sent, core=1).astype(f32)).astype(whole.dtype)

        def piece(b, r):
            half_piece = lax.dynamic_index_in_dim(pair, side ^ b, 1, keepdims=False)
            return lax.dynamic_index_in_dim(half_piece, row ^ r, 1, keepdims=False)

        got = plane_swap(piece)
        total = sum(part.astype(f32) for part in got.values())
        return reduce_ep(total.astype(whole.dtype))

    summed_rest = reduce_heads(rest_pair)

    grad_four = grad_attended.reshape(2, half, 4, HEAD)
    grad_mine = jnp.transpose(grad_four[:, :, 0:2], (2, 0, 1, 3))
    grad_sent = jnp.transpose(grad_four[:, :, 2:4], (2, 0, 1, 3))
    grad_got = swap(grad_sent, core=1)
    grad_heads = jnp.stack([grad_mine, grad_got], axis=2).reshape(4, SLOTS, HEAD)
    grad_query, grad_key, grad_value = attend_back(
        queries, keys_four, values_four, key_bias, log_total, grad_heads
    )
    grad_query = jnp.concatenate(
        [grad_query[0:2].reshape(2 * SLOTS, HEAD), grad_query[2:4].reshape(2 * SLOTS, HEAD)], axis=1
    )
    grad_key = jnp.concatenate([grad_key[0] + grad_key[1], grad_key[2] + grad_key[3]], axis=1)
    grad_value = jnp.concatenate(
        [grad_value[0] + grad_value[1], grad_value[2] + grad_value[3]], axis=1
    )
    grad_prompt_key = grad_key[0:PROMPT]
    grad_prompt_value = grad_value[0:PROMPT]
    context_key = grad_key[PAD:].astype(bf16)
    context_value = grad_value[PAD:].astype(bf16)
    grad_wq = dot(rows_low, grad_query, ((0,), (0,)))
    grad_wk = dot(context_low, context_key, ((0,), (0,)))
    grad_wv = dot(context_low, context_value, ((0,), (0,)))
    grad_wk = grad_wk + split_dot(grad_prompt_key, prompt_low, ((0,), (1,))).T
    grad_wv = grad_wv + split_dot(grad_prompt_value, prompt_low, ((0,), (1,))).T
    grad_prompt = (
        split_dot(grad_prompt_key, w_key, ((1,), (1,)))
        + split_dot(grad_prompt_value, w_value, ((1,), (1,)))
    ).T
    grad_bias_query = jnp.sum(grad_query.astype(f32), axis=0).reshape(2, HEAD)
    grad_bias_value = jnp.sum(context_value.astype(f32), axis=0) + jnp.sum(
        grad_prompt_value, axis=0
    )
    grad_bias_value = grad_bias_value.reshape(2, HEAD)

    back_rows = dot(grad_query, w_query, ((1,), (1,)))
    back_context = dot(context_key, w_key, ((1,), (1,))) + dot(context_value, w_value, ((1,), (1,)))
    back_rows = back_rows.reshape(2, 2, half, width)
    back_context = back_context.reshape(2, half, width)
    back_own = jnp.concatenate([back_rows[0, 0] + back_context[0], back_rows[1, 0]], axis=0)
    back_other = jnp.concatenate([back_rows[0, 1] + back_context[1], back_rows[1, 1]], axis=0)
    back_got = swap(back_other.astype(bf16), core=1).astype(f32)
    grad_input_low = (grad_one + back_own + back_got).astype(bf16)
    grad_encoder = feat_ratio * dot(grad_input_low, masked_own, ((0,), (0,)))
    grad_embed_bias = jnp.sum(grad_input_low.astype(f32), axis=0)
    input_grad = feat_ratio * dot(grad_input_low, encoder_low, ((1,), (0,))) * mask_float
    input_final = from_chip(input_grad)

    project_pair = jnp.stack(
        [
            jnp.concatenate(
                [g[:, k * HEAD : (k + 1) * HEAD] for g in (grad_wq, grad_wk, grad_wv)], axis=1
            )
            for k in (0, 1)
        ]
    ).astype(bf16)
    summed_project = reduce_heads(project_pair)
    summed_block = jnp.concatenate([summed_project, summed_rest], axis=1)[:, None, :]

    grad_vectors = jnp.stack(
        [gain_one, shift_one, gain_two, shift_two, bias_out, bias_two, grad_embed_bias], axis=1
    )
    bias_slots_grad = jnp.concatenate(
        [
            jnp.pad(grad_bias_query, ((0, 2), (0, 0))),
            jnp.pad(grad_bias_value, ((0, 2), (0, 0))),
            grad_bias_hidden.reshape(4, HID),
        ],
        axis=1,
    )
    by_core = bias_slots_grad.reshape(2, 2, width)
    core_ordered = jnp.stack(pick(by_core[0], by_core[1], core), axis=1)
    bias_abs = jnp.stack(pick(core_ordered[0], core_ordered[1], row))
    bias_abs = bias_abs.reshape(2, 2, n_ep, 2, strip, slab // strip)
    bias_abs = jnp.transpose(bias_abs, (2, 3, 0, 1, 4, 5)).reshape(width, slab // strip)
    grad_small = jnp.concatenate([grad_encoder, grad_vectors, bias_abs], axis=1)
    grad_small = jnp.pad(grad_small, ((0, 0), (0, WIDE - grad_small.shape[1])))
    summed_small = reduce_strips(grad_small)
    summed_prompt = reduce_strips(grad_prompt.astype(bf16))
    summed_encoder = summed_small[:, 0:FEAT]
    summed_vectors = summed_small[:, FEAT : FEAT + 7]
    summed_bias = summed_small[:, FEAT + 7 : FEAT + 7 + slab // strip].reshape(slab, 1)

    local_squares = (
        jnp.sum(summed_block * summed_block)
        + jnp.sum(summed_small * summed_small)
        + jnp.sum(summed_prompt * summed_prompt)
    )
    square_tile = jnp.full((8, 128), local_squares)
    square_tile = square_tile + swap(square_tile, core=1)
    got = plane_swap(lambda b, r: square_tile)
    square_tile = (got[0, 0] + got[1, 0]) + (got[0, 1] + got[1, 1])
    if n_ep > 4:
        square_tile = lax.psum(square_tile, "ep")
    else:
        square_tile = jnp.sum(gather_ep(square_tile), axis=0)
    grad_norm = jnp.sqrt(square_tile[0, 0])
    factor = jnp.minimum(1.0, clip_norm / (grad_norm + 1e-06))
    block_out = adam_update(
        block_weights, block_moments, summed_block, factor, rate_matrix, weight_decay
    )
    bias_out_new = adam_update(head_biases, bias_moments, summed_bias, factor, rate_vector, 0.0)
    encoder_out = adam_update(
        encoder, encoder_moments, summed_encoder, factor, rate_matrix, weight_decay
    )
    vector_out = adam_update(
        shared_vectors, vector_moments, summed_vectors, factor, rate_vector, 0.0
    )
    prompt_out = adam_update(
        prompt, prompt_moments, summed_prompt, factor, rate_vector, weight_decay
    )
    return (
        (output_final, input_final, grad_norm)
        + block_out
        + bias_out_new
        + encoder_out
        + vector_out
        + prompt_out
    )


def solution(mesh):
    data = P("split", "ep", "tp", None)
    block = P(("ep", "split"), "tp", None)
    bias = P(("ep", "split"), "tp")
    strip = P(AXES, None)
    placed = (
        data,
        P("ep", None),
        P("ep", None),
        data,
        block,
        P(None, ("ep", "split"), "tp", None),
        bias,
        P(None, ("ep", "split"), "tp"),
        strip,
        P(None, AXES, None),
        strip,
        P(None, AXES, None),
        strip,
        P(None, AXES, None),
    )
    return jax.shard_map(
        shards,
        mesh=mesh,
        in_specs=placed,
        out_specs=(data, data, P()) + (block,) * 4 + (bias,) * 4 + (strip,) * 12,
        check_vma=False,
    )
```

time: 1630 us -> 442 us (0.27)
  waiting for transfers between devices: 1090 us -> 61.8 us
  blocking collectives: 175 us -> 0 us
  starting transfers between devices: 3.39 us -> 85.8 us
  other arithmetic: 123 us -> 77.7 us
  matrix products: 161 us -> 121 us
  local copies, waits for them, and re-layouts: 50.2 us -> 81.5 us
    reduce_scatter x8 -> x0, waiting for transfers between devices: 531 us -> none  [the longest x6 264 us: row_reduce(): lax.psum_scatter(partial_sum.astype(jnp.bfloat16), 'tp', scatter_dimensio...]
    unnamed x23 -> x0, waiting for transfers between devices: 249 us -> none
    all_gather x7 -> x0, waiting for transfers between devices: 185 us -> none  [the longest x6 185 us: row_gather(): return lax.all_gather(rows_low, 'tp', axis=1, tiled=True)]
    all_gather x3 -> x0, blocking collectives: 121 us -> none  [the longest x1 43.5 us: shards(): lax.all_gather(shared_vectors.astype(jnp.bfloat16), ('ep', 'split', 'tp')...]
    ppermute x1 -> x77, starting transfers between devices: 1.28 us -> 85.8 us  [swap(): return lax.ppermute(value, AXES, pairs)]
    psum x2 -> x0, waiting for transfers between devices: 78.4 us -> none  [broadcast(): return lax.psum(jnp.where(mine, array, jnp.zeros_like(array)), axis)]
    dot_general x64 -> x59, matrix products: 161 us -> 121 us  [dot(): return lax.dot_general(a, b, (dims, ((), ())), preferred_element_type=f32)]
    psum x1 -> x0, blocking collectives: 36.8 us -> none  [shards(): grad_norm = jnp.sqrt(lax.psum(local_squares, ('ep', 'split', 'tp')))]
  transfers between devices with their start and end apart: 21 -> 77, of which waited for: 20 -> 33; matrix products, arithmetic and copies ran while one was open for 5% -> 51% of each run, Pallas kernels for 0% -> 0%
where the time goes in v1:
time: 442 us; the launch traced here: 436 us
  matrix products  121 us (27%)
  starting transfers between devices  85.8 us (19%)
  local copies, waits for them, and re-layouts  81.5 us (18%)
  other arithmetic  77.7 us (18%)
  waiting for transfers between devices  61.8 us (14%)
  between operations  7.55 us (2%)
    dot_general x59, matrix products, dot(): return lax.dot_general(a, b, (dims, ((), ())), preferred_element_type=f32)  121 us
    ppermute x77, starting transfers between devices, swap(): return lax.ppermute(value, AXES, pairs)  85.8 us
    ppermute x77, waiting for transfers between devices, swap(): return lax.ppermute(value, AXES, pairs)  61.8 us
    unnamed x209, local copies, waits for them, and re-layouts  13.4 us
    convert_element_type x4, other arithmetic, one(): grad_scores = (probs * (grad_probs - delta)).astype(bf16)  10.3 us
    reduce_sum x4, other arithmetic, one(): total = jnp.sum(raised, axis=-1, keepdims=True)  8.94 us
  transfers between devices with their start and end apart: 77, of which 33 were waited for; matrix products, arithmetic and copies ran while one was open for 51% of the time, Pallas kernels for 0%

profile of v1, /device:TPU:0, one launch (start us, length us, event | category | flops | bytes accessed | tf_op | source)
XLA Modules:
  0.0 436.1 jit_solution(11175159530743655446)
XLA Ops:
  3.2 4.0 collective-permute-start.5
  46.2 3.2 collective-permute-done
  64.5 3.2 collective-permute-done.20
  69.3 4.4 %collective-permute-done.21 = bf16[4,16,1000]{2,1,0:T(8,128)(2,1)S(1)} collective-permute-done((bf16[4,16,1000]{2,1,0:T(8,128)(2,1)S(1)}, bf16[4,16,1000]{2,1,0:T(8,128)(2,1)S(1)}, u32[]{:S(2)}, u32[]{:S(2)}) %collective-permute-start.21) | collective-permute-done | bytes 128032 | tf_op jit(solution)/shard_map/ppermute | solution.py:39
  93.8 4.9 %collective-permute-done.29 = bf16[4,64,640]{2,1,0:T(8,128)(2,1)S(1)} collective-permute-done((bf16[4,64,640]{2,1,0:T(8,128)(2,1)}, bf16[4,64,640]{2,1,0:T(8,128)(2,1)S(1)}, u32[]{:S(2)}, u32[]{:S(2)}) %collective-permute-start.29) | collective-permute-done | bytes 327712 | tf_op jit(solution)/shard_map/ppermute | solution.py:39
  105.6 33.7 %while.26 = (s32[]{:T(128)}, bf16[4,1024,128]{2,1,0:T(8,128)(2,1)}, f32[4,1024,1]{1,2,0:T(1,128)}, bf16[4,1024,128]{2,1,0:T(8,128)(2,1)S(1)}, bf16[4,2048,128]{2...) while((s32[]{:T(128)}, bf16[4,1024,128]{2,1,0:T(8,128)(2,1)}, ...), condition=%wide.region_4.5_spmd, body=%wide.region_1.4_spmd.sunk | while | flops 1099037696 | bytes 26806368 | solution.py:135
  109.2 4.1 fusion.267
  117.5 4.1 fusion.267
  125.8 4.1 fusion.267
  134.2 4.1 fusion.267
  146.5 9.7 %multiply_convert_fusion.1 = (bf16[1024,1024]{1,0:T(8,128)(2,1)S(1)}, f32[1024,1024]{1,0:T(8,128)S(1)}, f32[1024,1024]{1,0:T(8,128)S(1)}) fusion(f32[1024]{0:T(1024)S(1)} %bitcast.639, bf16[512,256]{1,0:T(8,128)(2,1)S(1)} %get-tuple-element.500, bf16[512,256]{1,0:T(8,128)(2,1)S(1)} %get-tuple-element.501, bf16[512,256]{1,0:T(8,128)(2,1)S(1)} %get-tuple-element.543, ...), kind=kOutput, calls=%fused_computation.62 | convolution fusion | flops 1149763584 | bytes 13647872 | tf_op jit(solution)/shard_map/dot_general | solution.py:114
  162.0 3.3 convert_reduce_fusion.3
  168.3 3.2 convert_reduce_fusion
  173.9 3.2 fusion.218
  192.8 3.5 slice_bitcast_fusion.4
  214.6 61.5 %while.27 = (s32[]{:T(128)}, bf16[4,1024,128]{2,1,0:T(8,128)(2,1)}, f32[4,2048,128]{2,1,0:T(8,128)}, f32[4,2048,128]{2,1,0:T(8,128)}, bf16[4,1024,128]{2,1,0:T(8...) while((s32[]{:T(128)}, bf16[4,1024,128]{2,1,0:T(8,128)(2,1)}, ...), condition=%wide.region_15.16_spmd, body=%wide.region_13.15_spmd.sunk | while | flops 2716335104 | bytes 72148112 | solution.py:153
  219.7 3.4 multiply_reduce_fusion.12
  235.0 3.4 multiply_reduce_fusion.12
  250.2 3.4 multiply_reduce_fusion.12
  265.5 3.4 multiply_reduce_fusion.12
  322.2 4.3 add_convert_fusion.1
  339.3 4.9 %collective-permute-start.48 = (bf16[64,384]{1,0:T(8,128)(2,1)S(1)}, bf16[64,384]{1,0:T(8,128)(2,1)S(1)}, u32[]{:S(2)}, u32[]{:S(2)}) collective-permute-start(bf16[64,384]{1,0:T(8,128)(2,1)S(1)} %get-tuple-element.617), channel_id=1, source_target_pairs={{0,24},{1,25},{2,26},{3,27},{4,28},{5,29},{6,30},{7,31},{8,16},{9,... | collective-permute-start | bytes 147464 | tf_op jit(solution)/shard_map/ppermute | solution.py:39
  355.3 3.5 collective-permute-start.69
  379.0 5.2 %collective-permute-done.50 = bf16[4,64,640]{2,1,0:T(8,128)(2,1)S(1)} collective-permute-done((bf16[4,64,640]{2,1,0:T(8,128)(2,1)}, bf16[4,64,640]{2,1,0:T(8,128)(2,1)S(1)}, u32[]{:S(2)}, u32[]{:S(2)}) %collective-permute-start.50) | collective-permute-done | bytes 327712 | tf_op jit(solution)/shard_map/ppermute | solution.py:39
  (661 shorter events, 337.2 us)
Async XLA Ops:
  3.2 19.4 %collective-permute-start.5 = (bf16[16,128]{1,0:T(8,128)(2,1)S(1)}, bf16[16,128]{1,0:T(8,128)(2,1)S(1)}, u32[]{:S(2)}, u32[]{:S(2)}) collective-permute-start(bf16[16,128]{1,0:T(8,128)(2,1)S(1)} %fusion.145), channel_id=1, source_target_pairs={{0,16},{1,17},{2,18},{3,19},{4,20},{5,21},{6,22},{7,23},{8,24},{9,... | collective-permute-start | bytes 12296 | tf_op jit(solution)/shard_map/ppermute | solution.py:39
  7.2 15.9 %collective-permute-start.4 = (bf16[16,128]{1,0:T(8,128)(2,1)S(1)}, bf16[16,128]{1,0:T(8,128)(2,1)S(1)}, u32[]{:S(2)}, u32[]{:S(2)}) collective-permute-start(bf16[16,128]{1,0:T(8,128)(2,1)S(1)} %fusion.145), channel_id=1, source_target_pairs={{0,8},{1,9},{2,10},{3,11},{4,12},{5,13},{6,14},{7,15},{8,0},{9,1},... | collective-permute-start | bytes 12296 | tf_op jit(solution)/shard_map/ppermute | solution.py:39
  9.6 28.9 %collective-permute-start.18 = (bf16[16,1000]{1,0:T(8,128)(2,1)S(1)}, bf16[16,1000]{1,0:T(8,128)(2,1)S(1)}, u32[]{:S(2)}, u32[]{:S(2)}) collective-permute-start(bf16[16,1000]{1,0:T(8,128)(2,1)S(1)} %convert_element_type.307), channel_id=1, source_target_pairs={{0,16},{1,17},{2,18},{3,19},{4,20},{5,21},{6,22},{7,23},{8,24},{9,... | collective-permute-start | bytes 96008 | tf_op jit(solution)/shard_map/ppermute | solution.py:39
  11.5 27.1 %collective-permute-start.19 = (bf16[16,1000]{1,0:T(8,128)(2,1)S(1)}, bf16[16,1000]{1,0:T(8,128)(2,1)S(1)}, u32[]{:S(2)}, u32[]{:S(2)}) collective-permute-start(bf16[16,1000]{1,0:T(8,128)(2,1)S(1)} %convert_element_type.307), channel_id=1, source_target_pairs={{0,24},{1,25},{2,26},{3,27},{4,28},{5,29},{6,30},{7,31},{8,16},{9,... | collective-permute-start | bytes 96008 | tf_op jit(solution)/shard_map/ppermute | solution.py:39
  22.6 18.5 %collective-permute-start.17 = (bf16[16,1000]{1,0:T(8,128)(2,1)S(1)}, bf16[16,1000]{1,0:T(8,128)(2,1)S(1)}, u32[]{:S(2)}, u32[]{:S(2)}) collective-permute-start(bf16[16,1000]{1,0:T(8,128)(2,1)S(1)} %convert_element_type.307), channel_id=1, source_target_pairs={{0,8},{1,9},{2,10},{3,11},{4,12},{5,13},{6,14},{7,15},{8,0},{9,1},... | collective-permute-start | bytes 96008 | tf_op jit(solution)/shard_map/ppermute | solution.py:39
  38.6 17.3 %collective-permute-start.26 = (bf16[64,640]{1,0:T(8,128)(2,1)S(1)}, bf16[64,640]{1,0:T(8,128)(2,1)S(1)}, u32[]{:S(2)}, u32[]{:S(2)}) collective-permute-start(bf16[64,640]{1,0:T(8,128)(2,1)S(1)} %slice.555), channel_id=1, source_target_pairs={{0,16},{1,17},{2,18},{3,19},{4,20},{5,21},{6,22},{7,23},{8,24},{9,... | collective-permute-start | bytes 245768 | tf_op jit(solution)/shard_map/ppermute | solution.py:39
  41.1 16.4 %collective-permute-start.27 = (bf16[64,640]{1,0:T(8,128)(2,1)S(1)}, bf16[64,640]{1,0:T(8,128)(2,1)S(1)}, u32[]{:S(2)}, u32[]{:S(2)}) collective-permute-start(bf16[64,640]{1,0:T(8,128)(2,1)S(1)} %slice.555), channel_id=1, source_target_pairs={{0,24},{1,25},{2,26},{3,27},{4,28},{5,29},{6,30},{7,31},{8,16},{9,... | collective-permute-start | bytes 245768 | tf_op jit(solution)/shard_map/ppermute | solution.py:39
  51.0 40.5 %collective-permute-start.35 = (bf16[256,512]{1,0:T(8,128)(2,1)}, bf16[256,512]{1,0:T(8,128)(2,1)}, u32[]{:S(2)}, u32[]{:S(2)}) collective-permute-start(bf16[256,512]{1,0:T(8,128)(2,1)} %get-tuple-element.516), channel_id=1, source_target_pairs={{0,2},{1,3},{2,0},{3,1},{4,6},{5,7},{6,4},{7,5},{8,10},{9,11},{10,... | collective-permute-start | bytes 786440 | tf_op jit(solution)/shard_map/ppermute | solution.py:39
  54.2 34.8 %collective-permute-start.37 = (bf16[256,512]{1,0:T(8,128)(2,1)}, bf16[256,512]{1,0:T(8,128)(2,1)}, u32[]{:S(2)}, u32[]{:S(2)}) collective-permute-start(bf16[256,512]{1,0:T(8,128)(2,1)} %get-tuple-element.517), channel_id=1, source_target_pairs={{0,6},{1,7},{2,4},{3,5},{4,2},{5,3},{6,0},{7,1},{8,14},{9,15},{10,... | collective-permute-start | bytes 786440 | tf_op jit(solution)/shard_map/ppermute | solution.py:39
  55.9 34.6 %collective-permute-start.36 = (bf16[256,512]{1,0:T(8,128)(2,1)}, bf16[256,512]{1,0:T(8,128)(2,1)}, u32[]{:S(2)}, u32[]{:S(2)}) collective-permute-start(bf16[256,512]{1,0:T(8,128)(2,1)} %get-tuple-element.518), channel_id=1, source_target_pairs={{0,4},{1,5},{2,6},{3,7},{4,0},{5,1},{6,2},{7,3},{8,12},{9,13},{10,... | collective-permute-start | bytes 786440 | tf_op jit(solution)/shard_map/ppermute | solution.py:39
  84.1 14.6 %collective-permute-start.29 = (bf16[4,64,640]{2,1,0:T(8,128)(2,1)}, bf16[4,64,640]{2,1,0:T(8,128)(2,1)S(1)}, u32[]{:S(2)}, u32[]{:S(2)}) collective-permute-start(bf16[4,64,640]{2,1,0:T(8,128)(2,1)} %pad_maximum_fusion.28), channel_id=1, source_target_pairs={{0,2},{1,3},{2,0},{3,1},{4,6},{5,7},{6,4},{7,5},{8,10},{9,11},{10,... | collective-permute-start | bytes 983048 | tf_op jit(solution)/shard_map/ppermute | solution.py:39
  100.5 42.4 %collective-permute-start.31 = (bf16[2,512,640]{2,1,0:T(8,128)(2,1)}, bf16[2,512,640]{2,1,0:T(8,128)(2,1)}, u32[]{:S(2)}, u32[]{:S(2)}) collective-permute-start(bf16[2,512,640]{2,1,0:T(8,128)(2,1)} %pad_maximum_fusion.2), channel_id=1, source_target_pairs={{0,1},{1,0},{2,3},{3,2},{4,5},{5,4},{6,7},{7,6},{8,9},{9,8},{10,11... | collective-permute-start | bytes 3932168 | tf_op jit(solution)/shard_map/ppermute | solution.py:39
  184.2 24.4 %collective-permute-start.32 = (bf16[256,512]{1,0:T(8,128)(2,1)}, bf16[256,512]{1,0:T(8,128)(2,1)}, u32[]{:S(2)}, u32[]{:S(2)}) collective-permute-start(bf16[256,512]{1,0:T(8,128)(2,1)} %get-tuple-element.521), channel_id=1, source_target_pairs={{0,2},{1,3},{2,0},{3,1},{4,6},{5,7},{6,4},{7,5},{8,10},{9,11},{10,... | collective-permute-start | bytes 786440 | tf_op jit(solution)/shard_map/ppermute | solution.py:39
  184.8 22.7 %collective-permute-start.34 = (bf16[256,512]{1,0:T(8,128)(2,1)}, bf16[256,512]{1,0:T(8,128)(2,1)}, u32[]{:S(2)}, u32[]{:S(2)}) collective-permute-start(bf16[256,512]{1,0:T(8,128)(2,1)} %get-tuple-element.522), channel_id=1, source_target_pairs={{0,6},{1,7},{2,4},{3,5},{4,2},{5,3},{6,0},{7,1},{8,14},{9,15},{10,... | collective-permute-start | bytes 786440 | tf_op jit(solution)/shard_map/ppermute | solution.py:39
  186.3 21.2 %collective-permute-start.33 = (bf16[256,512]{1,0:T(8,128)(2,1)}, bf16[256,512]{1,0:T(8,128)(2,1)}, u32[]{:S(2)}, u32[]{:S(2)}) collective-permute-start(bf16[256,512]{1,0:T(8,128)(2,1)} %get-tuple-element.523), channel_id=1, source_target_pairs={{0,4},{1,5},{2,6},{3,7},{4,0},{5,1},{6,2},{7,3},{8,12},{9,13},{10,... | collective-permute-start | bytes 786440 | tf_op jit(solution)/shard_map/ppermute | solution.py:39
  204.9 160.1 %collective-permute-start.49 = (bf16[2,512,640]{2,1,0:T(8,128)(2,1)}, bf16[2,512,640]{2,1,0:T(8,128)(2,1)}, u32[]{:S(2)}, u32[]{:S(2)}) collective-permute-start(bf16[2,512,640]{2,1,0:T(8,128)(2,1)} %pad_maximum_fusion.3), channel_id=1, source_target_pairs={{0,1},{1,0},{2,3},{3,2},{4,5},{5,4},{6,7},{7,6},{8,9},{9,8},{10,11... | collective-permute-start | bytes 3932168 | tf_op jit(solution)/shard_map/ppermute | solution.py:39
  318.7 16.7 %collective-permute-start.44 = (bf16[4,64,384]{2,1,0:T(8,128)(2,1)}, bf16[4,64,384]{2,1,0:T(8,128)(2,1)}, u32[]{:S(2)}, u32[]{:S(2)}) collective-permute-start(bf16[4,64,384]{2,1,0:T(8,128)(2,1)} %dynamic-slice_bitcast_fusion.11), channel_id=1, source_target_pairs={{0,4},{1,5},{2,6},{3,7},{4,0},{5,1},{6,2},{7,3},{8,12},{9,13},{10,... | collective-permute-start | bytes 589832 | tf_op jit(solution)/shard_map/ppermute | solution.py:39
  319.3 16.7 %collective-permute-start.43 = (bf16[4,64,384]{2,1,0:T(8,128)(2,1)}, bf16[4,64,384]{2,1,0:T(8,128)(2,1)}, u32[]{:S(2)}, u32[]{:S(2)}) collective-permute-start(bf16[4,64,384]{2,1,0:T(8,128)(2,1)} %get-tuple-element.569), channel_id=1, source_target_pairs={{0,2},{1,3},{2,0},{3,1},{4,6},{5,7},{6,4},{7,5},{8,10},{9,11},{10,... | collective-permute-start | bytes 589832 | tf_op jit(solution)/shard_map/ppermute | solution.py:39
  320.8 15.1 %collective-permute-start.45 = (bf16[4,64,384]{2,1,0:T(8,128)(2,1)}, bf16[4,64,384]{2,1,0:T(8,128)(2,1)}, u32[]{:S(2)}, u32[]{:S(2)}) collective-permute-start(bf16[4,64,384]{2,1,0:T(8,128)(2,1)} %get-tuple-element.570), channel_id=1, source_target_pairs={{0,6},{1,7},{2,4},{3,5},{4,2},{5,3},{6,0},{7,1},{8,14},{9,15},{10,... | collective-permute-start | bytes 589832 | tf_op jit(solution)/shard_map/ppermute | solution.py:39
  335.4 35.7 %collective-permute-start.39 = (bf16[1024,512]{1,0:T(8,128)(2,1)S(1)}, bf16[1024,512]{1,0:T(8,128)(2,1)S(1)}, u32[]{:S(2)}, u32[]{:S(2)}) collective-permute-start(bf16[1024,512]{1,0:T(8,128)(2,1)S(1)} %pad_maximum_fusion.12), channel_id=1, source_target_pairs={{0,1},{1,0},{2,3},{3,2},{4,5},{5,4},{6,7},{7,6},{8,9},{9,8},{10,11... | collective-permute-start | bytes 3145736 | tf_op jit(solution)/shard_map/ppermute | solution.py:39
  369.0 15.2 %collective-permute-start.50 = (bf16[4,64,640]{2,1,0:T(8,128)(2,1)}, bf16[4,64,640]{2,1,0:T(8,128)(2,1)S(1)}, u32[]{:S(2)}, u32[]{:S(2)}) collective-permute-start(bf16[4,64,640]{2,1,0:T(8,128)(2,1)} %get-tuple-element.538), channel_id=1, source_target_pairs={{0,2},{1,3},{2,0},{3,1},{4,6},{5,7},{6,4},{7,5},{8,10},{9,11},{10,... | collective-permute-start | bytes 983048 | tf_op jit(solution)/shard_map/ppermute | solution.py:39
  369.7 14.5 %collective-permute-start.52 = (bf16[4,64,640]{2,1,0:T(8,128)(2,1)S(1)}, bf16[4,64,640]{2,1,0:T(8,128)(2,1)}, u32[]{:S(2)}, u32[]{:S(2)}) collective-permute-start(bf16[4,64,640]{2,1,0:T(8,128)(2,1)S(1)} %get-tuple-element.539), channel_id=1, source_target_pairs={{0,6},{1,7},{2,4},{3,5},{4,2},{5,3},{6,0},{7,1},{8,14},{9,15},{10,... | collective-permute-start | bytes 983048 | tf_op jit(solution)/shard_map/ppermute | solution.py:39
  376.4 35.9 %collective-permute-start.41 = (f32[256,100]{0,1:T(8,128)}, f32[256,100]{0,1:T(8,128)}, u32[]{:S(2)}, u32[]{:S(2)}) collective-permute-start(f32[256,100]{0,1:T(8,128)} %bitcast.520), channel_id=1, source_target_pairs={{0,4},{1,5},{2,6},{3,7},{4,0},{5,1},{6,2},{7,3},{8,12},{9,13},{10,... | collective-permute-start | bytes 307208 | tf_op jit(solution)/shard_map/ppermute | solution.py:39
  377.5 34.8 %collective-permute-start.42 = (f32[256,100]{0,1:T(8,128)}, f32[256,100]{0,1:T(8,128)S(1)}, u32[]{:S(2)}, u32[]{:S(2)}) collective-permute-start(f32[256,100]{0,1:T(8,128)} %bitcast.519), channel_id=1, source_target_pairs={{0,6},{1,7},{2,4},{3,5},{4,2},{5,3},{6,0},{7,1},{8,14},{9,15},{10,... | collective-permute-start | bytes 307208 | tf_op jit(solution)/shard_map/ppermute | solution.py:39
  (152 other events, 1080.2 us)

commit v2 on v1

v2 whole, which is shorter than its diff:
```python
import functools

import jax
import jax.numpy as jnp
from jax import lax
from jax.experimental import pallas as pl
from jax.experimental.pallas import tpu as pltpu
from jax.sharding import PartitionSpec as P

HEADS = 4
HEAD = 128
FF = 1024
HID = FF // HEADS
FEAT = 100
PROMPT = 1000
SLOTS = 1024
ADAM_STEP = 10
PAD = 1024
WIDE = 128

ln_eps = 1e-05
neg_big = -1e30
clip_norm = 1.0
beta_one = 0.9
beta_two = 0.999
adam_eps = 1e-08
rate_matrix = 0.15
rate_vector = 0.5
weight_decay = 0.01
AXES = ("ep", "split", "tp")
bf16 = jnp.bfloat16
f32 = jnp.float32
score_scale = HEAD**-0.5


def swap(value, ep=0, split=0, row=0, core=0):
    sizes = [lax.axis_size(a) for a in AXES]
    pairs = []
    for a in range(sizes[0]):
        for b in range(sizes[1]):
            for t in range(sizes[2]):
                other = ((a ^ ep) * sizes[1] + (b ^ split)) * sizes[2] + (t ^ (2 * row + core))
                pairs.append(((a * sizes[1] + b) * sizes[2] + t, other))
    return lax.ppermute(value, AXES, pairs)


def pick(low, high, bit):
    return jnp.where(bit == 0, low, high), jnp.where(bit == 0, high, low)


def plane_swap(piece):
    got = {}
    for b in (0, 1):
        for r in (0, 1):
            sent = piece(b, r)
            got[b, r] = sent if (b, r) == (0, 0) else swap(sent, split=b, row=r)
    return got


def tie(value, other):
    return lax.optimization_barrier((value, other))[0]


def gather_ep(shard, name):
    count = lax.axis_size("ep")
    if count > 4:
        return lax.all_gather(shard, "ep", axis=0)
    parts = [shard] + [swap(shard, ep=k) for k in range(1, count)]
    return place(parts, lax.axis_index("ep"), name)


def reduce_plane(parts, places, name):
    count = parts[0].shape[0]
    if count > 4:
        total = sum(part.astype(f32) for part in parts)
        return [lax.psum_scatter(total, "ep", scatter_dimension=0, tiled=True)[0]]
    pieces = sum_plane(parts, places, name)
    return [pieces[0]] + [swap(pieces[k], ep=k) for k in range(1, count)]


def adam_update(weight, moments, gradient, factor, step_rate, decay_rate):
    clipped = gradient * factor
    first_moment = beta_one * moments[0] + (1.0 - beta_one) * clipped
    second_moment = beta_two * moments[1] + (1.0 - beta_two) * clipped * clipped
    first_hat = first_moment / (1.0 - beta_one**ADAM_STEP)
    second_hat = second_moment / (1.0 - beta_two**ADAM_STEP)
    updated = weight - step_rate * (
        first_hat / (jnp.sqrt(second_hat) + adam_eps) + decay_rate * weight
    )
    return (updated, first_moment, second_moment, updated.astype(bf16))


def dot(a, b, dims):
    return lax.dot_general(a, b, (dims, ((), ())), preferred_element_type=f32)


NN = ((1,), (0,))
NT = ((1,), (1,))
TN = ((0,), (0,))


def cost(micros):
    return pl.CostEstimate(flops=int(micros * 1e9), transcendentals=0, bytes_accessed=int(micros * 3e6))


def whole():
    return pl.BlockSpec(memory_space=pltpu.VMEM)


def shape_of(shape, dtype):
    return jax.ShapeDtypeStruct(shape, dtype)


def project_body(ratio, own, other, enc, vec, wp, bias, prompt, x_ref, q_ref, k_ref, kt_ref, v_ref, vt_ref):
    step = pl.program_id(0)
    rows = jnp.where(step < 2, own[...], other[...])
    low = (ratio[0] * dot(rows, enc[...], NT) + vec[6:7, :]).astype(bf16)
    x_ref[...] = low
    for h in range(2):
        q_ref[h] = (dot(low, wp[h, :, 0:HEAD], NN) + bias[h : h + 1, 0:HEAD]).astype(bf16)

    def keys_from(source):
        for h in range(2):
            key = dot(source, wp[h, :, HEAD : 2 * HEAD], NN).astype(bf16)
            shift = bias[h : h + 1, HEAD : 2 * HEAD]
            value = (dot(source, wp[h, :, 2 * HEAD : 3 * HEAD], NN) + shift).astype(bf16)
            k_ref[h] = key
            v_ref[h] = value
            kt_ref[h] = key.T
            vt_ref[h] = value.T

    @pl.when(step % 2 == 0)
    def _():
        keys_from(low)

    @pl.when(step % 2 == 1)
    def _():
        keys_from(prompt[...].T)


def project(ratio, own, other, enc, vec, wp, bias, prompt):
    half = own.shape[0] // 2
    width = enc.shape[0]
    keys = PAD + SLOTS
    spot = lambda i: jnp.where(i % 2 == 0, 2 + i // 2, i // 2)
    tall = pl.BlockSpec((2, half, HEAD), lambda i: (0, spot(i), 0))
    flat = pl.BlockSpec((2, HEAD, half), lambda i: (0, 0, spot(i)))
    return pl.pallas_call(
        project_body,
        grid=(4,),
        in_specs=[
            pl.BlockSpec(memory_space=pltpu.SMEM),
            pl.BlockSpec((half, WIDE), lambda i: (jnp.minimum(i, 1), 0)),
            pl.BlockSpec((half, WIDE), lambda i: (jnp.maximum(i - 2, 0), 0)),
            whole(),
            whole(),
            whole(),
            whole(),
            pl.BlockSpec((width, half), lambda i: (0, i // 2)),
        ],
        out_specs=[
            pl.BlockSpec((half, width), lambda i: (i, 0)),
            pl.BlockSpec((2, half, HEAD), lambda i: (0, i, 0)),
            tall,
            flat,
            tall,
            flat,
        ],
        out_shape=[
            shape_of((4 * half, width), bf16),
            shape_of((2, 4 * half, HEAD), bf16),
            shape_of((2, keys, HEAD), bf16),
            shape_of((2, HEAD, keys), bf16),
            shape_of((2, keys, HEAD), bf16),
            shape_of((2, HEAD, keys), bf16),
        ],
        cost_estimate=cost(9),
        name="project",
    )(ratio, own, other, enc, vec, wp, bias, prompt)


def attend_body(q_ref, k_ref, vt_ref, bias_ref, o_ref, lse_ref):
    scores = dot(k_ref[0], q_ref[0], NT) * score_scale + bias_ref[...]
    top = jnp.max(scores, axis=0, keepdims=True)
    raised = jnp.exp(scores - top)
    total = jnp.sum(raised, axis=0, keepdims=True)
    out = dot(vt_ref[0], raised.astype(bf16), NN) / total
    o_ref[...] = out.T.astype(bf16)
    lse_ref[0] = top + jnp.log(total)


def attend(q, k, vt, bias, which):
    size = 512
    blocks = SLOTS // size
    keys = k.shape[1]
    return pl.pallas_call(
        attend_body,
        grid=(2, blocks),
        in_specs=[
            pl.BlockSpec((1, size, HEAD), lambda h, i: (h, which * blocks + i, 0)),
            pl.BlockSpec((1, keys, HEAD), lambda h, i: (h, 0, 0)),
            pl.BlockSpec((1, HEAD, keys), lambda h, i: (h, 0, 0)),
            pl.BlockSpec((keys, 1), lambda h, i: (0, 0)),
        ],
        out_specs=[
            pl.BlockSpec((size, HEAD), lambda h, i: (i, h)),
            pl.BlockSpec((1, 1, size), lambda h, i: (h, 0, i)),
        ],
        out_shape=[shape_of((SLOTS, 2 * HEAD), bf16), shape_of((2, 1, SLOTS), f32)],
        cost_estimate=cost(10),
        name="attend",
    )(q, k, vt, bias)


def attend_back_body(q_ref, k_ref, kt_ref, v_ref, bias_ref, la_ref, lb_ref, da_ref, db_ref, dq_ref, dk_ref, dv_ref):
    step = pl.program_id(1)
    mine = step < 2
    query = q_ref[0]
    grad = jnp.where(mine, da_ref[...], db_ref[...])
    lse = jnp.where(mine, la_ref[0], lb_ref[0])
    probs = jnp.exp(dot(k_ref[0], query, NT) * score_scale + (bias_ref[...] - lse))
    grad_probs = dot(v_ref[0], grad, NT)
    delta = jnp.sum(probs * grad_probs, axis=0, keepdims=True)
    grad_scores = (probs * (grad_probs - delta)).astype(bf16)
    back = dot(kt_ref[0], grad_scores, NN) * score_scale
    dq_ref[...] = back.T.astype(bf16)
    grad_key = dot(grad_scores, query, NN) * score_scale
    grad_value = dot(probs.astype(bf16), grad, NN)

    @pl.when(step == 0)
    def _():
        dk_ref[0] = grad_key
        dv_ref[0] = grad_value

    @pl.when(step > 0)
    def _():
        dk_ref[0] += grad_key
        dv_ref[0] += grad_value


def attend_back(q, k, kt, v, bias, lse_own, lse_other, grad_own, grad_other):
    size = 512
    keys = k.shape[1]
    tall = pl.BlockSpec((1, keys, HEAD), lambda h, i: (h, 0, 0))
    first = lambda i: jnp.minimum(i, 1)
    second = lambda i: jnp.maximum(i - 2, 0)
    return pl.pallas_call(
        attend_back_body,
        grid=(2, 2 * SLOTS // size),
        in_specs=[
            pl.BlockSpec((1, size, HEAD), lambda h, i: (h, i, 0)),
            tall,
            pl.BlockSpec((1, HEAD, keys), lambda h, i: (h, 0, 0)),
            tall,
            pl.BlockSpec((keys, 1), lambda h, i: (0, 0)),
            pl.BlockSpec((1, 1, size), lambda h, i: (h, 0, first(i))),
            pl.BlockSpec((1, 1, size), lambda h, i: (h, 0, second(i))),
            pl.BlockSpec((size, HEAD), lambda h, i: (first(i), h)),
            pl.BlockSpec((size, HEAD), lambda h, i: (second(i), h)),
        ],
        out_specs=[pl.BlockSpec((size, HEAD), lambda h, i: (i, h)), tall, tall],
        out_shape=[
            shape_of((2 * SLOTS, 2 * HEAD), bf16),
            shape_of((2, keys, HEAD), f32),
            shape_of((2, keys, HEAD), f32),
        ],
        cost_estimate=cost(32),
        name="attend_back",
    )(q, k, kt, v, bias, lse_own, lse_other, grad_own, grad_other)


erfc_terms = (
    -1.26551223,
    1.00002368,
    0.37409196,
    0.09678418,
    -0.18628806,
    0.27886807,
    -1.13520398,
    1.48851587,
    -0.82215223,
    0.17087277,
)


def gelu_pair(t):
    z = jnp.abs(t) * (0.5**0.5)
    k = 1.0 / (1.0 + 0.5 * z)
    series = jnp.full_like(t, erfc_terms[-1])
    for term in erfc_terms[-2::-1]:
        series = series * k + term
    tail = 0.5 * k * jnp.exp(series - z * z)
    cumulative = jnp.where(t >= 0.0, 1.0 - tail, tail)
    density = jnp.exp(-0.5 * t * t) * 0.3989422804014327
    return t * cumulative, cumulative + t * density


def middle_body(
    sc,
    ratio,
    rows_ref,
    oa_ref,
    ob_ref,
    c0,
    c1,
    c2,
    c3,
    enc,
    vec,
    b1,
    ra,
    rb,
    y0,
    y1,
    y2,
    y3,
    da_ref,
    db_ref,
    dr_ref,
    ga,
    gb,
    gvec,
    gb1,
    cot,
    acc,
):
    step = pl.program_id(0)
    count = rows_ref.shape[0]
    for k, ref in enumerate((c0, c1, c2, c3)):

        @pl.when(step == k)
        def _(ref=ref):
            cot[...] = ref[...]

    @pl.when(step == 0)
    def _():
        acc[...] = jnp.zeros_like(acc)
        gvec[...] = jnp.zeros_like(gvec)
        gb1[...] = jnp.zeros_like(gb1)

    group = sc[0] ^ (step // 2)
    quarter = 2 * (sc[1] ^ (step % 2)) + sc[2]
    limit = jnp.where(group == 0, sc[4], sc[5])
    slot = quarter * count + lax.broadcasted_iota(jnp.int32, (count, 1), 0)
    live = (slot < limit).astype(f32)

    def weight(k, low, high):
        return (ra if k < 2 else rb)[k % 2, :, low:high]

    def row(k):
        return vec[k : k + 1, :]

    gain_one, shift_one, gain_two, shift_two, b_out, b_two, b_enc = (row(k) for k in range(7))
    embedded = ratio[0] * dot(rows_ref[...], enc[...], NT) + b_enc
    out_pair = [
        jnp.concatenate([weight(2 * k, 0, HEAD), weight(2 * k + 1, 0, HEAD)], axis=1)
        for k in (0, 1)
    ]
    attn = dot(oa_ref[...], out_pair[0], NT) + dot(ob_ref[...], out_pair[1], NT) + b_out

    def norm(residual):
        centred = residual - jnp.mean(residual, axis=-1, keepdims=True)
        inverse = lax.rsqrt(jnp.mean(centred * centred, axis=-1, keepdims=True) + ln_eps)
        return centred * inverse, inverse

    def back(grad, normed, inverse, gain):
        scaled = grad * gain
        plain = jnp.mean(scaled, axis=-1, keepdims=True)
        mixed = jnp.mean(scaled * normed, axis=-1, keepdims=True)
        return inverse * (scaled - plain - normed * mixed)

    def add_row(k, value):
        gvec[k : k + 1, :] += jnp.sum(value, axis=0, keepdims=True)

    normed_one, inverse_one = norm(embedded + attn)
    first = normed_one * gain_one + shift_one
    first_low = first.astype(bf16)
    mlp = b_two
    acts, slopes = [], []
    for k in range(4):
        pre = dot(first_low, weight(k, HEAD, HEAD + HID), NN) + b1[k : k + 1, 2 * HEAD :]
        act, slope = gelu_pair(pre)
        acts.append(act.astype(bf16))
        slopes.append(slope)
        mlp = mlp + dot(acts[k], weight(k, HEAD + HID, HEAD + 2 * HID), NT)
    normed_two, inverse_two = norm(first + mlp)
    out = ((normed_two * gain_two + shift_two) * live).astype(bf16)
    for k, ref in enumerate((y0, y1, y2, y3)):

        @pl.when(step == k)
        def _(ref=ref):
            ref[...] = out

    grad_y = cot[...].astype(f32) * live
    add_row(2, grad_y * normed_two)
    add_row(3, grad_y)
    grad_two = back(grad_y, normed_two, inverse_two, gain_two)
    grad_low = grad_two.astype(bf16)
    add_row(5, grad_low.astype(f32))
    grad_flip = grad_low.T
    first_flip = first_low.T
    grad_first = grad_two
    for k in range(4):
        acc[k, :, HEAD + HID :] += dot(grad_flip, acts[k], NN)
        grad_act = dot(grad_low, weight(k, HEAD + HID, HEAD + 2 * HID), NN)
        grad_pre = (grad_act * slopes[k]).astype(bf16)
        gb1[k : k + 1, :] += jnp.sum(grad_pre.astype(f32), axis=0, keepdims=True)
        acc[k, :, HEAD : HEAD + HID] += dot(first_flip, grad_pre, NN)
        grad_first = grad_first + dot(grad_pre, weight(k, HEAD, HEAD + HID), NT)
    add_row(0, grad_first * normed_one)
    add_row(1, grad_first)
    grad_one = back(grad_first, normed_one, inverse_one, gain_one)
    dr_ref[...] = grad_one
    attn_low = grad_one.astype(bf16)
    add_row(4, attn_low.astype(f32))
    attn_flip = attn_low.T
    for k, (source, target) in enumerate(((oa_ref, da_ref), (ob_ref, db_ref))):
        both = dot(attn_flip, source[...], NN)
        acc[2 * k, :, 0:HEAD] += both[:, 0:HEAD]
        acc[2 * k + 1, :, 0:HEAD] += both[:, HEAD:]
        target[...] = dot(attn_low, out_pair[k], NN).astype(bf16)

    @pl.when(step == 3)
    def _():
        ga[...] = acc[0:2].astype(bf16)
        gb[...] = acc[2:4].astype(bf16)


def middle(sc, ratio, rows, o_own, o_other, cots, enc, vec, b1, rest_own, rest_other):
    size = rows.shape[0] // 4
    width = enc.shape[0]
    spot = lambda i, sc: (2 * (sc[0] ^ (i // 2)) + (sc[1] ^ (i % 2)), 0)
    pair = pl.BlockSpec((size, 2 * HEAD), spot)
    smem = pl.BlockSpec(memory_space=pltpu.SMEM)
    fixed = pl.BlockSpec((size, width), lambda i, sc: (0, 0))
    weight = rest_own.shape
    return pl.pallas_call(
        middle_body,
        grid_spec=pltpu.PrefetchScalarGridSpec(
            num_scalar_prefetch=1,
            grid=(4,),
            in_specs=[smem, pl.BlockSpec((size, WIDE), spot), pair, pair]
            + [fixed] * 4
            + [whole()] * 5,
            out_specs=[fixed] * 4
            + [pair, pair, pl.BlockSpec((size, width), spot)]
            + [
                pl.BlockSpec(weight, lambda i, sc: (0, 0, 0)),
                pl.BlockSpec(weight, lambda i, sc: (0, 0, 0)),
                pl.BlockSpec((8, width), lambda i, sc: (0, 0)),
                pl.BlockSpec((4, HID), lambda i, sc: (0, 0)),
            ],
            scratch_shapes=[
                pltpu.VMEM((size, width), bf16),
                pltpu.VMEM((4,) + weight[1:], f32),
            ],
        ),
        out_shape=[shape_of((size, width), bf16)] * 4
        + [
            shape_of((4 * size, 2 * HEAD), bf16),
            shape_of((4 * size, 2 * HEAD), bf16),
            shape_of((4 * size, width), f32),
            shape_of(weight, bf16),
            shape_of(weight, bf16),
            shape_of((8, width), f32),
            shape_of((4, HID), f32),
        ],
        cost_estimate=cost(25),
        name="middle",
    )(sc, ratio, rows, o_own, o_other, *cots, enc, vec, b1, rest_own, rest_other)


def simple(body, out_shape, *args, scalars=None, scratch=(), name=None):
    specs = [whole()] * len(args)
    if scalars is not None:
        specs = [pl.BlockSpec(memory_space=pltpu.SMEM)] + specs
        args = (scalars,) + args
    many = isinstance(out_shape, (list, tuple))
    return pl.pallas_call(
        body,
        in_specs=specs,
        out_specs=[whole()] * len(out_shape) if many else whole(),
        out_shape=out_shape,
        scratch_shapes=scratch,
        cost_estimate=cost(2),
        name=name,
    )(*args)


def place(parts, index, name):
    def body(sc, *refs):
        for k, ref in enumerate(refs[:-1]):
            refs[-1][sc[0] ^ k] = ref[...]

    first = parts[0]
    return simple(
        body,
        shape_of((len(parts),) + first.shape, first.dtype),
        *parts,
        scalars=index.reshape(1).astype(jnp.int32),
        name=name,
    )


TAIL = 3 * HEAD
VEC = 104


def with_bias(prompt, bias):
    wide = jnp.pad(prompt, [(0, 0)] * (prompt.ndim - 1) + [(0, 3 * TAIL - prompt.shape[-1])])
    row = jnp.pad(
        bias[..., None, :].astype(prompt.dtype),
        [(0, 0)] * (bias.ndim - 1)
        + [(0, prompt.shape[-2] - 1), (PAD, 3 * TAIL - PAD - bias.shape[-1])],
    )
    return wide + row


def in_chunks(wide):
    lead, strip = wide.shape[:-2], wide.shape[-2]
    parts = jnp.swapaxes(wide.reshape(lead + (strip, 3, TAIL)), -3, -2)
    return parts.reshape(lead + (3 * strip, TAIL))


def small_tile(encoder, vectors):
    return jnp.concatenate(
        [
            jnp.pad(encoder, ((0, 0), (0, VEC - FEAT))),
            jnp.pad(vectors, ((0, 0), (0, WIDE - VEC - 7))),
        ],
        axis=1,
    )


def pack_parts(block, prompt, encoder, vectors, biases):
    slab, strip = block.shape[0], prompt.shape[0]
    flat = block.reshape(slab * 8, HEAD)
    out = [shape_of((slab + 4 * strip, TAIL), bf16), shape_of((slab, 8 * HEAD - TAIL), bf16)]
    if 2 * slab != WIDE:
        low = block.reshape(slab, 8 * HEAD).astype(bf16)
        chunks = in_chunks(with_bias(prompt.astype(bf16), biases[:, 0]))
        small = jnp.pad(small_tile(encoder, vectors), ((0, 0), (0, TAIL - WIDE))).astype(bf16)
        return jnp.concatenate([low[:, 0:TAIL], chunks, small], axis=0), low[:, TAIL:]

    def body(block_ref, prompt_ref, enc_ref, vec_ref, bias_ref, main_ref, rest_ref, tall, tile):
        for j in range(8):
            lanes = block_ref[pl.ds(j, slab, stride=8), :].astype(bf16)
            if j < 3:
                main_ref[0:slab, j * HEAD : (j + 1) * HEAD] = lanes
            else:
                rest_ref[:, (j - 3) * HEAD : (j - 2) * HEAD] = lanes
        low = prompt_ref[...].astype(bf16)
        for k in range(2):
            rows = slice(slab + k * strip, slab + (k + 1) * strip)
            main_ref[rows, :] = low[:, k * TAIL : (k + 1) * TAIL]
        rows = slice(slab + 2 * strip, slab + 3 * strip)
        main_ref[rows, WIDE : 2 * WIDE] = jnp.zeros((strip, WIDE), bf16)
        main_ref[rows, 0 : PROMPT - 2 * TAIL] = low[:, 2 * TAIL :]
        tile[...] = jnp.zeros_like(tile)
        tile[0:1, 0:slab] = bias_ref[...]
        main_ref[rows, 2 * WIDE :] = tile[...].astype(bf16)
        tall[...] = jnp.zeros_like(tall)
        tall[VEC : VEC + 7, :] = vec_ref[...]
        tile[...] = tall[...].T
        tile[:, 0:FEAT] = enc_ref[...]
        rows = slice(slab + 3 * strip, slab + 4 * strip)
        main_ref[rows, 0:WIDE] = tile[...].astype(bf16)
        main_ref[rows, WIDE:] = jnp.zeros((strip, TAIL - WIDE), bf16)

    return simple(
        body,
        out,
        flat,
        prompt,
        encoder,
        vectors.T,
        biases.T,
        scratch=[pltpu.VMEM((WIDE, strip), f32), pltpu.VMEM((strip, WIDE), f32)],
        name="pack_parts",
    )


def unpack_main(tops, lows, places, slab, strip):
    n_ep = tops[0].shape[0]
    if 2 * slab != WIDE:
        side, row, core = places[0], places[1], places[2]

        def ordered(parts, axis):
            cores = []
            for group in parts:
                sides = []
                for b in (0, 1):
                    sides.append(jnp.stack(pick(group[2 * b], group[2 * b + 1], row), axis=axis))
                cores.append(jnp.stack(pick(sides[0], sides[1], side), axis=axis))
            return jnp.stack(pick(cores[0], cores[1], core), axis=axis + 2)

        heads = [
            jnp.stack(pick(tops[r][:, 0:slab], tops[2 + r][:, 0:slab], side), axis=1) for r in (0, 1)
        ]
        whole_low = ordered([[t[:, slab:] for t in tops], [t[:, slab:] for t in lows]], 1)
        chunks = whole_low[..., 0 : 3 * strip, :].reshape((n_ep, 2, 2, 2, 3, strip, TAIL))
        wide = jnp.swapaxes(chunks, -3, -2).reshape((n_ep, 2, 2, 2, strip, 3 * TAIL))
        small = whole_low[..., 3 * strip :, 0:WIDE]
        vec = small.reshape(n_ep * 8 * strip, WIDE).astype(f32).T[VEC : VEC + 8]
        biases = []
        for group in (tops, lows):
            for r in (0, 1):
                spot = slab + 2 * strip
                pair = [
                    group[2 * b + r][:, spot, PAD - 2 * TAIL : PAD - 2 * TAIL + slab] for b in (0, 1)
                ]
                biases.append(jnp.stack(pick(pair[0], pair[1], side), axis=1).reshape(-1))
        return jnp.stack(heads), wide, small, vec, jnp.stack(biases).astype(f32)

    def body(sc, t0, t1, t2, t3, l0, l1, l2, l3, wp_ref, prompt_ref, small_ref, vec_ref, bias_ref):
        side, row, core = sc[0], sc[1], sc[2]
        refs = (t0, t1, t2, t3)
        low_refs = (l0, l1, l2, l3)
        bias_tiles = {}
        for b in range(2):
            for r in range(2):
                k = 2 * b + r
                wp_ref[r, :, side ^ b] = refs[k][:, 0:slab, :]
                for other in range(2):
                    spot = core ^ other
                    part = (low_refs if other else refs)[k][:, slab:, :]
                    for j in range(3):
                        lanes = slice(j * TAIL, (j + 1) * TAIL)
                        rows = slice(j * strip, (j + 1) * strip)
                        prompt_ref[:, side ^ b, row ^ r, spot, :, lanes] = part[:, rows, :]
                    small_ref[:, side ^ b, row ^ r, spot] = part[:, 3 * strip :, 0:WIDE]
                    bias_tiles[b, r, other] = part[:, 2 * strip : 2 * strip + 8, TAIL - WIDE :].astype(f32)
        flip = small_ref[...].reshape(n_ep * 8 * strip, WIDE).astype(f32).T
        vec_ref[...] = flip[VEC : VEC + 8]
        low_half = lax.broadcasted_iota(jnp.int32, (1, WIDE), 1) < slab
        for r in range(2):
            for other in range(2):
                for e in range(n_ep):
                    mine = bias_tiles[0, r, other][e, 0:1]
                    theirs = bias_tiles[1, r, other][e, 0:1]
                    first = jnp.where(side == 0, mine, theirs)
                    second = jnp.where(side == 0, theirs, mine)
                    row_tile = jnp.where(low_half, first, pltpu.roll(second, slab, 1))
                    k = r + 2 * other
                    bias_ref[k : k + 1, e * WIDE : (e + 1) * WIDE] = row_tile

    return simple(
        body,
        [
            shape_of((2, n_ep, 2, slab, TAIL), bf16),
            shape_of((n_ep, 2, 2, 2, strip, 3 * TAIL), bf16),
            shape_of((n_ep, 2, 2, 2, strip, WIDE), bf16),
            shape_of((8, n_ep * 2 * slab), f32),
            shape_of((4, n_ep * 2 * slab), f32),
        ],
        *tops,
        *lows,
        scalars=places,
        name="unpack_main",
    )


def unpack_rest(tops, places):
    n_ep, slab, width = tops[0].shape

    def body(sc, t0, t1, t2, t3, out_ref):
        for k, ref in enumerate((t0, t1, t2, t3)):
            out_ref[k % 2, :, sc[0] ^ (k // 2)] = ref[...]

    return simple(
        body, shape_of((2, n_ep, 2, slab, width), bf16), *tops, scalars=places, name="unpack_rest"
    )


def back_body(order, dq_ref, dk_ref, dv_ref, wp, other_ref, own_ref):
    step = pl.program_id(0)

    def columns(k):
        return jnp.concatenate([wp[h, :, k * HEAD : (k + 1) * HEAD] for h in range(2)], axis=1)

    def both(ref):
        return jnp.concatenate([ref[h].astype(bf16) for h in range(2)], axis=1)

    base = dot(dq_ref[...], columns(0), NT)

    def store(value):
        @pl.when(step < 2)
        def _():
            other_ref[...] = value.astype(bf16)

        @pl.when(step >= 2)
        def _():
            own_ref[...] = value

    @pl.when(step % 2 == 0)
    def _():
        store(base + dot(both(dk_ref), columns(1), NT) + dot(both(dv_ref), columns(2), NT))

    @pl.when(step % 2 == 1)
    def _():
        store(base)


def back_rows(dq, dk, dv, wp):
    half = dq.shape[0] // 4
    width = wp.shape[1]
    turn = lambda i: (i + 2) % 4
    key = pl.BlockSpec((2, half, HEAD), lambda i: (0, 3 - i // 2, 0))
    return pl.pallas_call(
        functools.partial(back_body, None),
        grid=(4,),
        in_specs=[pl.BlockSpec((half, 2 * HEAD), lambda i: (turn(i), 0)), key, key, whole()],
        out_specs=[
            pl.BlockSpec((half, width), lambda i: (jnp.minimum(i, 1), 0)),
            pl.BlockSpec((half, width), lambda i: (jnp.maximum(i - 2, 0), 0)),
        ],
        out_shape=[shape_of((2 * half, width), bf16), shape_of((2 * half, width), f32)],
        cost_estimate=cost(6),
        name="back_rows",
    )(dq, dk, dv, wp)


def weight_body(x_ref, dq_ref, dk_ref, dv_ref, prompt, wp, gb1, gw_ref, gp_ref, gb_ref, acc, gq_ref, gv_ref):
    step = pl.program_id(0)

    @pl.when(step == 0)
    def _():
        acc[...] = jnp.zeros_like(acc)
        gq_ref[...] = jnp.zeros_like(gq_ref)
        gv_ref[...] = jnp.zeros_like(gv_ref)

    flip = x_ref[...].T
    acc[0] += dot(flip, dq_ref[...], NN)
    gq_ref[...] += jnp.sum(dq_ref[...].astype(f32), axis=0, keepdims=True)
    grad_key = jnp.concatenate([dk_ref[h] for h in range(2)], axis=1)
    grad_value = jnp.concatenate([dv_ref[h] for h in range(2)], axis=1)
    key_high = grad_key.astype(bf16)
    value_high = grad_value.astype(bf16)

    @pl.when(step % 2 == 0)
    def _():
        acc[1] += dot(flip, key_high, NN)
        acc[2] += dot(flip, value_high, NN)
        gv_ref[...] += jnp.sum(value_high.astype(f32), axis=0, keepdims=True)

    @pl.when(step % 2 == 1)
    def _():
        key_low = (grad_key - key_high.astype(f32)).astype(bf16)
        value_low = (grad_value - value_high.astype(f32)).astype(bf16)
        source = prompt[...]
        acc[1] += dot(source, key_high, NN) + dot(source, key_low, NN)
        acc[2] += dot(source, value_high, NN) + dot(source, value_low, NN)
        gv_ref[...] += jnp.sum(grad_value, axis=0, keepdims=True)
        w_key, w_value = (
            jnp.concatenate([wp[h, :, k * HEAD : (k + 1) * HEAD] for h in range(2)], axis=1)
            for k in (1, 2)
        )
        total = dot(w_key, key_high, NT) + dot(w_key, key_low, NT)
        total = total + dot(w_value, value_high, NT) + dot(w_value, value_low, NT)
        gp_ref[...] = total.astype(bf16)

    @pl.when(step == 3)
    def _():
        for h in range(2):
            for k in range(3):
                lanes = slice(h * HEAD, (h + 1) * HEAD)
                gw_ref[h, :, k * HEAD : (k + 1) * HEAD] = acc[k, :, lanes].astype(bf16)
            gb_ref[h : h + 1, 0:HEAD] = gq_ref[:, h * HEAD : (h + 1) * HEAD]
            gb_ref[h : h + 1, HEAD : 2 * HEAD] = gv_ref[:, h * HEAD : (h + 1) * HEAD]
        gb_ref[2:4, 0 : 2 * HEAD] = jnp.zeros((2, 2 * HEAD), f32)
        gb_ref[:, 2 * HEAD :] = gb1[...]


def weight_grads(x, dq, dk, dv, prompt, wp, gb1):
    half = dq.shape[0] // 4
    width = wp.shape[1]
    spot = lambda i: jnp.where(i % 2 == 0, 2 + i // 2, i // 2)
    key = pl.BlockSpec((2, half, HEAD), lambda i: (0, spot(i), 0))
    return pl.pallas_call(
        weight_body,
        grid=(4,),
        in_specs=[
            pl.BlockSpec((half, width), lambda i: (i, 0)),
            pl.BlockSpec((half, 2 * HEAD), lambda i: (i, 0)),
            key,
            key,
            pl.BlockSpec((width, half), lambda i: (0, i // 2)),
            whole(),
            whole(),
        ],
        out_specs=[
            pl.BlockSpec((2, width, TAIL), lambda i: (0, 0, 0)),
            pl.BlockSpec((width, half), lambda i: (0, i // 2)),
            pl.BlockSpec((4, width), lambda i: (0, 0)),
        ],
        out_shape=[
            shape_of((2, width, TAIL), bf16),
            shape_of((width, PAD), bf16),
            shape_of((4, width), f32),
        ],
        scratch_shapes=[pltpu.VMEM((3, width, 2 * HEAD), f32)]
        + [pltpu.VMEM((1, 2 * HEAD), f32)] * 2,
        cost_estimate=cost(9),
        name="weight_grads",
    )(x, dq, dk, dv, prompt, wp, gb1)


def input_body(sc, ratio, dr_ref, own_ref, got_ref, rows_ref, enc, mask, rows_grad, i0, i1, i2, i3, small_ref, acc, bias):
    step = pl.program_id(0)
    low = (dr_ref[...] + own_ref[...] + got_ref[...].astype(f32)).astype(bf16)
    part = dot(low.T, rows_ref[...], NN) * ratio[0]
    part_bias = jnp.sum(low.astype(f32), axis=0, keepdims=True)

    @pl.when(step == 0)
    def _():
        acc[...] = part
        bias[...] = part_bias

    @pl.when(step > 0)
    def _():
        acc[...] += part
        bias[...] += part_bias

    grad = dot(enc[...].T, low, NT) * ratio[0] * mask[...]
    for k, ref in enumerate((i0, i1, i2, i3)):

        @pl.when(step == k)
        def _(ref=ref):
            ref[...] = grad[0:VEC]

    @pl.when(step == 3)
    def _():
        width = acc.shape[0]
        rows = jnp.concatenate(
            [
                jnp.zeros((VEC, width), f32),
                rows_grad[0:6],
                bias[...],
                jnp.zeros((WIDE - VEC - 7, width), f32),
            ],
            axis=0,
        )
        small_ref[...] = (acc[...] + rows.T).astype(bf16)


def input_grads(sc, ratio, dr, own, got, rows, enc, mask, rows_grad):
    size = rows.shape[0] // 4
    width = enc.shape[0]
    spot = lambda i, sc: (2 * (sc[0] ^ (i // 2)) + (sc[1] ^ (i % 2)), 0)
    block = pl.BlockSpec((size, width), spot)
    fixed = pl.BlockSpec((VEC, size), lambda i, sc: (0, 0))
    return pl.pallas_call(
        input_body,
        grid_spec=pltpu.PrefetchScalarGridSpec(
            num_scalar_prefetch=1,
            grid=(4,),
            in_specs=[
                pl.BlockSpec(memory_space=pltpu.SMEM),
                block,
                block,
                block,
                pl.BlockSpec((size, WIDE), spot),
                whole(),
                whole(),
                whole(),
            ],
            out_specs=[fixed] * 4 + [pl.BlockSpec((width, WIDE), lambda i, sc: (0, 0))],
            scratch_shapes=[pltpu.VMEM((width, WIDE), f32), pltpu.VMEM((1, width), f32)],
        ),
        out_shape=[shape_of((VEC, size), f32)] * 4 + [shape_of((width, WIDE), bf16)],
        cost_estimate=cost(6),
        name="input_grads",
    )(sc, ratio, dr, own, got, rows, enc, mask, rows_grad)


def split_prompt(grad, bias_rows, places, n_ep, strip):
    blocks = grad.reshape(n_ep, 2, 2, 2, strip, PAD)
    if 8 * strip != WIDE:
        row, core = places[1], places[2]
        table = bias_rows.reshape(2, 2, n_ep, 2, 4 * strip)
        both = []
        for other in (0, 1):
            by_row = jnp.stack(pick(table[other, 0], table[other, 1], row), axis=2)
            part = lax.dynamic_index_in_dim(blocks, core ^ other, 3, keepdims=False)
            both.append(in_chunks(with_bias(part, by_row)))
        return both

    def body(sc, grad_ref, bias_ref, mine_ref, sent_ref):
        row, core = sc[1], sc[2]
        first = lax.broadcasted_iota(jnp.int32, (strip, WIDE), 0) == 0
        low_half = lax.broadcasted_iota(jnp.int32, (1, WIDE), 1) < 4 * strip
        for s in range(2):
            for r in range(2):
                for other, ref in enumerate((mine_ref, sent_ref)):
                    for j in range(3):
                        rows = slice(j * strip, (j + 1) * strip)
                        high = min(PAD, (j + 1) * TAIL)
                        part = grad_ref[:, s, row ^ r, core ^ other, :, j * TAIL : high]
                        ref[:, s, row ^ r, rows, 0 : high - j * TAIL] = part
                    for e in range(n_ep):
                        k = r + 2 * other
                        tile = bias_ref[k : k + 1, e * WIDE : (e + 1) * WIDE]
                        if s == 1:
                            tile = pltpu.roll(tile, WIDE - 4 * strip, 1)
                        tile = jnp.where(low_half, tile, 0.0)
                        tile = jnp.where(first, tile, 0.0).astype(bf16)
                        ref[e, s, row ^ r, 2 * strip : 3 * strip, PAD - 2 * TAIL :] = tile

    shape = shape_of((n_ep, 2, 2, 3 * strip, TAIL), bf16)
    return simple(body, [shape, shape], blocks, bias_rows, scalars=places, name="split_prompt")


def split_small(grad, places, n_ep, strip):
    blocks = grad.reshape(n_ep * 4, 2, strip, WIDE)

    def body(sc, grad_ref, mine_ref, sent_ref):
        mine_ref[...] = grad_ref[:, sc[2]]
        sent_ref[...] = grad_ref[:, 1 - sc[2]]

    shape = shape_of((n_ep * 4, strip, WIDE), bf16)
    return simple(body, [shape, shape], blocks, scalars=places, name="split_small")


def pack_main(gw, mine, got, small_mine, small_got, places, slab, strip):
    n_ep = mine.shape[0]
    heads = gw.reshape(2, n_ep, 2, slab, TAIL)
    small_mine = small_mine.reshape(n_ep, 2, 2, strip, WIDE)
    small_got = small_got.reshape(n_ep, 2, 2, strip, WIDE)
    if 2 * slab != WIDE:
        pair = (mine.astype(f32) + got.astype(f32)).astype(bf16)
        small = (small_mine.astype(f32) + small_got.astype(f32)).astype(bf16)
        small = jnp.pad(small, [(0, 0)] * 4 + [(0, TAIL - WIDE)])
        low = jnp.concatenate([pair, small], axis=3)
        outs = []
        for b in (0, 1):
            for r in (0, 1):
                side, row = places[0] ^ b, places[1] ^ r
                part = lax.dynamic_index_in_dim(low, side, 1, keepdims=False)
                part = lax.dynamic_index_in_dim(part, row, 1, keepdims=False)
                head = lax.dynamic_index_in_dim(heads[r], side, 1, keepdims=False)
                outs.append(jnp.concatenate([head, part], axis=1))
        return outs

    def body(sc, gw_ref, a_ref, b_ref, c_ref, d_ref, *outs):
        for b in range(2):
            for r in range(2):
                out = outs[2 * b + r]
                side, row = sc[0] ^ b, sc[1] ^ r
                out[:, 0:slab, :] = gw_ref[r, :, side]
                pair = a_ref[:, side, row].astype(f32) + b_ref[:, side, row].astype(f32)
                out[:, slab : slab + 3 * strip, :] = pair.astype(bf16)
                pair = c_ref[:, side, row].astype(f32) + d_ref[:, side, row].astype(f32)
                out[:, slab + 3 * strip :, 0:WIDE] = pair.astype(bf16)
                out[:, slab + 3 * strip :, WIDE:] = jnp.zeros((n_ep, strip, TAIL - WIDE), bf16)

    shape = shape_of((n_ep, slab + 4 * strip, TAIL), bf16)
    return simple(
        body, [shape] * 4, heads, mine, got, small_mine, small_got, scalars=places, name="pack_main"
    )


def pack_rest(mine, got, places, n_ep, slab):
    width = mine.shape[-1]
    mine = mine.reshape(2, n_ep, 2, slab, width)
    got = got.reshape(2, n_ep, 2, slab, width)

    def body(sc, a_ref, b_ref, *outs):
        for b in range(2):
            for r in range(2):
                pair = a_ref[r, :, sc[0] ^ b].astype(f32) + b_ref[r, :, sc[0] ^ b].astype(f32)
                outs[2 * b + r][...] = pair.astype(bf16)

    shape = shape_of((n_ep, slab, width), bf16)
    return simple(body, [shape] * 4, mine, got, scalars=places, name="pack_rest")


def sum_plane(parts, places, name):
    n_ep = parts[0].shape[0]

    def body(sc, *refs):
        ins, outs = refs[: len(parts)], refs[len(parts) :]
        for k, out in enumerate(outs):
            spot = sc[6] ^ k
            total = ins[0][spot].astype(f32)
            for ref in ins[1:]:
                total = total + ref[spot].astype(f32)
            out[...] = total.astype(bf16)

    shape = shape_of(parts[0].shape[1:], bf16)
    return simple(body, [shape] * n_ep, *parts, scalars=places, name=name)


def final_sums(mains, rests, slab, strip):
    def body(*refs):
        main_refs, rest_refs = refs[: len(mains)], refs[len(mains) : len(mains) + len(rests)]
        block_ref, prompt_ref, small_ref, bias_ref, square_ref = refs[len(mains) + len(rests) :]

        def added(group):
            total = group[0][...].astype(f32)
            for ref in group[1:]:
                total = total + ref[...].astype(f32)
            return total

        main, rest = added(main_refs), added(rest_refs)
        square = jnp.sum(jnp.sum(main * main, axis=0, keepdims=True), axis=1, keepdims=True)
        square = square + jnp.sum(
            jnp.sum(rest * rest, axis=0, keepdims=True), axis=1, keepdims=True
        )
        for j in range(8):
            if j < 3:
                tile = main[0:slab, j * HEAD : (j + 1) * HEAD]
            else:
                tile = rest[:, (j - 3) * HEAD : (j - 2) * HEAD]
            block_ref[pl.ds(j, slab, stride=8), :] = tile
        for j in range(3):
            part = main[slab + j * strip : slab + (j + 1) * strip]
            high = min(PROMPT, (j + 1) * TAIL)
            prompt_ref[:, j * TAIL : high] = part[:, 0 : high - j * TAIL]
        small_ref[...] = main[slab + 3 * strip :, 0:WIDE]
        bias_ref[...] = main[slab + 2 * strip : slab + 2 * strip + 1, TAIL - WIDE :]
        square_ref[...] = jnp.broadcast_to(square, (8, 128))

    return simple(
        body,
        [
            shape_of((slab * 8, HEAD), f32),
            shape_of((strip, PROMPT), f32),
            shape_of((strip, WIDE), f32),
            shape_of((1, WIDE), f32),
            shape_of((8, 128), f32),
        ],
        *mains,
        *rests,
        name="final_sums",
    )


def adam_all(squares, params, moments, grads):
    slab = params[0].shape[0] // 8
    rates = (rate_matrix, rate_vector, rate_matrix, rate_vector, rate_vector)
    decays = (weight_decay, weight_decay, weight_decay, 0.0, 0.0)
    count = squares.shape[0]

    def body(sq_ref, *refs):
        weights, moment_refs, grad_refs, outs = refs[0:5], refs[5:10], refs[10:14], refs[14:]
        total = sq_ref[0, 0:1, 0:1]
        for k in range(1, count):
            total = total + sq_ref[k, 0:1, 0:1]
        norm = jnp.sqrt(total)
        outs[0][...] = norm
        factor = jnp.minimum(1.0, clip_norm / (norm + 1e-06))
        small = grad_refs[2][...]
        picked = (
            grad_refs[0][...],
            grad_refs[1][...],
            small[:, 0:FEAT],
            small.T[VEC : VEC + 7],
            grad_refs[3][:, 0:slab],
        )
        for k in range(5):
            both = moment_refs[k]
            pair = (both[:, 0], both[:, 1]) if k == 3 else (both[0], both[1])
            news = adam_update(weights[k][...], pair, picked[k], factor, rates[k], decays[k])
            for m in range(3):
                outs[1 + 4 * k + m][...] = news[m]
            if k > 0:
                outs[4 + 4 * k][...] = news[3]
        for j in range(8):
            tile = outs[1][pl.ds(j, slab, stride=8), :]
            outs[4][:, j * HEAD : (j + 1) * HEAD] = tile.astype(bf16)

    shapes = [shape_of((1, 1), f32)]
    for k, param in enumerate(params):
        low = (slab, 8 * HEAD) if k == 0 else param.shape
        shapes += [shape_of(param.shape, f32)] * 3 + [shape_of(low, bf16)]
    return simple(body, shapes, squares, *params, *moments, *grads, name="adam_all")


def shards(
    feats,
    counts,
    feat_mask,
    cotangent,
    block_weights,
    block_moments,
    head_biases,
    bias_moments,
    encoder,
    encoder_moments,
    shared_vectors,
    vector_moments,
    prompt,
    prompt_moments,
):
    n_ep = lax.axis_size("ep")
    side = lax.axis_index("split")
    row = lax.axis_index("tp") // 2
    core = lax.axis_index("tp") % 2
    chip = side * 2 + row
    rows = feats.shape[2]
    width = cotangent.shape[3]
    slab = block_weights.shape[0]
    strip = encoder.shape[0]
    quad = [(b, r) for b in (0, 1) for r in (0, 1)]

    mask_row = lax.dynamic_index_in_dim(feat_mask, chip, 0, keepdims=False)
    count_pair = lax.dynamic_index_in_dim(counts, chip, 0, keepdims=False)
    mask_float = mask_row.astype(f32)
    ratio = (FEAT / jnp.sum(mask_float)).reshape(1)
    spot = jnp.arange(8, dtype=jnp.int32)
    places = jnp.pad(count_pair, (4, 2)).astype(jnp.int32)
    for k, value in ((0, side), (1, row), (2, core), (3, chip), (6, lax.axis_index("ep"))):
        places = places + jnp.where(spot == k, value, 0)

    def canonical(got):
        first = [jnp.concatenate(pick(got[b, 0], got[b, 1], row), axis=0) for b in (0, 1)]
        return jnp.concatenate(pick(first[0], first[1], side), axis=0)

    def to_chip(array):
        return plane_swap(
            lambda b, r: lax.dynamic_index_in_dim(array[0], chip ^ (2 * b + r), 0, keepdims=False)
        )

    main_part, rest_part = pack_parts(
        block_weights, prompt, encoder, shared_vectors, head_biases
    )
    got = to_chip(feats)
    main_along = gather_ep(main_part, "stack_main")
    feats_own = canonical(got)
    masked_own = jnp.pad(feats_own * mask_row.astype(bf16), ((0, 0), (0, WIDE - FEAT)))
    masked_other = swap(masked_own, core=1)
    tops = plane_swap(lambda b, r: main_along)
    tops = [tops[key] for key in quad]
    lows = [swap(top, core=1) for top in tops]
    w_project, prompt_low, small_low, vector_rows, bias_rows = unpack_main(
        tops, lows, places, slab, strip
    )
    w_project = w_project.reshape(2, width, TAIL)
    prompt_low = prompt_low.reshape(width, 3 * TAIL)
    encoder_low = small_low.reshape(width, WIDE)

    rest_part = tie(rest_part, main_along)
    rest_along = gather_ep(rest_part, "stack_rest")
    rest_along = tie(rest_along, tops[3])
    rest_tops = plane_swap(lambda b, r: rest_along)
    rest_own = unpack_rest([rest_tops[key] for key in quad], places)
    rest_own = rest_own.reshape(2, width, -1)
    rest_other = swap(rest_own, core=1)

    lane = jnp.arange(rows, dtype=jnp.int32)

    def slots_of(which_core):
        return jnp.concatenate([which_core * rows + lane, (2 + which_core) * rows + lane])

    key_slots = jnp.concatenate([slots_of(core), slots_of(1 - core)])
    key_live = jnp.concatenate([jnp.arange(PAD) < PROMPT, key_slots < count_pair[0]])
    key_bias = jnp.where(key_live, 0.0, neg_big)[:, None].astype(f32)
    rows_low, query, keys, keys_flip, values, values_flip = project(
        ratio,
        masked_own,
        masked_other,
        encoder_low,
        vector_rows,
        w_project,
        bias_rows,
        prompt_low,
    )
    attended_other, lse_other = attend(query, keys, values_flip, key_bias, 1)
    attended_got = swap(attended_other, core=1)
    attended_own, lse_own = attend(query, keys, values_flip, key_bias, 0)
    cots = to_chip(tie(cotangent, tops[3]))
    (y0, y1, y2, y3, grad_own, grad_sent, grad_one, rest_mine, rest_sent, grad_rows, grad_hidden_row) = middle(
        places,
        ratio,
        masked_own,
        attended_own,
        attended_got,
        [cots[key] for key in quad],
        encoder_low,
        vector_rows,
        bias_rows,
        rest_own,
        rest_other,
    )
    grad_got = swap(grad_sent, core=1)
    rest_got = swap(rest_sent, core=1)
    outs = (y0, y1, y2, y3)
    outs = plane_swap(lambda b, r: outs[2 * b + r])
    output_final = place([outs[key] for key in quad], chip, "place_output")[None]
    rest_parts = pack_rest(rest_mine, rest_got, places, n_ep, slab)
    rest_tops = plane_swap(lambda b, r: rest_parts[2 * b + r])
    rest_pieces = reduce_plane([rest_tops[key] for key in quad], places, "sum_rest")

    query_again, *unused = lax.optimization_barrier((query, *rest_parts))
    grad_query, grad_key, grad_value = attend_back(
        query_again, keys, keys_flip, values, key_bias, lse_own, lse_other, grad_own, grad_got
    )
    back_other, back_own = back_rows(grad_query, grad_key, grad_value, w_project)
    back_got = swap(back_other, core=1)
    grad_project, grad_prompt, grad_bias = weight_grads(
        rows_low, grad_query, grad_key, grad_value, prompt_low, w_project, grad_hidden_row
    )
    prompt_mine, prompt_sent = split_prompt(grad_prompt, grad_bias, places, n_ep, strip)
    prompt_got = swap(prompt_sent, core=1)
    i0, i1, i2, i3, grad_small = input_grads(
        places,
        ratio,
        grad_one,
        back_own,
        back_got,
        masked_own,
        encoder_low,
        jnp.pad(mask_float, (0, WIDE - FEAT)).reshape(WIDE, 1),
        grad_rows,
    )
    small_mine, small_sent = split_small(grad_small, places, n_ep, strip)
    small_got = swap(small_sent, core=1)
    main_parts = pack_main(
        grad_project, prompt_mine, prompt_got, small_mine, small_got, places, slab, strip
    )
    main_tops = plane_swap(lambda b, r: main_parts[2 * b + r])
    ins = (i0, i1, i2, i3)
    ins = plane_swap(lambda b, r: ins[2 * b + r])
    main_pieces = reduce_plane([main_tops[key] for key in quad], places, "sum_main")
    input_final = place([ins[key] for key in quad], chip, "place_input")
    input_final = jnp.transpose(input_final[:, 0:FEAT], (0, 2, 1))[None]

    grad_block, grad_prompt_own, grad_small_own, grad_bias_own, square_tile = final_sums(
        main_pieces, rest_pieces, slab, strip
    )
    square_tile = square_tile + swap(square_tile, core=1)
    got = plane_swap(lambda b, r: square_tile)
    square_tile = (got[0, 0] + got[1, 0]) + (got[0, 1] + got[1, 1])
    if n_ep > 4:
        squares = lax.psum(square_tile, "ep")[None]
    else:
        squares = gather_ep(square_tile, "stack_square")
    grad_norm, *news = adam_all(
        squares,
        (
            block_weights.reshape(slab * 8, HEAD),
            prompt,
            encoder,
            shared_vectors.T,
            head_biases.T,
        ),
        (
            block_moments.reshape(2, slab * 8, HEAD),
            prompt_moments,
            encoder_moments,
            jnp.transpose(vector_moments, (2, 0, 1)),
            jnp.transpose(bias_moments, (0, 2, 1)),
        ),
        (grad_block, grad_prompt_own, grad_small_own, grad_bias_own),
    )
    block_out = tuple(part.reshape(block_weights.shape) for part in news[0:4])
    prompt_out = tuple(news[4:8])
    encoder_out = tuple(news[8:12])
    vector_out = tuple(part.T for part in news[12:16])
    bias_out = tuple(part.T for part in news[16:20])
    return (
        (output_final, input_final, grad_norm.reshape(()))
        + block_out
        + bias_out
        + encoder_out
        + vector_out
        + prompt_out
    )


def solution(mesh):
    data = P("split", "ep", "tp", None)
    block = P(("ep", "split"), "tp", None)
    bias = P(("ep", "split"), "tp")
    strip = P(AXES, None)
    placed = (
        data,
        P("ep", None),
        P("ep", None),
        data,
        block,
        P(None, ("ep", "split"), "tp", None),
        bias,
        P(None, ("ep", "split"), "tp"),
        strip,
        P(None, AXES, None),
        strip,
        P(None, AXES, None),
        strip,
        P(None, AXES, None),
    )
    return jax.shard_map(
        shards,
        mesh=mesh,
        in_specs=placed,
        out_specs=(data, data, P()) + (block,) * 4 + (bias,) * 4 + (strip,) * 12,
        check_vma=False,
    )
```

time: 442 us -> 284 us (0.64); the launches traced: 436 us -> 283 us
  Pallas kernels: 0 us -> 145 us
  matrix products: 121 us -> 0 us
  other arithmetic: 77.7 us -> 3.18 us
  local copies, waits for them, and re-layouts: 81.5 us -> 15.5 us
  starting transfers between devices: 85.8 us -> 58.6 us
  between operations: 7.55 us -> 2.06 us
    pallas_call x0 -> x24, Pallas kernels: none -> 145 us  [the longest x16 35.5 us: simple(): pl.pallas_call(body, in_specs=specs, out_specs=[whole()] * len(out_shape)...]
    dot_general x59 -> x0, matrix products: 121 us -> none  [dot(): return lax.dot_general(a, b, (dims, ((), ())), preferred_element_type=f32)]
    ppermute x77 -> x55, starting transfers between devices: 85.8 us -> 58.6 us  [swap(): return lax.ppermute(value, AXES, pairs)]
    reduce_sum x18 -> x1, other arithmetic: 22.1 us -> 0.61 us  [shards(): ratio = (FEAT / jnp.sum(mask_float)).reshape(1)]
    convert_element_type x18 -> x1, other arithmetic: 20.7 us -> 0.01 us  [shards(): mask_float = mask_row.astype(f32)]
    slice x29 -> x1, local copies, waits for them, and re-layouts: 19.8 us -> 0.52 us  [shards(): count_pair[0]]
    squeeze x25 -> x0, local copies, waits for them, and re-layouts: 15 us -> none  [the longest x4 4.25 us: reduce_heads(): lax.dynamic_index_in_dim(blocks[r], side ^ b, 1, keepdims=False)]
    another operation x44 -> x0, other arithmetic: 14.4 us -> none  [the longest x4 3.09 us: from_chip(): first = [jnp.stack(pick(got[b, 0], got[b, 1], row)) for b in (0, 1)]]
  transfers between devices with their start and end apart: 77 -> 55, of which waited for: 33 -> 19; matrix products, arithmetic and copies ran while one was open for 51% -> 3% of each run, Pallas kernels for 0% -> 26%
where the time goes in v2:
time: 284 us; the launch traced here: 283 us
  Pallas kernels  145 us (51%)
  waiting for transfers between devices  59.3 us (21%)
  starting transfers between devices  58.6 us (21%)
  local copies, waits for them, and re-layouts  15.5 us (5%)
  other arithmetic  3.18 us (1%)
    ppermute x55, waiting for transfers between devices, swap(): return lax.ppermute(value, AXES, pairs)  59.3 us
    ppermute x55, starting transfers between devices, swap(): return lax.ppermute(value, AXES, pairs)  58.6 us
    pallas_call x16, Pallas kernels, simple(): pl.pallas_call(body, in_specs=specs, out_specs=[whole()] * len(out_shape)...  35.5 us
    pallas_call x1, Pallas kernels, attend_back(): pl.pallas_call(attend_back_body, grid=(2, 2 * SLOTS // size), in_specs=[p...  32.1 us
    pallas_call x1, Pallas kernels, middle(): pl.pallas_call(middle_body, grid_spec=pltpu.PrefetchScalarGridSpec(num_sc...  25.5 us
    pallas_call x2, Pallas kernels, attend(): pl.pallas_call(attend_body, grid=(2, blocks), in_specs=[pl.BlockSpec((1,...  20.4 us
    unnamed x127, local copies, waits for them, and re-layouts  10.7 us
    pallas_call x1, Pallas kernels, weight_grads(): pl.pallas_call(weight_body, grid=(4,), in_specs=[pl.BlockSpec((half, widt...  9.09 us
  transfers between devices with their start and end apart: 55, of which 19 were waited for; matrix products, arithmetic and copies ran while one was open for 3% of the time, Pallas kernels for 26%

profile of v2, /device:TPU:0, one launch (start us, length us, event | category | flops | bytes accessed | tf_op | source)
XLA Modules:
  0.0 283.3 jit_solution(10012878922047359100)
XLA Ops:
  2.5 3.0 %collective-permute-start.4 = (bf16[128,384]{1,0:T(8,128)(2,1)}, bf16[128,384]{1,0:T(8,128)(2,1)S(1)}, u32[]{:S(2)}, u32[]{:S(2)}) collective-permute-start(bf16[128,384]{1,0:T(8,128)(2,1)} %get-tuple-element.114.refs_0_), channel_id=1, source_target_pairs={{0,8},{1,9},{2,10},{3,11},{4,12},{5,13},{6,14},{7,15},{8,0},{9,1},... | collective-permute-start | bytes 294920 | tf_op jit(solution)/shard_map/ppermute | solution.py:44
  20.6 3.5 %collective-permute-start.19 = (bf16[64,640]{1,0:T(8,128)(2,1)S(1)}, bf16[64,640]{1,0:T(8,128)(2,1)S(1)}, u32[]{:S(2)}, u32[]{:S(2)}) collective-permute-start(bf16[64,640]{1,0:T(8,128)(2,1)S(1)} %copy-done.50), channel_id=1, source_target_pairs={{0,16},{1,17},{2,18},{3,19},{4,20},{5,21},{6,22},{7,23},{8,24},{9,... | collective-permute-start | bytes 245768 | tf_op jit(solution)/shard_map/ppermute | solution.py:44
  32.7 4.8 %collective-permute-done.9.t3 = bf16[4,128,384]{2,1,0:T(8,128)(2,1)S(1)} collective-permute-done((bf16[4,128,384]{2,1,0:T(8,128)(2,1)}, bf16[4,128,384]{2,1,0:T(8,128)(2,1)S(1)}, u32[]{:S(2)}, u32[]{:S(2)}) %collective-permute-start.9) | collective-permute-done | bytes 393248 | tf_op jit(solution)/shard_map/ppermute | solution.py:44
  39.5 4.6 %collective-permute-done.7.t1 = bf16[4,128,384]{2,1,0:T(8,128)(2,1)S(1)} collective-permute-done((bf16[4,128,384]{2,1,0:T(8,128)(2,1)}, bf16[4,128,384]{2,1,0:T(8,128)(2,1)S(1)}, u32[]{:S(2)}, u32[]{:S(2)}) %collective-permute-start.7) | collective-permute-done | bytes 393248 | tf_op jit(solution)/shard_map/ppermute | solution.py:44
  46.4 7.8 %collective-permute-done.21.t1 = bf16[4,64,640]{2,1,0:T(8,128)(2,1)S(1)} collective-permute-done((bf16[4,64,640]{2,1,0:T(8,128)(2,1)}, bf16[4,64,640]{2,1,0:T(8,128)(2,1)S(1)}, u32[]{:S(2)}, u32[]{:S(2)}) %collective-permute-start.21) | collective-permute-done | bytes 327712 | tf_op jit(solution)/shard_map/ppermute | solution.py:44
  64.9 3.3 %unpack_main.1 = (bf16[2,4,2,64,384]{4,3,2,1,0:T(8,128)(2,1)}, bf16[4,2,2,2,16,1152]{5,4,3,2,1,0:T(8,128)(2,1)}, bf16[4,2,2,2,16,128]{5,4,3,2,1,0:T(8,128)(2,1)}, f32[8,512]{1,0:T(8,128)}, f32[4,512]{1,0:T(4,128)}) custom-call(s32[8]{0:T(128)} %fusion.4.sc, bf16[4,128,384]{2,1,0:T(8,128)(2,1)} %stack_main.1.t0, bf16[4,128,384]{2,1,0:T(8,128)(2,1)} %copy-done.15, ...), custom_call_target="tpu_custom_call" | custom-call | flops 2000000000 | bytes 6000000 | tf_op jit(solution)/shard_map/unpack_main/pallas_call | solution.py:479
  68.2 8.9 %project.1 = (bf16[2048,512]{1,0:T(8,128)(2,1)}, bf16[2,2048,128]{2,1,0:T(8,128)(2,1)}, bf16[2,2048,128]{2,1,0:T(8,128)(2,1)}, bf16[2,128,2048]{2,1,0:T(8,128)(2...) custom-call(f32[1]{0:T(128)} %bitcast.1.ratio, bf16[1024,128]{1,0:T(8,128)(2,1)} %copy-done.2, ...), custom_call_target="tpu_custom_call" | custom-call | flops 8999999488 | bytes 27000000 | tf_op jit(solution)/shard_map/project/pallas_call | solution.py:148
  77.2 10.2 %attend.3 = (bf16[1024,256]{1,0:T(8,128)(2,1)}, f32[2,1,1024]{2,1,0:T(1,128)}) custom-call(bf16[2,2048,128]{2,1,0:T(8,128)(2,1)} %get-tuple-element.140.q_ref, bf16[2,2048,128]{2,1,0:T(8,128)(2,1)} %get-tuple-element.121.k_ref, bf16[2,128,2048]{2,1,0:T(8,128)(2,1)} %get-tuple-element.122.vt_ref, f32[2048,1]{1,0:T(8,128)} %broadcast_select_fusion.bias_ref), custom_call_target="tpu_custom_call" | custom-call | flops 10000000000 | bytes 30000000 | tf_op jit(solution)/shard_map/attend/pallas_call | solution.py:196
  87.9 10.2 %attend.2 = (bf16[1024,256]{1,0:T(8,128)(2,1)}, f32[2,1,1024]{2,1,0:T(1,128)}) custom-call(bf16[2,2048,128]{2,1,0:T(8,128)(2,1)} %get-tuple-element.140.q_ref, bf16[2,2048,128]{2,1,0:T(8,128)(2,1)} %get-tuple-element.121.k_ref, bf16[2,128,2048]{2,1,0:T(8,128)(2,1)} %get-tuple-element.122.vt_ref, f32[2048,1]{1,0:T(8,128)} %broadcast_select_fusion.bias_ref), custom_call_target="tpu_custom_call" | custom-call | flops 10000000000 | bytes 30000000 | tf_op jit(solution)/shard_map/attend/pallas_call | solution.py:196
  99.5 25.5 %middle.1 = (bf16[256,512]{1,0:T(8,128)(2,1)}, bf16[256,512]{1,0:T(8,128)(2,1)}, bf16[256,512]{1,0:T(8,128)(2,1)}, bf16[256,512]{1,0:T(8,128)(2,1)}, bf16[1024,2...) custom-call(s32[8]{0:T(128)} %fusion.4.sc, ...), custom_call_target="tpu_custom_call" | custom-call | flops 24999999488 | bytes 75000000 | tf_op jit(solution)/shard_map/middle/pallas_call | solution.py:437
  129.4 2.9 %pack_rest.1 = (bf16[4,64,640]{2,1,0:T(8,128)(2,1)}, bf16[4,64,640]{2,1,0:T(8,128)(2,1)}, bf16[4,64,640]{2,1,0:T(8,128)(2,1)}, bf16[4,64,640]{2,1,0:T(8,128)(2,1)}) custom-call(s32[8]{0:T(128)} %fusion.4.sc, bf16[2,4,2,64,640]{4,3,2,1,0:T(8,128)(2,1)} %bitcast.77, bf16[2,4,2,64,640]{4,3,2,1,0:T(8,128)(2,1)} %bitcast.66), custom_call_target="tpu_custom_call" | custom-call | flops 2000000000 | bytes 6000000 | tf_op jit(solution)/shard_map/pack_rest/pallas_call | solution.py:479
  133.1 32.1 %attend_back.1 = (bf16[2048,256]{1,0:T(8,128)(2,1)}, f32[2,2048,128]{2,1,0:T(8,128)}, f32[2,2048,128]{2,1,0:T(8,128)}) custom-call(bf16[2,2048,128]{2,1,0:T(8,128)(2,1)} %get-tuple-element.140.q_ref, bf16[2,2048,128]{2,1,0:T(8,128)(2,1)} %get-tuple-element.121.k_ref, bf16[2,128,2048]{2,1,0:T(8,128)(2,1)} %get-tuple-element.141.kt_ref, ...), custom_call_target="tpu_custom_call" | custom-call | flops 32000000000 | bytes 96000000 | tf_op jit(solution)/shard_map/attend_back/pallas_call | solution.py:247
  165.2 6.5 %back_rows.1 = (bf16[1024,512]{1,0:T(8,128)(2,1)}, f32[1024,512]{1,0:T(8,128)}) custom-call(bf16[2048,256]{1,0:T(8,128)(2,1)} %get-tuple-element.147.dq_ref, f32[2,2048,128]{2,1,0:T(8,128)} %get-tuple-element.148.dk_ref, f32[2,2048,128]{2,1,0:T(8,128)} %get-tuple-element.149.dv_ref, bf16[2,512,384]{2,1,0:T(8,128)(2,1)} %bitcast.83), custom_call_target="tpu_custom_call" | custom-call | flops 6000000000 | bytes 18000000 | tf_op jit(solution)/shard_map/back_rows/pallas_call | solution.py:709
  173.2 9.1 %weight_grads.1 = (bf16[2,512,384]{2,1,0:T(8,128)(2,1)}, bf16[512,1024]{1,0:T(8,128)(2,1)}, f32[4,512]{1,0:T(4,128)}) custom-call(bf16[2048,512]{1,0:T(8,128)(2,1)} %get-tuple-element.157.x_ref, bf16[2048,256]{1,0:T(8,128)(2,1)} %get-tuple-element.147.dq_ref, f32[2,2048,128]{2,1,0:T(8,128)} %get-tuple-element.148.dk_ref, ...), custom_call_target="tpu_custom_call" | custom-call | flops 8999999488 | bytes 27000000 | tf_op jit(solution)/shard_map/weight_grads/pallas_call | solution.py:779
  185.7 6.6 %input_grads.1 = (f32[104,256]{1,0:T(8,128)}, f32[104,256]{1,0:T(8,128)}, f32[104,256]{1,0:T(8,128)}, f32[104,256]{1,0:T(8,128)}, bf16[512,128]{1,0:T(8,128)(2,1)}) custom-call(s32[8]{0:T(128)} %fusion.4.sc, f32[1]{0:T(128)} %bitcast.1.ratio, f32[1024,512]{1,0:T(8,128)} %get-tuple-element.133.dr_ref, f32[1024,512]{1,0:T(8,128)} %get-tuple-element.150.own_ref, ...), custom_call_target="tpu_custom_call" | custom-call | flops 6000000000 | bytes 18000000 | tf_op jit(solution)/shard_map/input_grads/pallas_call | solution.py:852
  198.1 2.8 pack_main.1
  205.0 8.1 %collective-permute-done.44.refs_3_ = bf16[4,64,640]{2,1,0:T(8,128)(2,1)} collective-permute-done((bf16[4,64,640]{2,1,0:T(8,128)(2,1)S(1)}, bf16[4,64,640]{2,1,0:T(8,128)(2,1)}, u32[]{:S(2)}, u32[]{:S(2)}) %collective-permute-start.44) | collective-permute-done | bytes 327712 | tf_op jit(solution)/shard_map/ppermute | solution.py:44
  215.7 3.1 %collective-permute-done.36.refs_1_ = bf16[4,128,384]{2,1,0:T(8,128)(2,1)S(1)} collective-permute-done((bf16[4,128,384]{2,1,0:T(8,128)(2,1)}, bf16[4,128,384]{2,1,0:T(8,128)(2,1)S(1)}, u32[]{:S(2)}, u32[]{:S(2)}) %collective-permute-start.36) | collective-permute-done | bytes 393248 | tf_op jit(solution)/shard_map/ppermute | solution.py:44
  220.5 8.4 %collective-permute-done.38.refs_3_ = bf16[4,128,384]{2,1,0:T(8,128)(2,1)S(1)} collective-permute-done((bf16[4,128,384]{2,1,0:T(8,128)(2,1)}, bf16[4,128,384]{2,1,0:T(8,128)(2,1)S(1)}, u32[]{:S(2)}, u32[]{:S(2)}) %collective-permute-start.38) | collective-permute-done | bytes 393248 | tf_op jit(solution)/shard_map/ppermute | solution.py:44
  232.6 3.5 %collective-permute-start.46 = (bf16[64,640]{1,0:T(8,128)(2,1)S(1)}, bf16[64,640]{1,0:T(8,128)(2,1)S(1)}, u32[]{:S(2)}, u32[]{:S(2)}) collective-permute-start(bf16[64,640]{1,0:T(8,128)(2,1)S(1)} %copy-done.55), channel_id=1, source_target_pairs={{0,16},{1,17},{2,18},{3,19},{4,20},{5,21},{6,22},{7,23},{8,24},{9,... | collective-permute-start | bytes 245768 | tf_op jit(solution)/shard_map/ppermute | solution.py:44
  240.0 6.5 %collective-permute-done.46.refs_6_ = bf16[64,640]{1,0:T(8,128)(2,1)S(1)} collective-permute-done((bf16[64,640]{1,0:T(8,128)(2,1)S(1)}, bf16[64,640]{1,0:T(8,128)(2,1)S(1)}, u32[]{:S(2)}, u32[]{:S(2)}) %collective-permute-start.46) | collective-permute-done | bytes 81952 | tf_op jit(solution)/shard_map/ppermute | solution.py:44
  256.2 3.4 %collective-permute-done.27.refs_3_ = bf16[256,512]{1,0:T(8,128)(2,1)S(1)} collective-permute-done((bf16[256,512]{1,0:T(8,128)(2,1)S(1)}, bf16[256,512]{1,0:T(8,128)(2,1)S(1)}, u32[]{:S(2)}, u32[]{:S(2)}) %collective-permute-start.27) | collective-permute-done | bytes 262176 | tf_op jit(solution)/shard_map/ppermute | solution.py:44
  268.6 3.7 %collective-permute-start.52 = (f32[8,128]{1,0:T(8,128)S(1)}, f32[8,128]{1,0:T(8,128)S(1)}, u32[]{:S(2)}, u32[]{:S(2)}) collective-permute-start(f32[8,128]{1,0:T(8,128)S(1)} %add_add_fusion.refs_0_), channel_id=1, source_target_pairs={{0,8},{1,9},{2,10},{3,11},{4,12},{5,13},{6,14},{7,15},{8,0},{9,1},... | collective-permute-start | bytes 12296 | tf_op jit(solution)/shard_map/ppermute | solution.py:44
  280.4 2.8 adam_all.1
  (268 shorter events, 100.1 us)
Async XLA Ops:
  2.5 14.9 %collective-permute-start.4 = (bf16[128,384]{1,0:T(8,128)(2,1)}, bf16[128,384]{1,0:T(8,128)(2,1)S(1)}, u32[]{:S(2)}, u32[]{:S(2)}) collective-permute-start(bf16[128,384]{1,0:T(8,128)(2,1)} %get-tuple-element.114.refs_0_), channel_id=1, source_target_pairs={{0,8},{1,9},{2,10},{3,11},{4,12},{5,13},{6,14},{7,15},{8,0},{9,1},... | collective-permute-start | bytes 294920 | tf_op jit(solution)/shard_map/ppermute | solution.py:44
  8.7 15.7 %collective-permute-start = (bf16[256,100]{1,0:T(8,128)(2,1)S(1)}, bf16[256,100]{1,0:T(8,128)(2,1)S(1)}, u32[]{:S(2)}, u32[]{:S(2)}) collective-permute-start(bf16[256,100]{1,0:T(8,128)(2,1)S(1)} %bitcast.63), channel_id=1, source_target_pairs={{0,2},{1,3},{2,0},{3,1},{4,6},{5,7},{6,4},{7,5},{8,10},{9,11},{10,... | collective-permute-start | bytes 153608 | tf_op jit(solution)/shard_map/ppermute | solution.py:44
  10.6 27.4 %collective-permute-start.1 = (bf16[256,100]{1,0:T(8,128)(2,1)S(1)}, bf16[256,100]{1,0:T(8,128)(2,1)S(1)}, u32[]{:S(2)}, u32[]{:S(2)}) collective-permute-start(bf16[256,100]{1,0:T(8,128)(2,1)S(1)} %bitcast.61), channel_id=1, source_target_pairs={{0,4},{1,5},{2,6},{3,7},{4,0},{5,1},{6,2},{7,3},{8,12},{9,13},{10,... | collective-permute-start | bytes 153608 | tf_op jit(solution)/shard_map/ppermute | solution.py:44
  28.4 15.7 %collective-permute-start.7 = (bf16[4,128,384]{2,1,0:T(8,128)(2,1)}, bf16[4,128,384]{2,1,0:T(8,128)(2,1)S(1)}, u32[]{:S(2)}, u32[]{:S(2)}) collective-permute-start(bf16[4,128,384]{2,1,0:T(8,128)(2,1)} %stack_main.1.t0), channel_id=1, source_target_pairs={{0,2},{1,3},{2,0},{3,1},{4,6},{5,7},{6,4},{7,5},{8,10},{9,11},{10,... | collective-permute-start | bytes 1179656 | tf_op jit(solution)/shard_map/ppermute | solution.py:44
  30.3 16.1 %collective-permute-start.8 = (bf16[4,128,384]{2,1,0:T(8,128)(2,1)}, bf16[4,128,384]{2,1,0:T(8,128)(2,1)S(1)}, u32[]{:S(2)}, u32[]{:S(2)}) collective-permute-start(bf16[4,128,384]{2,1,0:T(8,128)(2,1)} %stack_main.1.t0), channel_id=1, source_target_pairs={{0,4},{1,5},{2,6},{3,7},{4,0},{5,1},{6,2},{7,3},{8,12},{9,13},{10,... | collective-permute-start | bytes 1179656 | tf_op jit(solution)/shard_map/ppermute | solution.py:44
  37.5 16.7 %collective-permute-start.21 = (bf16[4,64,640]{2,1,0:T(8,128)(2,1)}, bf16[4,64,640]{2,1,0:T(8,128)(2,1)S(1)}, u32[]{:S(2)}, u32[]{:S(2)}) collective-permute-start(bf16[4,64,640]{2,1,0:T(8,128)(2,1)} %stack_rest.1.t0), channel_id=1, source_target_pairs={{0,2},{1,3},{2,0},{3,1},{4,6},{5,7},{6,4},{7,5},{8,10},{9,11},{10,... | collective-permute-start | bytes 983048 | tf_op jit(solution)/shard_map/ppermute | solution.py:44
  38.0 16.2 %collective-permute-start.22 = (bf16[4,64,640]{2,1,0:T(8,128)(2,1)}, bf16[4,64,640]{2,1,0:T(8,128)(2,1)S(1)}, u32[]{:S(2)}, u32[]{:S(2)}) collective-permute-start(bf16[4,64,640]{2,1,0:T(8,128)(2,1)} %stack_rest.1.t0), channel_id=1, source_target_pairs={{0,4},{1,5},{2,6},{3,7},{4,0},{5,1},{6,2},{7,3},{8,12},{9,13},{10,... | collective-permute-start | bytes 983048 | tf_op jit(solution)/shard_map/ppermute | solution.py:44
  39.4 21.8 %collective-permute-start.10 = (bf16[4,128,384]{2,1,0:T(8,128)(2,1)S(1)}, bf16[4,128,384]{2,1,0:T(8,128)(2,1)S(1)}, u32[]{:S(2)}, u32[]{:S(2)}) collective-permute-start(bf16[4,128,384]{2,1,0:T(8,128)(2,1)S(1)} %copy-done.13), channel_id=1, source_target_pairs={{0,1},{1,0},{2,3},{3,2},{4,5},{5,4},{6,7},{7,6},{8,9},{9,8},{10,11... | collective-permute-start | bytes 1179656 | tf_op jit(solution)/shard_map/ppermute | solution.py:44
  44.0 14.0 %collective-permute-start.23 = (bf16[4,64,640]{2,1,0:T(8,128)(2,1)}, bf16[4,64,640]{2,1,0:T(8,128)(2,1)S(1)}, u32[]{:S(2)}, u32[]{:S(2)}) collective-permute-start(bf16[4,64,640]{2,1,0:T(8,128)(2,1)} %stack_rest.1.t0), channel_id=1, source_target_pairs={{0,6},{1,7},{2,4},{3,5},{4,2},{5,3},{6,0},{7,1},{8,14},{9,15},{10,... | collective-permute-start | bytes 983048 | tf_op jit(solution)/shard_map/ppermute | solution.py:44
  46.4 15.4 %collective-permute-start.13 = (bf16[4,128,384]{2,1,0:T(8,128)(2,1)S(1)}, bf16[4,128,384]{2,1,0:T(8,128)(2,1)S(1)}, u32[]{:S(2)}, u32[]{:S(2)}) collective-permute-start(bf16[4,128,384]{2,1,0:T(8,128)(2,1)S(1)} %collective-permute-done.9.t3), channel_id=1, source_target_pairs={{0,1},{1,0},{2,3},{3,2},{4,5},{5,4},{6,7},{7,6},{8,9},{9,8},{10,11... | collective-permute-start | bytes 1179656 | tf_op jit(solution)/shard_map/ppermute | solution.py:44
  61.2 36.8 %collective-permute-start.15 = (bf16[256,512]{1,0:T(8,128)(2,1)S(1)}, bf16[256,512]{1,0:T(8,128)(2,1)}, u32[]{:S(2)}, u32[]{:S(2)}) collective-permute-start(bf16[256,512]{1,0:T(8,128)(2,1)S(1)} %get-tuple-element.278), channel_id=1, source_target_pairs={{0,2},{1,3},{2,0},{3,1},{4,6},{5,7},{6,4},{7,5},{8,10},{9,11},{10,... | collective-permute-start | bytes 786440 | tf_op jit(solution)/shard_map/ppermute | solution.py:44
  61.8 36.2 %collective-permute-start.16 = (bf16[256,512]{1,0:T(8,128)(2,1)S(1)}, bf16[256,512]{1,0:T(8,128)(2,1)S(1)}, u32[]{:S(2)}, u32[]{:S(2)}) collective-permute-start(bf16[256,512]{1,0:T(8,128)(2,1)S(1)} %get-tuple-element.277), channel_id=1, source_target_pairs={{0,4},{1,5},{2,6},{3,7},{4,0},{5,1},{6,2},{7,3},{8,12},{9,13},{10,... | collective-permute-start | bytes 786440 | tf_op jit(solution)/shard_map/ppermute | solution.py:44
  63.2 34.9 %collective-permute-start.17 = (bf16[256,512]{1,0:T(8,128)(2,1)S(1)}, bf16[256,512]{1,0:T(8,128)(2,1)S(1)}, u32[]{:S(2)}, u32[]{:S(2)}) collective-permute-start(bf16[256,512]{1,0:T(8,128)(2,1)S(1)} %get-tuple-element.276), channel_id=1, source_target_pairs={{0,6},{1,7},{2,4},{3,5},{4,2},{5,3},{6,0},{7,1},{8,14},{9,15},{10,... | collective-permute-start | bytes 786440 | tf_op jit(solution)/shard_map/ppermute | solution.py:44
  64.8 33.3 %collective-permute-start.24 = (bf16[2,512,640]{2,1,0:T(8,128)(2,1)}, bf16[2,512,640]{2,1,0:T(8,128)(2,1)S(1)}, u32[]{:S(2)}, u32[]{:S(2)}) collective-permute-start(bf16[2,512,640]{2,1,0:T(8,128)(2,1)} %bitcast.64), channel_id=1, source_target_pairs={{0,1},{1,0},{2,3},{3,2},{4,5},{5,4},{6,7},{7,6},{8,9},{9,8},{10,11... | collective-permute-start | bytes 3932168 | tf_op jit(solution)/shard_map/ppermute | solution.py:44
  172.6 30.2 %collective-permute-start.42 = (bf16[4,64,640]{2,1,0:T(8,128)(2,1)S(1)}, bf16[4,64,640]{2,1,0:T(8,128)(2,1)S(1)}, u32[]{:S(2)}, u32[]{:S(2)}) collective-permute-start(bf16[4,64,640]{2,1,0:T(8,128)(2,1)S(1)} %copy-done.24), channel_id=1, source_target_pairs={{0,2},{1,3},{2,0},{3,1},{4,6},{5,7},{6,4},{7,5},{8,10},{9,11},{10,... | collective-permute-start | bytes 983048 | tf_op jit(solution)/shard_map/ppermute | solution.py:44
  195.7 17.3 %collective-permute-start.44 = (bf16[4,64,640]{2,1,0:T(8,128)(2,1)S(1)}, bf16[4,64,640]{2,1,0:T(8,128)(2,1)}, u32[]{:S(2)}, u32[]{:S(2)}) collective-permute-start(bf16[4,64,640]{2,1,0:T(8,128)(2,1)S(1)} %copy-done.22), channel_id=1, source_target_pairs={{0,6},{1,7},{2,4},{3,5},{4,2},{5,3},{6,0},{7,1},{8,14},{9,15},{10,... | collective-permute-start | bytes 983048 | tf_op jit(solution)/shard_map/ppermute | solution.py:44
  200.9 17.8 %collective-permute-start.36 = (bf16[4,128,384]{2,1,0:T(8,128)(2,1)}, bf16[4,128,384]{2,1,0:T(8,128)(2,1)S(1)}, u32[]{:S(2)}, u32[]{:S(2)}) collective-permute-start(bf16[4,128,384]{2,1,0:T(8,128)(2,1)} %get-tuple-element.168), channel_id=1, source_target_pairs={{0,2},{1,3},{2,0},{3,1},{4,6},{5,7},{6,4},{7,5},{8,10},{9,11},{10,... | collective-permute-start | bytes 1179656 | tf_op jit(solution)/shard_map/ppermute | solution.py:44
  201.5 18.9 %collective-permute-start.37 = (bf16[4,128,384]{2,1,0:T(8,128)(2,1)}, bf16[4,128,384]{2,1,0:T(8,128)(2,1)S(1)}, u32[]{:S(2)}, u32[]{:S(2)}) collective-permute-start(bf16[4,128,384]{2,1,0:T(8,128)(2,1)} %get-tuple-element.169), channel_id=1, source_target_pairs={{0,4},{1,5},{2,6},{3,7},{4,0},{5,1},{6,2},{7,3},{8,12},{9,13},{10,... | collective-permute-start | bytes 1179656 | tf_op jit(solution)/shard_map/ppermute | solution.py:44
  202.8 26.1 %collective-permute-start.38 = (bf16[4,128,384]{2,1,0:T(8,128)(2,1)}, bf16[4,128,384]{2,1,0:T(8,128)(2,1)S(1)}, u32[]{:S(2)}, u32[]{:S(2)}) collective-permute-start(bf16[4,128,384]{2,1,0:T(8,128)(2,1)} %get-tuple-element.170), channel_id=1, source_target_pairs={{0,6},{1,7},{2,4},{3,5},{4,2},{5,3},{6,0},{7,1},{8,14},{9,15},{10,... | collective-permute-start | bytes 1179656 | tf_op jit(solution)/shard_map/ppermute | solution.py:44
  215.1 22.5 %collective-permute-start.45 = (bf16[64,640]{1,0:T(8,128)(2,1)}, bf16[64,640]{1,0:T(8,128)(2,1)S(1)}, u32[]{:S(2)}, u32[]{:S(2)}) collective-permute-start(bf16[64,640]{1,0:T(8,128)(2,1)} %get-tuple-element.176), channel_id=1, source_target_pairs={{0,8},{1,9},{2,10},{3,11},{4,12},{5,13},{6,14},{7,15},{8,0},{9,1},... | collective-permute-start | bytes 245768 | tf_op jit(solution)/shard_map/ppermute | solution.py:44
  232.0 15.8 %collective-permute-start.39 = (bf16[128,384]{1,0:T(8,128)(2,1)}, bf16[128,384]{1,0:T(8,128)(2,1)S(1)}, u32[]{:S(2)}, u32[]{:S(2)}) collective-permute-start(bf16[128,384]{1,0:T(8,128)(2,1)} %get-tuple-element.172), channel_id=1, source_target_pairs={{0,8},{1,9},{2,10},{3,11},{4,12},{5,13},{6,14},{7,15},{8,0},{9,1},... | collective-permute-start | bytes 294920 | tf_op jit(solution)/shard_map/ppermute | solution.py:44
  232.6 13.9 %collective-permute-start.46 = (bf16[64,640]{1,0:T(8,128)(2,1)S(1)}, bf16[64,640]{1,0:T(8,128)(2,1)S(1)}, u32[]{:S(2)}, u32[]{:S(2)}) collective-permute-start(bf16[64,640]{1,0:T(8,128)(2,1)S(1)} %copy-done.55), channel_id=1, source_target_pairs={{0,16},{1,17},{2,18},{3,19},{4,20},{5,21},{6,22},{7,23},{8,24},{9,... | collective-permute-start | bytes 245768 | tf_op jit(solution)/shard_map/ppermute | solution.py:44
  236.4 14.0 %collective-permute-start.40 = (bf16[128,384]{1,0:T(8,128)(2,1)}, bf16[128,384]{1,0:T(8,128)(2,1)S(1)}, u32[]{:S(2)}, u32[]{:S(2)}) collective-permute-start(bf16[128,384]{1,0:T(8,128)(2,1)} %get-tuple-element.173), channel_id=1, source_target_pairs={{0,16},{1,17},{2,18},{3,19},{4,20},{5,21},{6,22},{7,23},{8,24},{9,... | collective-permute-start | bytes 294920 | tf_op jit(solution)/shard_map/ppermute | solution.py:44
  251.0 15.1 %collective-permute-start.32 = (f32[104,256]{1,0:T(8,128)S(1)}, f32[104,256]{1,0:T(8,128)S(1)}, u32[]{:S(2)}, u32[]{:S(2)}) collective-permute-start(f32[104,256]{1,0:T(8,128)S(1)} %copy-done.39), channel_id=1, source_target_pairs={{0,4},{1,5},{2,6},{3,7},{4,0},{5,1},{6,2},{7,3},{8,12},{9,13},{10,... | collective-permute-start | bytes 319496 | tf_op jit(solution)/shard_map/ppermute | solution.py:44
  (94 other events, 634.5 us)

commit v3 on v2

--- a/solution.py
+++ b/solution.py
@@ -61,20 +61,21 @@
     return lax.optimization_barrier((value, other))[0]
 
 
-def gather_ep(shard, name):
+def gather_ep(shard):
     count = lax.axis_size("ep")
     if count > 4:
-        return lax.all_gather(shard, "ep", axis=0)
-    parts = [shard] + [swap(shard, ep=k) for k in range(1, count)]
-    return place(parts, lax.axis_index("ep"), name)
-
-
-def reduce_plane(parts, places, name):
-    count = parts[0].shape[0]
+        return [lax.all_gather(shard, "ep", axis=0)]
+    return [shard] + [swap(shard, ep=k) for k in range(1, count)]
+
+
+def stack_ep(parts, name):
+    return parts[0] if len(parts) == 1 else place(parts, lax.axis_index("ep"), name)
+
+
+def reduce_ep(total, pieces):
+    count = lax.axis_size("ep")
     if count > 4:
-        total = sum(part.astype(f32) for part in parts)
         return [lax.psum_scatter(total, "ep", scatter_dimension=0, tiled=True)[0]]
-    pieces = sum_plane(parts, places, name)
     return [pieces[0]] + [swap(pieces[k], ep=k) for k in range(1, count)]
 
 
@@ -100,7 +101,7 @@
 
 
 def cost(micros):
-    return pl.CostEstimate(flops=int(micros * 1e9), transcendentals=0, bytes_accessed=int(micros * 3e6))
+    return pl.CostEstimate(flops=int(micros * 3e8), transcendentals=0, bytes_accessed=int(micros * 1e6))
 
 
 def whole():
@@ -111,8 +112,25 @@
     return jax.ShapeDtypeStruct(shape, dtype)
 
 
-def project_body(ratio, own, other, enc, vec, wp, bias, prompt, x_ref, q_ref, k_ref, kt_ref, v_ref, vt_ref):
+def project_body(ratio, sc, own, other, enc, vec, wp, bias, prompt, x_ref, q_ref, k_ref, kt_ref, v_ref, vt_ref, extra_ref):
     step = pl.program_id(0)
+
+    @pl.when(step == 0)
+    def _():
+        half = own.shape[0]
+        size = half // 2
+        key = lax.broadcasted_iota(jnp.int32, extra_ref.shape[1:], 0)
+        lane = lax.broadcasted_iota(jnp.int32, extra_ref.shape[1:], 1)
+        inner = key - PAD
+        place = inner % half
+        slot = (2 * (place // size) + (sc[2] ^ (inner // half))) * size + place % size
+        limit = jnp.where(key < PAD, PROMPT, sc[4])
+        bias = jnp.where(jnp.where(key < PAD, key, slot) >= limit, neg_big, 0.0)
+        bias = jnp.where(lane == 3, bias, 0.0)
+        for h in range(2):
+            ones = jnp.where((lane >= 4 * h) & (lane < 4 * h + 3), 1.0, 0.0)
+            extra_ref[h] = (bias + ones).astype(bf16)
+
     rows = jnp.where(step < 2, own[...], other[...])
     low = (ratio[0] * dot(rows, enc[...], NT) + vec[6:7, :]).astype(bf16)
     x_ref[...] = low
@@ -138,7 +156,7 @@
         keys_from(prompt[...].T)
 
 
-def project(ratio, own, other, enc, vec, wp, bias, prompt):
+def project(ratio, places, own, other, enc, vec, wp, bias, prompt):
     half = own.shape[0] // 2
     width = enc.shape[0]
     keys = PAD + SLOTS
@@ -149,6 +167,7 @@
         project_body,
         grid=(4,),
         in_specs=[
+            pl.BlockSpec(memory_space=pltpu.SMEM),
             pl.BlockSpec(memory_space=pltpu.SMEM),
             pl.BlockSpec((half, WIDE), lambda i: (jnp.minimum(i, 1), 0)),
             pl.BlockSpec((half, WIDE), lambda i: (jnp.maximum(i - 2, 0), 0)),
@@ -165,108 +184,197 @@
             flat,
             tall,
             flat,
+            pl.BlockSpec((2, keys, WIDE), lambda i: (0, 0, 0)),
         ],
         out_shape=[
-            shape_of((4 * half, width), bf16),
-            shape_of((2, 4 * half, HEAD), bf16),
-            shape_of((2, keys, HEAD), bf16),
-            shape_of((2, HEAD, keys), bf16),
-            shape_of((2, keys, HEAD), bf16),
-            shape_of((2, HEAD, keys), bf16),
+            pltpu.HBM((4 * half, width), bf16),
+            pltpu.HBM((2, 4 * half, HEAD), bf16),
+            pltpu.HBM((2, keys, HEAD), bf16),
+            pltpu.HBM((2, HEAD, keys), bf16),
+            pltpu.HBM((2, keys, HEAD), bf16),
+            pltpu.HBM((2, HEAD, keys), bf16),
+            pltpu.HBM((2, keys, WIDE), bf16),
         ],
+        compiler_params=pltpu.CompilerParams(vmem_limit_bytes=32 << 20),
         cost_estimate=cost(9),
         name="project",
-    )(ratio, own, other, enc, vec, wp, bias, prompt)
-
-
-def attend_body(q_ref, k_ref, vt_ref, bias_ref, o_ref, lse_ref):
-    scores = dot(k_ref[0], q_ref[0], NT) * score_scale + bias_ref[...]
-    top = jnp.max(scores, axis=0, keepdims=True)
-    raised = jnp.exp(scores - top)
-    total = jnp.sum(raised, axis=0, keepdims=True)
-    out = dot(vt_ref[0], raised.astype(bf16), NN) / total
-    o_ref[...] = out.T.astype(bf16)
-    lse_ref[0] = top + jnp.log(total)
-
-
-def attend(q, k, vt, bias, which):
-    size = 512
-    blocks = SLOTS // size
+    )(ratio, places, *held((own, other, enc, vec, wp, bias, prompt)))
+
+
+CHUNK = 1024
+base_two = 1.4426950408889634
+
+
+def three_terms(value):
+    high = value.astype(bf16).astype(f32)
+    middle = (value - high).astype(bf16).astype(f32)
+    return high, middle, value - high - middle
+
+
+def attend_body(q_ref, k_ref, x_ref, vt_ref, o_ref, extra_ref, *scratch):
+    head = pl.program_id(0)
+    keys, size = scratch[0].shape
+    count = q_ref.shape[1] // size
+    steepness = score_scale * base_two
+    lane = lax.broadcasted_iota(jnp.int32, (size, WIDE), 1)
+    place = lax.broadcasted_iota(jnp.int32, (WIDE, size), 0)
+    one = jnp.where(lane == 3, 1.0, 0.0).astype(bf16)
+    top = None
+    for b in range(count + 1):
+        fresh_ref, old_ref = scratch[b % 2], scratch[(b + 1) % 2]
+        if b < count:
+            query = jnp.concatenate([q_ref[0, b * size : (b + 1) * size], one], axis=1)
+            partial = jnp.full((8, size), -jnp.inf, f32)
+        if b > 0:
+            shift = top * steepness
+            total = jnp.zeros((8, size), f32)
+            out = jnp.zeros((HEAD, size), f32)
+        for c in range(keys // CHUNK):
+            span = slice(c * CHUNK, (c + 1) * CHUNK)
+            if b < count:
+                wide = jnp.concatenate([k_ref[0, span], x_ref[0, span]], axis=1)
+                fresh = dot(wide, query, NT)
+                fresh_ref[span] = fresh
+                partial = jnp.maximum(partial, jnp.max(fresh.reshape(CHUNK // 8, 8, size), axis=0))
+            if b > 0:
+                raised = jnp.exp2(old_ref[span] * steepness - shift)
+                total = total + jnp.sum(raised.reshape(CHUNK // 8, 8, size), axis=0)
+                out = out + dot(vt_ref[0, :, span], raised.astype(bf16), NN)
+        if b > 0:
+            rows = slice((b - 1) * size, b * size)
+            total = jnp.sum(total, axis=0, keepdims=True)
+            o_ref[rows] = (out / total).T.astype(bf16)
+            terms = three_terms(-(top + jnp.log(total) / score_scale))
+            tile = jnp.where(place == 3, 1.0, 0.0)
+            for k in range(3):
+                tile = tile + jnp.where(place == 4 * head + k, terms[k], 0.0)
+            extra_ref[0, rows] = tile.T.astype(bf16)
+        if b < count:
+            top = jnp.max(partial, axis=0, keepdims=True)
+
+
+BLOCK = 512
+
+
+def attend(q, k, extra, vt, which):
     keys = k.shape[1]
+    tall = pl.BlockSpec((1, keys, HEAD), lambda h: (h, 0, 0))
     return pl.pallas_call(
         attend_body,
-        grid=(2, blocks),
+        grid=(2,),
         in_specs=[
-            pl.BlockSpec((1, size, HEAD), lambda h, i: (h, which * blocks + i, 0)),
-            pl.BlockSpec((1, keys, HEAD), lambda h, i: (h, 0, 0)),
-            pl.BlockSpec((1, HEAD, keys), lambda h, i: (h, 0, 0)),
-            pl.BlockSpec((keys, 1), lambda h, i: (0, 0)),
+            pl.BlockSpec((1, SLOTS, HEAD), lambda h: (h, which, 0)),
+            tall,
+            pl.BlockSpec((1, keys, WIDE), lambda h: (0, 0, 0)),
+            pl.BlockSpec((1, HEAD, keys), lambda h: (h, 0, 0)),
         ],
         out_specs=[
-            pl.BlockSpec((size, HEAD), lambda h, i: (i, h)),
-            pl.BlockSpec((1, 1, size), lambda h, i: (h, 0, i)),
+            pl.BlockSpec((SLOTS, HEAD), lambda h: (0, h)),
+            pl.BlockSpec((1, SLOTS, WIDE), lambda h: (h, 0, 0)),
         ],
-        out_shape=[shape_of((SLOTS, 2 * HEAD), bf16), shape_of((2, 1, SLOTS), f32)],
-        cost_estimate=cost(10),
+        out_shape=[shape_of((SLOTS, 2 * HEAD), bf16), shape_of((2, SLOTS, WIDE), bf16)],
+        scratch_shapes=[pltpu.VMEM((keys, BLOCK), f32)] * 2,
+        cost_estimate=cost(6),
         name="attend",
-    )(q, k, vt, bias)
-
-
-def attend_back_body(q_ref, k_ref, kt_ref, v_ref, bias_ref, la_ref, lb_ref, da_ref, db_ref, dq_ref, dk_ref, dv_ref):
-    step = pl.program_id(1)
-    mine = step < 2
-    query = q_ref[0]
-    grad = jnp.where(mine, da_ref[...], db_ref[...])
-    lse = jnp.where(mine, la_ref[0], lb_ref[0])
-    probs = jnp.exp(dot(k_ref[0], query, NT) * score_scale + (bias_ref[...] - lse))
-    grad_probs = dot(v_ref[0], grad, NT)
-    delta = jnp.sum(probs * grad_probs, axis=0, keepdims=True)
-    grad_scores = (probs * (grad_probs - delta)).astype(bf16)
-    back = dot(kt_ref[0], grad_scores, NN) * score_scale
-    dq_ref[...] = back.T.astype(bf16)
-    grad_key = dot(grad_scores, query, NN) * score_scale
-    grad_value = dot(probs.astype(bf16), grad, NN)
-
-    @pl.when(step == 0)
+    )(q, k, extra, vt)
+
+
+BACK_BLOCK = 256
+BACK_CHUNK = 1024
+
+
+def attend_back_body(q_ref, k_ref, x_ref, kt_ref, v_ref, qa_ref, qb_ref, da_ref, db_ref, ea_ref, eb_ref, dq_ref, dk_ref, dv_ref, *scratch):
+    size = scratch[0].shape[1]
+    keys = k_ref.shape[1]
+    rows = q_ref.shape[1]
+    count = rows // size
+    steepness = score_scale * base_two
+    mine = pl.program_id(1) == 0
+
+    @pl.when(mine)
     def _():
-        dk_ref[0] = grad_key
-        dv_ref[0] = grad_value
-
-    @pl.when(step > 0)
-    def _():
-        dk_ref[0] += grad_key
-        dv_ref[0] += grad_value
-
-
-def attend_back(q, k, kt, v, bias, lse_own, lse_other, grad_own, grad_other):
-    size = 512
+        dk_ref[...] = jnp.zeros_like(dk_ref)
+        dv_ref[...] = jnp.zeros_like(dv_ref)
+
+    for b in range(count + 1):
+        probs_ref, slopes_ref = scratch[2 * (b % 2) : 2 * (b % 2) + 2]
+        old_probs, old_slopes = scratch[2 - 2 * (b % 2) : 4 - 2 * (b % 2)]
+        if b < count:
+            span = slice(b * size, (b + 1) * size)
+            query = q_ref[0, span]
+            grad = jnp.where(mine, da_ref[span], db_ref[span])
+            aside = jnp.where(mine, qa_ref[0, span], qb_ref[0, span])
+            sums = jnp.where(mine, ea_ref[span], eb_ref[span])
+            query_wide = jnp.concatenate([query, aside], axis=1)
+            grad_wide = jnp.concatenate([grad, sums], axis=1)
+        if b > 0:
+            back = jnp.zeros((HEAD, size), f32)
+        for c in range(keys // BACK_CHUNK):
+            span = slice(c * BACK_CHUNK, (c + 1) * BACK_CHUNK)
+            if b < count:
+                extra = x_ref[0, span]
+                scores = dot(jnp.concatenate([k_ref[0, span], extra], axis=1), query_wide, NT)
+                slopes = dot(jnp.concatenate([v_ref[0, span], extra], axis=1), grad_wide, NT)
+                probs = jnp.exp2(scores * steepness)
+                probs_ref[span] = probs.astype(bf16)
+                slopes_ref[span] = (probs * slopes).astype(bf16)
+            if b > 0:
+                back = back + dot(kt_ref[0, :, span], old_slopes[span], NN)
+                grad_key = dot(query_flip, old_slopes[span], NT) * score_scale
+                grad_value = dot(grad_flip, old_probs[span], NT)
+                dk_ref[0, :, span] += grad_key
+                dv_ref[0, :, span] += grad_value
+        if b > 0:
+            dq_ref[(b - 1) * size : b * size] = (back * score_scale).T.astype(bf16)
+        if b < count:
+            query_flip, grad_flip = query.T, grad.T
+
+
+def attend_back(q, k, extra, kt, v, extra_own, extra_other, grad_own, grad_other):
     keys = k.shape[1]
     tall = pl.BlockSpec((1, keys, HEAD), lambda h, i: (h, 0, 0))
-    first = lambda i: jnp.minimum(i, 1)
-    second = lambda i: jnp.maximum(i - 2, 0)
+    flat = pl.BlockSpec((1, HEAD, keys), lambda h, i: (h, 0, 0))
+    aside = pl.BlockSpec((1, SLOTS, WIDE), lambda h, i: (h, 0, 0))
+    grad = pl.BlockSpec((SLOTS, HEAD), lambda h, i: (0, h))
+    sums = pl.BlockSpec((SLOTS, HEAD), lambda h, i: (0, 2))
     return pl.pallas_call(
         attend_back_body,
-        grid=(2, 2 * SLOTS // size),
+        grid=(2, 2),
         in_specs=[
-            pl.BlockSpec((1, size, HEAD), lambda h, i: (h, i, 0)),
+            pl.BlockSpec((1, SLOTS, HEAD), lambda h, i: (h, i, 0)),
             tall,
-            pl.BlockSpec((1, HEAD, keys), lambda h, i: (h, 0, 0)),
             tall,
-            pl.BlockSpec((keys, 1), lambda h, i: (0, 0)),
-            pl.BlockSpec((1, 1, size), lambda h, i: (h, 0, first(i))),
-            pl.BlockSpec((1, 1, size), lambda h, i: (h, 0, second(i))),
-            pl.BlockSpec((size, HEAD), lambda h, i: (first(i), h)),
-            pl.BlockSpec((size, HEAD), lambda h, i: (second(i), h)),
+            flat,
+            tall,
+            aside,
+            aside,
+            grad,
+            grad,
+            sums,
+            sums,
         ],
-        out_specs=[pl.BlockSpec((size, HEAD), lambda h, i: (i, h)), tall, tall],
+        out_specs=[pl.BlockSpec((SLOTS, HEAD), lambda h, i: (i, h)), flat, flat],
         out_shape=[
             shape_of((2 * SLOTS, 2 * HEAD), bf16),
-            shape_of((2, keys, HEAD), f32),
-            shape_of((2, keys, HEAD), f32),
+            shape_of((2, HEAD, keys), f32),
+            shape_of((2, HEAD, keys), f32),
         ],
-        cost_estimate=cost(32),
+        scratch_shapes=[pltpu.VMEM((keys, BACK_BLOCK), bf16)] * 4,
+        cost_estimate=cost(20),
         name="attend_back",
-    )(q, k, kt, v, bias, lse_own, lse_other, grad_own, grad_other)
+    )(
+        q,
+        k,
+        extra,
+        kt,
+        v,
+        extra_own,
+        extra_other,
+        grad_own,
+        grad_other,
+        grad_own,
+        grad_other,
+    )
 
 
 erfc_terms = (
@@ -418,7 +526,16 @@
         both = dot(attn_flip, source[...], NN)
         acc[2 * k, :, 0:HEAD] += both[:, 0:HEAD]
         acc[2 * k + 1, :, 0:HEAD] += both[:, HEAD:]
-        target[...] = dot(attn_low, out_pair[k], NN).astype(bf16)
+        both = dot(attn_low, out_pair[k], NN).astype(bf16)
+        target[:, 0 : 2 * HEAD] = both
+        product = both.astype(f32) * source[...].astype(f32)
+        lane = lax.broadcasted_iota(jnp.int32, (count, WIDE), 1)
+        tile = jnp.zeros((count, WIDE), f32)
+        for h in range(2):
+            sums = jnp.sum(product[:, h * HEAD : (h + 1) * HEAD], axis=1, keepdims=True)
+            for m, term in enumerate(three_terms(-sums)):
+                tile = tile + jnp.where(lane == 4 * h + m, term, 0.0)
+        target[:, 2 * HEAD :] = tile.astype(bf16)
 
     @pl.when(step == 3)
     def _():
@@ -443,7 +560,8 @@
             + [fixed] * 4
             + [whole()] * 5,
             out_specs=[fixed] * 4
-            + [pair, pair, pl.BlockSpec((size, width), spot)]
+            + [pl.BlockSpec((size, 3 * HEAD), spot)] * 2
+            + [pl.BlockSpec((size, width), spot)]
             + [
                 pl.BlockSpec(weight, lambda i, sc: (0, 0, 0)),
                 pl.BlockSpec(weight, lambda i, sc: (0, 0, 0)),
@@ -455,39 +573,50 @@
                 pltpu.VMEM((4,) + weight[1:], f32),
             ],
         ),
-        out_shape=[shape_of((size, width), bf16)] * 4
+        out_shape=[pltpu.VMEM((size, width), bf16)] * 4
         + [
-            shape_of((4 * size, 2 * HEAD), bf16),
-            shape_of((4 * size, 2 * HEAD), bf16),
-            shape_of((4 * size, width), f32),
-            shape_of(weight, bf16),
-            shape_of(weight, bf16),
-            shape_of((8, width), f32),
-            shape_of((4, HID), f32),
+            pltpu.HBM((4 * size, 3 * HEAD), bf16),
+            pltpu.HBM((4 * size, 3 * HEAD), bf16),
+            pltpu.HBM((4 * size, width), f32),
+            pltpu.VMEM(weight, bf16),
+            pltpu.VMEM(weight, bf16),
+            pltpu.HBM((8, width), f32),
+            pltpu.HBM((4, HID), f32),
         ],
+        compiler_params=pltpu.CompilerParams(vmem_limit_bytes=44 << 20),
         cost_estimate=cost(25),
         name="middle",
-    )(sc, ratio, rows, o_own, o_other, *cots, enc, vec, b1, rest_own, rest_other)
-
-
-def simple(body, out_shape, *args, scalars=None, scratch=(), name=None):
+    )(sc, ratio, rows, o_own, o_other, *cots, enc, vec, b1, *held((rest_own, rest_other)))
+
+
+def held(args, near=True):
+    space = pltpu.VMEM if near else pltpu.HBM
+    return tuple(pltpu.with_memory_space_constraint(arg, space) for arg in args)
+
+
+def simple(body, out_shape, *args, scalars=None, scratch=(), near=(True, True), name=None):
     specs = [whole()] * len(args)
+    args = held(args, near[0])
     if scalars is not None:
         specs = [pl.BlockSpec(memory_space=pltpu.SMEM)] + specs
         args = (scalars,) + args
     many = isinstance(out_shape, (list, tuple))
+    if near[1]:
+        kept = lambda shape: pltpu.VMEM(shape.shape, shape.dtype)
+        out_shape = [kept(shape) for shape in out_shape] if many else kept(out_shape)
     return pl.pallas_call(
         body,
         in_specs=specs,
         out_specs=[whole()] * len(out_shape) if many else whole(),
         out_shape=out_shape,
         scratch_shapes=scratch,
+        compiler_params=pltpu.CompilerParams(vmem_limit_bytes=16 << 20),
         cost_estimate=cost(2),
         name=name,
     )(*args)
 
 
-def place(parts, index, name):
+def place(parts, index, name, near=(True, True)):
     def body(sc, *refs):
         for k, ref in enumerate(refs[:-1]):
             refs[-1][sc[0] ^ k] = ref[...]
@@ -498,22 +627,34 @@
         shape_of((len(parts),) + first.shape, first.dtype),
         *parts,
         scalars=index.reshape(1).astype(jnp.int32),
+        near=near,
         name=name,
     )
 
 
 TAIL = 3 * HEAD
+FEAT_ROWS = 112
+LAST = 112
 VEC = 104
 
 
+def spread(row):
+    parts = row.reshape(row.shape[:-1] + (4, row.shape[-1] // 4))
+    room = WIDE - LAST - parts.shape[-1]
+    return jnp.pad(parts, [(0, 0)] * (parts.ndim - 1) + [(LAST, room)])
+
+
+def widened(prompt):
+    return jnp.pad(prompt, [(0, 0)] * (prompt.ndim - 1) + [(0, 3 * TAIL - prompt.shape[-1])])
+
+
 def with_bias(prompt, bias):
-    wide = jnp.pad(prompt, [(0, 0)] * (prompt.ndim - 1) + [(0, 3 * TAIL - prompt.shape[-1])])
     row = jnp.pad(
         bias[..., None, :].astype(prompt.dtype),
         [(0, 0)] * (bias.ndim - 1)
         + [(0, prompt.shape[-2] - 1), (PAD, 3 * TAIL - PAD - bias.shape[-1])],
     )
-    return wide + row
+    return widened(prompt) + row
 
 
 def in_chunks(wide):
@@ -522,27 +663,26 @@
     return parts.reshape(lead + (3 * strip, TAIL))
 
 
-def small_tile(encoder, vectors):
-    return jnp.concatenate(
-        [
-            jnp.pad(encoder, ((0, 0), (0, VEC - FEAT))),
-            jnp.pad(vectors, ((0, 0), (0, WIDE - VEC - 7))),
-        ],
-        axis=1,
-    )
-
-
 def pack_parts(block, prompt, encoder, vectors, biases):
     slab, strip = block.shape[0], prompt.shape[0]
     flat = block.reshape(slab * 8, HEAD)
-    out = [shape_of((slab + 4 * strip, TAIL), bf16), shape_of((slab, 8 * HEAD - TAIL), bf16)]
+    out = [shape_of((slab + 3 * strip, TAIL), bf16), shape_of((slab, 8 * HEAD - TAIL), bf16)]
     if 2 * slab != WIDE:
         low = block.reshape(slab, 8 * HEAD).astype(bf16)
-        chunks = in_chunks(with_bias(prompt.astype(bf16), biases[:, 0]))
-        small = jnp.pad(small_tile(encoder, vectors), ((0, 0), (0, TAIL - WIDE))).astype(bf16)
-        return jnp.concatenate([low[:, 0:TAIL], chunks, small], axis=0), low[:, TAIL:]
-
-    def body(block_ref, prompt_ref, enc_ref, vec_ref, bias_ref, main_ref, rest_ref, tall, tile):
+        small = jnp.concatenate(
+            [
+                jnp.pad(encoder, ((0, 0), (0, VEC - FEAT))),
+                jnp.pad(vectors, ((0, 0), (0, LAST - VEC - 7))),
+                jnp.pad(biases.reshape(strip, 4), ((0, 0), (0, WIDE - LAST - 4))),
+            ],
+            axis=1,
+        )
+        chunks = in_chunks(
+            jnp.concatenate([jnp.pad(prompt, ((0, 0), (0, PAD - PROMPT))), small], axis=1)
+        )
+        return jnp.concatenate([low[:, 0:TAIL], chunks.astype(bf16)], axis=0), low[:, TAIL:]
+
+    def body(block_ref, prompt_ref, enc_ref, vec_ref, bias_ref, main_ref, rest_ref, tall, tile, line):
         for j in range(8):
             lanes = block_ref[pl.ds(j, slab, stride=8), :].astype(bf16)
             if j < 3:
@@ -556,16 +696,13 @@
         rows = slice(slab + 2 * strip, slab + 3 * strip)
         main_ref[rows, WIDE : 2 * WIDE] = jnp.zeros((strip, WIDE), bf16)
         main_ref[rows, 0 : PROMPT - 2 * TAIL] = low[:, 2 * TAIL :]
-        tile[...] = jnp.zeros_like(tile)
-        tile[0:1, 0:slab] = bias_ref[...]
-        main_ref[rows, 2 * WIDE :] = tile[...].astype(bf16)
         tall[...] = jnp.zeros_like(tall)
         tall[VEC : VEC + 7, :] = vec_ref[...]
         tile[...] = tall[...].T
         tile[:, 0:FEAT] = enc_ref[...]
-        rows = slice(slab + 3 * strip, slab + 4 * strip)
-        main_ref[rows, 0:WIDE] = tile[...].astype(bf16)
-        main_ref[rows, WIDE:] = jnp.zeros((strip, TAIL - WIDE), bf16)
+        line[...] = jnp.zeros_like(line)
+        line[:, 0:slab] = bias_ref[...]
+        main_ref[rows, 2 * WIDE :] = (tile[...] + spread_row(line[...], strip)).astype(bf16)
 
     return simple(
         body,
@@ -575,14 +712,69 @@
         encoder,
         vectors.T,
         biases.T,
-        scratch=[pltpu.VMEM((WIDE, strip), f32), pltpu.VMEM((strip, WIDE), f32)],
+        near=(False, True),
+        scratch=[
+            pltpu.VMEM((WIDE, strip), f32),
+            pltpu.VMEM((strip, WIDE), f32),
+            pltpu.VMEM((1, WIDE), f32),
+        ],
         name="pack_parts",
     )
 
 
-def unpack_main(tops, lows, places, slab, strip):
+def spread_row(row, strip):
+    place = lax.broadcasted_iota(jnp.int32, (strip, WIDE), 0)
+    lane = lax.broadcasted_iota(jnp.int32, (strip, WIDE), 1)
+    total = jnp.zeros((strip, WIDE), f32)
+    for k in range(4):
+        turned = jnp.broadcast_to(pltpu.roll(row, LAST - k * strip, 1), (strip, WIDE))
+        total = total + jnp.where((place == k) & (lane >= LAST), turned, 0.0)
+    return total
+
+
+def gathered_row(tile, strip):
+    lane = lax.broadcasted_iota(jnp.int32, (1, WIDE), 1)
+    total = jnp.zeros((1, WIDE), f32)
+    for k in range(4):
+        turned = pltpu.roll(tile[k : k + 1], (k * strip - LAST) % WIDE, 1)
+        total = total + jnp.where(lane // strip == k, turned, 0.0)
+    return total
+
+
+def join_features(parts, places):
+    feats, rows = parts[0].shape
+
+    def body(sc, *refs):
+        for k, ref in enumerate(refs[:-1]):
+            spot = 2 * (sc[0] ^ (k // 2)) + (sc[1] ^ (k % 2))
+            refs[-1][spot, 0:feats] = ref[...]
+
+    return simple(
+        body, shape_of((4, FEAT_ROWS, rows), bf16), *parts, scalars=places, name="join_features"
+    )
+
+
+def unpack_main(tops, lows, feats, feats_low, mask, places, slab, strip):
     n_ep = tops[0].shape[0]
-    if 2 * slab != WIDE:
+    rows = feats.shape[2]
+    plain = 2 * slab != WIDE
+    shapes = [
+        shape_of((2, n_ep, 2, slab, TAIL), bf16),
+        shape_of((n_ep, 2, 2, 2, strip, 3 * TAIL), bf16),
+        shape_of((n_ep, 2, 2, 2, strip, WIDE), bf16),
+        shape_of((8, n_ep * 2 * slab), f32),
+        shape_of((4, n_ep * 2 * slab), f32),
+        shape_of((4 * rows, WIDE), bf16),
+        shape_of((4 * rows, WIDE), bf16),
+    ]
+
+    def features(mask_ref, source, target):
+        for p in range(4):
+            flip = jnp.concatenate([source[p], jnp.zeros((WIDE - FEAT_ROWS, rows), bf16)], axis=0)
+            piece = jnp.where(mask_ref[...] > 0.0, flip.T.astype(f32), 0.0).astype(bf16)
+            target[p * rows : (p + 1) * rows, :] = piece
+
+    if plain:
         side, row, core = places[0], places[1], places[2]
 
         def ordered(parts, axis):
@@ -597,66 +789,71 @@
         heads = [
             jnp.stack(pick(tops[r][:, 0:slab], tops[2 + r][:, 0:slab], side), axis=1) for r in (0, 1)
         ]
-        whole_low = ordered([[t[:, slab:] for t in tops], [t[:, slab:] for t in lows]], 1)
-        chunks = whole_low[..., 0 : 3 * strip, :].reshape((n_ep, 2, 2, 2, 3, strip, TAIL))
+        chunks = ordered([[t[:, slab:] for t in tops], [t[:, slab:] for t in lows]], 1)
+        chunks = chunks.reshape((n_ep, 2, 2, 2, 3, strip, TAIL))
         wide = jnp.swapaxes(chunks, -3, -2).reshape((n_ep, 2, 2, 2, strip, 3 * TAIL))
-        small = whole_low[..., 3 * strip :, 0:WIDE]
+        small = wide[..., PAD:]
         vec = small.reshape(n_ep * 8 * strip, WIDE).astype(f32).T[VEC : VEC + 8]
         biases = []
         for group in (tops, lows):
             for r in (0, 1):
-                spot = slab + 2 * strip
                 pair = [
-                    group[2 * b + r][:, spot, PAD - 2 * TAIL : PAD - 2 * TAIL + slab] for b in (0, 1)
+                    group[2 * b + r][:, slab + 2 * strip :, PAD - 2 * TAIL + LAST :][..., 0:4]
+                    for b in (0, 1)
                 ]
                 biases.append(jnp.stack(pick(pair[0], pair[1], side), axis=1).reshape(-1))
-        return jnp.stack(heads), wide, small, vec, jnp.stack(biases).astype(f32)
-
-    def body(sc, t0, t1, t2, t3, l0, l1, l2, l3, wp_ref, prompt_ref, small_ref, vec_ref, bias_ref):
+        def both(mask_ref, a, b, c, d):
+            features(mask_ref, a, c)
+            features(mask_ref, b, d)
+
+        masked = simple(
+            both,
+            shapes[5:],
+            mask,
+            feats,
+            feats_low,
+            near=(False, False),
+            name="features",
+        )
+        return [jnp.stack(heads), wide, small, vec, jnp.stack(biases).astype(f32), *masked]
+
+    def body(sc, t0, t1, t2, t3, l0, l1, l2, l3, fa, fb, mask_ref, *outs):
+        wp_ref, prompt_ref, small_ref, vec_ref, bias_ref, own_ref, other_ref = outs
         side, row, core = sc[0], sc[1], sc[2]
-        refs = (t0, t1, t2, t3)
-        low_refs = (l0, l1, l2, l3)
+        groups = ((t0, t1, t2, t3), (l0, l1, l2, l3))
         bias_tiles = {}
         for b in range(2):
             for r in range(2):
                 k = 2 * b + r
-                wp_ref[r, :, side ^ b] = refs[k][:, 0:slab, :]
+                wp_ref[r, :, side ^ b] = groups[0][k][:, 0:slab, :]
                 for other in range(2):
                     spot = core ^ other
-                    part = (low_refs if other else refs)[k][:, slab:, :]
+                    part = groups[other][k][:, slab:, :]
                     for j in range(3):
                         lanes = slice(j * TAIL, (j + 1) * TAIL)
-                        rows = slice(j * strip, (j + 1) * strip)
-                        prompt_ref[:, side ^ b, row ^ r, spot, :, lanes] = part[:, rows, :]
-                    small_ref[:, side ^ b, row ^ r, spot] = part[:, 3 * strip :, 0:WIDE]
-                    bias_tiles[b, r, other] = part[:, 2 * strip : 2 * strip + 8, TAIL - WIDE :].astype(f32)
+                        span = slice(j * strip, (j + 1) * strip)
+                        prompt_ref[:, side ^ b, row ^ r, spot, :, lanes] = part[:, span, :]
+                    tile = part[:, 2 * strip :, TAIL - WIDE :]
+                    small_ref[:, side ^ b, row ^ r, spot] = tile
+                    bias_tiles[b, r, other] = tile.astype(f32)
         flip = small_ref[...].reshape(n_ep * 8 * strip, WIDE).astype(f32).T
         vec_ref[...] = flip[VEC : VEC + 8]
         low_half = lax.broadcasted_iota(jnp.int32, (1, WIDE), 1) < slab
         for r in range(2):
             for other in range(2):
                 for e in range(n_ep):
-                    mine = bias_tiles[0, r, other][e, 0:1]
-                    theirs = bias_tiles[1, r, other][e, 0:1]
+                    mine = gathered_row(bias_tiles[0, r, other][e], strip)
+                    theirs = gathered_row(bias_tiles[1, r, other][e], strip)
                     first = jnp.where(side == 0, mine, theirs)
                     second = jnp.where(side == 0, theirs, mine)
                     row_tile = jnp.where(low_half, first, pltpu.roll(second, slab, 1))
                     k = r + 2 * other
                     bias_ref[k : k + 1, e * WIDE : (e + 1) * WIDE] = row_tile
+        features(mask_ref, fa, own_ref)
+        features(mask_ref, fb, other_ref)
 
     return simple(
-        body,
-        [
-            shape_of((2, n_ep, 2, slab, TAIL), bf16),
-            shape_of((n_ep, 2, 2, 2, strip, 3 * TAIL), bf16),
-            shape_of((n_ep, 2, 2, 2, strip, WIDE), bf16),
-            shape_of((8, n_ep * 2 * slab), f32),
-            shape_of((4, n_ep * 2 * slab), f32),
-        ],
-        *tops,
-        *lows,
-        scalars=places,
-        name="unpack_main",
+        body, shapes, *tops, *lows, feats, feats_low, mask, scalars=places, name="unpack_main"
     )
 
 
@@ -672,52 +869,39 @@
     )
 
 
-def back_body(order, dq_ref, dk_ref, dv_ref, wp, other_ref, own_ref):
-    step = pl.program_id(0)
-
+def back_body(dq_ref, dk_ref, dv_ref, wp, out_ref):
     def columns(k):
         return jnp.concatenate([wp[h, :, k * HEAD : (k + 1) * HEAD] for h in range(2)], axis=1)
 
     def both(ref):
-        return jnp.concatenate([ref[h].astype(bf16) for h in range(2)], axis=1)
-
-    base = dot(dq_ref[...], columns(0), NT)
-
-    def store(value):
-        @pl.when(step < 2)
-        def _():
-            other_ref[...] = value.astype(bf16)
-
-        @pl.when(step >= 2)
-        def _():
-            own_ref[...] = value
-
-    @pl.when(step % 2 == 0)
+        return jnp.concatenate([ref[h].astype(bf16) for h in range(2)], axis=0).T
+
+    total = dot(dq_ref[...], columns(0), NT)
+
+    @pl.when(pl.program_id(0) == 0)
     def _():
-        store(base + dot(both(dk_ref), columns(1), NT) + dot(both(dv_ref), columns(2), NT))
-
-    @pl.when(step % 2 == 1)
+        more = dot(both(dk_ref), columns(1), NT) + dot(both(dv_ref), columns(2), NT)
+        out_ref[...] = (total + more).astype(out_ref.dtype)
+
+    @pl.when(pl.program_id(0) == 1)
     def _():
-        store(base)
-
-
-def back_rows(dq, dk, dv, wp):
+        out_ref[...] = total.astype(out_ref.dtype)
+
+
+def back_rows(dq, dk, dv, wp, which, dtype):
     half = dq.shape[0] // 4
     width = wp.shape[1]
-    turn = lambda i: (i + 2) % 4
-    key = pl.BlockSpec((2, half, HEAD), lambda i: (0, 3 - i // 2, 0))
+    key = pl.BlockSpec((2, HEAD, half), lambda i: (0, 0, 2 + which))
     return pl.pallas_call(
-        functools.partial(back_body, None),
-        grid=(4,),
-        in_specs=[pl.BlockSpec((half, 2 * HEAD), lambda i: (turn(i), 0)), key, key, whole()],
-        out_specs=[
-            pl.BlockSpec((half, width), lambda i: (jnp.minimum(i, 1), 0)),
-            pl.BlockSpec((half, width), lambda i: (jnp.maximum(i - 2, 0), 0)),
-        ],
-        out_shape=[shape_of((2 * half, width), bf16), shape_of((2 * half, width), f32)],
-        cost_estimate=cost(6),
+        back_body,
+        grid=(2,),
+        in_specs=[pl.BlockSpec((half, 2 * HEAD), lambda i: (2 * which + i, 0)), key, key, whole()],
+        out_specs=pl.BlockSpec((half, width), lambda i: (i, 0)),
+        out_shape=pltpu.HBM((2 * half, width), dtype),
+        compiler_params=pltpu.CompilerParams(vmem_limit_bytes=32 << 20),
+        cost_estimate=cost(3),
         name="back_rows",
-    )(dq, dk, dv, wp)
+    )(*held((dq, dk, dv, wp), False))
 
 
 def weight_body(x_ref, dq_ref, dk_ref, dv_ref, prompt, wp, gb1, gw_ref, gp_ref, gb_ref, acc, gq_ref, gv_ref):
@@ -732,31 +916,32 @@
     flip = x_ref[...].T
     acc[0] += dot(flip, dq_ref[...], NN)
     gq_ref[...] += jnp.sum(dq_ref[...].astype(f32), axis=0, keepdims=True)
-    grad_key = jnp.concatenate([dk_ref[h] for h in range(2)], axis=1)
-    grad_value = jnp.concatenate([dv_ref[h] for h in range(2)], axis=1)
+    grad_key = jnp.concatenate([dk_ref[h] for h in range(2)], axis=0)
+    grad_value = jnp.concatenate([dv_ref[h] for h in range(2)], axis=0)
     key_high = grad_key.astype(bf16)
     value_high = grad_value.astype(bf16)
+    ones = jnp.ones((8, grad_key.shape[1]), bf16)
+    gv_ref[...] += dot(ones, value_high, NT)[0:1]
 
     @pl.when(step % 2 == 0)
     def _():
-        acc[1] += dot(flip, key_high, NN)
-        acc[2] += dot(flip, value_high, NN)
-        gv_ref[...] += jnp.sum(value_high.astype(f32), axis=0, keepdims=True)
+        acc[1] += dot(flip, key_high, NT)
+        acc[2] += dot(flip, value_high, NT)
 
     @pl.when(step % 2 == 1)
     def _():
         key_low = (grad_key - key_high.astype(f32)).astype(bf16)
         value_low = (grad_value - value_high.astype(f32)).astype(bf16)
         source = prompt[...]
-        acc[1] += dot(source, key_high, NN) + dot(source, key_low, NN)
-        acc[2] += dot(source, value_high, NN) + dot(source, value_low, NN)
-        gv_ref[...] += jnp.sum(grad_value, axis=0, keepdims=True)
+        acc[1] += dot(source, key_high, NT) + dot(source, key_low, NT)
+        acc[2] += dot(source, value_high, NT) + dot(source, value_low, NT)
+        gv_ref[...] += dot(ones, value_low, NT)[0:1]
         w_key, w_value = (
             jnp.concatenate([wp[h, :, k * HEAD : (k + 1) * HEAD] for h in range(2)], axis=1)
             for k in (1, 2)
         )
-        total = dot(w_key, key_high, NT) + dot(w_key, key_low, NT)
-        total = total + dot(w_value, value_high, NT) + dot(w_value, value_low, NT)
+        total = dot(w_key, key_high, NN) + dot(w_key, key_low, NN)
+        total = total + dot(w_value, value_high, NN) + dot(w_value, value_low, NN)
         gp_ref[...] = total.astype(bf16)
 
     @pl.when(step == 3)
@@ -775,7 +960,7 @@
     half = dq.shape[0] // 4
     width = wp.shape[1]
     spot = lambda i: jnp.where(i % 2 == 0, 2 + i // 2, i // 2)
-    key = pl.BlockSpec((2, half, HEAD), lambda i: (0, spot(i), 0))
+    key = pl.BlockSpec((2, HEAD, half), lambda i: (0, 0, spot(i)))
     return pl.pallas_call(
         weight_body,
         grid=(4,),
@@ -794,15 +979,16 @@
             pl.BlockSpec((4, width), lambda i: (0, 0)),
         ],
         out_shape=[
-            shape_of((2, width, TAIL), bf16),
-            shape_of((width, PAD), bf16),
-            shape_of((4, width), f32),
+            pltpu.VMEM((2, width, TAIL), bf16),
+            pltpu.VMEM((width, PAD), bf16),
+            pltpu.VMEM((4, width), f32),
         ],
+        compiler_params=pltpu.CompilerParams(vmem_limit_bytes=40 << 20),
         scratch_shapes=[pltpu.VMEM((3, width, 2 * HEAD), f32)]
         + [pltpu.VMEM((1, 2 * HEAD), f32)] * 2,
         cost_estimate=cost(9),
         name="weight_grads",
-    )(x, dq, dk, dv, prompt, wp, gb1)
+    )(*held((x, dq, dk, dv, prompt, wp), False), gb1)
 
 
 def input_body(sc, ratio, dr_ref, own_ref, got_ref, rows_ref, enc, mask, rows_grad, i0, i1, i2, i3, small_ref, acc, bias):
@@ -826,7 +1012,7 @@
 
         @pl.when(step == k)
         def _(ref=ref):
-            ref[...] = grad[0:VEC]
+            ref[...] = grad[0:FEAT_ROWS].astype(bf16)
 
     @pl.when(step == 3)
     def _():
@@ -848,7 +1034,7 @@
     width = enc.shape[0]
     spot = lambda i, sc: (2 * (sc[0] ^ (i // 2)) + (sc[1] ^ (i % 2)), 0)
     block = pl.BlockSpec((size, width), spot)
-    fixed = pl.BlockSpec((VEC, size), lambda i, sc: (0, 0))
+    fixed = pl.BlockSpec((FEAT_ROWS, size), lambda i, sc: (0, 0))
     return pl.pallas_call(
         input_body,
         grid_spec=pltpu.PrefetchScalarGridSpec(
@@ -867,10 +1053,11 @@
             out_specs=[fixed] * 4 + [pl.BlockSpec((width, WIDE), lambda i, sc: (0, 0))],
             scratch_shapes=[pltpu.VMEM((width, WIDE), f32), pltpu.VMEM((1, width), f32)],
         ),
-        out_shape=[shape_of((VEC, size), f32)] * 4 + [shape_of((width, WIDE), bf16)],
+        out_shape=[pltpu.VMEM((FEAT_ROWS, size), bf16)] * 4 + [pltpu.VMEM((width, WIDE), bf16)],
+        compiler_params=pltpu.CompilerParams(vmem_limit_bytes=32 << 20),
         cost_estimate=cost(6),
         name="input_grads",
-    )(sc, ratio, dr, own, got, rows, enc, mask, rows_grad)
+    )(sc, ratio, *held((dr, own, got, rows), False), enc, mask, rows_grad)
 
 
 def split_prompt(grad, bias_rows, places, n_ep, strip):
@@ -921,27 +1108,22 @@
     return simple(body, [shape, shape], blocks, scalars=places, name="split_small")
 
 
-def pack_main(gw, mine, got, small_mine, small_got, places, slab, strip):
+def pack_main(gw, mine, got, places, slab, strip):
     n_ep = mine.shape[0]
     heads = gw.reshape(2, n_ep, 2, slab, TAIL)
-    small_mine = small_mine.reshape(n_ep, 2, 2, strip, WIDE)
-    small_got = small_got.reshape(n_ep, 2, 2, strip, WIDE)
     if 2 * slab != WIDE:
         pair = (mine.astype(f32) + got.astype(f32)).astype(bf16)
-        small = (small_mine.astype(f32) + small_got.astype(f32)).astype(bf16)
-        small = jnp.pad(small, [(0, 0)] * 4 + [(0, TAIL - WIDE)])
-        low = jnp.concatenate([pair, small], axis=3)
         outs = []
         for b in (0, 1):
             for r in (0, 1):
                 side, row = places[0] ^ b, places[1] ^ r
-                part = lax.dynamic_index_in_dim(low, side, 1, keepdims=False)
+                part = lax.dynamic_index_in_dim(pair, side, 1, keepdims=False)
                 part = lax.dynamic_index_in_dim(part, row, 1, keepdims=False)
                 head = lax.dynamic_index_in_dim(heads[r], side, 1, keepdims=False)
                 outs.append(jnp.concatenate([head, part], axis=1))
         return outs
 
-    def body(sc, gw_ref, a_ref, b_ref, c_ref, d_ref, *outs):
+    def body(sc, gw_ref, a_ref, b_ref, *outs):
         for b in range(2):
             for r in range(2):
                 out = outs[2 * b + r]
@@ -949,45 +1131,119 @@
                 out[:, 0:slab, :] = gw_ref[r, :, side]
                 pair = a_ref[:, side, row].astype(f32) + b_ref[:, side, row].astype(f32)
                 out[:, slab : slab + 3 * strip, :] = pair.astype(bf16)
-                pair = c_ref[:, side, row].astype(f32) + d_ref[:, side, row].astype(f32)
-                out[:, slab + 3 * strip :, 0:WIDE] = pair.astype(bf16)
-                out[:, slab + 3 * strip :, WIDE:] = jnp.zeros((n_ep, strip, TAIL - WIDE), bf16)
-
-    shape = shape_of((n_ep, slab + 4 * strip, TAIL), bf16)
+
+    shape = shape_of((n_ep, slab + 3 * strip, TAIL), bf16)
+    return simple(body, [shape] * 4, heads, mine, got, scalars=places, name="pack_main")
+
+
+def pack_small(ins, mine, got, places, n_ep, strip):
+    rows = ins[0].shape[1]
+    mine = mine.reshape(n_ep, 2, 2, strip, WIDE)
+    got = got.reshape(n_ep, 2, 2, strip, WIDE)
+    total = FEAT_ROWS + n_ep * strip
+    if 8 * strip != WIDE:
+        pair = (mine.astype(f32) + got.astype(f32)).astype(bf16)
+        outs = []
+        for k in range(4):
+            part = lax.dynamic_index_in_dim(pair, places[0] ^ (k // 2), 1, keepdims=False)
+            part = lax.dynamic_index_in_dim(part, places[1] ^ (k % 2), 1, keepdims=False)
+            part = jnp.pad(part.reshape(n_ep * strip, WIDE), ((0, 0), (0, rows - WIDE)))
+            outs.append(jnp.concatenate([ins[k], part], axis=0))
+        return outs
+
+    def body(sc, *refs):
+        in_refs, a_ref, b_ref, outs = refs[0:4], refs[4], refs[5], refs[6:]
+        for k in range(4):
+            side, row = sc[0] ^ (k // 2), sc[1] ^ (k % 2)
+            outs[k][0:FEAT_ROWS] = in_refs[k][...]
+            pair = a_ref[:, side, row].astype(f32) + b_ref[:, side, row].astype(f32)
+            outs[k][FEAT_ROWS:, 0:WIDE] = pair.reshape(n_ep * strip, WIDE).astype(bf16)
+
     return simple(
-        body, [shape] * 4, heads, mine, got, small_mine, small_got, scalars=places, name="pack_main"
-    )
-
-
-def pack_rest(mine, got, places, n_ep, slab):
+        body, [shape_of((total, rows), bf16)] * 4, *ins, mine, got, scalars=places, name="pack_small"
+    )
+
+
+def pack_rest(mine, got, outs, places, n_ep, slab):
     width = mine.shape[-1]
+    rows, lanes = outs[0].shape
+    count = n_ep * slab
     mine = mine.reshape(2, n_ep, 2, slab, width)
     got = got.reshape(2, n_ep, 2, slab, width)
 
-    def body(sc, a_ref, b_ref, *outs):
-        for b in range(2):
-            for r in range(2):
-                pair = a_ref[r, :, sc[0] ^ b].astype(f32) + b_ref[r, :, sc[0] ^ b].astype(f32)
-                outs[2 * b + r][...] = pair.astype(bf16)
-
-    shape = shape_of((n_ep, slab, width), bf16)
-    return simple(body, [shape] * 4, mine, got, scalars=places, name="pack_rest")
-
-
-def sum_plane(parts, places, name):
-    n_ep = parts[0].shape[0]
+    def body(sc, a_ref, b_ref, *refs):
+        for k in range(4):
+            side = sc[0] ^ (k // 2)
+            pair = a_ref[k % 2, :, side].astype(f32) + b_ref[k % 2, :, side].astype(f32)
+            refs[4 + k][0:count] = pair.reshape(count, width).astype(bf16)
+            refs[4 + k][count:, 0:lanes] = refs[k][...]
+
+    shape = shape_of((count + rows, width), bf16)
+    return simple(body, [shape] * 4, mine, got, *outs, scalars=places, name="pack_rest")
+
+
+def sum_rest(parts, places, n_ep, slab):
+    width = parts[0].shape[1]
+    if n_ep > 4:
+        total = sum(part[0 : n_ep * slab].astype(f32) for part in parts)
+        return reduce_ep(total.reshape(n_ep, slab, width), None)
 
     def body(sc, *refs):
         ins, outs = refs[: len(parts)], refs[len(parts) :]
         for k, out in enumerate(outs):
+            spot = pl.multiple_of((sc[6] ^ k) * slab, slab)
+            total = ins[0][pl.ds(spot, slab), :].astype(f32)
+            for ref in ins[1:]:
+                total = total + ref[pl.ds(spot, slab), :].astype(f32)
+            out[...] = total.astype(bf16)
+
+    pieces = simple(
+        body, [shape_of((slab, width), bf16)] * n_ep, *parts, scalars=places, name="sum_rest"
+    )
+    return reduce_ep(None, pieces)
+
+
+def sum_main(mains, smalls, places, slab, strip):
+    n_ep = mains[0].shape[0]
+    if n_ep > 4:
+        total = sum(part.astype(f32) for part in mains)
+        small = sum(part[FEAT_ROWS:, 0:WIDE].astype(f32) for part in smalls)
+        small = jnp.pad(small.reshape(n_ep, strip, WIDE), ((0, 0), (0, 0), (0, TAIL - WIDE)))
+        return reduce_ep(jnp.concatenate([total, small], axis=1), None)
+
+    def body(sc, *refs):
+        main_refs, small_refs, outs = refs[0:4], refs[4:8], refs[8:]
+        for k, out in enumerate(outs):
             spot = sc[6] ^ k
-            total = ins[0][spot].astype(f32)
-            for ref in ins[1:]:
+            total = main_refs[0][spot].astype(f32)
+            for ref in main_refs[1:]:
                 total = total + ref[spot].astype(f32)
-            out[...] = total.astype(bf16)
-
-    shape = shape_of(parts[0].shape[1:], bf16)
-    return simple(body, [shape] * n_ep, *parts, scalars=places, name=name)
+            out[0 : slab + 3 * strip] = total.astype(bf16)
+            where = pl.multiple_of(FEAT_ROWS + spot * strip, strip)
+            total = small_refs[0][pl.ds(where, strip), 0:WIDE].astype(f32)
+            for ref in small_refs[1:]:
+                total = total + ref[pl.ds(where, strip), 0:WIDE].astype(f32)
+            out[slab + 3 * strip :, 0:WIDE] = total.astype(bf16)
+            out[slab + 3 * strip :, WIDE:] = jnp.zeros((strip, TAIL - WIDE), bf16)
+
+    shape = shape_of((slab + 4 * strip, TAIL), bf16)
+    pieces = simple(body, [shape] * n_ep, *mains, *smalls, scalars=places, name="sum_main")
+    return reduce_ep(None, pieces)
+
+
+def place_rows(parts, index, begin, shape, dtype, name):
+    def body(sc, *refs):
+        for k, ref in enumerate(refs[:-1]):
+            refs[-1][sc[0] ^ k] = ref[begin : begin + shape[0], 0 : shape[1]].astype(dtype)
+
+    return simple(
+        body,
+        shape_of((len(parts),) + shape, dtype),
+        *parts,
+        scalars=index.reshape(1).astype(jnp.int32),
+        near=(True, False),
+        name=name,
+    )
 
 
 def final_sums(mains, rests, slab, strip):
@@ -1073,7 +1329,7 @@
     for k, param in enumerate(params):
         low = (slab, 8 * HEAD) if k == 0 else param.shape
         shapes += [shape_of(param.shape, f32)] * 3 + [shape_of(low, bf16)]
-    return simple(body, shapes, squares, *params, *moments, *grads, name="adam_all")
+    return simple(body, shapes, squares, *params, *moments, *grads, near=(True, False), name="adam_all")
 
 
 def shards(
@@ -1101,7 +1357,6 @@
     width = cotangent.shape[3]
     slab = block_weights.shape[0]
     strip = encoder.shape[0]
-    quad = [(b, r) for b in (0, 1) for r in (0, 1)]
 
     mask_row = lax.dynamic_index_in_dim(feat_mask, chip, 0, keepdims=False)
     count_pair = lax.dynamic_index_in_dim(counts, chip, 0, keepdims=False)
@@ -1112,51 +1367,43 @@
     for k, value in ((0, side), (1, row), (2, core), (3, chip), (6, lax.axis_index("ep"))):
         places = places + jnp.where(spot == k, value, 0)
 
-    def canonical(got):
-        first = [jnp.concatenate(pick(got[b, 0], got[b, 1], row), axis=0) for b in (0, 1)]
-        return jnp.concatenate(pick(first[0], first[1], side), axis=0)
-
     def to_chip(array):
-        return plane_swap(
-            lambda b, r: lax.dynamic_index_in_dim(array[0], chip ^ (2 * b + r), 0, keepdims=False)
+        return plane_list(
+            [lax.dynamic_index_in_dim(array[0], chip ^ k, 0, keepdims=False) for k in range(4)]
         )
+
+    def plane_list(parts):
+        got = plane_swap(lambda b, r: parts[2 * b + r])
+        return [got[b, r] for b in (0, 1) for r in (0, 1)]
 
     main_part, rest_part = pack_parts(
         block_weights, prompt, encoder, shared_vectors, head_biases
     )
-    got = to_chip(feats)
-    main_along = gather_ep(main_part, "stack_main")
-    feats_own = canonical(got)
-    masked_own = jnp.pad(feats_own * mask_row.astype(bf16), ((0, 0), (0, WIDE - FEAT)))
-    masked_other = swap(masked_own, core=1)
-    tops = plane_swap(lambda b, r: main_along)
-    tops = [tops[key] for key in quad]
+    mask_wide = jnp.pad(mask_float, (0, WIDE - FEAT)).reshape(1, WIDE)
+    flipped = jnp.transpose(feats[0], (0, 2, 1))
+    main_pieces = gather_ep(main_part)
+    feats_parts = plane_list(
+        [lax.dynamic_index_in_dim(flipped, chip ^ k, 0, keepdims=False) for k in range(4)]
+    )
+    main_pieces, feats_parts = lax.optimization_barrier((main_pieces, feats_parts))
+    feats_own = join_features(feats_parts, places)
+    feats_other = swap(feats_own, core=1)
+    main_along = stack_ep(main_pieces, "stack_main")
+    tops = plane_list([main_along] * 4)
     lows = [swap(top, core=1) for top in tops]
-    w_project, prompt_low, small_low, vector_rows, bias_rows = unpack_main(
-        tops, lows, places, slab, strip
+    w_project, prompt_low, small_low, vector_rows, bias_rows, masked_own, masked_other = unpack_main(
+        tops, lows, feats_own, feats_other, mask_wide, places, slab, strip
     )
     w_project = w_project.reshape(2, width, TAIL)
     prompt_low = prompt_low.reshape(width, 3 * TAIL)
     encoder_low = small_low.reshape(width, WIDE)
 
-    rest_part = tie(rest_part, main_along)
-    rest_along = gather_ep(rest_part, "stack_rest")
-    rest_along = tie(rest_along, tops[3])
-    rest_tops = plane_swap(lambda b, r: rest_along)
-    rest_own = unpack_rest([rest_tops[key] for key in quad], places)
-    rest_own = rest_own.reshape(2, width, -1)
-    rest_other = swap(rest_own, core=1)
-
-    lane = jnp.arange(rows, dtype=jnp.int32)
-
-    def slots_of(which_core):
-        return jnp.concatenate([which_core * rows + lane, (2 + which_core) * rows + lane])
-
-    key_slots = jnp.concatenate([slots_of(core), slots_of(1 - core)])
-    key_live = jnp.concatenate([jnp.arange(PAD) < PROMPT, key_slots < count_pair[0]])
-    key_bias = jnp.where(key_live, 0.0, neg_big)[:, None].astype(f32)
-    rows_low, query, keys, keys_flip, values, values_flip = project(
+    rest_along = stack_ep(gather_ep(tie(rest_part, feats_other)), "stack_rest")
+    cots = to_chip(tie(cotangent, w_project))
+
+    rows_low, query, keys, keys_flip, values, values_flip, key_extra = project(
         ratio,
+        places,
         masked_own,
         masked_other,
         encoder_low,
@@ -1165,17 +1412,22 @@
         bias_rows,
         prompt_low,
     )
-    attended_other, lse_other = attend(query, keys, values_flip, key_bias, 1)
+    query, rest_along, cots = lax.optimization_barrier((query, rest_along, cots))
+    rest_tops = plane_list([rest_along] * 4)
+    attended_other, extra_other = attend(query, keys, key_extra, values_flip, 1)
     attended_got = swap(attended_other, core=1)
-    attended_own, lse_own = attend(query, keys, values_flip, key_bias, 0)
-    cots = to_chip(tie(cotangent, tops[3]))
+    query_own = tie(query, (attended_other, rest_tops[1]))
+    attended_own, extra_own = attend(query_own, keys, key_extra, values_flip, 0)
+    rest_own = unpack_rest(tie(rest_tops, attended_own), places)
+    rest_own = rest_own.reshape(2, width, -1)
+    rest_other = swap(rest_own, core=1)
     (y0, y1, y2, y3, grad_own, grad_sent, grad_one, rest_mine, rest_sent, grad_rows, grad_hidden_row) = middle(
         places,
         ratio,
         masked_own,
         attended_own,
         attended_got,
-        [cots[key] for key in quad],
+        cots,
         encoder_low,
         vector_rows,
         bias_rows,
@@ -1184,24 +1436,34 @@
     )
     grad_got = swap(grad_sent, core=1)
     rest_got = swap(rest_sent, core=1)
-    outs = (y0, y1, y2, y3)
-    outs = plane_swap(lambda b, r: outs[2 * b + r])
-    output_final = place([outs[key] for key in quad], chip, "place_output")[None]
-    rest_parts = pack_rest(rest_mine, rest_got, places, n_ep, slab)
-    rest_tops = plane_swap(lambda b, r: rest_parts[2 * b + r])
-    rest_pieces = reduce_plane([rest_tops[key] for key in quad], places, "sum_rest")
-
+    rest_parts = pack_rest(rest_mine, rest_got, (y0, y1, y2, y3), places, n_ep, slab)
+    rest_tops = plane_list(rest_parts)
     query_again, *unused = lax.optimization_barrier((query, *rest_parts))
     grad_query, grad_key, grad_value = attend_back(
-        query_again, keys, keys_flip, values, key_bias, lse_own, lse_other, grad_own, grad_got
-    )
-    back_other, back_own = back_rows(grad_query, grad_key, grad_value, w_project)
-    back_got = swap(back_other, core=1)
+        query_again,
+        keys,
+        key_extra,
+        keys_flip,
+        values,
+        extra_own,
+        extra_other,
+        grad_own,
+        grad_got,
+    )
+    rest_tops, grad_query = lax.optimization_barrier((rest_tops, grad_query))
+    rest_pieces = sum_rest(rest_tops, places, n_ep, slab)
     grad_project, grad_prompt, grad_bias = weight_grads(
         rows_low, grad_query, grad_key, grad_value, prompt_low, w_project, grad_hidden_row
     )
     prompt_mine, prompt_sent = split_prompt(grad_prompt, grad_bias, places, n_ep, strip)
     prompt_got = swap(prompt_sent, core=1)
+    back_other = back_rows(grad_query, grad_key, grad_value, w_project, 1, bf16)
+    back_got = swap(back_other, core=1)
+    prompt_got = tie(prompt_got, back_other)
+    main_parts = pack_main(grad_project, prompt_mine, prompt_got, places, slab, strip)
+    main_tops = plane_list(main_parts)
+    grad_query, *unused = lax.optimization_barrier((grad_query, *main_parts))
+    back_own = back_rows(grad_query, grad_key, grad_value, w_project, 0, f32)
     i0, i1, i2, i3, grad_small = input_grads(
         places,
         ratio,
@@ -1210,19 +1472,21 @@
         back_got,
         masked_own,
         encoder_low,
-        jnp.pad(mask_float, (0, WIDE - FEAT)).reshape(WIDE, 1),
+        mask_wide.reshape(WIDE, 1),
         grad_rows,
     )
+    grad_small, rest_pieces = lax.optimization_barrier((grad_small, rest_pieces))
     small_mine, small_sent = split_small(grad_small, places, n_ep, strip)
     small_got = swap(small_sent, core=1)
-    main_parts = pack_main(
-        grad_project, prompt_mine, prompt_got, small_mine, small_got, places, slab, strip
-    )
-    main_tops = plane_swap(lambda b, r: main_parts[2 * b + r])
-    ins = (i0, i1, i2, i3)
-    ins = plane_swap(lambda b, r: ins[2 * b + r])
-    main_pieces = reduce_plane([main_tops[key] for key in quad], places, "sum_main")
-    input_final = place([ins[key] for key in quad], chip, "place_input")
+    small_tops = plane_list(
+        pack_small((i0, i1, i2, i3), small_mine, small_got, places, n_ep, strip)
+    )
+    output_final = place_rows(
+        rest_tops, chip, n_ep * slab, (rows, width), bf16, "place_output"
+    )
+    main_tops, output_final = lax.optimization_barrier((main_tops, output_final))
+    main_pieces = sum_main(main_tops, small_tops, places, slab, strip)
+    input_final = place_rows(small_tops, chip, 0, (FEAT_ROWS, rows), f32, "place_input")
     input_final = jnp.transpose(input_final[:, 0:FEAT], (0, 2, 1))[None]
 
     grad_block, grad_prompt_own, grad_small_own, grad_bias_own, square_tile = final_sums(
@@ -1234,7 +1498,7 @@
     if n_ep > 4:
         squares = lax.psum(square_tile, "ep")[None]
     else:
-        squares = gather_ep(square_tile, "stack_square")
+        squares = stack_ep(gather_ep(square_tile), "stack_square")
     grad_norm, *news = adam_all(
         squares,
         (
@@ -1259,7 +1523,7 @@
     vector_out = tuple(part.T for part in news[12:16])
     bias_out = tuple(part.T for part in news[16:20])
     return (
-        (output_final, input_final, grad_norm.reshape(()))
+        (output_final[None], input_final, grad_norm.reshape(()))
         + block_out
         + bias_out
         + encoder_out

time: 284 us -> 223 us (0.79)
  Pallas kernels: 145 us -> 110 us
  waiting for transfers between devices: 59.3 us -> 47.2 us
  local copies, waits for them, and re-layouts: 15.5 us -> 7.69 us
  starting transfers between devices: 58.6 us -> 54.1 us
    pallas_call x16 -> x18, Pallas kernels: 35.5 us -> 15.2 us  [simple(): pl.pallas_call(body, in_specs=specs, out_specs=[whole()] * len(out_shape)...]
    ppermute x55 -> x52, waiting for transfers between devices: 59.3 us -> 47.2 us  [swap(): return lax.ppermute(value, AXES, pairs)]
    pallas_call x4 -> x5, Pallas kernels: 59 us -> 50.4 us  [the longest x1 25.5 us: attend_back(): pl.pallas_call(attend_back_body, grid=(2, 2), in_specs=[pl.BlockSpec((1,...]
    unnamed x127 -> x71, local copies, waits for them, and re-layouts: 10.7 us -> 5.39 us
    ppermute x55 -> x52, starting transfers between devices: 58.6 us -> 54.1 us  [swap(): return lax.ppermute(value, AXES, pairs)]
    pallas_call x1, Pallas kernels: 25.5 us -> 22.4 us  [middle(): pl.pallas_call(middle_body, grid_spec=pltpu.PrefetchScalarGridSpec(num_sc...]
  transfers between devices with their start and end apart: 55 -> 52, of which waited for: 19 -> 21; matrix products, arithmetic and copies ran while one was open for 3% -> 1% of each run, Pallas kernels for 26% -> 37%
where the time goes in v3:
time: 223 us; the launch traced here: 222 us
  Pallas kernels  110 us (49%)
  starting transfers between devices  54.1 us (24%)
  waiting for transfers between devices  47.2 us (21%)
  local copies, waits for them, and re-layouts  7.69 us (3%)
    ppermute x52, starting transfers between devices, swap(): return lax.ppermute(value, AXES, pairs)  54.1 us
    ppermute x52, waiting for transfers between devices, swap(): return lax.ppermute(value, AXES, pairs)  47.2 us
    pallas_call x1, Pallas kernels, attend_back(): pl.pallas_call(attend_back_body, grid=(2, 2), in_specs=[pl.BlockSpec((1,...  25.5 us
    pallas_call x1, Pallas kernels, middle(): pl.pallas_call(middle_body, grid_spec=pltpu.PrefetchScalarGridSpec(num_sc...  22.4 us
    pallas_call x2, Pallas kernels, attend(): pl.pallas_call(attend_body, grid=(2,), in_specs=[pl.BlockSpec((1, SLOTS,...  17.5 us
    pallas_call x18, Pallas kernels, simple(): pl.pallas_call(body, in_specs=specs, out_specs=[whole()] * len(out_shape)...  15.2 us
    pallas_call x1, Pallas kernels, project(): pl.pallas_call(project_body, grid=(4,), in_specs=[pl.BlockSpec(memory_spa...  8.8 us
    pallas_call x1, Pallas kernels, weight_grads(): pl.pallas_call(weight_body, grid=(4,), in_specs=[pl.BlockSpec((half, widt...  8.13 us
  transfers between devices with their start and end apart: 52, of which 21 were waited for; matrix products, arithmetic and copies ran while one was open for 1% of the time, Pallas kernels for 37%

profile of v3, /device:TPU:0, one launch (start us, length us, event | category | flops | bytes accessed | tf_op | source)
XLA Modules:
  0.0 222.4 jit_solution(571657156122353317)
XLA Ops:
  2.6 3.0 %collective-permute-start.3 = (bf16[100,256]{1,0:T(8,128)(2,1)S(1)}, bf16[100,256]{1,0:T(8,128)(2,1)S(1)}, u32[]{:S(2)}, u32[]{:S(2)}) collective-permute-start(bf16[100,256]{1,0:T(8,128)(2,1)S(1)} %bitcast.111), channel_id=1, source_target_pairs={{0,2},{1,3},{2,0},{3,1},{4,6},{5,7},{6,4},{7,5},{8,10},{9,11},{10,... | collective-permute-start | bytes 153608 | tf_op jit(solution)/shard_map/ppermute | solution.py:44
  8.9 2.6 %collective-permute-start.1 = (bf16[112,384]{1,0:T(8,128)(2,1)S(1)}, bf16[112,384]{1,0:T(8,128)(2,1)S(1)}, u32[]{:S(2)}, u32[]{:S(2)}) collective-permute-start(bf16[112,384]{1,0:T(8,128)(2,1)S(1)} %get-tuple-element.155.refs_0_), channel_id=1, source_target_pairs={{0,16},{1,17},{2,18},{3,19},{4,20},{5,21},{6,22},{7,23},{8,24},{9,... | collective-permute-start | bytes 258056 | tf_op jit(solution)/shard_map/ppermute | solution.py:44
  13.7 2.3 %collective-permute-done.4.refs_2_ = bf16[100,256]{1,0:T(8,128)(2,1)S(1)} collective-permute-done((bf16[100,256]{1,0:T(8,128)(2,1)S(1)}, bf16[100,256]{1,0:T(8,128)(2,1)S(1)}, u32[]{:S(2)}, u32[]{:S(2)}) %collective-permute-start.4) | collective-permute-done | bytes 51232 | tf_op jit(solution)/shard_map/ppermute | solution.py:44
  16.0 2.5 %collective-permute-done.5.refs_3_ = bf16[100,256]{1,0:T(8,128)(2,1)S(1)} collective-permute-done((bf16[100,256]{1,0:T(8,128)(2,1)S(1)}, bf16[100,256]{1,0:T(8,128)(2,1)S(1)}, u32[]{:S(2)}, u32[]{:S(2)}) %collective-permute-start.5) | collective-permute-done | bytes 51232 | tf_op jit(solution)/shard_map/ppermute | solution.py:44
  22.3 6.3 %collective-permute-done.6.t1 = bf16[4,112,384]{2,1,0:T(8,128)(2,1)S(1)} collective-permute-done((bf16[4,112,384]{2,1,0:T(8,128)(2,1)S(1)}, bf16[4,112,384]{2,1,0:T(8,128)(2,1)S(1)}, u32[]{:S(2)}, u32[]{:S(2)}) %collective-permute-start.6) | collective-permute-done | bytes 344096 | tf_op jit(solution)/shard_map/ppermute | solution.py:44
  30.1 4.9 %collective-permute-done.8.t3 = bf16[4,112,384]{2,1,0:T(8,128)(2,1)S(1)} collective-permute-done((bf16[4,112,384]{2,1,0:T(8,128)(2,1)S(1)}, bf16[4,112,384]{2,1,0:T(8,128)(2,1)S(1)}, u32[]{:S(2)}, u32[]{:S(2)}) %collective-permute-start.8) | collective-permute-done | bytes 344096 | tf_op jit(solution)/shard_map/ppermute | solution.py:44
  39.0 2.3 %collective-permute-start.14 = (bf16[64,640]{1,0:T(8,128)(2,1)}, bf16[64,640]{1,0:T(8,128)(2,1)S(1)}, u32[]{:S(2)}, u32[]{:S(2)}) collective-permute-start(bf16[64,640]{1,0:T(8,128)(2,1)} %get-tuple-element.173.refs_0_), channel_id=1, source_target_pairs={{0,8},{1,9},{2,10},{3,11},{4,12},{5,13},{6,14},{7,15},{8,0},{9,1},... | collective-permute-start | bytes 245768 | tf_op jit(solution)/shard_map/ppermute | solution.py:44
  52.1 8.8 %project.1 = (bf16[2048,512]{1,0:T(8,128)(2,1)}, bf16[2,2048,128]{2,1,0:T(8,128)(2,1)}, bf16[2,2048,128]{2,1,0:T(8,128)(2,1)}, bf16[2,128,2048]{2,1,0:T(8,128)(2...) custom-call(f32[1]{0:T(128)} %bitcast.ratio, s32[8]{0:T(128)S(1)} %fusion.5.sc, ...), custom_call_target="tpu_custom_call" | custom-call | flops 2700000000 | bytes 9000000 | tf_op jit(solution)/shard_map/project/pallas_call | solution.py:166
  65.6 8.8 %attend.2 = (bf16[1024,256]{1,0:T(8,128)(2,1)}, bf16[2,1024,128]{2,1,0:T(8,128)(2,1)}) custom-call(bf16[2,2048,128]{2,1,0:T(8,128)(2,1)} %get-tuple-element.201.q_ref, bf16[2,2048,128]{2,1,0:T(8,128)(2,1)} %get-tuple-element.176.k_ref, bf16[2,2048,128]{2,1,0:T(8,128)(2,1)} %get-tuple-element.177.x_ref, bf16[2,128,2048]{2,1,0:T(8,128)(2,1)} %get-tuple-element.178.vt_ref), custom_call_target="tpu_custom_call" | custom-call | flops 1800000000 | bytes 6000000 | tf_op jit(solution)/shard_map/attend/pallas_call | solution.py:262
  74.3 8.8 %attend.3 = (bf16[1024,256]{1,0:T(8,128)(2,1)}, bf16[2,1024,128]{2,1,0:T(8,128)(2,1)}) custom-call(bf16[2,2048,128]{2,1,0:T(8,128)(2,1)} %get-tuple-element.201.q_ref, bf16[2,2048,128]{2,1,0:T(8,128)(2,1)} %get-tuple-element.176.k_ref, bf16[2,2048,128]{2,1,0:T(8,128)(2,1)} %get-tuple-element.177.x_ref, bf16[2,128,2048]{2,1,0:T(8,128)(2,1)} %get-tuple-element.178.vt_ref), custom_call_target="tpu_custom_call" | custom-call | flops 1800000000 | bytes 6000000 | tf_op jit(solution)/shard_map/attend/pallas_call | solution.py:262
  84.4 3.3 %collective-permute-done.21.ob_ref = bf16[1024,256]{1,0:T(8,128)(2,1)S(1)} collective-permute-done((bf16[1024,256]{1,0:T(8,128)(2,1)S(1)}, bf16[1024,256]{1,0:T(8,128)(2,1)S(1)}, u32[]{:S(2)}, u32[]{:S(2)}) %collective-permute-start.21) | collective-permute-done | bytes 524320 | tf_op jit(solution)/shard_map/ppermute | solution.py:44
  87.7 22.4 %middle.1 = (bf16[256,512]{1,0:T(8,128)(2,1)S(1)}, bf16[256,512]{1,0:T(8,128)(2,1)S(1)}, bf16[256,512]{1,0:T(8,128)(2,1)S(1)}, bf16[256,512]{1,0:T(8,128)(2,1)S(...) custom-call(s32[8]{0:T(128)S(1)} %fusion.5.sc, ...), custom_call_target="tpu_custom_call" | custom-call | flops 7500000256 | bytes 25000000 | tf_op jit(solution)/shard_map/middle/pallas_call | solution.py:554
  110.7 3.0 %collective-permute-done.25 = bf16[2,512,640]{2,1,0:T(8,128)(2,1)S(1)} collective-permute-done((bf16[2,512,640]{2,1,0:T(8,128)(2,1)S(1)}, bf16[2,512,640]{2,1,0:T(8,128)(2,1)S(1)}, u32[]{:S(2)}, u32[]{:S(2)}) %collective-permute-start.25) | collective-permute-done | bytes 1310752 | tf_op jit(solution)/shard_map/ppermute | solution.py:44
  119.1 25.5 %attend_back.1 = (bf16[2048,256]{1,0:T(8,128)(2,1)}, f32[2,128,2048]{2,1,0:T(8,128)}, f32[2,128,2048]{2,1,0:T(8,128)}) custom-call(bf16[2,2048,128]{2,1,0:T(8,128)(2,1)} %get-tuple-element.201.q_ref, bf16[2,2048,128]{2,1,0:T(8,128)(2,1)} %get-tuple-element.176.k_ref, bf16[2,2048,128]{2,1,0:T(8,128)(2,1)} %get-tuple-element.177.x_ref, ...), custom_call_target="tpu_custom_call" | custom-call | flops 6000000000 | bytes 20000000 | tf_op jit(solution)/shard_map/attend_back/pallas_call | solution.py:340
  144.6 3.2 %collective-permute-done.28.refs_3_ = bf16[512,640]{1,0:T(8,128)(2,1)S(1)} collective-permute-done((bf16[512,640]{1,0:T(8,128)(2,1)S(1)}, bf16[512,640]{1,0:T(8,128)(2,1)S(1)}, u32[]{:S(2)}, u32[]{:S(2)}) %collective-permute-start.28) | collective-permute-done | bytes 655392 | tf_op jit(solution)/shard_map/ppermute | solution.py:44
  147.8 3.6 %back_rows.2 = bf16[1024,512]{1,0:T(8,128)(2,1)} custom-call(bf16[2048,256]{1,0:T(8,128)(2,1)} %get-tuple-element.229.dq_ref, f32[2,128,2048]{2,1,0:T(8,128)} %get-tuple-element.210.dk_ref, f32[2,128,2048]{2,1,0:T(8,128)} %get-tuple-element.211.dv_ref, bf16[2,512,384]{2,1,0:T(8,128)(2,1)} %bitcast.83), custom_call_target="tpu_custom_call" | custom-call | flops 900000000 | bytes 3000000 | tf_op jit(solution)/shard_map/back_rows/pallas_call | solution.py:895
  151.4 8.1 %weight_grads.1 = (bf16[2,512,384]{2,1,0:T(8,128)(2,1)S(1)}, bf16[512,1024]{1,0:T(8,128)(2,1)S(1)}, f32[4,512]{1,0:T(4,128)S(1)}) custom-call(bf16[2048,512]{1,0:T(8,128)(2,1)} %get-tuple-element.170.x_ref, bf16[2048,256]{1,0:T(8,128)(2,1)} %get-tuple-element.229.dq_ref, f32[2,128,2048]{2,1,0:T(8,128)} %get-tuple-element.210.dk_ref, ...), custom_call_target="tpu_custom_call" | custom-call | flops 2700000000 | bytes 9000000 | tf_op jit(solution)/shard_map/weight_grads/pallas_call | solution.py:964
  164.1 2.9 %collective-permute-start.36 = (bf16[64,640]{1,0:T(8,128)(2,1)S(1)}, bf16[64,640]{1,0:T(8,128)(2,1)S(1)}, u32[]{:S(2)}, u32[]{:S(2)}) collective-permute-start(bf16[64,640]{1,0:T(8,128)(2,1)S(1)} %get-tuple-element.238), channel_id=1, source_target_pairs={{0,16},{1,17},{2,18},{3,19},{4,20},{5,21},{6,22},{7,23},{8,24},{9,... | collective-permute-start | bytes 245768 | tf_op jit(solution)/shard_map/ppermute | solution.py:44
  168.9 3.8 %back_rows.3.own_ref = f32[1024,512]{1,0:T(8,128)} custom-call(bf16[2048,256]{1,0:T(8,128)(2,1)} %get-tuple-element.229.dq_ref, f32[2,128,2048]{2,1,0:T(8,128)} %get-tuple-element.210.dk_ref, f32[2,128,2048]{2,1,0:T(8,128)} %get-tuple-element.211.dv_ref, bf16[2,512,384]{2,1,0:T(8,128)(2,1)} %bitcast.85), custom_call_target="tpu_custom_call" | custom-call | flops 900000000 | bytes 3000000 | tf_op jit(solution)/shard_map/back_rows/pallas_call | solution.py:895
  175.7 5.4 %input_grads.1 = (bf16[112,256]{1,0:T(8,128)(2,1)S(1)}, bf16[112,256]{1,0:T(8,128)(2,1)S(1)}, bf16[112,256]{1,0:T(8,128)(2,1)S(1)}, bf16[112,256]{1,0:T(8,128)(2,1)S(1)}, bf16[512,128]{1,0:T(8,128)(2,1)S(1)}) custom-call(s32[8]{0:T(128)S(1)} %fusion.5.sc, f32[1]{0:T(128)} %bitcast.ratio, f32[1024,512]{1,0:T(8,128)} %get-tuple-element.228.dr_ref, ...), custom_call_target="tpu_custom_call" | custom-call | flops 1800000000 | bytes 6000000 | tf_op jit(solution)/shard_map/input_grads/pallas_call | solution.py:1038
  188.3 3.7 %collective-permute-done.33.refs_3_ = bf16[4,112,384]{2,1,0:T(8,128)(2,1)S(1)} collective-permute-done((bf16[4,112,384]{2,1,0:T(8,128)(2,1)S(1)}, bf16[4,112,384]{2,1,0:T(8,128)(2,1)S(1)}, u32[]{:S(2)}, u32[]{:S(2)}) %collective-permute-start.33) | collective-permute-done | bytes 344096 | tf_op jit(solution)/shard_map/ppermute | solution.py:44
  194.9 3.5 %collective-permute-start.43 = (bf16[128,384]{1,0:T(8,128)(2,1)S(1)}, bf16[128,384]{1,0:T(8,128)(2,1)S(1)}, u32[]{:S(2)}, u32[]{:S(2)}) collective-permute-start(bf16[128,384]{1,0:T(8,128)(2,1)S(1)} %get-tuple-element.253), channel_id=1, source_target_pairs={{0,16},{1,17},{2,18},{3,19},{4,20},{5,21},{6,22},{7,23},{8,24},{9,... | collective-permute-start | bytes 294920 | tf_op jit(solution)/shard_map/ppermute | solution.py:44
  200.2 5.2 %collective-permute-done.43.refs_2_ = bf16[128,384]{1,0:T(8,128)(2,1)S(1)} collective-permute-done((bf16[128,384]{1,0:T(8,128)(2,1)S(1)}, bf16[128,384]{1,0:T(8,128)(2,1)S(1)}, u32[]{:S(2)}, u32[]{:S(2)}) %collective-permute-start.43) | collective-permute-done | bytes 98336 | tf_op jit(solution)/shard_map/ppermute | solution.py:44
  207.8 2.5 %collective-permute-start.48 = (f32[8,128]{1,0:T(8,128)S(1)}, f32[8,128]{1,0:T(8,128)S(1)}, u32[]{:S(2)}, u32[]{:S(2)}) collective-permute-start(f32[8,128]{1,0:T(8,128)S(1)} %add.72), channel_id=1, source_target_pairs={{0,6},{1,7},{2,4},{3,5},{4,2},{5,3},{6,0},{7,1},{8,14},{9,15},{10,... | collective-permute-start | bytes 12296 | tf_op jit(solution)/shard_map/ppermute | solution.py:44
  (189 shorter events, 73.7 us)
Async XLA Ops:
  2.6 10.7 %collective-permute-start.3 = (bf16[100,256]{1,0:T(8,128)(2,1)S(1)}, bf16[100,256]{1,0:T(8,128)(2,1)S(1)}, u32[]{:S(2)}, u32[]{:S(2)}) collective-permute-start(bf16[100,256]{1,0:T(8,128)(2,1)S(1)} %bitcast.111), channel_id=1, source_target_pairs={{0,2},{1,3},{2,0},{3,1},{4,6},{5,7},{6,4},{7,5},{8,10},{9,11},{10,... | collective-permute-start | bytes 153608 | tf_op jit(solution)/shard_map/ppermute | solution.py:44
  7.4 11.1 %collective-permute-start = (bf16[112,384]{1,0:T(8,128)(2,1)S(1)}, bf16[112,384]{1,0:T(8,128)(2,1)S(1)}, u32[]{:S(2)}, u32[]{:S(2)}) collective-permute-start(bf16[112,384]{1,0:T(8,128)(2,1)S(1)} %get-tuple-element.155.refs_0_), channel_id=1, source_target_pairs={{0,8},{1,9},{2,10},{3,11},{4,12},{5,13},{6,14},{7,15},{8,0},{9,1},... | collective-permute-start | bytes 258056 | tf_op jit(solution)/shard_map/ppermute | solution.py:44
  19.1 11.0 %collective-permute-start.7 = (bf16[4,112,384]{2,1,0:T(8,128)(2,1)S(1)}, bf16[4,112,384]{2,1,0:T(8,128)(2,1)S(1)}, u32[]{:S(2)}, u32[]{:S(2)}) collective-permute-start(bf16[4,112,384]{2,1,0:T(8,128)(2,1)S(1)} %stack_main.1.t0), channel_id=1, source_target_pairs={{0,4},{1,5},{2,6},{3,7},{4,0},{5,1},{6,2},{7,3},{8,12},{9,13},{10,... | collective-permute-start | bytes 1032200 | tf_op jit(solution)/shard_map/ppermute | solution.py:44
  20.3 14.8 %collective-permute-start.8 = (bf16[4,112,384]{2,1,0:T(8,128)(2,1)S(1)}, bf16[4,112,384]{2,1,0:T(8,128)(2,1)S(1)}, u32[]{:S(2)}, u32[]{:S(2)}) collective-permute-start(bf16[4,112,384]{2,1,0:T(8,128)(2,1)S(1)} %stack_main.1.t0), channel_id=1, source_target_pairs={{0,6},{1,7},{2,4},{3,5},{4,2},{5,3},{6,0},{7,1},{8,14},{9,15},{10,... | collective-permute-start | bytes 1032200 | tf_op jit(solution)/shard_map/ppermute | solution.py:44
  22.2 19.1 %collective-permute-start.9 = (bf16[4,112,384]{2,1,0:T(8,128)(2,1)S(1)}, bf16[4,112,384]{2,1,0:T(8,128)(2,1)S(1)}, u32[]{:S(2)}, u32[]{:S(2)}) collective-permute-start(bf16[4,112,384]{2,1,0:T(8,128)(2,1)S(1)} %stack_main.1.t0), channel_id=1, source_target_pairs={{0,1},{1,0},{2,3},{3,2},{4,5},{5,4},{6,7},{7,6},{8,9},{9,8},{10,11... | collective-permute-start | bytes 1032200 | tf_op jit(solution)/shard_map/ppermute | solution.py:44
  28.7 14.7 %collective-permute-start.10 = (bf16[4,112,384]{2,1,0:T(8,128)(2,1)S(1)}, bf16[4,112,384]{2,1,0:T(8,128)(2,1)S(1)}, u32[]{:S(2)}, u32[]{:S(2)}) collective-permute-start(bf16[4,112,384]{2,1,0:T(8,128)(2,1)S(1)} %collective-permute-done.6.t1), channel_id=1, source_target_pairs={{0,1},{1,0},{2,3},{3,2},{4,5},{5,4},{6,7},{7,6},{8,9},{9,8},{10,11... | collective-permute-start | bytes 1032200 | tf_op jit(solution)/shard_map/ppermute | solution.py:44
  30.1 13.6 %collective-permute-start.11 = (bf16[4,112,384]{2,1,0:T(8,128)(2,1)S(1)}, bf16[4,112,384]{2,1,0:T(8,128)(2,1)S(1)}, u32[]{:S(2)}, u32[]{:S(2)}) collective-permute-start(bf16[4,112,384]{2,1,0:T(8,128)(2,1)S(1)} %collective-permute-done.7.t2), channel_id=1, source_target_pairs={{0,1},{1,0},{2,3},{3,2},{4,5},{5,4},{6,7},{7,6},{8,9},{9,8},{10,11... | collective-permute-start | bytes 1032200 | tf_op jit(solution)/shard_map/ppermute | solution.py:44
  39.0 10.4 %collective-permute-start.14 = (bf16[64,640]{1,0:T(8,128)(2,1)}, bf16[64,640]{1,0:T(8,128)(2,1)S(1)}, u32[]{:S(2)}, u32[]{:S(2)}) collective-permute-start(bf16[64,640]{1,0:T(8,128)(2,1)} %get-tuple-element.173.refs_0_), channel_id=1, source_target_pairs={{0,8},{1,9},{2,10},{3,11},{4,12},{5,13},{6,14},{7,15},{8,0},{9,1},... | collective-permute-start | bytes 245768 | tf_op jit(solution)/shard_map/ppermute | solution.py:44
  47.6 13.3 %collective-permute-start.17 = (bf16[256,512]{1,0:T(8,128)(2,1)S(1)}, bf16[256,512]{1,0:T(8,128)(2,1)S(1)}, u32[]{:S(2)}, u32[]{:S(2)}) collective-permute-start(bf16[256,512]{1,0:T(8,128)(2,1)S(1)} %get-tuple-element.333), channel_id=1, source_target_pairs={{0,2},{1,3},{2,0},{3,1},{4,6},{5,7},{6,4},{7,5},{8,10},{9,11},{10,... | collective-permute-start | bytes 786440 | tf_op jit(solution)/shard_map/ppermute | solution.py:44
  48.1 12.8 %collective-permute-start.18 = (bf16[256,512]{1,0:T(8,128)(2,1)S(1)}, bf16[256,512]{1,0:T(8,128)(2,1)S(1)}, u32[]{:S(2)}, u32[]{:S(2)}) collective-permute-start(bf16[256,512]{1,0:T(8,128)(2,1)S(1)} %get-tuple-element.332), channel_id=1, source_target_pairs={{0,4},{1,5},{2,6},{3,7},{4,0},{5,1},{6,2},{7,3},{8,12},{9,13},{10,... | collective-permute-start | bytes 786440 | tf_op jit(solution)/shard_map/ppermute | solution.py:44
  49.4 12.7 %collective-permute-start.19 = (bf16[256,512]{1,0:T(8,128)(2,1)S(1)}, bf16[256,512]{1,0:T(8,128)(2,1)S(1)}, u32[]{:S(2)}, u32[]{:S(2)}) collective-permute-start(bf16[256,512]{1,0:T(8,128)(2,1)S(1)} %get-tuple-element.331), channel_id=1, source_target_pairs={{0,6},{1,7},{2,4},{3,5},{4,2},{5,3},{6,0},{7,1},{8,14},{9,15},{10,... | collective-permute-start | bytes 786440 | tf_op jit(solution)/shard_map/ppermute | solution.py:44
  62.1 12.2 %collective-permute-start.20 = (bf16[4,64,640]{2,1,0:T(8,128)(2,1)S(1)}, bf16[4,64,640]{2,1,0:T(8,128)(2,1)S(1)}, u32[]{:S(2)}, u32[]{:S(2)}) collective-permute-start(bf16[4,64,640]{2,1,0:T(8,128)(2,1)S(1)} %stack_rest.1.t0), channel_id=1, source_target_pairs={{0,2},{1,3},{2,0},{3,1},{4,6},{5,7},{6,4},{7,5},{8,10},{9,11},{10,... | collective-permute-start | bytes 983048 | tf_op jit(solution)/shard_map/ppermute | solution.py:44
  62.6 20.5 %collective-permute-start.22 = (bf16[4,64,640]{2,1,0:T(8,128)(2,1)S(1)}, bf16[4,64,640]{2,1,0:T(8,128)(2,1)S(1)}, u32[]{:S(2)}, u32[]{:S(2)}) collective-permute-start(bf16[4,64,640]{2,1,0:T(8,128)(2,1)S(1)} %stack_rest.1.t0), channel_id=1, source_target_pairs={{0,4},{1,5},{2,6},{3,7},{4,0},{5,1},{6,2},{7,3},{8,12},{9,13},{10,... | collective-permute-start | bytes 983048 | tf_op jit(solution)/shard_map/ppermute | solution.py:44
  63.8 19.3 %collective-permute-start.23 = (bf16[4,64,640]{2,1,0:T(8,128)(2,1)S(1)}, bf16[4,64,640]{2,1,0:T(8,128)(2,1)S(1)}, u32[]{:S(2)}, u32[]{:S(2)}) collective-permute-start(bf16[4,64,640]{2,1,0:T(8,128)(2,1)S(1)} %stack_rest.1.t0), channel_id=1, source_target_pairs={{0,6},{1,7},{2,4},{3,5},{4,2},{5,3},{6,0},{7,1},{8,14},{9,15},{10,... | collective-permute-start | bytes 983048 | tf_op jit(solution)/shard_map/ppermute | solution.py:44
  115.6 29.0 %collective-permute-start.26 = (bf16[512,640]{1,0:T(8,128)(2,1)}, bf16[512,640]{1,0:T(8,128)(2,1)S(1)}, u32[]{:S(2)}, u32[]{:S(2)}) collective-permute-start(bf16[512,640]{1,0:T(8,128)(2,1)} %get-tuple-element.198), channel_id=1, source_target_pairs={{0,2},{1,3},{2,0},{3,1},{4,6},{5,7},{6,4},{7,5},{8,10},{9,11},{10,... | collective-permute-start | bytes 1966088 | tf_op jit(solution)/shard_map/ppermute | solution.py:44
  116.1 28.5 %collective-permute-start.27 = (bf16[512,640]{1,0:T(8,128)(2,1)}, bf16[512,640]{1,0:T(8,128)(2,1)S(1)}, u32[]{:S(2)}, u32[]{:S(2)}) collective-permute-start(bf16[512,640]{1,0:T(8,128)(2,1)} %get-tuple-element.199), channel_id=1, source_target_pairs={{0,4},{1,5},{2,6},{3,7},{4,0},{5,1},{6,2},{7,3},{8,12},{9,13},{10,... | collective-permute-start | bytes 1966088 | tf_op jit(solution)/shard_map/ppermute | solution.py:44
  117.3 30.5 %collective-permute-start.28 = (bf16[512,640]{1,0:T(8,128)(2,1)S(1)}, bf16[512,640]{1,0:T(8,128)(2,1)S(1)}, u32[]{:S(2)}, u32[]{:S(2)}) collective-permute-start(bf16[512,640]{1,0:T(8,128)(2,1)S(1)} %get-tuple-element.200), channel_id=1, source_target_pairs={{0,6},{1,7},{2,4},{3,5},{4,2},{5,3},{6,0},{7,1},{8,14},{9,15},{10,... | collective-permute-start | bytes 1966088 | tf_op jit(solution)/shard_map/ppermute | solution.py:44
  151.4 22.6 %collective-permute-start.34 = (bf16[1024,512]{1,0:T(8,128)(2,1)}, bf16[1024,512]{1,0:T(8,128)(2,1)}, u32[]{:S(2)}, u32[]{:S(2)}) collective-permute-start(bf16[1024,512]{1,0:T(8,128)(2,1)} %back_rows.2), channel_id=1, source_target_pairs={{0,1},{1,0},{2,3},{3,2},{4,5},{5,4},{6,7},{7,6},{8,9},{9,8},{10,11... | collective-permute-start | bytes 3145736 | tf_op jit(solution)/shard_map/ppermute | solution.py:44
  164.1 17.1 %collective-permute-start.36 = (bf16[64,640]{1,0:T(8,128)(2,1)S(1)}, bf16[64,640]{1,0:T(8,128)(2,1)S(1)}, u32[]{:S(2)}, u32[]{:S(2)}) collective-permute-start(bf16[64,640]{1,0:T(8,128)(2,1)S(1)} %get-tuple-element.238), channel_id=1, source_target_pairs={{0,16},{1,17},{2,18},{3,19},{4,20},{5,21},{6,22},{7,23},{8,24},{9,... | collective-permute-start | bytes 245768 | tf_op jit(solution)/shard_map/ppermute | solution.py:44
  167.0 14.2 %collective-permute-start.37 = (bf16[64,640]{1,0:T(8,128)(2,1)S(1)}, bf16[64,640]{1,0:T(8,128)(2,1)S(1)}, u32[]{:S(2)}, u32[]{:S(2)}) collective-permute-start(bf16[64,640]{1,0:T(8,128)(2,1)S(1)} %get-tuple-element.239), channel_id=1, source_target_pairs={{0,24},{1,25},{2,26},{3,27},{4,28},{5,29},{6,30},{7,31},{8,16},{9,... | collective-permute-start | bytes 245768 | tf_op jit(solution)/shard_map/ppermute | solution.py:44
  168.3 17.1 %collective-permute-start.31 = (bf16[4,112,384]{2,1,0:T(8,128)(2,1)S(1)}, bf16[4,112,384]{2,1,0:T(8,128)(2,1)S(1)}, u32[]{:S(2)}, u32[]{:S(2)}) collective-permute-start(bf16[4,112,384]{2,1,0:T(8,128)(2,1)S(1)} %get-tuple-element.220), channel_id=1, source_target_pairs={{0,2},{1,3},{2,0},{3,1},{4,6},{5,7},{6,4},{7,5},{8,10},{9,11},{10,... | collective-permute-start | bytes 1032200 | tf_op jit(solution)/shard_map/ppermute | solution.py:44
  172.7 15.5 %collective-permute-start.32 = (bf16[4,112,384]{2,1,0:T(8,128)(2,1)S(1)}, bf16[4,112,384]{2,1,0:T(8,128)(2,1)S(1)}, u32[]{:S(2)}, u32[]{:S(2)}) collective-permute-start(bf16[4,112,384]{2,1,0:T(8,128)(2,1)S(1)} %get-tuple-element.221), channel_id=1, source_target_pairs={{0,4},{1,5},{2,6},{3,7},{4,0},{5,1},{6,2},{7,3},{8,12},{9,13},{10,... | collective-permute-start | bytes 1032200 | tf_op jit(solution)/shard_map/ppermute | solution.py:44
  174.0 18.0 %collective-permute-start.33 = (bf16[4,112,384]{2,1,0:T(8,128)(2,1)S(1)}, bf16[4,112,384]{2,1,0:T(8,128)(2,1)S(1)}, u32[]{:S(2)}, u32[]{:S(2)}) collective-permute-start(bf16[4,112,384]{2,1,0:T(8,128)(2,1)S(1)} %get-tuple-element.222), channel_id=1, source_target_pairs={{0,6},{1,7},{2,4},{3,5},{4,2},{5,3},{6,0},{7,1},{8,14},{9,15},{10,... | collective-permute-start | bytes 1032200 | tf_op jit(solution)/shard_map/ppermute | solution.py:44
  194.9 10.5 %collective-permute-start.43 = (bf16[128,384]{1,0:T(8,128)(2,1)S(1)}, bf16[128,384]{1,0:T(8,128)(2,1)S(1)}, u32[]{:S(2)}, u32[]{:S(2)}) collective-permute-start(bf16[128,384]{1,0:T(8,128)(2,1)S(1)} %get-tuple-element.253), channel_id=1, source_target_pairs={{0,16},{1,17},{2,18},{3,19},{4,20},{5,21},{6,22},{7,23},{8,24},{9,... | collective-permute-start | bytes 294920 | tf_op jit(solution)/shard_map/ppermute | solution.py:44
  (61 other events, 309.0 us)

commit v4 on v3

--- a/solution.py
+++ b/solution.py
@@ -272,11 +272,12 @@
             pl.BlockSpec((SLOTS, HEAD), lambda h: (0, h)),
             pl.BlockSpec((1, SLOTS, WIDE), lambda h: (h, 0, 0)),
         ],
-        out_shape=[shape_of((SLOTS, 2 * HEAD), bf16), shape_of((2, SLOTS, WIDE), bf16)],
+        out_shape=[pltpu.HBM((SLOTS, 2 * HEAD), bf16), pltpu.HBM((2, SLOTS, WIDE), bf16)],
         scratch_shapes=[pltpu.VMEM((keys, BLOCK), f32)] * 2,
+        compiler_params=pltpu.CompilerParams(vmem_limit_bytes=32 << 20),
         cost_estimate=cost(6),
         name="attend",
-    )(q, k, extra, vt)
+    )(*held((q, k, extra, vt), False))
 
 
 BACK_BLOCK = 256
@@ -355,25 +356,17 @@
         ],
         out_specs=[pl.BlockSpec((SLOTS, HEAD), lambda h, i: (i, h)), flat, flat],
         out_shape=[
-            shape_of((2 * SLOTS, 2 * HEAD), bf16),
-            shape_of((2, HEAD, keys), f32),
-            shape_of((2, HEAD, keys), f32),
+            pltpu.HBM((2 * SLOTS, 2 * HEAD), bf16),
+            pltpu.HBM((2, HEAD, keys), f32),
+            pltpu.HBM((2, HEAD, keys), f32),
         ],
         scratch_shapes=[pltpu.VMEM((keys, BACK_BLOCK), bf16)] * 4,
+        compiler_params=pltpu.CompilerParams(vmem_limit_bytes=40 << 20),
         cost_estimate=cost(20),
         name="attend_back",
     )(
-        q,
-        k,
-        extra,
-        kt,
-        v,
-        extra_own,
-        extra_other,
-        grad_own,
-        grad_other,
-        grad_own,
-        grad_other,
+        *held((q, k, extra, kt, v, extra_own, extra_other), False),
+        *held((grad_own, grad_other, grad_own, grad_other), (False, True, False, True)),
     )
 
 
@@ -586,12 +579,25 @@
         compiler_params=pltpu.CompilerParams(vmem_limit_bytes=44 << 20),
         cost_estimate=cost(25),
         name="middle",
-    )(sc, ratio, rows, o_own, o_other, *cots, enc, vec, b1, *held((rest_own, rest_other)))
+    )(
+        sc,
+        ratio,
+        rows,
+        o_own,
+        o_other,
+        *held(cots),
+        enc,
+        vec,
+        b1,
+        *held((rest_own, rest_other)),
+    )
 
 
 def held(args, near=True):
-    space = pltpu.VMEM if near else pltpu.HBM
-    return tuple(pltpu.with_memory_space_constraint(arg, space) for arg in args)
+    if isinstance(near, bool):
+        near = [near] * len(args)
+    spaces = [pltpu.VMEM if flag else pltpu.HBM for flag in near]
+    return tuple(map(pltpu.with_memory_space_constraint, args, spaces))
 
 
 def simple(body, out_shape, *args, scalars=None, scratch=(), near=(True, True), name=None):
@@ -741,6 +747,33 @@
     return total
 
 
+FEAT_SPAN = 80
+FEAT_CUTS = ((0, 0, 0, 0, 80), (1, 0, 0, 80, 112), (1, 32, 1, 0, 48), (2, 0, 1, 48, 112))
+
+
+def build_main(parts, flipped, places):
+    count = len(parts)
+    size, lanes = parts[0].shape
+    feats, rows = flipped.shape[1:]
+
+    def body(sc, *refs):
+        ins, flip_ref, outs = refs[:count], refs[count], refs[count + 1 :]
+        for k, out in enumerate(outs):
+            for e, ref in enumerate(ins):
+                at = pl.multiple_of((sc[6] ^ e) * size, 16)
+                out[pl.ds(at, size), :] = ref[...]
+            wide = jnp.concatenate(
+                [flip_ref[sc[3] ^ k], jnp.zeros((FEAT_ROWS - feats, rows), bf16)], axis=0
+            )
+            for column, row, tile, begin, end in FEAT_CUTS:
+                at = slice(count * size + row, count * size + row + end - begin)
+                part = wide[begin:end, tile * WIDE : (tile + 1) * WIDE]
+                out[at, column * WIDE : (column + 1) * WIDE] = part
+
+    shape = shape_of((count * size + FEAT_SPAN, lanes), bf16)
+    return simple(body, [shape] * 4, *parts, flipped, scalars=places, name="build_main")
+
+
 def join_features(parts, places):
     feats, rows = parts[0].shape
 
@@ -754,10 +787,9 @@
     )
 
 
-def unpack_main(tops, lows, feats, feats_low, mask, places, slab, strip):
-    n_ep = tops[0].shape[0]
-    rows = feats.shape[2]
+def unpack_main(tops, lows, feats, feats_low, mask, places, n_ep, slab, strip, rows):
     plain = 2 * slab != WIDE
+    size = slab + 3 * strip
     shapes = [
         shape_of((2, n_ep, 2, slab, TAIL), bf16),
         shape_of((n_ep, 2, 2, 2, strip, 3 * TAIL), bf16),
@@ -817,7 +849,7 @@
         )
         return [jnp.stack(heads), wide, small, vec, jnp.stack(biases).astype(f32), *masked]
 
-    def body(sc, t0, t1, t2, t3, l0, l1, l2, l3, fa, fb, mask_ref, *outs):
+    def body(sc, t0, t1, t2, t3, l0, l1, l2, l3, mask_ref, *outs):
         wp_ref, prompt_ref, small_ref, vec_ref, bias_ref, own_ref, other_ref = outs
         side, row, core = sc[0], sc[1], sc[2]
         groups = ((t0, t1, t2, t3), (l0, l1, l2, l3))
@@ -825,10 +857,23 @@
         for b in range(2):
             for r in range(2):
                 k = 2 * b + r
-                wp_ref[r, :, side ^ b] = groups[0][k][:, 0:slab, :]
                 for other in range(2):
                     spot = core ^ other
-                    part = groups[other][k][:, slab:, :]
+                    source = groups[other][k]
+                    full = source[0 : n_ep * size].reshape(n_ep, size, TAIL)
+                    if other == 0:
+                        wp_ref[r, :, side ^ b] = full[:, 0:slab, :]
+                    part = full[:, slab:, :]
+                    tiles = ([], [])
+                    for column, line, tile, begin, end in FEAT_CUTS:
+                        at = slice(n_ep * size + line, n_ep * size + line + end - begin)
+                        tiles[tile].append(source[at, column * WIDE : (column + 1) * WIDE])
+                    blank = jnp.zeros((WIDE - FEAT_ROWS, rows), bf16)
+                    flip = jnp.concatenate([jnp.concatenate(t, axis=0) for t in tiles], axis=1)
+                    flip = jnp.concatenate([flip, blank], axis=0)
+                    piece = jnp.where(mask_ref[...] > 0.0, flip.T.astype(f32), 0.0).astype(bf16)
+                    at = pl.multiple_of((2 * (side ^ b) + (row ^ r)) * rows, rows)
+                    (other_ref if other else own_ref)[pl.ds(at, rows), :] = piece
                     for j in range(3):
                         lanes = slice(j * TAIL, (j + 1) * TAIL)
                         span = slice(j * strip, (j + 1) * strip)
@@ -849,12 +894,8 @@
                     row_tile = jnp.where(low_half, first, pltpu.roll(second, slab, 1))
                     k = r + 2 * other
                     bias_ref[k : k + 1, e * WIDE : (e + 1) * WIDE] = row_tile
-        features(mask_ref, fa, own_ref)
-        features(mask_ref, fb, other_ref)
-
-    return simple(
-        body, shapes, *tops, *lows, feats, feats_low, mask, scalars=places, name="unpack_main"
-    )
+
+    return simple(body, shapes, *tops, *lows, mask, scalars=places, name="unpack_main")
 
 
 def unpack_rest(tops, places):
@@ -869,42 +910,7 @@
     )
 
 
-def back_body(dq_ref, dk_ref, dv_ref, wp, out_ref):
-    def columns(k):
-        return jnp.concatenate([wp[h, :, k * HEAD : (k + 1) * HEAD] for h in range(2)], axis=1)
-
-    def both(ref):
-        return jnp.concatenate([ref[h].astype(bf16) for h in range(2)], axis=0).T
-
-    total = dot(dq_ref[...], columns(0), NT)
-
-    @pl.when(pl.program_id(0) == 0)
-    def _():
-        more = dot(both(dk_ref), columns(1), NT) + dot(both(dv_ref), columns(2), NT)
-        out_ref[...] = (total + more).astype(out_ref.dtype)
-
-    @pl.when(pl.program_id(0) == 1)
-    def _():
-        out_ref[...] = total.astype(out_ref.dtype)
-
-
-def back_rows(dq, dk, dv, wp, which, dtype):
-    half = dq.shape[0] // 4
-    width = wp.shape[1]
-    key = pl.BlockSpec((2, HEAD, half), lambda i: (0, 0, 2 + which))
-    return pl.pallas_call(
-        back_body,
-        grid=(2,),
-        in_specs=[pl.BlockSpec((half, 2 * HEAD), lambda i: (2 * which + i, 0)), key, key, whole()],
-        out_specs=pl.BlockSpec((half, width), lambda i: (i, 0)),
-        out_shape=pltpu.HBM((2 * half, width), dtype),
-        compiler_params=pltpu.CompilerParams(vmem_limit_bytes=32 << 20),
-        cost_estimate=cost(3),
-        name="back_rows",
-    )(*held((dq, dk, dv, wp), False))
-
-
-def weight_body(x_ref, dq_ref, dk_ref, dv_ref, prompt, wp, gb1, gw_ref, gp_ref, gb_ref, acc, gq_ref, gv_ref):
+def weight_body(n_ep, strip, sc, x_ref, dq_ref, dk_ref, dv_ref, prompt, wp, gb1, gw_ref, mine_ref, sent_ref, own_ref, other_ref, acc, gq_ref, gv_ref, gp_ref, gb_ref):
     step = pl.program_id(0)
 
     @pl.when(step == 0)
@@ -913,36 +919,48 @@
         gq_ref[...] = jnp.zeros_like(gq_ref)
         gv_ref[...] = jnp.zeros_like(gv_ref)
 
+    def columns(k):
+        return jnp.concatenate([wp[h, :, k * HEAD : (k + 1) * HEAD] for h in range(2)], axis=1)
+
     flip = x_ref[...].T
-    acc[0] += dot(flip, dq_ref[...], NN)
-    gq_ref[...] += jnp.sum(dq_ref[...].astype(f32), axis=0, keepdims=True)
+    grad_query = dq_ref[...]
+    acc[0] += dot(flip, grad_query, NN)
+    gq_ref[...] += jnp.sum(grad_query.astype(f32), axis=0, keepdims=True)
     grad_key = jnp.concatenate([dk_ref[h] for h in range(2)], axis=0)
     grad_value = jnp.concatenate([dv_ref[h] for h in range(2)], axis=0)
     key_high = grad_key.astype(bf16)
     value_high = grad_value.astype(bf16)
     ones = jnp.ones((8, grad_key.shape[1]), bf16)
     gv_ref[...] += dot(ones, value_high, NT)[0:1]
+    back = dot(grad_query, columns(0), NT)
+
+    def store(value):
+        @pl.when(step < 2)
+        def _():
+            own_ref[...] = value
+
+        @pl.when(step >= 2)
+        def _():
+            other_ref[...] = value.astype(bf16)
 
     @pl.when(step % 2 == 0)
     def _():
         acc[1] += dot(flip, key_high, NT)
         acc[2] += dot(flip, value_high, NT)
+        store(back + dot(key_high.T, columns(1), NT) + dot(value_high.T, columns(2), NT))
 
     @pl.when(step % 2 == 1)
     def _():
+        store(back)
         key_low = (grad_key - key_high.astype(f32)).astype(bf16)
         value_low = (grad_value - value_high.astype(f32)).astype(bf16)
         source = prompt[...]
         acc[1] += dot(source, key_high, NT) + dot(source, key_low, NT)
         acc[2] += dot(source, value_high, NT) + dot(source, value_low, NT)
         gv_ref[...] += dot(ones, value_low, NT)[0:1]
-        w_key, w_value = (
-            jnp.concatenate([wp[h, :, k * HEAD : (k + 1) * HEAD] for h in range(2)], axis=1)
-            for k in (1, 2)
-        )
-        total = dot(w_key, key_high, NN) + dot(w_key, key_low, NN)
-        total = total + dot(w_value, value_high, NN) + dot(w_value, value_low, NN)
-        gp_ref[...] = total.astype(bf16)
+        total = dot(columns(1), key_high, NN) + dot(columns(1), key_low, NN)
+        total = total + dot(columns(2), value_high, NN) + dot(columns(2), value_low, NN)
+        gp_ref[step // 2] = total.astype(bf16)
 
     @pl.when(step == 3)
     def _():
@@ -954,17 +972,55 @@
             gb_ref[h : h + 1, HEAD : 2 * HEAD] = gv_ref[:, h * HEAD : (h + 1) * HEAD]
         gb_ref[2:4, 0 : 2 * HEAD] = jnp.zeros((2, 2 * HEAD), f32)
         gb_ref[:, 2 * HEAD :] = gb1[...]
-
-
-def weight_grads(x, dq, dk, dv, prompt, wp, gb1):
-    half = dq.shape[0] // 4
+        if strip % 16:
+            mine_ref[...] = gp_ref[...]
+            sent_ref[...] = gb_ref[...]
+            return
+        half = gp_ref.shape[2]
+        row, core = sc[1], sc[2]
+        first = lax.broadcasted_iota(jnp.int32, (strip, WIDE), 0) == 0
+        low_half = lax.broadcasted_iota(jnp.int32, (1, WIDE), 1) < 4 * strip
+        for other, ref in enumerate((mine_ref, sent_ref)):
+            for e in range(n_ep):
+                for s in range(2):
+                    for r in range(2):
+                        y = row ^ r
+                        at = ((e * 2 + s) * 2 + y) * 2 + (core ^ other)
+                        at = pl.ds(pl.multiple_of(at * strip, strip), strip)
+                        for tile in range(PAD // WIDE):
+                            lanes = slice(tile * WIDE % half, tile * WIDE % half + WIDE)
+                            j, place = tile // 3, tile % 3
+                            rows = slice(j * strip, (j + 1) * strip)
+                            to = slice(place * WIDE, (place + 1) * WIDE)
+                            ref[e, s, y, rows, to] = gp_ref[tile * WIDE // half, at, lanes]
+                        k = r + 2 * other
+                        tile = gb_ref[k : k + 1, e * WIDE : (e + 1) * WIDE]
+                        if s == 1:
+                            tile = pltpu.roll(tile, WIDE - 4 * strip, 1)
+                        tile = jnp.where(low_half, tile, 0.0)
+                        tile = jnp.where(first, tile, 0.0).astype(bf16)
+                        ref[e, s, y, 2 * strip : 3 * strip, 2 * WIDE :] = tile
+
+
+def weight_grads(places, x, dq, dk, dv, prompt, wp, gb1, n_ep, strip):
+    half = x.shape[0] // 4
     width = wp.shape[1]
     spot = lambda i: jnp.where(i % 2 == 0, 2 + i // 2, i // 2)
     key = pl.BlockSpec((2, HEAD, half), lambda i: (0, 0, spot(i)))
-    return pl.pallas_call(
-        weight_body,
+    if strip % 16:
+        shapes = [pltpu.VMEM((2, width, half), bf16), pltpu.VMEM((4, width), f32)]
+    else:
+        strips = (n_ep, 2, 2, 3 * strip, TAIL)
+        shapes = [pltpu.HBM(strips, bf16), pltpu.VMEM(strips, bf16)]
+    fixed = [
+        pl.BlockSpec(shape.shape, functools.partial(lambda n, i: (0,) * n, len(shape.shape)))
+        for shape in shapes
+    ]
+    out = pl.pallas_call(
+        functools.partial(weight_body, n_ep, strip),
         grid=(4,),
         in_specs=[
+            pl.BlockSpec(memory_space=pltpu.SMEM),
             pl.BlockSpec((half, width), lambda i: (i, 0)),
             pl.BlockSpec((half, 2 * HEAD), lambda i: (i, 0)),
             key,
@@ -973,22 +1029,35 @@
             whole(),
             whole(),
         ],
-        out_specs=[
-            pl.BlockSpec((2, width, TAIL), lambda i: (0, 0, 0)),
-            pl.BlockSpec((width, half), lambda i: (0, i // 2)),
-            pl.BlockSpec((4, width), lambda i: (0, 0)),
+        out_specs=[pl.BlockSpec((2, width, TAIL), lambda i: (0, 0, 0))]
+        + fixed
+        + [
+            pl.BlockSpec((half, width), lambda i: (jnp.minimum(i, 1), 0)),
+            pl.BlockSpec((half, width), lambda i: (jnp.maximum(i - 2, 0), 0)),
         ],
-        out_shape=[
-            pltpu.VMEM((2, width, TAIL), bf16),
-            pltpu.VMEM((width, PAD), bf16),
-            pltpu.VMEM((4, width), f32),
-        ],
+        out_shape=[pltpu.HBM((2, width, TAIL), bf16)]
+        + shapes
+        + [pltpu.HBM((2 * half, width), f32), pltpu.HBM((2 * half, width), bf16)],
+        scratch_shapes=[pltpu.VMEM((3, width, 2 * HEAD), f32)]
+        + [pltpu.VMEM((1, 2 * HEAD), f32)] * 2
+        + [pltpu.VMEM((2, width, half), bf16), pltpu.VMEM((4, width), f32)],
         compiler_params=pltpu.CompilerParams(vmem_limit_bytes=40 << 20),
-        scratch_shapes=[pltpu.VMEM((3, width, 2 * HEAD), f32)]
-        + [pltpu.VMEM((1, 2 * HEAD), f32)] * 2,
         cost_estimate=cost(9),
         name="weight_grads",
-    )(*held((x, dq, dk, dv, prompt, wp), False), gb1)
+    )(places, *held((x, dq, dk, dv, prompt, wp), False), gb1)
+    grad_project, mine, sent, back_own, back_other = out
+    if strip % 16:
+        row, core = places[1], places[2]
+        grad = jnp.concatenate([mine[0], mine[1]], axis=1)
+        blocks = grad.reshape(n_ep, 2, 2, 2, strip, PAD)
+        table = sent.reshape(2, 2, n_ep, 2, 4 * strip)
+        both = []
+        for other in (0, 1):
+            by_row = jnp.stack(pick(table[other, 0], table[other, 1], row), axis=2)
+            part = lax.dynamic_index_in_dim(blocks, core ^ other, 3, keepdims=False)
+            both.append(in_chunks(with_bias(part, by_row)))
+        mine, sent = both
+    return grad_project, mine, sent, back_own, back_other
 
 
 def input_body(sc, ratio, dr_ref, own_ref, got_ref, rows_ref, enc, mask, rows_grad, i0, i1, i2, i3, small_ref, acc, bias):
@@ -1060,43 +1129,6 @@
     )(sc, ratio, *held((dr, own, got, rows), False), enc, mask, rows_grad)
 
 
-def split_prompt(grad, bias_rows, places, n_ep, strip):
-    blocks = grad.reshape(n_ep, 2, 2, 2, strip, PAD)
-    if 8 * strip != WIDE:
-        row, core = places[1], places[2]
-        table = bias_rows.reshape(2, 2, n_ep, 2, 4 * strip)
-        both = []
-        for other in (0, 1):
-            by_row = jnp.stack(pick(table[other, 0], table[other, 1], row), axis=2)
-            part = lax.dynamic_index_in_dim(blocks, core ^ other, 3, keepdims=False)
-            both.append(in_chunks(with_bias(part, by_row)))
-        return both
-
-    def body(sc, grad_ref, bias_ref, mine_ref, sent_ref):
-        row, core = sc[1], sc[2]
-        first = lax.broadcasted_iota(jnp.int32, (strip, WIDE), 0) == 0
-        low_half = lax.broadcasted_iota(jnp.int32, (1, WIDE), 1) < 4 * strip
-        for s in range(2):
-            for r in range(2):
-                for other, ref in enumerate((mine_ref, sent_ref)):
-                    for j in range(3):
-                        rows = slice(j * strip, (j + 1) * strip)
-                        high = min(PAD, (j + 1) * TAIL)
-                        part = grad_ref[:, s, row ^ r, core ^ other, :, j * TAIL : high]
-                        ref[:, s, row ^ r, rows, 0 : high - j * TAIL] = part
-                    for e in range(n_ep):
-                        k = r + 2 * other
-                        tile = bias_ref[k : k + 1, e * WIDE : (e + 1) * WIDE]
-                        if s == 1:
-                            tile = pltpu.roll(tile, WIDE - 4 * strip, 1)
-                        tile = jnp.where(low_half, tile, 0.0)
-                        tile = jnp.where(first, tile, 0.0).astype(bf16)
-                        ref[e, s, row ^ r, 2 * strip : 3 * strip, PAD - 2 * TAIL :] = tile
-
-    shape = shape_of((n_ep, 2, 2, 3 * strip, TAIL), bf16)
-    return simple(body, [shape, shape], blocks, bias_rows, scalars=places, name="split_prompt")
-
-
 def split_small(grad, places, n_ep, strip):
     blocks = grad.reshape(n_ep * 4, 2, strip, WIDE)
 
@@ -1133,7 +1165,16 @@
                 out[:, slab : slab + 3 * strip, :] = pair.astype(bf16)
 
     shape = shape_of((n_ep, slab + 3 * strip, TAIL), bf16)
-    return simple(body, [shape] * 4, heads, mine, got, scalars=places, name="pack_main")
+    return simple(
+        body,
+        [shape] * 4,
+        heads,
+        mine,
+        got,
+        scalars=places,
+        near=((False, False, True), True),
+        name="pack_main",
+    )
 
 
 def pack_small(ins, mine, got, places, n_ep, strip):
@@ -1164,6 +1205,36 @@
     )
 
 
+def subtiles(rows, lanes, width):
+    out = []
+    across = width // WIDE
+    for n in range(rows // 16 * (lanes // WIDE)):
+        g, t = divmod(n, lanes // WIDE)
+        row, col = divmod(n, across)
+        here = (slice(16 * g, 16 * (g + 1)), slice(WIDE * t, WIDE * (t + 1)))
+        out.append((here, (16 * row, slice(WIDE * col, WIDE * (col + 1)))))
+    return out
+
+
+def place_tiles(parts, index, begin, rows, lanes, name):
+    width = parts[0].shape[1]
+
+    def body(sc, *refs):
+        for k, ref in enumerate(refs[:-1]):
+            for here, there in subtiles(rows, lanes, width):
+                tile = ref[begin + there[0] : begin + there[0] + 16, there[1]]
+                refs[-1][sc[0] ^ k, here[0], here[1]] = tile
+
+    return simple(
+        body,
+        shape_of((len(parts), rows, lanes), bf16),
+        *parts,
+        scalars=index.reshape(1).astype(jnp.int32),
+        near=(True, False),
+        name=name,
+    )
+
+
 def pack_rest(mine, got, outs, places, n_ep, slab):
     width = mine.shape[-1]
     rows, lanes = outs[0].shape
@@ -1176,31 +1247,42 @@
             side = sc[0] ^ (k // 2)
             pair = a_ref[k % 2, :, side].astype(f32) + b_ref[k % 2, :, side].astype(f32)
             refs[4 + k][0:count] = pair.reshape(count, width).astype(bf16)
-            refs[4 + k][count:, 0:lanes] = refs[k][...]
-
-    shape = shape_of((count + rows, width), bf16)
+            for here, there in subtiles(rows, lanes, width):
+                refs[4 + k][count + there[0] : count + there[0] + 16, there[1]] = refs[k][here]
+
+    extra = subtiles(rows, lanes, width)[-1][1][0] + 16
+    shape = shape_of((count + extra, width), bf16)
     return simple(body, [shape] * 4, mine, got, *outs, scalars=places, name="pack_rest")
 
 
-def sum_rest(parts, places, n_ep, slab):
+def sum_rest(parts, later, places, n_ep, slab):
     width = parts[0].shape[1]
-    if n_ep > 4:
+    if n_ep != 4:
         total = sum(part[0 : n_ep * slab].astype(f32) for part in parts)
-        return reduce_ep(total.reshape(n_ep, slab, width), None)
+        total = total.reshape(n_ep, slab, width)
+        return [lax.psum_scatter(total, "ep", scatter_dimension=0, tiled=True)[0]]
 
     def body(sc, *refs):
         ins, outs = refs[: len(parts)], refs[len(parts) :]
-        for k, out in enumerate(outs):
+        for k in range(4):
             spot = pl.multiple_of((sc[6] ^ k) * slab, slab)
             total = ins[0][pl.ds(spot, slab), :].astype(f32)
             for ref in ins[1:]:
                 total = total + ref[pl.ds(spot, slab), :].astype(f32)
-            out[...] = total.astype(bf16)
-
-    pieces = simple(
-        body, [shape_of((slab, width), bf16)] * n_ep, *parts, scalars=places, name="sum_rest"
-    )
-    return reduce_ep(None, pieces)
+            outs[k // 2][k % 2] = total.astype(bf16)
+
+    near, far = simple(
+        body, [shape_of((2, slab, width), bf16)] * 2, *parts, scalars=places, name="sum_rest"
+    )
+    got = swap(far, ep=2)
+
+    def added(a_ref, b_ref, own_ref, sent_ref):
+        own_ref[...] = (a_ref[0].astype(f32) + b_ref[0].astype(f32)).astype(bf16)
+        sent_ref[...] = (a_ref[1].astype(f32) + b_ref[1].astype(f32)).astype(bf16)
+
+    got = tie(got, later)
+    own, sent = simple(added, [shape_of((slab, width), bf16)] * 2, near, got, name="add_rest")
+    return [own, swap(sent, ep=1)]
 
 
 def sum_main(mains, smalls, places, slab, strip):
@@ -1380,27 +1462,32 @@
         block_weights, prompt, encoder, shared_vectors, head_biases
     )
     mask_wide = jnp.pad(mask_float, (0, WIDE - FEAT)).reshape(1, WIDE)
-    flipped = jnp.transpose(feats[0], (0, 2, 1))
+    flipped = jnp.transpose(tie(feats, main_part)[0], (0, 2, 1))
     main_pieces = gather_ep(main_part)
-    feats_parts = plane_list(
-        [lax.dynamic_index_in_dim(flipped, chip ^ k, 0, keepdims=False) for k in range(4)]
-    )
-    main_pieces, feats_parts = lax.optimization_barrier((main_pieces, feats_parts))
-    feats_own = join_features(feats_parts, places)
-    feats_other = swap(feats_own, core=1)
-    main_along = stack_ep(main_pieces, "stack_main")
-    tops = plane_list([main_along] * 4)
+    feats_own, feats_other = None, None
+    if 2 * slab == WIDE:
+        tops = plane_list(build_main(main_pieces, flipped, places))
+    else:
+        feats_own = join_features(
+            plane_list(
+                [lax.dynamic_index_in_dim(flipped, chip ^ k, 0, keepdims=False) for k in range(4)]
+            ),
+            places,
+        )
+        feats_other = swap(feats_own, core=1)
+        tops = plane_list([stack_ep(main_pieces, "stack_main")] * 4)
     lows = [swap(top, core=1) for top in tops]
     w_project, prompt_low, small_low, vector_rows, bias_rows, masked_own, masked_other = unpack_main(
-        tops, lows, feats_own, feats_other, mask_wide, places, slab, strip
+        tops, lows, feats_own, feats_other, mask_wide, places, n_ep, slab, strip, rows
     )
     w_project = w_project.reshape(2, width, TAIL)
     prompt_low = prompt_low.reshape(width, 3 * TAIL)
     encoder_low = small_low.reshape(width, WIDE)
 
-    rest_along = stack_ep(gather_ep(tie(rest_part, feats_other)), "stack_rest")
+    rest_along = stack_ep(gather_ep(tie(rest_part, lows[0])), "stack_rest")
+    lows, rest_along = lax.optimization_barrier((lows, rest_along))
+
     cots = to_chip(tie(cotangent, w_project))
-
     rows_low, query, keys, keys_flip, values, values_flip, key_extra = project(
         ratio,
         places,
@@ -1451,19 +1538,23 @@
         grad_got,
     )
     rest_tops, grad_query = lax.optimization_barrier((rest_tops, grad_query))
-    rest_pieces = sum_rest(rest_tops, places, n_ep, slab)
-    grad_project, grad_prompt, grad_bias = weight_grads(
-        rows_low, grad_query, grad_key, grad_value, prompt_low, w_project, grad_hidden_row
-    )
-    prompt_mine, prompt_sent = split_prompt(grad_prompt, grad_bias, places, n_ep, strip)
+    grad_project, prompt_mine, prompt_sent, back_own, back_other = weight_grads(
+        places,
+        rows_low,
+        grad_query,
+        grad_key,
+        grad_value,
+        prompt_low,
+        w_project,
+        grad_hidden_row,
+        n_ep,
+        strip,
+    )
     prompt_got = swap(prompt_sent, core=1)
-    back_other = back_rows(grad_query, grad_key, grad_value, w_project, 1, bf16)
     back_got = swap(back_other, core=1)
-    prompt_got = tie(prompt_got, back_other)
     main_parts = pack_main(grad_project, prompt_mine, prompt_got, places, slab, strip)
     main_tops = plane_list(main_parts)
-    grad_query, *unused = lax.optimization_barrier((grad_query, *main_parts))
-    back_own = back_rows(grad_query, grad_key, grad_value, w_project, 0, f32)
+    back_own = tie(back_own, main_parts)
     i0, i1, i2, i3, grad_small = input_grads(
         places,
         ratio,
@@ -1475,16 +1566,15 @@
         mask_wide.reshape(WIDE, 1),
         grad_rows,
     )
-    grad_small, rest_pieces = lax.optimization_barrier((grad_small, rest_pieces))
     small_mine, small_sent = split_small(grad_small, places, n_ep, strip)
     small_got = swap(small_sent, core=1)
-    small_tops = plane_list(
-        pack_small((i0, i1, i2, i3), small_mine, small_got, places, n_ep, strip)
-    )
-    output_final = place_rows(
-        rest_tops, chip, n_ep * slab, (rows, width), bf16, "place_output"
-    )
-    main_tops, output_final = lax.optimization_barrier((main_tops, output_final))
+    small_parts = pack_small((i0, i1, i2, i3), small_mine, small_got, places, n_ep, strip)
+    small_tops = plane_list(small_parts)
+    rest_pieces = sum_rest(tie(rest_tops, main_parts), grad_small, places, n_ep, slab)
+    output_final = place_tiles(rest_tops, chip, n_ep * slab, rows, width, "place_output")
+    main_tops, output_final, rest_pieces = lax.optimization_barrier(
+        (main_tops, output_final, rest_pieces)
+    )
     main_pieces = sum_main(main_tops, small_tops, places, slab, strip)
     input_final = place_rows(small_tops, chip, 0, (FEAT_ROWS, rows), f32, "place_input")
     input_final = jnp.transpose(input_final[:, 0:FEAT], (0, 2, 1))[None]

time: 223 us -> 210 us (0.942)
  Pallas kernels: 110 us -> 104 us
  local copies, waits for them, and re-layouts: 7.69 us -> 1.75 us
  starting transfers between devices: 54.1 us -> 48.6 us
  waiting for transfers between devices: 47.2 us -> 52.5 us
    ppermute x52 -> x47, starting transfers between devices: 54.1 us -> 48.6 us  [swap(): return lax.ppermute(value, AXES, pairs)]
    ppermute x52 -> x47, waiting for transfers between devices: 47.2 us -> 52.5 us  [swap(): return lax.ppermute(value, AXES, pairs)]
    pallas_call x3 -> x1, Pallas kernels: 15.5 us -> 11.2 us  [weight_grads(): pl.pallas_call(functools.partial(weight_body, n_ep, strip), grid=(4,), in...]
    unnamed x71 -> x47, local copies, waits for them, and re-layouts: 5.39 us -> 1.32 us
    pallas_call x18 -> x17, Pallas kernels: 15.2 us -> 13.7 us  [simple(): pl.pallas_call(body, in_specs=specs, out_specs=[whole()] * len(out_shape)...]
  transfers between devices with their start and end apart: 52 -> 47, of which waited for: 21 -> 20; matrix products, arithmetic and copies ran while one was open for 1% -> 1% of each run, Pallas kernels for 37% -> 31%
where the time goes in v4:
time: 210 us
  Pallas kernels  104 us (50%)
  waiting for transfers between devices  52.5 us (25%)
  starting transfers between devices  48.6 us (23%)
    ppermute x47, waiting for transfers between devices, swap(): return lax.ppermute(value, AXES, pairs)  52.5 us
    ppermute x47, starting transfers between devices, swap(): return lax.ppermute(value, AXES, pairs)  48.6 us
    pallas_call x1, Pallas kernels, attend_back(): pl.pallas_call(attend_back_body, grid=(2, 2), in_specs=[pl.BlockSpec((1,...  25.5 us
    pallas_call x1, Pallas kernels, middle(): pl.pallas_call(middle_body, grid_spec=pltpu.PrefetchScalarGridSpec(num_sc...  22.2 us
    pallas_call x2, Pallas kernels, attend(): pl.pallas_call(attend_body, grid=(2,), in_specs=[pl.BlockSpec((1, SLOTS,...  17.6 us
    pallas_call x17, Pallas kernels, simple(): pl.pallas_call(body, in_specs=specs, out_specs=[whole()] * len(out_shape)...  13.7 us
    pallas_call x1, Pallas kernels, weight_grads(): pl.pallas_call(functools.partial(weight_body, n_ep, strip), grid=(4,), in...  11.2 us
    pallas_call x1, Pallas kernels, project(): pl.pallas_call(project_body, grid=(4,), in_specs=[pl.BlockSpec(memory_spa...  8.58 us
  transfers between devices with their start and end apart: 47, of which 20 were waited for; matrix products, arithmetic and copies ran while one was open for 1% of the time, Pallas kernels for 31%

profile of v4, /device:TPU:0, one launch (start us, length us, event | category | flops | bytes accessed | tf_op | source)
XLA Modules:
  0.0 209.8 jit_solution(11032053894346913481)
XLA Ops:
  2.4 3.0 %collective-permute-start = (bf16[112,384]{1,0:T(8,128)(2,1)S(1)}, bf16[112,384]{1,0:T(8,128)(2,1)S(1)}, u32[]{:S(2)}, u32[]{:S(2)}) collective-permute-start(bf16[112,384]{1,0:T(8,128)(2,1)S(1)} %get-tuple-element.153.refs_0_), channel_id=1, source_target_pairs={{0,8},{1,9},{2,10},{3,11},{4,12},{5,13},{6,14},{7,15},{8,0},{9,1},... | collective-permute-start | bytes 258056 | tf_op jit(solution)/shard_map/ppermute | solution.py:44
  5.5 2.6 %collective-permute-start.1 = (bf16[112,384]{1,0:T(8,128)(2,1)S(1)}, bf16[112,384]{1,0:T(8,128)(2,1)S(1)}, u32[]{:S(2)}, u32[]{:S(2)}) collective-permute-start(bf16[112,384]{1,0:T(8,128)(2,1)S(1)} %get-tuple-element.153.refs_0_), channel_id=1, source_target_pairs={{0,16},{1,17},{2,18},{3,19},{4,20},{5,21},{6,22},{7,23},{8,24},{9,... | collective-permute-start | bytes 258056 | tf_op jit(solution)/shard_map/ppermute | solution.py:44
  8.4 6.6 %collective-permute-done.1.refs_2_ = bf16[112,384]{1,0:T(8,128)(2,1)S(1)} collective-permute-done((bf16[112,384]{1,0:T(8,128)(2,1)S(1)}, bf16[112,384]{1,0:T(8,128)(2,1)S(1)}, u32[]{:S(2)}, u32[]{:S(2)}) %collective-permute-start.1) | collective-permute-done | bytes 86048 | tf_op jit(solution)/shard_map/ppermute | solution.py:44
  19.2 7.9 %collective-permute-done.3.t1 = bf16[528,384]{1,0:T(8,128)(2,1)S(1)} collective-permute-done((bf16[528,384]{1,0:T(8,128)(2,1)S(1)}, bf16[528,384]{1,0:T(8,128)(2,1)S(1)}, u32[]{:S(2)}, u32[]{:S(2)}) %collective-permute-start.3) | collective-permute-done | bytes 405536 | tf_op jit(solution)/shard_map/ppermute | solution.py:44
  27.1 2.4 %collective-permute-done.4.t2 = bf16[528,384]{1,0:T(8,128)(2,1)S(1)} collective-permute-done((bf16[528,384]{1,0:T(8,128)(2,1)S(1)}, bf16[528,384]{1,0:T(8,128)(2,1)S(1)}, u32[]{:S(2)}, u32[]{:S(2)}) %collective-permute-start.4) | collective-permute-done | bytes 405536 | tf_op jit(solution)/shard_map/ppermute | solution.py:44
  29.6 5.1 %collective-permute-done.5.t3 = bf16[528,384]{1,0:T(8,128)(2,1)S(1)} collective-permute-done((bf16[528,384]{1,0:T(8,128)(2,1)S(1)}, bf16[528,384]{1,0:T(8,128)(2,1)S(1)}, u32[]{:S(2)}, u32[]{:S(2)}) %collective-permute-start.5) | collective-permute-done | bytes 405536 | tf_op jit(solution)/shard_map/ppermute | solution.py:44
  36.1 2.5 %collective-permute-start.10 = (bf16[64,640]{1,0:T(8,128)(2,1)}, bf16[64,640]{1,0:T(8,128)(2,1)S(1)}, u32[]{:S(2)}, u32[]{:S(2)}) collective-permute-start(bf16[64,640]{1,0:T(8,128)(2,1)} %get-tuple-element.169.refs_0_), channel_id=1, source_target_pairs={{0,8},{1,9},{2,10},{3,11},{4,12},{5,13},{6,14},{7,15},{8,0},{9,1},... | collective-permute-start | bytes 245768 | tf_op jit(solution)/shard_map/ppermute | solution.py:44
  46.4 2.0 collective-permute-done.11.refs_2_
  49.4 8.6 %project.1 = (bf16[2048,512]{1,0:T(8,128)(2,1)}, bf16[2,2048,128]{2,1,0:T(8,128)(2,1)}, bf16[2,2048,128]{2,1,0:T(8,128)(2,1)}, bf16[2,128,2048]{2,1,0:T(8,128)(2...) custom-call(f32[1]{0:T(128)} %bitcast.ratio, s32[8]{0:T(128)S(1)} %fusion.6.sc, ...), custom_call_target="tpu_custom_call" | custom-call | flops 2700000000 | bytes 9000000 | tf_op jit(solution)/shard_map/project/pallas_call | solution.py:166
  61.6 8.8 %attend.2 = (bf16[1024,256]{1,0:T(8,128)(2,1)}, bf16[2,1024,128]{2,1,0:T(8,128)(2,1)}) custom-call(bf16[2,2048,128]{2,1,0:T(8,128)(2,1)} %get-tuple-element.198.q_ref, bf16[2,2048,128]{2,1,0:T(8,128)(2,1)} %get-tuple-element.173.k_ref, bf16[2,2048,128]{2,1,0:T(8,128)(2,1)} %get-tuple-element.174.x_ref, bf16[2,128,2048]{2,1,0:T(8,128)(2,1)} %get-tuple-element.175.vt_ref), custom_call_target="tpu_custom_call" | custom-call | flops 1800000000 | bytes 6000000 | tf_op jit(solution)/shard_map/attend/pallas_call | solution.py:262
  70.3 8.8 %attend.3 = (bf16[1024,256]{1,0:T(8,128)(2,1)}, bf16[2,1024,128]{2,1,0:T(8,128)(2,1)}) custom-call(bf16[2,2048,128]{2,1,0:T(8,128)(2,1)} %get-tuple-element.198.q_ref, bf16[2,2048,128]{2,1,0:T(8,128)(2,1)} %get-tuple-element.173.k_ref, bf16[2,2048,128]{2,1,0:T(8,128)(2,1)} %get-tuple-element.174.x_ref, bf16[2,128,2048]{2,1,0:T(8,128)(2,1)} %get-tuple-element.175.vt_ref), custom_call_target="tpu_custom_call" | custom-call | flops 1800000000 | bytes 6000000 | tf_op jit(solution)/shard_map/attend/pallas_call | solution.py:262
  80.4 3.3 %collective-permute-done.17.ob_ref = bf16[1024,256]{1,0:T(8,128)(2,1)S(1)} collective-permute-done((bf16[1024,256]{1,0:T(8,128)(2,1)S(1)}, bf16[1024,256]{1,0:T(8,128)(2,1)S(1)}, u32[]{:S(2)}, u32[]{:S(2)}) %collective-permute-start.17) | collective-permute-done | bytes 524320 | tf_op jit(solution)/shard_map/ppermute | solution.py:44
  83.7 22.2 %middle.1 = (bf16[256,512]{1,0:T(8,128)(2,1)S(1)}, bf16[256,512]{1,0:T(8,128)(2,1)S(1)}, bf16[256,512]{1,0:T(8,128)(2,1)S(1)}, bf16[256,512]{1,0:T(8,128)(2,1)S(...) custom-call(s32[8]{0:T(128)S(1)} %fusion.6.sc, ...), custom_call_target="tpu_custom_call" | custom-call | flops 7500000256 | bytes 25000000 | tf_op jit(solution)/shard_map/middle/pallas_call | solution.py:547
  106.5 3.1 %collective-permute-done.21 = bf16[2,512,640]{2,1,0:T(8,128)(2,1)S(1)} collective-permute-done((bf16[2,512,640]{2,1,0:T(8,128)(2,1)S(1)}, bf16[2,512,640]{2,1,0:T(8,128)(2,1)S(1)}, u32[]{:S(2)}, u32[]{:S(2)}) %collective-permute-start.21) | collective-permute-done | bytes 1310752 | tf_op jit(solution)/shard_map/ppermute | solution.py:44
  114.1 25.5 %attend_back.1 = (bf16[2048,256]{1,0:T(8,128)(2,1)}, f32[2,128,2048]{2,1,0:T(8,128)}, f32[2,128,2048]{2,1,0:T(8,128)}) custom-call(bf16[2,2048,128]{2,1,0:T(8,128)(2,1)} %get-tuple-element.198.q_ref, bf16[2,2048,128]{2,1,0:T(8,128)(2,1)} %get-tuple-element.173.k_ref, bf16[2,2048,128]{2,1,0:T(8,128)(2,1)} %get-tuple-element.174.x_ref, ...), custom_call_target="tpu_custom_call" | custom-call | flops 6000000000 | bytes 20000000 | tf_op jit(solution)/shard_map/attend_back/pallas_call | solution.py:341
  140.0 11.2 %weight_grads.1 = (bf16[2,512,384]{2,1,0:T(8,128)(2,1)}, bf16[4,2,2,48,384]{4,3,2,1,0:T(8,128)(2,1)}, bf16[4,2,2,48,384]{4,3,2,1,0:T(8,128)(2,1)S(1)}, f32[1024,512]{1,0:T(8,128)}, bf16[1024,512]{1,0:T(8,128)(2,1)}) custom-call(s32[8]{0:T(128)S(1)} %fusion.6.sc, bf16[2048,512]{1,0:T(8,128)(2,1)} %get-tuple-element.166.x_ref, ...), custom_call_target="tpu_custom_call" | custom-call | flops 2700000000 | bytes 9000000 | tf_op jit(solution)/shard_map/weight_grads/pallas_call | solution.py:1019
  151.8 3.0 %collective-permute-done.26.b_ref = bf16[4,2,2,48,384]{4,3,2,1,0:T(8,128)(2,1)} collective-permute-done((bf16[4,2,2,48,384]{4,3,2,1,0:T(8,128)(2,1)S(1)}, bf16[4,2,2,48,384]{4,3,2,1,0:T(8,128)(2,1)}, u32[]{:S(2)}, u32[]{:S(2)}) %collective-permute-start.26) | collective-permute-done | bytes 589856 | tf_op jit(solution)/shard_map/ppermute | solution.py:44
  160.8 2.6 %collective-permute-start.30 = (bf16[2,64,640]{2,1,0:T(8,128)(2,1)S(1)}, bf16[2,64,640]{2,1,0:T(8,128)(2,1)S(1)}, u32[]{:S(2)}, u32[]{:S(2)}) collective-permute-start(bf16[2,64,640]{2,1,0:T(8,128)(2,1)S(1)} %get-tuple-element.226), channel_id=1, source_target_pairs={{0,16},{1,17},{2,18},{3,19},{4,20},{5,21},{6,22},{7,23},{8,24},{9,... | collective-permute-start | bytes 491528 | tf_op jit(solution)/shard_map/ppermute | solution.py:44
  163.3 5.5 %input_grads.1 = (bf16[112,256]{1,0:T(8,128)(2,1)S(1)}, bf16[112,256]{1,0:T(8,128)(2,1)S(1)}, bf16[112,256]{1,0:T(8,128)(2,1)S(1)}, bf16[112,256]{1,0:T(8,128)(2,1)S(1)}, bf16[512,128]{1,0:T(8,128)(2,1)S(1)}) custom-call(s32[8]{0:T(128)S(1)} %fusion.6.sc, f32[1]{0:T(128)} %bitcast.ratio, f32[1024,512]{1,0:T(8,128)} %get-tuple-element.227.dr_ref, ...), custom_call_target="tpu_custom_call" | custom-call | flops 1800000000 | bytes 6000000 | tf_op jit(solution)/shard_map/input_grads/pallas_call | solution.py:1107
  176.2 3.2 %collective-permute-done.32.refs_5_ = bf16[64,640]{1,0:T(8,128)(2,1)S(1)} collective-permute-done((bf16[64,640]{1,0:T(8,128)(2,1)S(1)}, bf16[64,640]{1,0:T(8,128)(2,1)S(1)}, u32[]{:S(2)}, u32[]{:S(2)}) %collective-permute-start.32) | collective-permute-done | bytes 81952 | tf_op jit(solution)/shard_map/ppermute | solution.py:44
  185.7 5.4 %collective-permute-done.38.refs_2_ = bf16[128,384]{1,0:T(8,128)(2,1)S(1)} collective-permute-done((bf16[128,384]{1,0:T(8,128)(2,1)S(1)}, bf16[128,384]{1,0:T(8,128)(2,1)S(1)}, u32[]{:S(2)}, u32[]{:S(2)}) %collective-permute-start.38) | collective-permute-done | bytes 98336 | tf_op jit(solution)/shard_map/ppermute | solution.py:44
  197.7 2.4 %collective-permute-done.43 = f32[8,128]{1,0:T(8,128)S(1)} collective-permute-done((f32[8,128]{1,0:T(8,128)S(1)}, f32[8,128]{1,0:T(8,128)S(1)}, u32[]{:S(2)}, u32[]{:S(2)}) %collective-permute-start.43) | collective-permute-done | bytes 4128 | tf_op jit(solution)/shard_map/ppermute | solution.py:44
  202.6 1.9 collective-permute-start.46
  206.2 1.8 collective-permute-done.46.refs_3_
  (152 shorter events, 58.4 us)
Async XLA Ops:
  5.5 9.5 %collective-permute-start.1 = (bf16[112,384]{1,0:T(8,128)(2,1)S(1)}, bf16[112,384]{1,0:T(8,128)(2,1)S(1)}, u32[]{:S(2)}, u32[]{:S(2)}) collective-permute-start(bf16[112,384]{1,0:T(8,128)(2,1)S(1)} %get-tuple-element.153.refs_0_), channel_id=1, source_target_pairs={{0,16},{1,17},{2,18},{3,19},{4,20},{5,21},{6,22},{7,23},{8,24},{9,... | collective-permute-start | bytes 258056 | tf_op jit(solution)/shard_map/ppermute | solution.py:44
  15.7 11.5 %collective-permute-start.3 = (bf16[528,384]{1,0:T(8,128)(2,1)S(1)}, bf16[528,384]{1,0:T(8,128)(2,1)S(1)}, u32[]{:S(2)}, u32[]{:S(2)}) collective-permute-start(bf16[528,384]{1,0:T(8,128)(2,1)S(1)} %get-tuple-element.156), channel_id=1, source_target_pairs={{0,2},{1,3},{2,0},{3,1},{4,6},{5,7},{6,4},{7,5},{8,10},{9,11},{10,... | collective-permute-start | bytes 1216520 | tf_op jit(solution)/shard_map/ppermute | solution.py:44
  17.3 12.3 %collective-permute-start.4 = (bf16[528,384]{1,0:T(8,128)(2,1)S(1)}, bf16[528,384]{1,0:T(8,128)(2,1)S(1)}, u32[]{:S(2)}, u32[]{:S(2)}) collective-permute-start(bf16[528,384]{1,0:T(8,128)(2,1)S(1)} %get-tuple-element.157), channel_id=1, source_target_pairs={{0,4},{1,5},{2,6},{3,7},{4,0},{5,1},{6,2},{7,3},{8,12},{9,13},{10,... | collective-permute-start | bytes 1216520 | tf_op jit(solution)/shard_map/ppermute | solution.py:44
  18.7 15.9 %collective-permute-start.5 = (bf16[528,384]{1,0:T(8,128)(2,1)S(1)}, bf16[528,384]{1,0:T(8,128)(2,1)S(1)}, u32[]{:S(2)}, u32[]{:S(2)}) collective-permute-start(bf16[528,384]{1,0:T(8,128)(2,1)S(1)} %get-tuple-element.158), channel_id=1, source_target_pairs={{0,6},{1,7},{2,4},{3,5},{4,2},{5,3},{6,0},{7,1},{8,14},{9,15},{10,... | collective-permute-start | bytes 1216520 | tf_op jit(solution)/shard_map/ppermute | solution.py:44
  19.2 16.8 %collective-permute-start.6 = (bf16[528,384]{1,0:T(8,128)(2,1)S(1)}, bf16[528,384]{1,0:T(8,128)(2,1)S(1)}, u32[]{:S(2)}, u32[]{:S(2)}) collective-permute-start(bf16[528,384]{1,0:T(8,128)(2,1)S(1)} %get-tuple-element.155.t0), channel_id=1, source_target_pairs={{0,1},{1,0},{2,3},{3,2},{4,5},{5,4},{6,7},{7,6},{8,9},{9,8},{10,11... | collective-permute-start | bytes 1216520 | tf_op jit(solution)/shard_map/ppermute | solution.py:44
  27.1 12.4 %collective-permute-start.7 = (bf16[528,384]{1,0:T(8,128)(2,1)S(1)}, bf16[528,384]{1,0:T(8,128)(2,1)S(1)}, u32[]{:S(2)}, u32[]{:S(2)}) collective-permute-start(bf16[528,384]{1,0:T(8,128)(2,1)S(1)} %collective-permute-done.3.t1), channel_id=1, source_target_pairs={{0,1},{1,0},{2,3},{3,2},{4,5},{5,4},{6,7},{7,6},{8,9},{9,8},{10,11... | collective-permute-start | bytes 1216520 | tf_op jit(solution)/shard_map/ppermute | solution.py:44
  29.6 11.5 %collective-permute-start.8 = (bf16[528,384]{1,0:T(8,128)(2,1)S(1)}, bf16[528,384]{1,0:T(8,128)(2,1)S(1)}, u32[]{:S(2)}, u32[]{:S(2)}) collective-permute-start(bf16[528,384]{1,0:T(8,128)(2,1)S(1)} %collective-permute-done.4.t2), channel_id=1, source_target_pairs={{0,1},{1,0},{2,3},{3,2},{4,5},{5,4},{6,7},{7,6},{8,9},{9,8},{10,11... | collective-permute-start | bytes 1216520 | tf_op jit(solution)/shard_map/ppermute | solution.py:44
  36.1 9.9 %collective-permute-start.10 = (bf16[64,640]{1,0:T(8,128)(2,1)}, bf16[64,640]{1,0:T(8,128)(2,1)S(1)}, u32[]{:S(2)}, u32[]{:S(2)}) collective-permute-start(bf16[64,640]{1,0:T(8,128)(2,1)} %get-tuple-element.169.refs_0_), channel_id=1, source_target_pairs={{0,8},{1,9},{2,10},{3,11},{4,12},{5,13},{6,14},{7,15},{8,0},{9,1},... | collective-permute-start | bytes 245768 | tf_op jit(solution)/shard_map/ppermute | solution.py:44
  38.6 9.8 %collective-permute-start.11 = (bf16[64,640]{1,0:T(8,128)(2,1)}, bf16[64,640]{1,0:T(8,128)(2,1)S(1)}, u32[]{:S(2)}, u32[]{:S(2)}) collective-permute-start(bf16[64,640]{1,0:T(8,128)(2,1)} %get-tuple-element.169.refs_0_), channel_id=1, source_target_pairs={{0,16},{1,17},{2,18},{3,19},{4,20},{5,21},{6,22},{7,23},{8,24},{9,... | collective-permute-start | bytes 245768 | tf_op jit(solution)/shard_map/ppermute | solution.py:44
  42.9 15.1 %collective-permute-start.13 = (bf16[256,512]{1,0:T(8,128)(2,1)S(1)}, bf16[256,512]{1,0:T(8,128)(2,1)S(1)}, u32[]{:S(2)}, u32[]{:S(2)}) collective-permute-start(bf16[256,512]{1,0:T(8,128)(2,1)S(1)} %get-tuple-element.308), channel_id=1, source_target_pairs={{0,2},{1,3},{2,0},{3,1},{4,6},{5,7},{6,4},{7,5},{8,10},{9,11},{10,... | collective-permute-start | bytes 786440 | tf_op jit(solution)/shard_map/ppermute | solution.py:44
  44.5 13.5 %collective-permute-start.14 = (bf16[256,512]{1,0:T(8,128)(2,1)S(1)}, bf16[256,512]{1,0:T(8,128)(2,1)S(1)}, u32[]{:S(2)}, u32[]{:S(2)}) collective-permute-start(bf16[256,512]{1,0:T(8,128)(2,1)S(1)} %get-tuple-element.307), channel_id=1, source_target_pairs={{0,4},{1,5},{2,6},{3,7},{4,0},{5,1},{6,2},{7,3},{8,12},{9,13},{10,... | collective-permute-start | bytes 786440 | tf_op jit(solution)/shard_map/ppermute | solution.py:44
  46.0 12.0 %collective-permute-start.15 = (bf16[256,512]{1,0:T(8,128)(2,1)S(1)}, bf16[256,512]{1,0:T(8,128)(2,1)S(1)}, u32[]{:S(2)}, u32[]{:S(2)}) collective-permute-start(bf16[256,512]{1,0:T(8,128)(2,1)S(1)} %get-tuple-element.306), channel_id=1, source_target_pairs={{0,6},{1,7},{2,4},{3,5},{4,2},{5,3},{6,0},{7,1},{8,14},{9,15},{10,... | collective-permute-start | bytes 786440 | tf_op jit(solution)/shard_map/ppermute | solution.py:44
  58.0 12.3 %collective-permute-start.16 = (bf16[4,64,640]{2,1,0:T(8,128)(2,1)S(1)}, bf16[4,64,640]{2,1,0:T(8,128)(2,1)S(1)}, u32[]{:S(2)}, u32[]{:S(2)}) collective-permute-start(bf16[4,64,640]{2,1,0:T(8,128)(2,1)S(1)} %stack_rest.1.t0), channel_id=1, source_target_pairs={{0,2},{1,3},{2,0},{3,1},{4,6},{5,7},{6,4},{7,5},{8,10},{9,11},{10,... | collective-permute-start | bytes 983048 | tf_op jit(solution)/shard_map/ppermute | solution.py:44
  59.6 19.5 %collective-permute-start.18 = (bf16[4,64,640]{2,1,0:T(8,128)(2,1)S(1)}, bf16[4,64,640]{2,1,0:T(8,128)(2,1)S(1)}, u32[]{:S(2)}, u32[]{:S(2)}) collective-permute-start(bf16[4,64,640]{2,1,0:T(8,128)(2,1)S(1)} %stack_rest.1.t0), channel_id=1, source_target_pairs={{0,4},{1,5},{2,6},{3,7},{4,0},{5,1},{6,2},{7,3},{8,12},{9,13},{10,... | collective-permute-start | bytes 983048 | tf_op jit(solution)/shard_map/ppermute | solution.py:44
  61.1 18.0 %collective-permute-start.19 = (bf16[4,64,640]{2,1,0:T(8,128)(2,1)S(1)}, bf16[4,64,640]{2,1,0:T(8,128)(2,1)S(1)}, u32[]{:S(2)}, u32[]{:S(2)}) collective-permute-start(bf16[4,64,640]{2,1,0:T(8,128)(2,1)S(1)} %stack_rest.1.t0), channel_id=1, source_target_pairs={{0,6},{1,7},{2,4},{3,5},{4,2},{5,3},{6,0},{7,1},{8,14},{9,15},{10,... | collective-permute-start | bytes 983048 | tf_op jit(solution)/shard_map/ppermute | solution.py:44
  110.5 29.1 %collective-permute-start.22 = (bf16[464,640]{1,0:T(8,128)(2,1)S(1)}, bf16[464,640]{1,0:T(8,128)(2,1)S(1)}, u32[]{:S(2)}, u32[]{:S(2)}) collective-permute-start(bf16[464,640]{1,0:T(8,128)(2,1)S(1)} %get-tuple-element.195), channel_id=1, source_target_pairs={{0,2},{1,3},{2,0},{3,1},{4,6},{5,7},{6,4},{7,5},{8,10},{9,11},{10,... | collective-permute-start | bytes 1781768 | tf_op jit(solution)/shard_map/ppermute | solution.py:44
  112.1 27.5 %collective-permute-start.23 = (bf16[464,640]{1,0:T(8,128)(2,1)S(1)}, bf16[464,640]{1,0:T(8,128)(2,1)S(1)}, u32[]{:S(2)}, u32[]{:S(2)}) collective-permute-start(bf16[464,640]{1,0:T(8,128)(2,1)S(1)} %get-tuple-element.196), channel_id=1, source_target_pairs={{0,4},{1,5},{2,6},{3,7},{4,0},{5,1},{6,2},{7,3},{8,12},{9,13},{10,... | collective-permute-start | bytes 1781768 | tf_op jit(solution)/shard_map/ppermute | solution.py:44
  113.6 26.4 %collective-permute-start.24 = (bf16[464,640]{1,0:T(8,128)(2,1)S(1)}, bf16[464,640]{1,0:T(8,128)(2,1)S(1)}, u32[]{:S(2)}, u32[]{:S(2)}) collective-permute-start(bf16[464,640]{1,0:T(8,128)(2,1)S(1)} %get-tuple-element.197), channel_id=1, source_target_pairs={{0,6},{1,7},{2,4},{3,5},{4,2},{5,3},{6,0},{7,1},{8,14},{9,15},{10,... | collective-permute-start | bytes 1781768 | tf_op jit(solution)/shard_map/ppermute | solution.py:44
  151.2 12.2 %collective-permute-start.31 = (bf16[1024,512]{1,0:T(8,128)(2,1)}, bf16[1024,512]{1,0:T(8,128)(2,1)}, u32[]{:S(2)}, u32[]{:S(2)}) collective-permute-start(bf16[1024,512]{1,0:T(8,128)(2,1)} %get-tuple-element.230), channel_id=1, source_target_pairs={{0,1},{1,0},{2,3},{3,2},{4,5},{5,4},{6,7},{7,6},{8,9},{9,8},{10,11... | collective-permute-start | bytes 3145736 | tf_op jit(solution)/shard_map/ppermute | solution.py:44
  156.5 17.9 %collective-permute-start.27 = (bf16[4,112,384]{2,1,0:T(8,128)(2,1)S(1)}, bf16[4,112,384]{2,1,0:T(8,128)(2,1)S(1)}, u32[]{:S(2)}, u32[]{:S(2)}) collective-permute-start(bf16[4,112,384]{2,1,0:T(8,128)(2,1)S(1)} %get-tuple-element.214), channel_id=1, source_target_pairs={{0,2},{1,3},{2,0},{3,1},{4,6},{5,7},{6,4},{7,5},{8,10},{9,11},{10,... | collective-permute-start | bytes 1032200 | tf_op jit(solution)/shard_map/ppermute | solution.py:44
  158.1 16.8 %collective-permute-start.28 = (bf16[4,112,384]{2,1,0:T(8,128)(2,1)S(1)}, bf16[4,112,384]{2,1,0:T(8,128)(2,1)S(1)}, u32[]{:S(2)}, u32[]{:S(2)}) collective-permute-start(bf16[4,112,384]{2,1,0:T(8,128)(2,1)S(1)} %get-tuple-element.215), channel_id=1, source_target_pairs={{0,4},{1,5},{2,6},{3,7},{4,0},{5,1},{6,2},{7,3},{8,12},{9,13},{10,... | collective-permute-start | bytes 1032200 | tf_op jit(solution)/shard_map/ppermute | solution.py:44
  159.5 16.7 %collective-permute-start.29 = (bf16[4,112,384]{2,1,0:T(8,128)(2,1)S(1)}, bf16[4,112,384]{2,1,0:T(8,128)(2,1)S(1)}, u32[]{:S(2)}, u32[]{:S(2)}) collective-permute-start(bf16[4,112,384]{2,1,0:T(8,128)(2,1)S(1)} %get-tuple-element.216), channel_id=1, source_target_pairs={{0,6},{1,7},{2,4},{3,5},{4,2},{5,3},{6,0},{7,1},{8,14},{9,15},{10,... | collective-permute-start | bytes 1032200 | tf_op jit(solution)/shard_map/ppermute | solution.py:44
  160.8 9.9 %collective-permute-start.30 = (bf16[2,64,640]{2,1,0:T(8,128)(2,1)S(1)}, bf16[2,64,640]{2,1,0:T(8,128)(2,1)S(1)}, u32[]{:S(2)}, u32[]{:S(2)}) collective-permute-start(bf16[2,64,640]{2,1,0:T(8,128)(2,1)S(1)} %get-tuple-element.226), channel_id=1, source_target_pairs={{0,16},{1,17},{2,18},{3,19},{4,20},{5,21},{6,22},{7,23},{8,24},{9,... | collective-permute-start | bytes 491528 | tf_op jit(solution)/shard_map/ppermute | solution.py:44
  181.5 9.6 %collective-permute-start.38 = (bf16[128,384]{1,0:T(8,128)(2,1)S(1)}, bf16[128,384]{1,0:T(8,128)(2,1)S(1)}, u32[]{:S(2)}, u32[]{:S(2)}) collective-permute-start(bf16[128,384]{1,0:T(8,128)(2,1)S(1)} %get-tuple-element.253), channel_id=1, source_target_pairs={{0,16},{1,17},{2,18},{3,19},{4,20},{5,21},{6,22},{7,23},{8,24},{9,... | collective-permute-start | bytes 294920 | tf_op jit(solution)/shard_map/ppermute | solution.py:44
  (46 other events, 327.3 us)

commit v5 on v4

--- a/solution.py
+++ b/solution.py
@@ -117,19 +117,19 @@
 
     @pl.when(step == 0)
     def _():
-        half = own.shape[0]
-        size = half // 2
-        key = lax.broadcasted_iota(jnp.int32, extra_ref.shape[1:], 0)
-        lane = lax.broadcasted_iota(jnp.int32, extra_ref.shape[1:], 1)
-        inner = key - PAD
-        place = inner % half
-        slot = (2 * (place // size) + (sc[2] ^ (inner // half))) * size + place % size
-        limit = jnp.where(key < PAD, PROMPT, sc[4])
-        bias = jnp.where(jnp.where(key < PAD, key, slot) >= limit, neg_big, 0.0)
-        bias = jnp.where(lane == 3, bias, 0.0)
-        for h in range(2):
-            ones = jnp.where((lane >= 4 * h) & (lane < 4 * h + 3), 1.0, 0.0)
-            extra_ref[h] = (bias + ones).astype(bf16)
+        size = own.shape[0] // 2
+        lane = lax.broadcasted_iota(jnp.int32, (size, WIDE), 1)
+        line = lax.broadcasted_iota(jnp.int32, (size, WIDE), 0)
+        ones = [jnp.where((lane >= 4 * h) & (lane < 4 * h + 3), 1.0, 0.0) for h in range(2)]
+        for begin in range(0, extra_ref.shape[1], size):
+            if begin < PAD:
+                left = PROMPT - begin
+            else:
+                other, quarter = divmod((begin - PAD) // size, 2)
+                left = sc[4] - (2 * quarter + (sc[2] ^ other)) * size
+            bias = jnp.where((lane == 3) & (line >= left), neg_big, 0.0)
+            for h in range(2):
+                extra_ref[h, begin : begin + size] = (bias + ones[h]).astype(bf16)
 
     rows = jnp.where(step < 2, own[...], other[...])
     low = (ratio[0] * dot(rows, enc[...], NT) + vec[6:7, :]).astype(bf16)
@@ -423,26 +423,34 @@
     gvec,
     gb1,
     cot,
+    late,
     acc,
 ):
     step = pl.program_id(0)
     count = rows_ref.shape[0]
+    part = count // 2
+
+    def quarter_rows(k):
+        return pl.ds(pl.multiple_of((sc[1] ^ (k % 2)) * part, part), part)
+
     for k, ref in enumerate((c0, c1, c2, c3)):
 
-        @pl.when(step == k)
-        def _(ref=ref):
-            cot[...] = ref[...]
+        @pl.when(step == k // 2)
+        def _(k=k, ref=ref):
+            cot[quarter_rows(k), :] = ref[...]
 
     @pl.when(step == 0)
     def _():
-        acc[...] = jnp.zeros_like(acc)
         gvec[...] = jnp.zeros_like(gvec)
         gb1[...] = jnp.zeros_like(gb1)
 
-    group = sc[0] ^ (step // 2)
-    quarter = 2 * (sc[1] ^ (step % 2)) + sc[2]
+    def gather(k, low, high, value):
+        acc[k, :, low:high] = jnp.where(step > 0, acc[k, :, low:high], 0.0) + value
+
+    group = sc[0] ^ step
     limit = jnp.where(group == 0, sc[4], sc[5])
-    slot = quarter * count + lax.broadcasted_iota(jnp.int32, (count, 1), 0)
+    line = lax.broadcasted_iota(jnp.int32, (count, 1), 0)
+    slot = line + sc[2] * part + jnp.where(line >= part, part, 0)
     live = (slot < limit).astype(f32)
 
     def weight(k, low, high):
@@ -485,12 +493,12 @@
         slopes.append(slope)
         mlp = mlp + dot(acts[k], weight(k, HEAD + HID, HEAD + 2 * HID), NT)
     normed_two, inverse_two = norm(first + mlp)
-    out = ((normed_two * gain_two + shift_two) * live).astype(bf16)
+    late[...] = ((normed_two * gain_two + shift_two) * live).astype(bf16)
     for k, ref in enumerate((y0, y1, y2, y3)):
 
-        @pl.when(step == k)
-        def _(ref=ref):
-            ref[...] = out
+        @pl.when(step == k // 2)
+        def _(k=k, ref=ref):
+            ref[...] = late[quarter_rows(k), :]
 
     grad_y = cot[...].astype(f32) * live
     add_row(2, grad_y * normed_two)
@@ -502,11 +510,11 @@
     first_flip = first_low.T
     grad_first = grad_two
     for k in range(4):
-        acc[k, :, HEAD + HID :] += dot(grad_flip, acts[k], NN)
+        gather(k, HEAD + HID, HEAD + 2 * HID, dot(grad_flip, acts[k], NN))
         grad_act = dot(grad_low, weight(k, HEAD + HID, HEAD + 2 * HID), NN)
         grad_pre = (grad_act * slopes[k]).astype(bf16)
         gb1[k : k + 1, :] += jnp.sum(grad_pre.astype(f32), axis=0, keepdims=True)
-        acc[k, :, HEAD : HEAD + HID] += dot(first_flip, grad_pre, NN)
+        gather(k, HEAD, HEAD + HID, dot(first_flip, grad_pre, NN))
         grad_first = grad_first + dot(grad_pre, weight(k, HEAD, HEAD + HID), NT)
     add_row(0, grad_first * normed_one)
     add_row(1, grad_first)
@@ -517,8 +525,8 @@
     attn_flip = attn_low.T
     for k, (source, target) in enumerate(((oa_ref, da_ref), (ob_ref, db_ref))):
         both = dot(attn_flip, source[...], NN)
-        acc[2 * k, :, 0:HEAD] += both[:, 0:HEAD]
-        acc[2 * k + 1, :, 0:HEAD] += both[:, HEAD:]
+        gather(2 * k, 0, HEAD, both[:, 0:HEAD])
+        gather(2 * k + 1, 0, HEAD, both[:, HEAD:])
         both = dot(attn_low, out_pair[k], NN).astype(bf16)
         target[:, 0 : 2 * HEAD] = both
         product = both.astype(f32) * source[...].astype(f32)
@@ -530,7 +538,7 @@
                 tile = tile + jnp.where(lane == 4 * h + m, term, 0.0)
         target[:, 2 * HEAD :] = tile.astype(bf16)
 
-    @pl.when(step == 3)
+    @pl.when(step == 1)
     def _():
         ga[...] = acc[0:2].astype(bf16)
         gb[...] = acc[2:4].astype(bf16)
@@ -538,9 +546,10 @@
 
 def middle(sc, ratio, rows, o_own, o_other, cots, enc, vec, b1, rest_own, rest_other):
     size = rows.shape[0] // 4
+    block = 2 * size
     width = enc.shape[0]
-    spot = lambda i, sc: (2 * (sc[0] ^ (i // 2)) + (sc[1] ^ (i % 2)), 0)
-    pair = pl.BlockSpec((size, 2 * HEAD), spot)
+    spot = lambda i, sc: (sc[0] ^ i, 0)
+    pair = pl.BlockSpec((block, 2 * HEAD), spot)
     smem = pl.BlockSpec(memory_space=pltpu.SMEM)
     fixed = pl.BlockSpec((size, width), lambda i, sc: (0, 0))
     weight = rest_own.shape
@@ -548,13 +557,13 @@
         middle_body,
         grid_spec=pltpu.PrefetchScalarGridSpec(
             num_scalar_prefetch=1,
-            grid=(4,),
-            in_specs=[smem, pl.BlockSpec((size, WIDE), spot), pair, pair]
+            grid=(2,),
+            in_specs=[smem, pl.BlockSpec((block, WIDE), spot), pair, pair]
             + [fixed] * 4
             + [whole()] * 5,
             out_specs=[fixed] * 4
-            + [pl.BlockSpec((size, 3 * HEAD), spot)] * 2
-            + [pl.BlockSpec((size, width), spot)]
+            + [pl.BlockSpec((block, 3 * HEAD), spot)] * 2
+            + [pl.BlockSpec((block, width), spot)]
             + [
                 pl.BlockSpec(weight, lambda i, sc: (0, 0, 0)),
                 pl.BlockSpec(weight, lambda i, sc: (0, 0, 0)),
@@ -562,7 +571,8 @@
                 pl.BlockSpec((4, HID), lambda i, sc: (0, 0)),
             ],
             scratch_shapes=[
-                pltpu.VMEM((size, width), bf16),
+                pltpu.VMEM((block, width), bf16),
+                pltpu.VMEM((block, width), bf16),
                 pltpu.VMEM((4,) + weight[1:], f32),
             ],
         ),
@@ -898,15 +908,20 @@
     return simple(body, shapes, *tops, *lows, mask, scalars=places, name="unpack_main")
 
 
-def unpack_rest(tops, places):
+def unpack_rest(tops, lows, places):
     n_ep, slab, width = tops[0].shape
 
-    def body(sc, t0, t1, t2, t3, out_ref):
-        for k, ref in enumerate((t0, t1, t2, t3)):
-            out_ref[k % 2, :, sc[0] ^ (k // 2)] = ref[...]
+    def body(sc, *refs):
+        for k in range(8):
+            refs[8 + k // 4][k % 2, :, sc[0] ^ (k % 4 // 2)] = refs[k][...]
 
     return simple(
-        body, shape_of((2, n_ep, 2, slab, width), bf16), *tops, scalars=places, name="unpack_rest"
+        body,
+        [shape_of((2, n_ep, 2, slab, width), bf16)] * 2,
+        *tops,
+        *lows,
+        scalars=places,
+        name="unpack_rest",
     )
 
 
@@ -1076,14 +1091,16 @@
         acc[...] += part
         bias[...] += part_bias
 
-    grad = dot(enc[...].T, low, NT) * ratio[0] * mask[...]
+    grad = dot(enc[...].T, low, NT)[0:FEAT_ROWS] * ratio[0] * mask[0:FEAT_ROWS]
     for k, ref in enumerate((i0, i1, i2, i3)):
 
-        @pl.when(step == k)
-        def _(ref=ref):
-            ref[...] = grad[0:FEAT_ROWS].astype(bf16)
-
-    @pl.when(step == 3)
+        @pl.when(step == k // 2)
+        def _(k=k, ref=ref):
+            first = sc[1] ^ (k % 2) == 0
+            part = ref.shape[1]
+            ref[...] = jnp.where(first, grad[:, 0:part], grad[:, part:]).astype(bf16)
+
+    @pl.when(step == 1)
     def _():
         width = acc.shape[0]
         rows = jnp.concatenate(
@@ -1101,20 +1118,20 @@
 def input_grads(sc, ratio, dr, own, got, rows, enc, mask, rows_grad):
     size = rows.shape[0] // 4
     width = enc.shape[0]
-    spot = lambda i, sc: (2 * (sc[0] ^ (i // 2)) + (sc[1] ^ (i % 2)), 0)
-    block = pl.BlockSpec((size, width), spot)
+    spot = lambda i, sc: (sc[0] ^ i, 0)
+    block = pl.BlockSpec((2 * size, width), spot)
     fixed = pl.BlockSpec((FEAT_ROWS, size), lambda i, sc: (0, 0))
     return pl.pallas_call(
         input_body,
         grid_spec=pltpu.PrefetchScalarGridSpec(
             num_scalar_prefetch=1,
-            grid=(4,),
+            grid=(2,),
             in_specs=[
                 pl.BlockSpec(memory_space=pltpu.SMEM),
                 block,
                 block,
                 block,
-                pl.BlockSpec((size, WIDE), spot),
+                pl.BlockSpec((2 * size, WIDE), spot),
                 whole(),
                 whole(),
                 whole(),
@@ -1505,9 +1522,11 @@
     attended_got = swap(attended_other, core=1)
     query_own = tie(query, (attended_other, rest_tops[1]))
     attended_own, extra_own = attend(query_own, keys, key_extra, values_flip, 0)
-    rest_own = unpack_rest(tie(rest_tops, attended_own), places)
+    rest_early = [swap(top, core=1) for top in rest_tops[0:2]]
+    rest_late = [swap(top, core=1) for top in tie(rest_tops[2:4], attended_own)]
+    rest_own, rest_other = unpack_rest(rest_tops, rest_early + rest_late, places)
     rest_own = rest_own.reshape(2, width, -1)
-    rest_other = swap(rest_own, core=1)
+    rest_other = rest_other.reshape(2, width, -1)
     (y0, y1, y2, y3, grad_own, grad_sent, grad_one, rest_mine, rest_sent, grad_rows, grad_hidden_row) = middle(
         places,
         ratio,
@@ -1521,8 +1540,8 @@
         rest_own,
         rest_other,
     )
-    grad_got = swap(grad_sent, core=1)
     rest_got = swap(rest_sent, core=1)
+    grad_got = swap(tie(grad_sent, rest_got), core=1)
     rest_parts = pack_rest(rest_mine, rest_got, (y0, y1, y2, y3), places, n_ep, slab)
     rest_tops = plane_list(rest_parts)
     query_again, *unused = lax.optimization_barrier((query, *rest_parts))
@@ -1551,7 +1570,7 @@
         strip,
     )
     prompt_got = swap(prompt_sent, core=1)
-    back_got = swap(back_other, core=1)
+    back_got = swap(tie(back_other, prompt_got), core=1)
     main_parts = pack_main(grad_project, prompt_mine, prompt_got, places, slab, strip)
     main_tops = plane_list(main_parts)
     back_own = tie(back_own, main_parts)

time: 210 us -> 205 us (0.976)
  Pallas kernels: 104 us -> 100 us
    pallas_call x1, Pallas kernels: 22.2 us -> 19.3 us  [middle(): pl.pallas_call(middle_body, grid_spec=pltpu.PrefetchScalarGridSpec(num_sc...]
    ppermute x47 -> x50, waiting for transfers between devices: 52.5 us -> 51.5 us  [swap(): return lax.ppermute(value, AXES, pairs)]
    ppermute x47 -> x50, starting transfers between devices: 48.6 us -> 48.5 us  [swap(): return lax.ppermute(value, AXES, pairs)]
  transfers between devices with their start and end apart: 47 -> 50, of which waited for: 20 -> 24; matrix products, arithmetic and copies ran while one was open for 1% -> 1% of each run, Pallas kernels for 31% -> 32%
where the time goes in v5:
time: 205 us; the launch traced here: 204 us
  Pallas kernels  100 us (49%)
  waiting for transfers between devices  51.5 us (25%)
  starting transfers between devices  48.5 us (24%)
  between operations  2.07 us (1%)
    ppermute x50, waiting for transfers between devices, swap(): return lax.ppermute(value, AXES, pairs)  51.5 us
    ppermute x50, starting transfers between devices, swap(): return lax.ppermute(value, AXES, pairs)  48.5 us
    pallas_call x1, Pallas kernels, attend_back(): pl.pallas_call(attend_back_body, grid=(2, 2), in_specs=[pl.BlockSpec((1,...  25.7 us
    pallas_call x1, Pallas kernels, middle(): pl.pallas_call(middle_body, grid_spec=pltpu.PrefetchScalarGridSpec(num_sc...  19.3 us
    pallas_call x2, Pallas kernels, attend(): pl.pallas_call(attend_body, grid=(2,), in_specs=[pl.BlockSpec((1, SLOTS,...  17.5 us
    pallas_call x17, Pallas kernels, simple(): pl.pallas_call(body, in_specs=specs, out_specs=[whole()] * len(out_shape)...  13.6 us
    pallas_call x1, Pallas kernels, weight_grads(): pl.pallas_call(functools.partial(weight_body, n_ep, strip), grid=(4,), in...  11 us
    pallas_call x1, Pallas kernels, project(): pl.pallas_call(project_body, grid=(4,), in_specs=[pl.BlockSpec(memory_spa...  8.34 us
  transfers between devices with their start and end apart: 50, of which 24 were waited for; matrix products, arithmetic and copies ran while one was open for 1% of the time, Pallas kernels for 32%

profile of v5, /device:TPU:0, one launch (start us, length us, event | category | flops | bytes accessed | tf_op | source)
XLA Modules:
  0.0 204.5 jit_solution(12592923260530240018)
XLA Ops:
  2.4 3.0 %collective-permute-start = (bf16[112,384]{1,0:T(8,128)(2,1)S(1)}, bf16[112,384]{1,0:T(8,128)(2,1)S(1)}, u32[]{:S(2)}, u32[]{:S(2)}) collective-permute-start(bf16[112,384]{1,0:T(8,128)(2,1)S(1)} %get-tuple-element.155.refs_0_), channel_id=1, source_target_pairs={{0,8},{1,9},{2,10},{3,11},{4,12},{5,13},{6,14},{7,15},{8,0},{9,1},... | collective-permute-start | bytes 258056 | tf_op jit(solution)/shard_map/ppermute | solution.py:44
  5.5 2.6 %collective-permute-start.1 = (bf16[112,384]{1,0:T(8,128)(2,1)S(1)}, bf16[112,384]{1,0:T(8,128)(2,1)S(1)}, u32[]{:S(2)}, u32[]{:S(2)}) collective-permute-start(bf16[112,384]{1,0:T(8,128)(2,1)S(1)} %get-tuple-element.155.refs_0_), channel_id=1, source_target_pairs={{0,16},{1,17},{2,18},{3,19},{4,20},{5,21},{6,22},{7,23},{8,24},{9,... | collective-permute-start | bytes 258056 | tf_op jit(solution)/shard_map/ppermute | solution.py:44
  8.4 6.6 %collective-permute-done.1.refs_2_ = bf16[112,384]{1,0:T(8,128)(2,1)S(1)} collective-permute-done((bf16[112,384]{1,0:T(8,128)(2,1)S(1)}, bf16[112,384]{1,0:T(8,128)(2,1)S(1)}, u32[]{:S(2)}, u32[]{:S(2)}) %collective-permute-start.1) | collective-permute-done | bytes 86048 | tf_op jit(solution)/shard_map/ppermute | solution.py:44
  19.2 7.9 %collective-permute-done.3.t1 = bf16[528,384]{1,0:T(8,128)(2,1)S(1)} collective-permute-done((bf16[528,384]{1,0:T(8,128)(2,1)S(1)}, bf16[528,384]{1,0:T(8,128)(2,1)S(1)}, u32[]{:S(2)}, u32[]{:S(2)}) %collective-permute-start.3) | collective-permute-done | bytes 405536 | tf_op jit(solution)/shard_map/ppermute | solution.py:44
  27.1 2.4 %collective-permute-done.4.t2 = bf16[528,384]{1,0:T(8,128)(2,1)S(1)} collective-permute-done((bf16[528,384]{1,0:T(8,128)(2,1)S(1)}, bf16[528,384]{1,0:T(8,128)(2,1)S(1)}, u32[]{:S(2)}, u32[]{:S(2)}) %collective-permute-start.4) | collective-permute-done | bytes 405536 | tf_op jit(solution)/shard_map/ppermute | solution.py:44
  29.6 5.1 %collective-permute-done.5.t3 = bf16[528,384]{1,0:T(8,128)(2,1)S(1)} collective-permute-done((bf16[528,384]{1,0:T(8,128)(2,1)S(1)}, bf16[528,384]{1,0:T(8,128)(2,1)S(1)}, u32[]{:S(2)}, u32[]{:S(2)}) %collective-permute-start.5) | collective-permute-done | bytes 405536 | tf_op jit(solution)/shard_map/ppermute | solution.py:44
  36.1 2.5 %collective-permute-start.10 = (bf16[64,640]{1,0:T(8,128)(2,1)}, bf16[64,640]{1,0:T(8,128)(2,1)S(1)}, u32[]{:S(2)}, u32[]{:S(2)}) collective-permute-start(bf16[64,640]{1,0:T(8,128)(2,1)} %get-tuple-element.171.refs_0_), channel_id=1, source_target_pairs={{0,8},{1,9},{2,10},{3,11},{4,12},{5,13},{6,14},{7,15},{8,0},{9,1},... | collective-permute-start | bytes 245768 | tf_op jit(solution)/shard_map/ppermute | solution.py:44
  46.4 2.0 collective-permute-done.11.refs_2_
  49.4 8.3 %project.1 = (bf16[2048,512]{1,0:T(8,128)(2,1)}, bf16[2,2048,128]{2,1,0:T(8,128)(2,1)}, bf16[2,2048,128]{2,1,0:T(8,128)(2,1)}, bf16[2,128,2048]{2,1,0:T(8,128)(2...) custom-call(f32[1]{0:T(128)} %bitcast.ratio, s32[8]{0:T(128)S(1)} %fusion.6.sc, ...), custom_call_target="tpu_custom_call" | custom-call | flops 2700000000 | bytes 9000000 | tf_op jit(solution)/shard_map/project/pallas_call | solution.py:166
  61.4 8.8 %attend.2 = (bf16[1024,256]{1,0:T(8,128)(2,1)}, bf16[2,1024,128]{2,1,0:T(8,128)(2,1)}) custom-call(bf16[2,2048,128]{2,1,0:T(8,128)(2,1)} %get-tuple-element.200.q_ref, bf16[2,2048,128]{2,1,0:T(8,128)(2,1)} %get-tuple-element.175.k_ref, bf16[2,2048,128]{2,1,0:T(8,128)(2,1)} %get-tuple-element.176.x_ref, bf16[2,128,2048]{2,1,0:T(8,128)(2,1)} %get-tuple-element.177.vt_ref), custom_call_target="tpu_custom_call" | custom-call | flops 1800000000 | bytes 6000000 | tf_op jit(solution)/shard_map/attend/pallas_call | solution.py:262
  70.7 8.8 %attend.3 = (bf16[1024,256]{1,0:T(8,128)(2,1)}, bf16[2,1024,128]{2,1,0:T(8,128)(2,1)}) custom-call(bf16[2,2048,128]{2,1,0:T(8,128)(2,1)} %get-tuple-element.200.q_ref, bf16[2,2048,128]{2,1,0:T(8,128)(2,1)} %get-tuple-element.175.k_ref, bf16[2,2048,128]{2,1,0:T(8,128)(2,1)} %get-tuple-element.176.x_ref, bf16[2,128,2048]{2,1,0:T(8,128)(2,1)} %get-tuple-element.177.vt_ref), custom_call_target="tpu_custom_call" | custom-call | flops 1800000000 | bytes 6000000 | tf_op jit(solution)/shard_map/attend/pallas_call | solution.py:262
  82.9 19.3 %middle.1 = (bf16[256,512]{1,0:T(8,128)(2,1)S(1)}, bf16[256,512]{1,0:T(8,128)(2,1)S(1)}, bf16[256,512]{1,0:T(8,128)(2,1)S(1)}, bf16[256,512]{1,0:T(8,128)(2,1)S(...) custom-call(s32[8]{0:T(128)S(1)} %fusion.6.sc, ...), custom_call_target="tpu_custom_call" | custom-call | flops 7500000256 | bytes 25000000 | tf_op jit(solution)/shard_map/middle/pallas_call | solution.py:556
  102.4 2.9 %collective-permute-done.24 = bf16[2,512,640]{2,1,0:T(8,128)(2,1)S(1)} collective-permute-done((bf16[2,512,640]{2,1,0:T(8,128)(2,1)S(1)}, bf16[2,512,640]{2,1,0:T(8,128)(2,1)S(1)}, u32[]{:S(2)}, u32[]{:S(2)}) %collective-permute-start.24) | collective-permute-done | bytes 1310752 | tf_op jit(solution)/shard_map/ppermute | solution.py:44
  109.9 25.7 %attend_back.1 = (bf16[2048,256]{1,0:T(8,128)(2,1)}, f32[2,128,2048]{2,1,0:T(8,128)}, f32[2,128,2048]{2,1,0:T(8,128)}) custom-call(bf16[2,2048,128]{2,1,0:T(8,128)(2,1)} %get-tuple-element.200.q_ref, bf16[2,2048,128]{2,1,0:T(8,128)(2,1)} %get-tuple-element.175.k_ref, bf16[2,2048,128]{2,1,0:T(8,128)(2,1)} %get-tuple-element.176.x_ref, ...), custom_call_target="tpu_custom_call" | custom-call | flops 6000000000 | bytes 20000000 | tf_op jit(solution)/shard_map/attend_back/pallas_call | solution.py:341
  136.0 11.0 %weight_grads.1 = (bf16[2,512,384]{2,1,0:T(8,128)(2,1)}, bf16[4,2,2,48,384]{4,3,2,1,0:T(8,128)(2,1)}, bf16[4,2,2,48,384]{4,3,2,1,0:T(8,128)(2,1)S(1)}, f32[1024,512]{1,0:T(8,128)}, bf16[1024,512]{1,0:T(8,128)(2,1)}) custom-call(s32[8]{0:T(128)S(1)} %fusion.6.sc, bf16[2048,512]{1,0:T(8,128)(2,1)} %get-tuple-element.168.x_ref, ...), custom_call_target="tpu_custom_call" | custom-call | flops 2700000000 | bytes 9000000 | tf_op jit(solution)/shard_map/weight_grads/pallas_call | solution.py:1034
  147.0 2.0 collective-permute-done.29.b_ref
  155.1 2.5 %collective-permute-start.33 = (bf16[2,64,640]{2,1,0:T(8,128)(2,1)S(1)}, bf16[2,64,640]{2,1,0:T(8,128)(2,1)S(1)}, u32[]{:S(2)}, u32[]{:S(2)}) collective-permute-start(bf16[2,64,640]{2,1,0:T(8,128)(2,1)S(1)} %get-tuple-element.229), channel_id=1, source_target_pairs={{0,16},{1,17},{2,18},{3,19},{4,20},{5,21},{6,22},{7,23},{8,24},{9,... | collective-permute-start | bytes 491528 | tf_op jit(solution)/shard_map/ppermute | solution.py:44
  157.6 4.6 %input_grads.1 = (bf16[112,256]{1,0:T(8,128)(2,1)S(1)}, bf16[112,256]{1,0:T(8,128)(2,1)S(1)}, bf16[112,256]{1,0:T(8,128)(2,1)S(1)}, bf16[112,256]{1,0:T(8,128)(2,1)S(1)}, bf16[512,128]{1,0:T(8,128)(2,1)S(1)}) custom-call(s32[8]{0:T(128)S(1)} %fusion.6.sc, f32[1]{0:T(128)} %bitcast.ratio, f32[1024,512]{1,0:T(8,128)} %get-tuple-element.230.dr_ref, ...), custom_call_target="tpu_custom_call" | custom-call | flops 1800000000 | bytes 6000000 | tf_op jit(solution)/shard_map/input_grads/pallas_call | solution.py:1124
  162.9 2.3 %collective-permute-done.33.b_ref = bf16[2,64,640]{2,1,0:T(8,128)(2,1)S(1)} collective-permute-done((bf16[2,64,640]{2,1,0:T(8,128)(2,1)S(1)}, bf16[2,64,640]{2,1,0:T(8,128)(2,1)S(1)}, u32[]{:S(2)}, u32[]{:S(2)}) %collective-permute-start.33) | collective-permute-done | bytes 163872 | tf_op jit(solution)/shard_map/ppermute | solution.py:44
  170.7 3.3 %collective-permute-done.35.refs_5_ = bf16[64,640]{1,0:T(8,128)(2,1)S(1)} collective-permute-done((bf16[64,640]{1,0:T(8,128)(2,1)S(1)}, bf16[64,640]{1,0:T(8,128)(2,1)S(1)}, u32[]{:S(2)}, u32[]{:S(2)}) %collective-permute-start.35) | collective-permute-done | bytes 81952 | tf_op jit(solution)/shard_map/ppermute | solution.py:44
  176.1 1.9 collective-permute-start.41
  180.6 5.3 %collective-permute-done.41.refs_2_ = bf16[128,384]{1,0:T(8,128)(2,1)S(1)} collective-permute-done((bf16[128,384]{1,0:T(8,128)(2,1)S(1)}, bf16[128,384]{1,0:T(8,128)(2,1)S(1)}, u32[]{:S(2)}, u32[]{:S(2)}) %collective-permute-start.41) | collective-permute-done | bytes 98336 | tf_op jit(solution)/shard_map/ppermute | solution.py:44
  192.4 2.4 %collective-permute-done.46 = f32[8,128]{1,0:T(8,128)S(1)} collective-permute-done((f32[8,128]{1,0:T(8,128)S(1)}, f32[8,128]{1,0:T(8,128)S(1)}, u32[]{:S(2)}, u32[]{:S(2)}) %collective-permute-start.46) | collective-permute-done | bytes 4128 | tf_op jit(solution)/shard_map/ppermute | solution.py:44
  197.3 1.9 collective-permute-start.49
  (156 shorter events, 59.2 us)
Async XLA Ops:
  15.7 11.5 %collective-permute-start.3 = (bf16[528,384]{1,0:T(8,128)(2,1)S(1)}, bf16[528,384]{1,0:T(8,128)(2,1)S(1)}, u32[]{:S(2)}, u32[]{:S(2)}) collective-permute-start(bf16[528,384]{1,0:T(8,128)(2,1)S(1)} %get-tuple-element.158), channel_id=1, source_target_pairs={{0,2},{1,3},{2,0},{3,1},{4,6},{5,7},{6,4},{7,5},{8,10},{9,11},{10,... | collective-permute-start | bytes 1216520 | tf_op jit(solution)/shard_map/ppermute | solution.py:44
  17.3 12.3 %collective-permute-start.4 = (bf16[528,384]{1,0:T(8,128)(2,1)S(1)}, bf16[528,384]{1,0:T(8,128)(2,1)S(1)}, u32[]{:S(2)}, u32[]{:S(2)}) collective-permute-start(bf16[528,384]{1,0:T(8,128)(2,1)S(1)} %get-tuple-element.159), channel_id=1, source_target_pairs={{0,4},{1,5},{2,6},{3,7},{4,0},{5,1},{6,2},{7,3},{8,12},{9,13},{10,... | collective-permute-start | bytes 1216520 | tf_op jit(solution)/shard_map/ppermute | solution.py:44
  18.7 15.9 %collective-permute-start.5 = (bf16[528,384]{1,0:T(8,128)(2,1)S(1)}, bf16[528,384]{1,0:T(8,128)(2,1)S(1)}, u32[]{:S(2)}, u32[]{:S(2)}) collective-permute-start(bf16[528,384]{1,0:T(8,128)(2,1)S(1)} %get-tuple-element.160), channel_id=1, source_target_pairs={{0,6},{1,7},{2,4},{3,5},{4,2},{5,3},{6,0},{7,1},{8,14},{9,15},{10,... | collective-permute-start | bytes 1216520 | tf_op jit(solution)/shard_map/ppermute | solution.py:44
  19.2 16.8 %collective-permute-start.6 = (bf16[528,384]{1,0:T(8,128)(2,1)S(1)}, bf16[528,384]{1,0:T(8,128)(2,1)S(1)}, u32[]{:S(2)}, u32[]{:S(2)}) collective-permute-start(bf16[528,384]{1,0:T(8,128)(2,1)S(1)} %get-tuple-element.157.t0), channel_id=1, source_target_pairs={{0,1},{1,0},{2,3},{3,2},{4,5},{5,4},{6,7},{7,6},{8,9},{9,8},{10,11... | collective-permute-start | bytes 1216520 | tf_op jit(solution)/shard_map/ppermute | solution.py:44
  27.1 12.4 %collective-permute-start.7 = (bf16[528,384]{1,0:T(8,128)(2,1)S(1)}, bf16[528,384]{1,0:T(8,128)(2,1)S(1)}, u32[]{:S(2)}, u32[]{:S(2)}) collective-permute-start(bf16[528,384]{1,0:T(8,128)(2,1)S(1)} %collective-permute-done.3.t1), channel_id=1, source_target_pairs={{0,1},{1,0},{2,3},{3,2},{4,5},{5,4},{6,7},{7,6},{8,9},{9,8},{10,11... | collective-permute-start | bytes 1216520 | tf_op jit(solution)/shard_map/ppermute | solution.py:44
  29.6 11.5 %collective-permute-start.8 = (bf16[528,384]{1,0:T(8,128)(2,1)S(1)}, bf16[528,384]{1,0:T(8,128)(2,1)S(1)}, u32[]{:S(2)}, u32[]{:S(2)}) collective-permute-start(bf16[528,384]{1,0:T(8,128)(2,1)S(1)} %collective-permute-done.4.t2), channel_id=1, source_target_pairs={{0,1},{1,0},{2,3},{3,2},{4,5},{5,4},{6,7},{7,6},{8,9},{9,8},{10,11... | collective-permute-start | bytes 1216520 | tf_op jit(solution)/shard_map/ppermute | solution.py:44
  36.1 9.9 %collective-permute-start.10 = (bf16[64,640]{1,0:T(8,128)(2,1)}, bf16[64,640]{1,0:T(8,128)(2,1)S(1)}, u32[]{:S(2)}, u32[]{:S(2)}) collective-permute-start(bf16[64,640]{1,0:T(8,128)(2,1)} %get-tuple-element.171.refs_0_), channel_id=1, source_target_pairs={{0,8},{1,9},{2,10},{3,11},{4,12},{5,13},{6,14},{7,15},{8,0},{9,1},... | collective-permute-start | bytes 245768 | tf_op jit(solution)/shard_map/ppermute | solution.py:44
  38.6 9.8 %collective-permute-start.11 = (bf16[64,640]{1,0:T(8,128)(2,1)}, bf16[64,640]{1,0:T(8,128)(2,1)S(1)}, u32[]{:S(2)}, u32[]{:S(2)}) collective-permute-start(bf16[64,640]{1,0:T(8,128)(2,1)} %get-tuple-element.171.refs_0_), channel_id=1, source_target_pairs={{0,16},{1,17},{2,18},{3,19},{4,20},{5,21},{6,22},{7,23},{8,24},{9,... | collective-permute-start | bytes 245768 | tf_op jit(solution)/shard_map/ppermute | solution.py:44
  42.9 14.8 %collective-permute-start.13 = (bf16[256,512]{1,0:T(8,128)(2,1)S(1)}, bf16[256,512]{1,0:T(8,128)(2,1)S(1)}, u32[]{:S(2)}, u32[]{:S(2)}) collective-permute-start(bf16[256,512]{1,0:T(8,128)(2,1)S(1)} %get-tuple-element.312), channel_id=1, source_target_pairs={{0,2},{1,3},{2,0},{3,1},{4,6},{5,7},{6,4},{7,5},{8,10},{9,11},{10,... | collective-permute-start | bytes 786440 | tf_op jit(solution)/shard_map/ppermute | solution.py:44
  44.5 13.3 %collective-permute-start.14 = (bf16[256,512]{1,0:T(8,128)(2,1)S(1)}, bf16[256,512]{1,0:T(8,128)(2,1)S(1)}, u32[]{:S(2)}, u32[]{:S(2)}) collective-permute-start(bf16[256,512]{1,0:T(8,128)(2,1)S(1)} %get-tuple-element.311), channel_id=1, source_target_pairs={{0,4},{1,5},{2,6},{3,7},{4,0},{5,1},{6,2},{7,3},{8,12},{9,13},{10,... | collective-permute-start | bytes 786440 | tf_op jit(solution)/shard_map/ppermute | solution.py:44
  46.0 11.9 %collective-permute-start.15 = (bf16[256,512]{1,0:T(8,128)(2,1)S(1)}, bf16[256,512]{1,0:T(8,128)(2,1)S(1)}, u32[]{:S(2)}, u32[]{:S(2)}) collective-permute-start(bf16[256,512]{1,0:T(8,128)(2,1)S(1)} %get-tuple-element.310), channel_id=1, source_target_pairs={{0,6},{1,7},{2,4},{3,5},{4,2},{5,3},{6,0},{7,1},{8,14},{9,15},{10,... | collective-permute-start | bytes 786440 | tf_op jit(solution)/shard_map/ppermute | solution.py:44
  57.9 12.8 %collective-permute-start.16 = (bf16[4,64,640]{2,1,0:T(8,128)(2,1)S(1)}, bf16[4,64,640]{2,1,0:T(8,128)(2,1)S(1)}, u32[]{:S(2)}, u32[]{:S(2)}) collective-permute-start(bf16[4,64,640]{2,1,0:T(8,128)(2,1)S(1)} %stack_rest.1.refs_0_), channel_id=1, source_target_pairs={{0,2},{1,3},{2,0},{3,1},{4,6},{5,7},{6,4},{7,5},{8,10},{9,11},{10,... | collective-permute-start | bytes 983048 | tf_op jit(solution)/shard_map/ppermute | solution.py:44
  59.4 20.0 %collective-permute-start.18 = (bf16[4,64,640]{2,1,0:T(8,128)(2,1)S(1)}, bf16[4,64,640]{2,1,0:T(8,128)(2,1)S(1)}, u32[]{:S(2)}, u32[]{:S(2)}) collective-permute-start(bf16[4,64,640]{2,1,0:T(8,128)(2,1)S(1)} %stack_rest.1.refs_0_), channel_id=1, source_target_pairs={{0,4},{1,5},{2,6},{3,7},{4,0},{5,1},{6,2},{7,3},{8,12},{9,13},{10,... | collective-permute-start | bytes 983048 | tf_op jit(solution)/shard_map/ppermute | solution.py:44
  60.9 18.5 %collective-permute-start.19 = (bf16[4,64,640]{2,1,0:T(8,128)(2,1)S(1)}, bf16[4,64,640]{2,1,0:T(8,128)(2,1)S(1)}, u32[]{:S(2)}, u32[]{:S(2)}) collective-permute-start(bf16[4,64,640]{2,1,0:T(8,128)(2,1)S(1)} %stack_rest.1.refs_0_), channel_id=1, source_target_pairs={{0,6},{1,7},{2,4},{3,5},{4,2},{5,3},{6,0},{7,1},{8,14},{9,15},{10,... | collective-permute-start | bytes 983048 | tf_op jit(solution)/shard_map/ppermute | solution.py:44
  61.4 18.7 %collective-permute-start.20 = (bf16[4,64,640]{2,1,0:T(8,128)(2,1)S(1)}, bf16[4,64,640]{2,1,0:T(8,128)(2,1)S(1)}, u32[]{:S(2)}, u32[]{:S(2)}) collective-permute-start(bf16[4,64,640]{2,1,0:T(8,128)(2,1)S(1)} %stack_rest.1.refs_0_), channel_id=1, source_target_pairs={{0,1},{1,0},{2,3},{3,2},{4,5},{5,4},{6,7},{7,6},{8,9},{9,8},{10,11... | collective-permute-start | bytes 983048 | tf_op jit(solution)/shard_map/ppermute | solution.py:44
  70.2 12.7 %collective-permute-start.17 = (bf16[1024,256]{1,0:T(8,128)(2,1)}, bf16[1024,256]{1,0:T(8,128)(2,1)S(1)}, u32[]{:S(2)}, u32[]{:S(2)}) collective-permute-start(bf16[1024,256]{1,0:T(8,128)(2,1)} %get-tuple-element.178), channel_id=1, source_target_pairs={{0,1},{1,0},{2,3},{3,2},{4,5},{5,4},{6,7},{7,6},{8,9},{9,8},{10,11... | collective-permute-start | bytes 1572872 | tf_op jit(solution)/shard_map/ppermute | solution.py:44
  106.4 29.3 %collective-permute-start.25 = (bf16[464,640]{1,0:T(8,128)(2,1)S(1)}, bf16[464,640]{1,0:T(8,128)(2,1)S(1)}, u32[]{:S(2)}, u32[]{:S(2)}) collective-permute-start(bf16[464,640]{1,0:T(8,128)(2,1)S(1)} %get-tuple-element.197), channel_id=1, source_target_pairs={{0,2},{1,3},{2,0},{3,1},{4,6},{5,7},{6,4},{7,5},{8,10},{9,11},{10,... | collective-permute-start | bytes 1781768 | tf_op jit(solution)/shard_map/ppermute | solution.py:44
  108.0 27.7 %collective-permute-start.26 = (bf16[464,640]{1,0:T(8,128)(2,1)S(1)}, bf16[464,640]{1,0:T(8,128)(2,1)S(1)}, u32[]{:S(2)}, u32[]{:S(2)}) collective-permute-start(bf16[464,640]{1,0:T(8,128)(2,1)S(1)} %get-tuple-element.198), channel_id=1, source_target_pairs={{0,4},{1,5},{2,6},{3,7},{4,0},{5,1},{6,2},{7,3},{8,12},{9,13},{10,... | collective-permute-start | bytes 1781768 | tf_op jit(solution)/shard_map/ppermute | solution.py:44
  109.4 26.6 %collective-permute-start.27 = (bf16[464,640]{1,0:T(8,128)(2,1)S(1)}, bf16[464,640]{1,0:T(8,128)(2,1)S(1)}, u32[]{:S(2)}, u32[]{:S(2)}) collective-permute-start(bf16[464,640]{1,0:T(8,128)(2,1)S(1)} %get-tuple-element.199), channel_id=1, source_target_pairs={{0,6},{1,7},{2,4},{3,5},{4,2},{5,3},{6,0},{7,1},{8,14},{9,15},{10,... | collective-permute-start | bytes 1781768 | tf_op jit(solution)/shard_map/ppermute | solution.py:44
  150.8 18.0 %collective-permute-start.30 = (bf16[4,112,384]{2,1,0:T(8,128)(2,1)S(1)}, bf16[4,112,384]{2,1,0:T(8,128)(2,1)S(1)}, u32[]{:S(2)}, u32[]{:S(2)}) collective-permute-start(bf16[4,112,384]{2,1,0:T(8,128)(2,1)S(1)} %get-tuple-element.217), channel_id=1, source_target_pairs={{0,2},{1,3},{2,0},{3,1},{4,6},{5,7},{6,4},{7,5},{8,10},{9,11},{10,... | collective-permute-start | bytes 1032200 | tf_op jit(solution)/shard_map/ppermute | solution.py:44
  152.4 17.0 %collective-permute-start.31 = (bf16[4,112,384]{2,1,0:T(8,128)(2,1)S(1)}, bf16[4,112,384]{2,1,0:T(8,128)(2,1)S(1)}, u32[]{:S(2)}, u32[]{:S(2)}) collective-permute-start(bf16[4,112,384]{2,1,0:T(8,128)(2,1)S(1)} %get-tuple-element.218), channel_id=1, source_target_pairs={{0,4},{1,5},{2,6},{3,7},{4,0},{5,1},{6,2},{7,3},{8,12},{9,13},{10,... | collective-permute-start | bytes 1032200 | tf_op jit(solution)/shard_map/ppermute | solution.py:44
  153.9 16.8 %collective-permute-start.32 = (bf16[4,112,384]{2,1,0:T(8,128)(2,1)S(1)}, bf16[4,112,384]{2,1,0:T(8,128)(2,1)S(1)}, u32[]{:S(2)}, u32[]{:S(2)}) collective-permute-start(bf16[4,112,384]{2,1,0:T(8,128)(2,1)S(1)} %get-tuple-element.219), channel_id=1, source_target_pairs={{0,6},{1,7},{2,4},{3,5},{4,2},{5,3},{6,0},{7,1},{8,14},{9,15},{10,... | collective-permute-start | bytes 1032200 | tf_op jit(solution)/shard_map/ppermute | solution.py:44
  155.1 10.1 %collective-permute-start.33 = (bf16[2,64,640]{2,1,0:T(8,128)(2,1)S(1)}, bf16[2,64,640]{2,1,0:T(8,128)(2,1)S(1)}, u32[]{:S(2)}, u32[]{:S(2)}) collective-permute-start(bf16[2,64,640]{2,1,0:T(8,128)(2,1)S(1)} %get-tuple-element.229), channel_id=1, source_target_pairs={{0,16},{1,17},{2,18},{3,19},{4,20},{5,21},{6,22},{7,23},{8,24},{9,... | collective-permute-start | bytes 491528 | tf_op jit(solution)/shard_map/ppermute | solution.py:44
  176.1 9.8 %collective-permute-start.41 = (bf16[128,384]{1,0:T(8,128)(2,1)S(1)}, bf16[128,384]{1,0:T(8,128)(2,1)S(1)}, u32[]{:S(2)}, u32[]{:S(2)}) collective-permute-start(bf16[128,384]{1,0:T(8,128)(2,1)S(1)} %get-tuple-element.257), channel_id=1, source_target_pairs={{0,16},{1,17},{2,18},{3,19},{4,20},{5,21},{6,22},{7,23},{8,24},{9,... | collective-permute-start | bytes 294920 | tf_op jit(solution)/shard_map/ppermute | solution.py:44
  (48 other events, 336.1 us)

commit v6 on v5

--- a/solution.py
+++ b/solution.py
@@ -281,7 +281,7 @@
 
 
 BACK_BLOCK = 256
-BACK_CHUNK = 1024
+BACK_CHUNK = 2048
 
 
 def attend_back_body(q_ref, k_ref, x_ref, kt_ref, v_ref, qa_ref, qb_ref, da_ref, db_ref, ea_ref, eb_ref, dq_ref, dk_ref, dv_ref, *scratch):
@@ -370,30 +370,30 @@
     )
 
 
-erfc_terms = (
-    -1.26551223,
-    1.00002368,
-    0.37409196,
-    0.09678418,
-    -0.18628806,
-    0.27886807,
-    -1.13520398,
-    1.48851587,
-    -0.82215223,
-    0.17087277,
+tail_slope = 0.32
+tail_terms = (
+    0.1276615327396569,
+    0.12766067896437439,
+    0.1146273959793329,
+    0.0877866398778977,
+    0.058846245380943685,
+    -0.009886160894676655,
+    0.0661375104847692,
+    -0.14747037514007924,
+    0.09579928012384316,
+    -0.02116276404130493,
 )
 
 
 def gelu_pair(t):
-    z = jnp.abs(t) * (0.5**0.5)
-    k = 1.0 / (1.0 + 0.5 * z)
-    series = jnp.full_like(t, erfc_terms[-1])
-    for term in erfc_terms[-2::-1]:
+    bell = jnp.exp2(t * t * (-0.5 * base_two))
+    k = 1.0 / (1.0 + tail_slope * jnp.abs(t))
+    series = jnp.full_like(t, tail_terms[-1])
+    for term in tail_terms[-2::-1]:
         series = series * k + term
-    tail = 0.5 * k * jnp.exp(series - z * z)
+    tail = series * k * bell
     cumulative = jnp.where(t >= 0.0, 1.0 - tail, tail)
-    density = jnp.exp(-0.5 * t * t) * 0.3989422804014327
-    return t * cumulative, cumulative + t * density
+    return t * cumulative, cumulative + t * (bell * 0.3989422804014327)
 
 
 def middle_body(

time: 205 us -> 204 us (level)
  no operation moved by 1% of the time
where the time goes in v6:
time: 204 us
  Pallas kernels  98.9 us (48%)
  waiting for transfers between devices  52 us (25%)
  starting transfers between devices  48.5 us (24%)
  between operations  2.07 us (1%)
    ppermute x50, waiting for transfers between devices, swap(): return lax.ppermute(value, AXES, pairs)  52 us
    ppermute x50, starting transfers between devices, swap(): return lax.ppermute(value, AXES, pairs)  48.5 us
    pallas_call x1, Pallas kernels, attend_back(): pl.pallas_call(attend_back_body, grid=(2, 2), in_specs=[pl.BlockSpec((1,...  25.2 us
    pallas_call x1, Pallas kernels, middle(): pl.pallas_call(middle_body, grid_spec=pltpu.PrefetchScalarGridSpec(num_sc...  18.5 us
    pallas_call x2, Pallas kernels, attend(): pl.pallas_call(attend_body, grid=(2,), in_specs=[pl.BlockSpec((1, SLOTS,...  17.5 us
    pallas_call x17, Pallas kernels, simple(): pl.pallas_call(body, in_specs=specs, out_specs=[whole()] * len(out_shape)...  13.6 us
    pallas_call x1, Pallas kernels, weight_grads(): pl.pallas_call(functools.partial(weight_body, n_ep, strip), grid=(4,), in...  11 us
    pallas_call x1, Pallas kernels, project(): pl.pallas_call(project_body, grid=(4,), in_specs=[pl.BlockSpec(memory_spa...  8.34 us
  transfers between devices with their start and end apart: 50, of which 24 were waited for; matrix products, arithmetic and copies ran while one was open for 1% of the time, Pallas kernels for 32%

profile of v6, /device:TPU:0, one launch (start us, length us, event | category | flops | bytes accessed | tf_op | source)
XLA Modules:
  0.0 203.7 jit_solution(12631898135507374847)
XLA Ops:
  2.4 3.0 %collective-permute-start = (bf16[112,384]{1,0:T(8,128)(2,1)S(1)}, bf16[112,384]{1,0:T(8,128)(2,1)S(1)}, u32[]{:S(2)}, u32[]{:S(2)}) collective-permute-start(bf16[112,384]{1,0:T(8,128)(2,1)S(1)} %get-tuple-element.155.refs_0_), channel_id=1, source_target_pairs={{0,8},{1,9},{2,10},{3,11},{4,12},{5,13},{6,14},{7,15},{8,0},{9,1},... | collective-permute-start | bytes 258056 | tf_op jit(solution)/shard_map/ppermute | solution.py:44
  5.5 2.6 %collective-permute-start.1 = (bf16[112,384]{1,0:T(8,128)(2,1)S(1)}, bf16[112,384]{1,0:T(8,128)(2,1)S(1)}, u32[]{:S(2)}, u32[]{:S(2)}) collective-permute-start(bf16[112,384]{1,0:T(8,128)(2,1)S(1)} %get-tuple-element.155.refs_0_), channel_id=1, source_target_pairs={{0,16},{1,17},{2,18},{3,19},{4,20},{5,21},{6,22},{7,23},{8,24},{9,... | collective-permute-start | bytes 258056 | tf_op jit(solution)/shard_map/ppermute | solution.py:44
  8.4 6.6 %collective-permute-done.1.refs_2_ = bf16[112,384]{1,0:T(8,128)(2,1)S(1)} collective-permute-done((bf16[112,384]{1,0:T(8,128)(2,1)S(1)}, bf16[112,384]{1,0:T(8,128)(2,1)S(1)}, u32[]{:S(2)}, u32[]{:S(2)}) %collective-permute-start.1) | collective-permute-done | bytes 86048 | tf_op jit(solution)/shard_map/ppermute | solution.py:44
  19.2 7.9 %collective-permute-done.3.t1 = bf16[528,384]{1,0:T(8,128)(2,1)S(1)} collective-permute-done((bf16[528,384]{1,0:T(8,128)(2,1)S(1)}, bf16[528,384]{1,0:T(8,128)(2,1)S(1)}, u32[]{:S(2)}, u32[]{:S(2)}) %collective-permute-start.3) | collective-permute-done | bytes 405536 | tf_op jit(solution)/shard_map/ppermute | solution.py:44
  27.1 2.4 %collective-permute-done.4.t2 = bf16[528,384]{1,0:T(8,128)(2,1)S(1)} collective-permute-done((bf16[528,384]{1,0:T(8,128)(2,1)S(1)}, bf16[528,384]{1,0:T(8,128)(2,1)S(1)}, u32[]{:S(2)}, u32[]{:S(2)}) %collective-permute-start.4) | collective-permute-done | bytes 405536 | tf_op jit(solution)/shard_map/ppermute | solution.py:44
  29.6 5.1 %collective-permute-done.5.t3 = bf16[528,384]{1,0:T(8,128)(2,1)S(1)} collective-permute-done((bf16[528,384]{1,0:T(8,128)(2,1)S(1)}, bf16[528,384]{1,0:T(8,128)(2,1)S(1)}, u32[]{:S(2)}, u32[]{:S(2)}) %collective-permute-start.5) | collective-permute-done | bytes 405536 | tf_op jit(solution)/shard_map/ppermute | solution.py:44
  36.1 2.5 %collective-permute-start.10 = (bf16[64,640]{1,0:T(8,128)(2,1)}, bf16[64,640]{1,0:T(8,128)(2,1)S(1)}, u32[]{:S(2)}, u32[]{:S(2)}) collective-permute-start(bf16[64,640]{1,0:T(8,128)(2,1)} %get-tuple-element.171.refs_0_), channel_id=1, source_target_pairs={{0,8},{1,9},{2,10},{3,11},{4,12},{5,13},{6,14},{7,15},{8,0},{9,1},... | collective-permute-start | bytes 245768 | tf_op jit(solution)/shard_map/ppermute | solution.py:44
  46.4 2.0 collective-permute-done.11.refs_2_
  49.4 8.3 %project.1 = (bf16[2048,512]{1,0:T(8,128)(2,1)}, bf16[2,2048,128]{2,1,0:T(8,128)(2,1)}, bf16[2,2048,128]{2,1,0:T(8,128)(2,1)}, bf16[2,128,2048]{2,1,0:T(8,128)(2...) custom-call(f32[1]{0:T(128)} %bitcast.ratio, s32[8]{0:T(128)S(1)} %fusion.6.sc, ...), custom_call_target="tpu_custom_call" | custom-call | flops 2700000000 | bytes 9000000 | tf_op jit(solution)/shard_map/project/pallas_call | solution.py:166
  61.4 8.8 %attend.2 = (bf16[1024,256]{1,0:T(8,128)(2,1)}, bf16[2,1024,128]{2,1,0:T(8,128)(2,1)}) custom-call(bf16[2,2048,128]{2,1,0:T(8,128)(2,1)} %get-tuple-element.200.q_ref, bf16[2,2048,128]{2,1,0:T(8,128)(2,1)} %get-tuple-element.175.k_ref, bf16[2,2048,128]{2,1,0:T(8,128)(2,1)} %get-tuple-element.176.x_ref, bf16[2,128,2048]{2,1,0:T(8,128)(2,1)} %get-tuple-element.177.vt_ref), custom_call_target="tpu_custom_call" | custom-call | flops 1800000000 | bytes 6000000 | tf_op jit(solution)/shard_map/attend/pallas_call | solution.py:262
  70.7 8.8 %attend.3 = (bf16[1024,256]{1,0:T(8,128)(2,1)}, bf16[2,1024,128]{2,1,0:T(8,128)(2,1)}) custom-call(bf16[2,2048,128]{2,1,0:T(8,128)(2,1)} %get-tuple-element.200.q_ref, bf16[2,2048,128]{2,1,0:T(8,128)(2,1)} %get-tuple-element.175.k_ref, bf16[2,2048,128]{2,1,0:T(8,128)(2,1)} %get-tuple-element.176.x_ref, bf16[2,128,2048]{2,1,0:T(8,128)(2,1)} %get-tuple-element.177.vt_ref), custom_call_target="tpu_custom_call" | custom-call | flops 1800000000 | bytes 6000000 | tf_op jit(solution)/shard_map/attend/pallas_call | solution.py:262
  82.9 18.5 %middle.1 = (bf16[256,512]{1,0:T(8,128)(2,1)S(1)}, bf16[256,512]{1,0:T(8,128)(2,1)S(1)}, bf16[256,512]{1,0:T(8,128)(2,1)S(1)}, bf16[256,512]{1,0:T(8,128)(2,1)S(...) custom-call(s32[8]{0:T(128)S(1)} %fusion.6.sc, ...), custom_call_target="tpu_custom_call" | custom-call | flops 7500000256 | bytes 25000000 | tf_op jit(solution)/shard_map/middle/pallas_call | solution.py:556
  101.6 2.9 %collective-permute-done.24 = bf16[2,512,640]{2,1,0:T(8,128)(2,1)S(1)} collective-permute-done((bf16[2,512,640]{2,1,0:T(8,128)(2,1)S(1)}, bf16[2,512,640]{2,1,0:T(8,128)(2,1)S(1)}, u32[]{:S(2)}, u32[]{:S(2)}) %collective-permute-start.24) | collective-permute-done | bytes 1310752 | tf_op jit(solution)/shard_map/ppermute | solution.py:44
  109.2 25.2 %attend_back.1 = (bf16[2048,256]{1,0:T(8,128)(2,1)}, f32[2,128,2048]{2,1,0:T(8,128)}, f32[2,128,2048]{2,1,0:T(8,128)}) custom-call(bf16[2,2048,128]{2,1,0:T(8,128)(2,1)} %get-tuple-element.200.q_ref, bf16[2,2048,128]{2,1,0:T(8,128)(2,1)} %get-tuple-element.175.k_ref, bf16[2,2048,128]{2,1,0:T(8,128)(2,1)} %get-tuple-element.176.x_ref, ...), custom_call_target="tpu_custom_call" | custom-call | flops 6000000000 | bytes 20000000 | tf_op jit(solution)/shard_map/attend_back/pallas_call | solution.py:341
  135.3 11.0 %weight_grads.1 = (bf16[2,512,384]{2,1,0:T(8,128)(2,1)}, bf16[4,2,2,48,384]{4,3,2,1,0:T(8,128)(2,1)}, bf16[4,2,2,48,384]{4,3,2,1,0:T(8,128)(2,1)S(1)}, f32[1024,512]{1,0:T(8,128)}, bf16[1024,512]{1,0:T(8,128)(2,1)}) custom-call(s32[8]{0:T(128)S(1)} %fusion.6.sc, bf16[2048,512]{1,0:T(8,128)(2,1)} %get-tuple-element.168.x_ref, ...), custom_call_target="tpu_custom_call" | custom-call | flops 2700000000 | bytes 9000000 | tf_op jit(solution)/shard_map/weight_grads/pallas_call | solution.py:1034
  146.2 2.0 collective-permute-done.29.b_ref
  154.3 2.5 %collective-permute-start.33 = (bf16[2,64,640]{2,1,0:T(8,128)(2,1)S(1)}, bf16[2,64,640]{2,1,0:T(8,128)(2,1)S(1)}, u32[]{:S(2)}, u32[]{:S(2)}) collective-permute-start(bf16[2,64,640]{2,1,0:T(8,128)(2,1)S(1)} %get-tuple-element.229), channel_id=1, source_target_pairs={{0,16},{1,17},{2,18},{3,19},{4,20},{5,21},{6,22},{7,23},{8,24},{9,... | collective-permute-start | bytes 491528 | tf_op jit(solution)/shard_map/ppermute | solution.py:44
  156.9 4.6 %input_grads.1 = (bf16[112,256]{1,0:T(8,128)(2,1)S(1)}, bf16[112,256]{1,0:T(8,128)(2,1)S(1)}, bf16[112,256]{1,0:T(8,128)(2,1)S(1)}, bf16[112,256]{1,0:T(8,128)(2,1)S(1)}, bf16[512,128]{1,0:T(8,128)(2,1)S(1)}) custom-call(s32[8]{0:T(128)S(1)} %fusion.6.sc, f32[1]{0:T(128)} %bitcast.ratio, f32[1024,512]{1,0:T(8,128)} %get-tuple-element.230.dr_ref, ...), custom_call_target="tpu_custom_call" | custom-call | flops 1800000000 | bytes 6000000 | tf_op jit(solution)/shard_map/input_grads/pallas_call | solution.py:1124
  162.1 2.3 %collective-permute-done.33.b_ref = bf16[2,64,640]{2,1,0:T(8,128)(2,1)S(1)} collective-permute-done((bf16[2,64,640]{2,1,0:T(8,128)(2,1)S(1)}, bf16[2,64,640]{2,1,0:T(8,128)(2,1)S(1)}, u32[]{:S(2)}, u32[]{:S(2)}) %collective-permute-start.33) | collective-permute-done | bytes 163872 | tf_op jit(solution)/shard_map/ppermute | solution.py:44
  169.9 3.3 %collective-permute-done.35.refs_5_ = bf16[64,640]{1,0:T(8,128)(2,1)S(1)} collective-permute-done((bf16[64,640]{1,0:T(8,128)(2,1)S(1)}, bf16[64,640]{1,0:T(8,128)(2,1)S(1)}, u32[]{:S(2)}, u32[]{:S(2)}) %collective-permute-start.35) | collective-permute-done | bytes 81952 | tf_op jit(solution)/shard_map/ppermute | solution.py:44
  175.3 1.9 collective-permute-start.41
  179.8 5.3 %collective-permute-done.41.refs_2_ = bf16[128,384]{1,0:T(8,128)(2,1)S(1)} collective-permute-done((bf16[128,384]{1,0:T(8,128)(2,1)S(1)}, bf16[128,384]{1,0:T(8,128)(2,1)S(1)}, u32[]{:S(2)}, u32[]{:S(2)}) %collective-permute-start.41) | collective-permute-done | bytes 98336 | tf_op jit(solution)/shard_map/ppermute | solution.py:44
  191.6 2.4 %collective-permute-done.46 = f32[8,128]{1,0:T(8,128)S(1)} collective-permute-done((f32[8,128]{1,0:T(8,128)S(1)}, f32[8,128]{1,0:T(8,128)S(1)}, u32[]{:S(2)}, u32[]{:S(2)}) %collective-permute-start.46) | collective-permute-done | bytes 4128 | tf_op jit(solution)/shard_map/ppermute | solution.py:44
  196.5 1.9 collective-permute-start.49
  (156 shorter events, 59.7 us)
Async XLA Ops:
  15.7 11.5 %collective-permute-start.3 = (bf16[528,384]{1,0:T(8,128)(2,1)S(1)}, bf16[528,384]{1,0:T(8,128)(2,1)S(1)}, u32[]{:S(2)}, u32[]{:S(2)}) collective-permute-start(bf16[528,384]{1,0:T(8,128)(2,1)S(1)} %get-tuple-element.158), channel_id=1, source_target_pairs={{0,2},{1,3},{2,0},{3,1},{4,6},{5,7},{6,4},{7,5},{8,10},{9,11},{10,... | collective-permute-start | bytes 1216520 | tf_op jit(solution)/shard_map/ppermute | solution.py:44
  17.3 12.3 %collective-permute-start.4 = (bf16[528,384]{1,0:T(8,128)(2,1)S(1)}, bf16[528,384]{1,0:T(8,128)(2,1)S(1)}, u32[]{:S(2)}, u32[]{:S(2)}) collective-permute-start(bf16[528,384]{1,0:T(8,128)(2,1)S(1)} %get-tuple-element.159), channel_id=1, source_target_pairs={{0,4},{1,5},{2,6},{3,7},{4,0},{5,1},{6,2},{7,3},{8,12},{9,13},{10,... | collective-permute-start | bytes 1216520 | tf_op jit(solution)/shard_map/ppermute | solution.py:44
  18.7 15.9 %collective-permute-start.5 = (bf16[528,384]{1,0:T(8,128)(2,1)S(1)}, bf16[528,384]{1,0:T(8,128)(2,1)S(1)}, u32[]{:S(2)}, u32[]{:S(2)}) collective-permute-start(bf16[528,384]{1,0:T(8,128)(2,1)S(1)} %get-tuple-element.160), channel_id=1, source_target_pairs={{0,6},{1,7},{2,4},{3,5},{4,2},{5,3},{6,0},{7,1},{8,14},{9,15},{10,... | collective-permute-start | bytes 1216520 | tf_op jit(solution)/shard_map/ppermute | solution.py:44
  19.2 16.8 %collective-permute-start.6 = (bf16[528,384]{1,0:T(8,128)(2,1)S(1)}, bf16[528,384]{1,0:T(8,128)(2,1)S(1)}, u32[]{:S(2)}, u32[]{:S(2)}) collective-permute-start(bf16[528,384]{1,0:T(8,128)(2,1)S(1)} %get-tuple-element.157.t0), channel_id=1, source_target_pairs={{0,1},{1,0},{2,3},{3,2},{4,5},{5,4},{6,7},{7,6},{8,9},{9,8},{10,11... | collective-permute-start | bytes 1216520 | tf_op jit(solution)/shard_map/ppermute | solution.py:44
  27.1 12.4 %collective-permute-start.7 = (bf16[528,384]{1,0:T(8,128)(2,1)S(1)}, bf16[528,384]{1,0:T(8,128)(2,1)S(1)}, u32[]{:S(2)}, u32[]{:S(2)}) collective-permute-start(bf16[528,384]{1,0:T(8,128)(2,1)S(1)} %collective-permute-done.3.t1), channel_id=1, source_target_pairs={{0,1},{1,0},{2,3},{3,2},{4,5},{5,4},{6,7},{7,6},{8,9},{9,8},{10,11... | collective-permute-start | bytes 1216520 | tf_op jit(solution)/shard_map/ppermute | solution.py:44
  29.6 11.5 %collective-permute-start.8 = (bf16[528,384]{1,0:T(8,128)(2,1)S(1)}, bf16[528,384]{1,0:T(8,128)(2,1)S(1)}, u32[]{:S(2)}, u32[]{:S(2)}) collective-permute-start(bf16[528,384]{1,0:T(8,128)(2,1)S(1)} %collective-permute-done.4.t2), channel_id=1, source_target_pairs={{0,1},{1,0},{2,3},{3,2},{4,5},{5,4},{6,7},{7,6},{8,9},{9,8},{10,11... | collective-permute-start | bytes 1216520 | tf_op jit(solution)/shard_map/ppermute | solution.py:44
  36.1 9.9 %collective-permute-start.10 = (bf16[64,640]{1,0:T(8,128)(2,1)}, bf16[64,640]{1,0:T(8,128)(2,1)S(1)}, u32[]{:S(2)}, u32[]{:S(2)}) collective-permute-start(bf16[64,640]{1,0:T(8,128)(2,1)} %get-tuple-element.171.refs_0_), channel_id=1, source_target_pairs={{0,8},{1,9},{2,10},{3,11},{4,12},{5,13},{6,14},{7,15},{8,0},{9,1},... | collective-permute-start | bytes 245768 | tf_op jit(solution)/shard_map/ppermute | solution.py:44
  38.6 9.8 %collective-permute-start.11 = (bf16[64,640]{1,0:T(8,128)(2,1)}, bf16[64,640]{1,0:T(8,128)(2,1)S(1)}, u32[]{:S(2)}, u32[]{:S(2)}) collective-permute-start(bf16[64,640]{1,0:T(8,128)(2,1)} %get-tuple-element.171.refs_0_), channel_id=1, source_target_pairs={{0,16},{1,17},{2,18},{3,19},{4,20},{5,21},{6,22},{7,23},{8,24},{9,... | collective-permute-start | bytes 245768 | tf_op jit(solution)/shard_map/ppermute | solution.py:44
  42.9 14.8 %collective-permute-start.13 = (bf16[256,512]{1,0:T(8,128)(2,1)S(1)}, bf16[256,512]{1,0:T(8,128)(2,1)S(1)}, u32[]{:S(2)}, u32[]{:S(2)}) collective-permute-start(bf16[256,512]{1,0:T(8,128)(2,1)S(1)} %get-tuple-element.312), channel_id=1, source_target_pairs={{0,2},{1,3},{2,0},{3,1},{4,6},{5,7},{6,4},{7,5},{8,10},{9,11},{10,... | collective-permute-start | bytes 786440 | tf_op jit(solution)/shard_map/ppermute | solution.py:44
  44.5 13.3 %collective-permute-start.14 = (bf16[256,512]{1,0:T(8,128)(2,1)S(1)}, bf16[256,512]{1,0:T(8,128)(2,1)S(1)}, u32[]{:S(2)}, u32[]{:S(2)}) collective-permute-start(bf16[256,512]{1,0:T(8,128)(2,1)S(1)} %get-tuple-element.311), channel_id=1, source_target_pairs={{0,4},{1,5},{2,6},{3,7},{4,0},{5,1},{6,2},{7,3},{8,12},{9,13},{10,... | collective-permute-start | bytes 786440 | tf_op jit(solution)/shard_map/ppermute | solution.py:44
  46.0 11.9 %collective-permute-start.15 = (bf16[256,512]{1,0:T(8,128)(2,1)S(1)}, bf16[256,512]{1,0:T(8,128)(2,1)S(1)}, u32[]{:S(2)}, u32[]{:S(2)}) collective-permute-start(bf16[256,512]{1,0:T(8,128)(2,1)S(1)} %get-tuple-element.310), channel_id=1, source_target_pairs={{0,6},{1,7},{2,4},{3,5},{4,2},{5,3},{6,0},{7,1},{8,14},{9,15},{10,... | collective-permute-start | bytes 786440 | tf_op jit(solution)/shard_map/ppermute | solution.py:44
  57.9 12.8 %collective-permute-start.16 = (bf16[4,64,640]{2,1,0:T(8,128)(2,1)S(1)}, bf16[4,64,640]{2,1,0:T(8,128)(2,1)S(1)}, u32[]{:S(2)}, u32[]{:S(2)}) collective-permute-start(bf16[4,64,640]{2,1,0:T(8,128)(2,1)S(1)} %stack_rest.1.refs_0_), channel_id=1, source_target_pairs={{0,2},{1,3},{2,0},{3,1},{4,6},{5,7},{6,4},{7,5},{8,10},{9,11},{10,... | collective-permute-start | bytes 983048 | tf_op jit(solution)/shard_map/ppermute | solution.py:44
  59.4 20.0 %collective-permute-start.18 = (bf16[4,64,640]{2,1,0:T(8,128)(2,1)S(1)}, bf16[4,64,640]{2,1,0:T(8,128)(2,1)S(1)}, u32[]{:S(2)}, u32[]{:S(2)}) collective-permute-start(bf16[4,64,640]{2,1,0:T(8,128)(2,1)S(1)} %stack_rest.1.refs_0_), channel_id=1, source_target_pairs={{0,4},{1,5},{2,6},{3,7},{4,0},{5,1},{6,2},{7,3},{8,12},{9,13},{10,... | collective-permute-start | bytes 983048 | tf_op jit(solution)/shard_map/ppermute | solution.py:44
  60.9 18.5 %collective-permute-start.19 = (bf16[4,64,640]{2,1,0:T(8,128)(2,1)S(1)}, bf16[4,64,640]{2,1,0:T(8,128)(2,1)S(1)}, u32[]{:S(2)}, u32[]{:S(2)}) collective-permute-start(bf16[4,64,640]{2,1,0:T(8,128)(2,1)S(1)} %stack_rest.1.refs_0_), channel_id=1, source_target_pairs={{0,6},{1,7},{2,4},{3,5},{4,2},{5,3},{6,0},{7,1},{8,14},{9,15},{10,... | collective-permute-start | bytes 983048 | tf_op jit(solution)/shard_map/ppermute | solution.py:44
  61.4 18.7 %collective-permute-start.20 = (bf16[4,64,640]{2,1,0:T(8,128)(2,1)S(1)}, bf16[4,64,640]{2,1,0:T(8,128)(2,1)S(1)}, u32[]{:S(2)}, u32[]{:S(2)}) collective-permute-start(bf16[4,64,640]{2,1,0:T(8,128)(2,1)S(1)} %stack_rest.1.refs_0_), channel_id=1, source_target_pairs={{0,1},{1,0},{2,3},{3,2},{4,5},{5,4},{6,7},{7,6},{8,9},{9,8},{10,11... | collective-permute-start | bytes 983048 | tf_op jit(solution)/shard_map/ppermute | solution.py:44
  70.2 12.7 %collective-permute-start.17 = (bf16[1024,256]{1,0:T(8,128)(2,1)}, bf16[1024,256]{1,0:T(8,128)(2,1)S(1)}, u32[]{:S(2)}, u32[]{:S(2)}) collective-permute-start(bf16[1024,256]{1,0:T(8,128)(2,1)} %get-tuple-element.178), channel_id=1, source_target_pairs={{0,1},{1,0},{2,3},{3,2},{4,5},{5,4},{6,7},{7,6},{8,9},{9,8},{10,11... | collective-permute-start | bytes 1572872 | tf_op jit(solution)/shard_map/ppermute | solution.py:44
  105.6 28.8 %collective-permute-start.25 = (bf16[464,640]{1,0:T(8,128)(2,1)S(1)}, bf16[464,640]{1,0:T(8,128)(2,1)S(1)}, u32[]{:S(2)}, u32[]{:S(2)}) collective-permute-start(bf16[464,640]{1,0:T(8,128)(2,1)S(1)} %get-tuple-element.197), channel_id=1, source_target_pairs={{0,2},{1,3},{2,0},{3,1},{4,6},{5,7},{6,4},{7,5},{8,10},{9,11},{10,... | collective-permute-start | bytes 1781768 | tf_op jit(solution)/shard_map/ppermute | solution.py:44
  107.2 27.2 %collective-permute-start.26 = (bf16[464,640]{1,0:T(8,128)(2,1)S(1)}, bf16[464,640]{1,0:T(8,128)(2,1)S(1)}, u32[]{:S(2)}, u32[]{:S(2)}) collective-permute-start(bf16[464,640]{1,0:T(8,128)(2,1)S(1)} %get-tuple-element.198), channel_id=1, source_target_pairs={{0,4},{1,5},{2,6},{3,7},{4,0},{5,1},{6,2},{7,3},{8,12},{9,13},{10,... | collective-permute-start | bytes 1781768 | tf_op jit(solution)/shard_map/ppermute | solution.py:44
  108.7 26.6 %collective-permute-start.27 = (bf16[464,640]{1,0:T(8,128)(2,1)S(1)}, bf16[464,640]{1,0:T(8,128)(2,1)S(1)}, u32[]{:S(2)}, u32[]{:S(2)}) collective-permute-start(bf16[464,640]{1,0:T(8,128)(2,1)S(1)} %get-tuple-element.199), channel_id=1, source_target_pairs={{0,6},{1,7},{2,4},{3,5},{4,2},{5,3},{6,0},{7,1},{8,14},{9,15},{10,... | collective-permute-start | bytes 1781768 | tf_op jit(solution)/shard_map/ppermute | solution.py:44
  150.0 18.1 %collective-permute-start.30 = (bf16[4,112,384]{2,1,0:T(8,128)(2,1)S(1)}, bf16[4,112,384]{2,1,0:T(8,128)(2,1)S(1)}, u32[]{:S(2)}, u32[]{:S(2)}) collective-permute-start(bf16[4,112,384]{2,1,0:T(8,128)(2,1)S(1)} %get-tuple-element.217), channel_id=1, source_target_pairs={{0,2},{1,3},{2,0},{3,1},{4,6},{5,7},{6,4},{7,5},{8,10},{9,11},{10,... | collective-permute-start | bytes 1032200 | tf_op jit(solution)/shard_map/ppermute | solution.py:44
  151.6 17.0 %collective-permute-start.31 = (bf16[4,112,384]{2,1,0:T(8,128)(2,1)S(1)}, bf16[4,112,384]{2,1,0:T(8,128)(2,1)S(1)}, u32[]{:S(2)}, u32[]{:S(2)}) collective-permute-start(bf16[4,112,384]{2,1,0:T(8,128)(2,1)S(1)} %get-tuple-element.218), channel_id=1, source_target_pairs={{0,4},{1,5},{2,6},{3,7},{4,0},{5,1},{6,2},{7,3},{8,12},{9,13},{10,... | collective-permute-start | bytes 1032200 | tf_op jit(solution)/shard_map/ppermute | solution.py:44
  153.1 16.7 %collective-permute-start.32 = (bf16[4,112,384]{2,1,0:T(8,128)(2,1)S(1)}, bf16[4,112,384]{2,1,0:T(8,128)(2,1)S(1)}, u32[]{:S(2)}, u32[]{:S(2)}) collective-permute-start(bf16[4,112,384]{2,1,0:T(8,128)(2,1)S(1)} %get-tuple-element.219), channel_id=1, source_target_pairs={{0,6},{1,7},{2,4},{3,5},{4,2},{5,3},{6,0},{7,1},{8,14},{9,15},{10,... | collective-permute-start | bytes 1032200 | tf_op jit(solution)/shard_map/ppermute | solution.py:44
  154.3 10.1 %collective-permute-start.33 = (bf16[2,64,640]{2,1,0:T(8,128)(2,1)S(1)}, bf16[2,64,640]{2,1,0:T(8,128)(2,1)S(1)}, u32[]{:S(2)}, u32[]{:S(2)}) collective-permute-start(bf16[2,64,640]{2,1,0:T(8,128)(2,1)S(1)} %get-tuple-element.229), channel_id=1, source_target_pairs={{0,16},{1,17},{2,18},{3,19},{4,20},{5,21},{6,22},{7,23},{8,24},{9,... | collective-permute-start | bytes 491528 | tf_op jit(solution)/shard_map/ppermute | solution.py:44
  175.3 9.8 %collective-permute-start.41 = (bf16[128,384]{1,0:T(8,128)(2,1)S(1)}, bf16[128,384]{1,0:T(8,128)(2,1)S(1)}, u32[]{:S(2)}, u32[]{:S(2)}) collective-permute-start(bf16[128,384]{1,0:T(8,128)(2,1)S(1)} %get-tuple-element.257), channel_id=1, source_target_pairs={{0,16},{1,17},{2,18},{3,19},{4,20},{5,21},{6,22},{7,23},{8,24},{9,... | collective-permute-start | bytes 294920 | tf_op jit(solution)/shard_map/ppermute | solution.py:44
  (48 other events, 336.1 us)

commit v7 on v6

--- a/solution.py
+++ b/solution.py
@@ -1286,12 +1286,12 @@
             total = ins[0][pl.ds(spot, slab), :].astype(f32)
             for ref in ins[1:]:
                 total = total + ref[pl.ds(spot, slab), :].astype(f32)
-            outs[k // 2][k % 2] = total.astype(bf16)
+            outs[k % 2][k // 2] = total.astype(bf16)
 
     near, far = simple(
         body, [shape_of((2, slab, width), bf16)] * 2, *parts, scalars=places, name="sum_rest"
     )
-    got = swap(far, ep=2)
+    got = swap(far, ep=1)
 
     def added(a_ref, b_ref, own_ref, sent_ref):
         own_ref[...] = (a_ref[0].astype(f32) + b_ref[0].astype(f32)).astype(bf16)
@@ -1299,7 +1299,7 @@
 
     got = tie(got, later)
     own, sent = simple(added, [shape_of((slab, width), bf16)] * 2, near, got, name="add_rest")
-    return [own, swap(sent, ep=1)]
+    return [own, swap(sent, ep=2)]
 
 
 def sum_main(mains, smalls, places, slab, strip):
@@ -1589,7 +1589,7 @@
     small_got = swap(small_sent, core=1)
     small_parts = pack_small((i0, i1, i2, i3), small_mine, small_got, places, n_ep, strip)
     small_tops = plane_list(small_parts)
-    rest_pieces = sum_rest(tie(rest_tops, main_parts), grad_small, places, n_ep, slab)
+    rest_pieces = sum_rest(tie(rest_tops, main_parts), small_parts, places, n_ep, slab)
     output_final = place_tiles(rest_tops, chip, n_ep * slab, rows, width, "place_output")
     main_tops, output_final, rest_pieces = lax.optimization_barrier(
         (main_tops, output_final, rest_pieces)

time: 204 us -> 204 us (level)
  transfers between devices with their start and end apart: 50 -> 50, of which waited for: 24 -> 23; matrix products, arithmetic and copies ran while one was open for 1% -> 1% of each run, Pallas kernels for 32% -> 32%
where the time goes in v7:
time: 204 us
  Pallas kernels  98.9 us (48%)
  waiting for transfers between devices  51.6 us (25%)
  starting transfers between devices  49 us (24%)
  between operations  2.06 us (1%)
    ppermute x50, waiting for transfers between devices, swap(): return lax.ppermute(value, AXES, pairs)  51.6 us
    ppermute x50, starting transfers between devices, swap(): return lax.ppermute(value, AXES, pairs)  49 us
    pallas_call x1, Pallas kernels, attend_back(): pl.pallas_call(attend_back_body, grid=(2, 2), in_specs=[pl.BlockSpec((1,...  25.2 us
    pallas_call x1, Pallas kernels, middle(): pl.pallas_call(middle_body, grid_spec=pltpu.PrefetchScalarGridSpec(num_sc...  18.5 us
    pallas_call x2, Pallas kernels, attend(): pl.pallas_call(attend_body, grid=(2,), in_specs=[pl.BlockSpec((1, SLOTS,...  17.5 us
    pallas_call x17, Pallas kernels, simple(): pl.pallas_call(body, in_specs=specs, out_specs=[whole()] * len(out_shape)...  13.6 us
    pallas_call x1, Pallas kernels, weight_grads(): pl.pallas_call(functools.partial(weight_body, n_ep, strip), grid=(4,), in...  11 us
    pallas_call x1, Pallas kernels, project(): pl.pallas_call(project_body, grid=(4,), in_specs=[pl.BlockSpec(memory_spa...  8.34 us
  transfers between devices with their start and end apart: 50, of which 23 were waited for; matrix products, arithmetic and copies ran while one was open for 1% of the time, Pallas kernels for 32%

profile of v7, /device:TPU:0, one launch (start us, length us, event | category | flops | bytes accessed | tf_op | source)
XLA Modules:
  0.0 203.7 jit_solution(5718377589427292393)
XLA Ops:
  0.7 1.8 pack_parts.1
  2.4 3.0 %collective-permute-start = (bf16[112,384]{1,0:T(8,128)(2,1)S(1)}, bf16[112,384]{1,0:T(8,128)(2,1)S(1)}, u32[]{:S(2)}, u32[]{:S(2)}) collective-permute-start(bf16[112,384]{1,0:T(8,128)(2,1)S(1)} %get-tuple-element.155.refs_0_), channel_id=1, source_target_pairs={{0,8},{1,9},{2,10},{3,11},{4,12},{5,13},{6,14},{7,15},{8,0},{9,1},... | collective-permute-start | bytes 258056 | tf_op jit(solution)/shard_map/ppermute | solution.py:44
  5.5 2.6 %collective-permute-start.1 = (bf16[112,384]{1,0:T(8,128)(2,1)S(1)}, bf16[112,384]{1,0:T(8,128)(2,1)S(1)}, u32[]{:S(2)}, u32[]{:S(2)}) collective-permute-start(bf16[112,384]{1,0:T(8,128)(2,1)S(1)} %get-tuple-element.155.refs_0_), channel_id=1, source_target_pairs={{0,16},{1,17},{2,18},{3,19},{4,20},{5,21},{6,22},{7,23},{8,24},{9,... | collective-permute-start | bytes 258056 | tf_op jit(solution)/shard_map/ppermute | solution.py:44
  8.4 6.6 %collective-permute-done.1.refs_2_ = bf16[112,384]{1,0:T(8,128)(2,1)S(1)} collective-permute-done((bf16[112,384]{1,0:T(8,128)(2,1)S(1)}, bf16[112,384]{1,0:T(8,128)(2,1)S(1)}, u32[]{:S(2)}, u32[]{:S(2)}) %collective-permute-start.1) | collective-permute-done | bytes 86048 | tf_op jit(solution)/shard_map/ppermute | solution.py:44
  19.2 7.9 %collective-permute-done.3.t1 = bf16[528,384]{1,0:T(8,128)(2,1)S(1)} collective-permute-done((bf16[528,384]{1,0:T(8,128)(2,1)S(1)}, bf16[528,384]{1,0:T(8,128)(2,1)S(1)}, u32[]{:S(2)}, u32[]{:S(2)}) %collective-permute-start.3) | collective-permute-done | bytes 405536 | tf_op jit(solution)/shard_map/ppermute | solution.py:44
  27.1 2.4 %collective-permute-done.4.t2 = bf16[528,384]{1,0:T(8,128)(2,1)S(1)} collective-permute-done((bf16[528,384]{1,0:T(8,128)(2,1)S(1)}, bf16[528,384]{1,0:T(8,128)(2,1)S(1)}, u32[]{:S(2)}, u32[]{:S(2)}) %collective-permute-start.4) | collective-permute-done | bytes 405536 | tf_op jit(solution)/shard_map/ppermute | solution.py:44
  29.6 5.1 %collective-permute-done.5.t3 = bf16[528,384]{1,0:T(8,128)(2,1)S(1)} collective-permute-done((bf16[528,384]{1,0:T(8,128)(2,1)S(1)}, bf16[528,384]{1,0:T(8,128)(2,1)S(1)}, u32[]{:S(2)}, u32[]{:S(2)}) %collective-permute-start.5) | collective-permute-done | bytes 405536 | tf_op jit(solution)/shard_map/ppermute | solution.py:44
  36.1 2.5 %collective-permute-start.10 = (bf16[64,640]{1,0:T(8,128)(2,1)}, bf16[64,640]{1,0:T(8,128)(2,1)S(1)}, u32[]{:S(2)}, u32[]{:S(2)}) collective-permute-start(bf16[64,640]{1,0:T(8,128)(2,1)} %get-tuple-element.171.refs_0_), channel_id=1, source_target_pairs={{0,8},{1,9},{2,10},{3,11},{4,12},{5,13},{6,14},{7,15},{8,0},{9,1},... | collective-permute-start | bytes 245768 | tf_op jit(solution)/shard_map/ppermute | solution.py:44
  41.0 1.7 unpack_main.1
  46.4 2.0 collective-permute-done.11.refs_2_
  49.4 8.3 %project.1 = (bf16[2048,512]{1,0:T(8,128)(2,1)}, bf16[2,2048,128]{2,1,0:T(8,128)(2,1)}, bf16[2,2048,128]{2,1,0:T(8,128)(2,1)}, bf16[2,128,2048]{2,1,0:T(8,128)(2...) custom-call(f32[1]{0:T(128)} %bitcast.ratio, s32[8]{0:T(128)S(1)} %fusion.6.sc, ...), custom_call_target="tpu_custom_call" | custom-call | flops 2700000000 | bytes 9000000 | tf_op jit(solution)/shard_map/project/pallas_call | solution.py:166
  61.4 8.8 %attend.2 = (bf16[1024,256]{1,0:T(8,128)(2,1)}, bf16[2,1024,128]{2,1,0:T(8,128)(2,1)}) custom-call(bf16[2,2048,128]{2,1,0:T(8,128)(2,1)} %get-tuple-element.200.q_ref, bf16[2,2048,128]{2,1,0:T(8,128)(2,1)} %get-tuple-element.175.k_ref, bf16[2,2048,128]{2,1,0:T(8,128)(2,1)} %get-tuple-element.176.x_ref, bf16[2,128,2048]{2,1,0:T(8,128)(2,1)} %get-tuple-element.177.vt_ref), custom_call_target="tpu_custom_call" | custom-call | flops 1800000000 | bytes 6000000 | tf_op jit(solution)/shard_map/attend/pallas_call | solution.py:262
  70.7 8.8 %attend.3 = (bf16[1024,256]{1,0:T(8,128)(2,1)}, bf16[2,1024,128]{2,1,0:T(8,128)(2,1)}) custom-call(bf16[2,2048,128]{2,1,0:T(8,128)(2,1)} %get-tuple-element.200.q_ref, bf16[2,2048,128]{2,1,0:T(8,128)(2,1)} %get-tuple-element.175.k_ref, bf16[2,2048,128]{2,1,0:T(8,128)(2,1)} %get-tuple-element.176.x_ref, bf16[2,128,2048]{2,1,0:T(8,128)(2,1)} %get-tuple-element.177.vt_ref), custom_call_target="tpu_custom_call" | custom-call | flops 1800000000 | bytes 6000000 | tf_op jit(solution)/shard_map/attend/pallas_call | solution.py:262
  82.9 18.5 %middle.1 = (bf16[256,512]{1,0:T(8,128)(2,1)S(1)}, bf16[256,512]{1,0:T(8,128)(2,1)S(1)}, bf16[256,512]{1,0:T(8,128)(2,1)S(1)}, bf16[256,512]{1,0:T(8,128)(2,1)S(...) custom-call(s32[8]{0:T(128)S(1)} %fusion.6.sc, ...), custom_call_target="tpu_custom_call" | custom-call | flops 7500000256 | bytes 25000000 | tf_op jit(solution)/shard_map/middle/pallas_call | solution.py:556
  101.6 2.9 %collective-permute-done.24 = bf16[2,512,640]{2,1,0:T(8,128)(2,1)S(1)} collective-permute-done((bf16[2,512,640]{2,1,0:T(8,128)(2,1)S(1)}, bf16[2,512,640]{2,1,0:T(8,128)(2,1)S(1)}, u32[]{:S(2)}, u32[]{:S(2)}) %collective-permute-start.24) | collective-permute-done | bytes 1310752 | tf_op jit(solution)/shard_map/ppermute | solution.py:44
  109.2 25.2 %attend_back.1 = (bf16[2048,256]{1,0:T(8,128)(2,1)}, f32[2,128,2048]{2,1,0:T(8,128)}, f32[2,128,2048]{2,1,0:T(8,128)}) custom-call(bf16[2,2048,128]{2,1,0:T(8,128)(2,1)} %get-tuple-element.200.q_ref, bf16[2,2048,128]{2,1,0:T(8,128)(2,1)} %get-tuple-element.175.k_ref, bf16[2,2048,128]{2,1,0:T(8,128)(2,1)} %get-tuple-element.176.x_ref, ...), custom_call_target="tpu_custom_call" | custom-call | flops 6000000000 | bytes 20000000 | tf_op jit(solution)/shard_map/attend_back/pallas_call | solution.py:341
  135.3 11.0 %weight_grads.1 = (bf16[2,512,384]{2,1,0:T(8,128)(2,1)}, bf16[4,2,2,48,384]{4,3,2,1,0:T(8,128)(2,1)}, bf16[4,2,2,48,384]{4,3,2,1,0:T(8,128)(2,1)S(1)}, f32[1024,512]{1,0:T(8,128)}, bf16[1024,512]{1,0:T(8,128)(2,1)}) custom-call(s32[8]{0:T(128)S(1)} %fusion.6.sc, bf16[2048,512]{1,0:T(8,128)(2,1)} %get-tuple-element.168.x_ref, ...), custom_call_target="tpu_custom_call" | custom-call | flops 2700000000 | bytes 9000000 | tf_op jit(solution)/shard_map/weight_grads/pallas_call | solution.py:1034
  146.2 2.0 collective-permute-done.29.b_ref
  156.0 4.6 %input_grads.1 = (bf16[112,256]{1,0:T(8,128)(2,1)S(1)}, bf16[112,256]{1,0:T(8,128)(2,1)S(1)}, bf16[112,256]{1,0:T(8,128)(2,1)S(1)}, bf16[112,256]{1,0:T(8,128)(2,1)S(1)}, bf16[512,128]{1,0:T(8,128)(2,1)S(1)}) custom-call(s32[8]{0:T(128)S(1)} %fusion.6.sc, f32[1]{0:T(128)} %bitcast.ratio, f32[1024,512]{1,0:T(8,128)} %get-tuple-element.230.dr_ref, ...), custom_call_target="tpu_custom_call" | custom-call | flops 1800000000 | bytes 6000000 | tf_op jit(solution)/shard_map/input_grads/pallas_call | solution.py:1124
  169.9 3.1 %collective-permute-done.36.refs_5_ = bf16[64,640]{1,0:T(8,128)(2,1)S(1)} collective-permute-done((bf16[64,640]{1,0:T(8,128)(2,1)S(1)}, bf16[64,640]{1,0:T(8,128)(2,1)S(1)}, u32[]{:S(2)}, u32[]{:S(2)}) %collective-permute-start.36) | collective-permute-done | bytes 81952 | tf_op jit(solution)/shard_map/ppermute | solution.py:44
  179.3 5.8 %collective-permute-done.41.refs_2_ = bf16[128,384]{1,0:T(8,128)(2,1)S(1)} collective-permute-done((bf16[128,384]{1,0:T(8,128)(2,1)S(1)}, bf16[128,384]{1,0:T(8,128)(2,1)S(1)}, u32[]{:S(2)}, u32[]{:S(2)}) %collective-permute-start.41) | collective-permute-done | bytes 98336 | tf_op jit(solution)/shard_map/ppermute | solution.py:44
  191.6 2.4 %collective-permute-done.46 = f32[8,128]{1,0:T(8,128)S(1)} collective-permute-done((f32[8,128]{1,0:T(8,128)S(1)}, f32[8,128]{1,0:T(8,128)S(1)}, u32[]{:S(2)}, u32[]{:S(2)}) %collective-permute-start.46) | collective-permute-done | bytes 4128 | tf_op jit(solution)/shard_map/ppermute | solution.py:44
  196.5 1.9 collective-permute-start.49
  200.2 1.8 collective-permute-done.49.refs_3_
  (156 shorter events, 60.9 us)
Async XLA Ops:
  15.7 11.5 %collective-permute-start.3 = (bf16[528,384]{1,0:T(8,128)(2,1)S(1)}, bf16[528,384]{1,0:T(8,128)(2,1)S(1)}, u32[]{:S(2)}, u32[]{:S(2)}) collective-permute-start(bf16[528,384]{1,0:T(8,128)(2,1)S(1)} %get-tuple-element.158), channel_id=1, source_target_pairs={{0,2},{1,3},{2,0},{3,1},{4,6},{5,7},{6,4},{7,5},{8,10},{9,11},{10,... | collective-permute-start | bytes 1216520 | tf_op jit(solution)/shard_map/ppermute | solution.py:44
  17.3 12.3 %collective-permute-start.4 = (bf16[528,384]{1,0:T(8,128)(2,1)S(1)}, bf16[528,384]{1,0:T(8,128)(2,1)S(1)}, u32[]{:S(2)}, u32[]{:S(2)}) collective-permute-start(bf16[528,384]{1,0:T(8,128)(2,1)S(1)} %get-tuple-element.159), channel_id=1, source_target_pairs={{0,4},{1,5},{2,6},{3,7},{4,0},{5,1},{6,2},{7,3},{8,12},{9,13},{10,... | collective-permute-start | bytes 1216520 | tf_op jit(solution)/shard_map/ppermute | solution.py:44
  18.7 15.9 %collective-permute-start.5 = (bf16[528,384]{1,0:T(8,128)(2,1)S(1)}, bf16[528,384]{1,0:T(8,128)(2,1)S(1)}, u32[]{:S(2)}, u32[]{:S(2)}) collective-permute-start(bf16[528,384]{1,0:T(8,128)(2,1)S(1)} %get-tuple-element.160), channel_id=1, source_target_pairs={{0,6},{1,7},{2,4},{3,5},{4,2},{5,3},{6,0},{7,1},{8,14},{9,15},{10,... | collective-permute-start | bytes 1216520 | tf_op jit(solution)/shard_map/ppermute | solution.py:44
  19.2 16.8 %collective-permute-start.6 = (bf16[528,384]{1,0:T(8,128)(2,1)S(1)}, bf16[528,384]{1,0:T(8,128)(2,1)S(1)}, u32[]{:S(2)}, u32[]{:S(2)}) collective-permute-start(bf16[528,384]{1,0:T(8,128)(2,1)S(1)} %get-tuple-element.157.t0), channel_id=1, source_target_pairs={{0,1},{1,0},{2,3},{3,2},{4,5},{5,4},{6,7},{7,6},{8,9},{9,8},{10,11... | collective-permute-start | bytes 1216520 | tf_op jit(solution)/shard_map/ppermute | solution.py:44
  27.1 12.4 %collective-permute-start.7 = (bf16[528,384]{1,0:T(8,128)(2,1)S(1)}, bf16[528,384]{1,0:T(8,128)(2,1)S(1)}, u32[]{:S(2)}, u32[]{:S(2)}) collective-permute-start(bf16[528,384]{1,0:T(8,128)(2,1)S(1)} %collective-permute-done.3.t1), channel_id=1, source_target_pairs={{0,1},{1,0},{2,3},{3,2},{4,5},{5,4},{6,7},{7,6},{8,9},{9,8},{10,11... | collective-permute-start | bytes 1216520 | tf_op jit(solution)/shard_map/ppermute | solution.py:44
  29.6 11.5 %collective-permute-start.8 = (bf16[528,384]{1,0:T(8,128)(2,1)S(1)}, bf16[528,384]{1,0:T(8,128)(2,1)S(1)}, u32[]{:S(2)}, u32[]{:S(2)}) collective-permute-start(bf16[528,384]{1,0:T(8,128)(2,1)S(1)} %collective-permute-done.4.t2), channel_id=1, source_target_pairs={{0,1},{1,0},{2,3},{3,2},{4,5},{5,4},{6,7},{7,6},{8,9},{9,8},{10,11... | collective-permute-start | bytes 1216520 | tf_op jit(solution)/shard_map/ppermute | solution.py:44
  36.1 9.9 %collective-permute-start.10 = (bf16[64,640]{1,0:T(8,128)(2,1)}, bf16[64,640]{1,0:T(8,128)(2,1)S(1)}, u32[]{:S(2)}, u32[]{:S(2)}) collective-permute-start(bf16[64,640]{1,0:T(8,128)(2,1)} %get-tuple-element.171.refs_0_), channel_id=1, source_target_pairs={{0,8},{1,9},{2,10},{3,11},{4,12},{5,13},{6,14},{7,15},{8,0},{9,1},... | collective-permute-start | bytes 245768 | tf_op jit(solution)/shard_map/ppermute | solution.py:44
  38.6 9.8 %collective-permute-start.11 = (bf16[64,640]{1,0:T(8,128)(2,1)}, bf16[64,640]{1,0:T(8,128)(2,1)S(1)}, u32[]{:S(2)}, u32[]{:S(2)}) collective-permute-start(bf16[64,640]{1,0:T(8,128)(2,1)} %get-tuple-element.171.refs_0_), channel_id=1, source_target_pairs={{0,16},{1,17},{2,18},{3,19},{4,20},{5,21},{6,22},{7,23},{8,24},{9,... | collective-permute-start | bytes 245768 | tf_op jit(solution)/shard_map/ppermute | solution.py:44
  42.9 14.8 %collective-permute-start.13 = (bf16[256,512]{1,0:T(8,128)(2,1)S(1)}, bf16[256,512]{1,0:T(8,128)(2,1)S(1)}, u32[]{:S(2)}, u32[]{:S(2)}) collective-permute-start(bf16[256,512]{1,0:T(8,128)(2,1)S(1)} %get-tuple-element.312), channel_id=1, source_target_pairs={{0,2},{1,3},{2,0},{3,1},{4,6},{5,7},{6,4},{7,5},{8,10},{9,11},{10,... | collective-permute-start | bytes 786440 | tf_op jit(solution)/shard_map/ppermute | solution.py:44
  44.5 13.3 %collective-permute-start.14 = (bf16[256,512]{1,0:T(8,128)(2,1)S(1)}, bf16[256,512]{1,0:T(8,128)(2,1)S(1)}, u32[]{:S(2)}, u32[]{:S(2)}) collective-permute-start(bf16[256,512]{1,0:T(8,128)(2,1)S(1)} %get-tuple-element.311), channel_id=1, source_target_pairs={{0,4},{1,5},{2,6},{3,7},{4,0},{5,1},{6,2},{7,3},{8,12},{9,13},{10,... | collective-permute-start | bytes 786440 | tf_op jit(solution)/shard_map/ppermute | solution.py:44
  46.0 11.9 %collective-permute-start.15 = (bf16[256,512]{1,0:T(8,128)(2,1)S(1)}, bf16[256,512]{1,0:T(8,128)(2,1)S(1)}, u32[]{:S(2)}, u32[]{:S(2)}) collective-permute-start(bf16[256,512]{1,0:T(8,128)(2,1)S(1)} %get-tuple-element.310), channel_id=1, source_target_pairs={{0,6},{1,7},{2,4},{3,5},{4,2},{5,3},{6,0},{7,1},{8,14},{9,15},{10,... | collective-permute-start | bytes 786440 | tf_op jit(solution)/shard_map/ppermute | solution.py:44
  57.9 12.8 %collective-permute-start.16 = (bf16[4,64,640]{2,1,0:T(8,128)(2,1)S(1)}, bf16[4,64,640]{2,1,0:T(8,128)(2,1)S(1)}, u32[]{:S(2)}, u32[]{:S(2)}) collective-permute-start(bf16[4,64,640]{2,1,0:T(8,128)(2,1)S(1)} %stack_rest.1.refs_0_), channel_id=1, source_target_pairs={{0,2},{1,3},{2,0},{3,1},{4,6},{5,7},{6,4},{7,5},{8,10},{9,11},{10,... | collective-permute-start | bytes 983048 | tf_op jit(solution)/shard_map/ppermute | solution.py:44
  59.4 20.0 %collective-permute-start.18 = (bf16[4,64,640]{2,1,0:T(8,128)(2,1)S(1)}, bf16[4,64,640]{2,1,0:T(8,128)(2,1)S(1)}, u32[]{:S(2)}, u32[]{:S(2)}) collective-permute-start(bf16[4,64,640]{2,1,0:T(8,128)(2,1)S(1)} %stack_rest.1.refs_0_), channel_id=1, source_target_pairs={{0,4},{1,5},{2,6},{3,7},{4,0},{5,1},{6,2},{7,3},{8,12},{9,13},{10,... | collective-permute-start | bytes 983048 | tf_op jit(solution)/shard_map/ppermute | solution.py:44
  60.9 18.5 %collective-permute-start.19 = (bf16[4,64,640]{2,1,0:T(8,128)(2,1)S(1)}, bf16[4,64,640]{2,1,0:T(8,128)(2,1)S(1)}, u32[]{:S(2)}, u32[]{:S(2)}) collective-permute-start(bf16[4,64,640]{2,1,0:T(8,128)(2,1)S(1)} %stack_rest.1.refs_0_), channel_id=1, source_target_pairs={{0,6},{1,7},{2,4},{3,5},{4,2},{5,3},{6,0},{7,1},{8,14},{9,15},{10,... | collective-permute-start | bytes 983048 | tf_op jit(solution)/shard_map/ppermute | solution.py:44
  61.4 18.7 %collective-permute-start.20 = (bf16[4,64,640]{2,1,0:T(8,128)(2,1)S(1)}, bf16[4,64,640]{2,1,0:T(8,128)(2,1)S(1)}, u32[]{:S(2)}, u32[]{:S(2)}) collective-permute-start(bf16[4,64,640]{2,1,0:T(8,128)(2,1)S(1)} %stack_rest.1.refs_0_), channel_id=1, source_target_pairs={{0,1},{1,0},{2,3},{3,2},{4,5},{5,4},{6,7},{7,6},{8,9},{9,8},{10,11... | collective-permute-start | bytes 983048 | tf_op jit(solution)/shard_map/ppermute | solution.py:44
  70.2 12.7 %collective-permute-start.17 = (bf16[1024,256]{1,0:T(8,128)(2,1)}, bf16[1024,256]{1,0:T(8,128)(2,1)S(1)}, u32[]{:S(2)}, u32[]{:S(2)}) collective-permute-start(bf16[1024,256]{1,0:T(8,128)(2,1)} %get-tuple-element.178), channel_id=1, source_target_pairs={{0,1},{1,0},{2,3},{3,2},{4,5},{5,4},{6,7},{7,6},{8,9},{9,8},{10,11... | collective-permute-start | bytes 1572872 | tf_op jit(solution)/shard_map/ppermute | solution.py:44
  105.6 28.8 %collective-permute-start.25 = (bf16[464,640]{1,0:T(8,128)(2,1)S(1)}, bf16[464,640]{1,0:T(8,128)(2,1)S(1)}, u32[]{:S(2)}, u32[]{:S(2)}) collective-permute-start(bf16[464,640]{1,0:T(8,128)(2,1)S(1)} %get-tuple-element.197), channel_id=1, source_target_pairs={{0,2},{1,3},{2,0},{3,1},{4,6},{5,7},{6,4},{7,5},{8,10},{9,11},{10,... | collective-permute-start | bytes 1781768 | tf_op jit(solution)/shard_map/ppermute | solution.py:44
  107.2 27.2 %collective-permute-start.26 = (bf16[464,640]{1,0:T(8,128)(2,1)S(1)}, bf16[464,640]{1,0:T(8,128)(2,1)S(1)}, u32[]{:S(2)}, u32[]{:S(2)}) collective-permute-start(bf16[464,640]{1,0:T(8,128)(2,1)S(1)} %get-tuple-element.198), channel_id=1, source_target_pairs={{0,4},{1,5},{2,6},{3,7},{4,0},{5,1},{6,2},{7,3},{8,12},{9,13},{10,... | collective-permute-start | bytes 1781768 | tf_op jit(solution)/shard_map/ppermute | solution.py:44
  108.7 26.6 %collective-permute-start.27 = (bf16[464,640]{1,0:T(8,128)(2,1)S(1)}, bf16[464,640]{1,0:T(8,128)(2,1)S(1)}, u32[]{:S(2)}, u32[]{:S(2)}) collective-permute-start(bf16[464,640]{1,0:T(8,128)(2,1)S(1)} %get-tuple-element.199), channel_id=1, source_target_pairs={{0,6},{1,7},{2,4},{3,5},{4,2},{5,3},{6,0},{7,1},{8,14},{9,15},{10,... | collective-permute-start | bytes 1781768 | tf_op jit(solution)/shard_map/ppermute | solution.py:44
  150.0 16.1 %collective-permute-start.30 = (bf16[4,112,384]{2,1,0:T(8,128)(2,1)S(1)}, bf16[4,112,384]{2,1,0:T(8,128)(2,1)S(1)}, u32[]{:S(2)}, u32[]{:S(2)}) collective-permute-start(bf16[4,112,384]{2,1,0:T(8,128)(2,1)S(1)} %get-tuple-element.217), channel_id=1, source_target_pairs={{0,2},{1,3},{2,0},{3,1},{4,6},{5,7},{6,4},{7,5},{8,10},{9,11},{10,... | collective-permute-start | bytes 1032200 | tf_op jit(solution)/shard_map/ppermute | solution.py:44
  151.6 15.1 %collective-permute-start.31 = (bf16[4,112,384]{2,1,0:T(8,128)(2,1)S(1)}, bf16[4,112,384]{2,1,0:T(8,128)(2,1)S(1)}, u32[]{:S(2)}, u32[]{:S(2)}) collective-permute-start(bf16[4,112,384]{2,1,0:T(8,128)(2,1)S(1)} %get-tuple-element.218), channel_id=1, source_target_pairs={{0,4},{1,5},{2,6},{3,7},{4,0},{5,1},{6,2},{7,3},{8,12},{9,13},{10,... | collective-permute-start | bytes 1032200 | tf_op jit(solution)/shard_map/ppermute | solution.py:44
  153.1 16.8 %collective-permute-start.32 = (bf16[4,112,384]{2,1,0:T(8,128)(2,1)S(1)}, bf16[4,112,384]{2,1,0:T(8,128)(2,1)S(1)}, u32[]{:S(2)}, u32[]{:S(2)}) collective-permute-start(bf16[4,112,384]{2,1,0:T(8,128)(2,1)S(1)} %get-tuple-element.219), channel_id=1, source_target_pairs={{0,6},{1,7},{2,4},{3,5},{4,2},{5,3},{6,0},{7,1},{8,14},{9,15},{10,... | collective-permute-start | bytes 1032200 | tf_op jit(solution)/shard_map/ppermute | solution.py:44
  154.3 10.3 %collective-permute-start.33 = (bf16[2,64,640]{2,1,0:T(8,128)(2,1)S(1)}, bf16[2,64,640]{2,1,0:T(8,128)(2,1)S(1)}, u32[]{:S(2)}, u32[]{:S(2)}) collective-permute-start(bf16[2,64,640]{2,1,0:T(8,128)(2,1)S(1)} %get-tuple-element.229), channel_id=1, source_target_pairs={{0,8},{1,9},{2,10},{3,11},{4,12},{5,13},{6,14},{7,15},{8,0},{9,1},... | collective-permute-start | bytes 491528 | tf_op jit(solution)/shard_map/ppermute | solution.py:44
  163.1 9.9 %collective-permute-start.37 = (bf16[176,256]{1,0:T(8,128)(2,1)S(1)}, bf16[176,256]{1,0:T(8,128)(2,1)S(1)}, u32[]{:S(2)}, u32[]{:S(2)}) collective-permute-start(bf16[176,256]{1,0:T(8,128)(2,1)S(1)} %get-tuple-element.244), channel_id=1, source_target_pairs={{0,2},{1,3},{2,0},{3,1},{4,6},{5,7},{6,4},{7,5},{8,10},{9,11},{10,... | collective-permute-start | bytes 270344 | tf_op jit(solution)/shard_map/ppermute | solution.py:44
  (48 other events, 339.5 us)
